TPU v7x, 32 devices: a whole 2x2x4 slice. The times are simulated.
32 devices in a mesh: bucket: 2 (over core), frame: 8 (over z, y), seq: 2 (over x).
Axes of the slice: x: 2, y: 2, z: 4, core: 2. Of those that a mesh axis runs over, the one named last changes fastest.
Arguments:
- latent: bfloat16 [2, 16, 1024, 1152], P('bucket', 'frame', 'seq'), may hold values from -6 to 6
- condition: bfloat16 [2, 1152], P('bucket'), may hold values from -6 to 6
- text: bfloat16 [2, 128, 4096], P('bucket'), may hold values from -6 to 6
- text_len: int32 [2], P('bucket'), may hold values from 16 to 128, as said below
- clip_ids: int32 [2, 16], P('bucket'), may hold values from 0 to 8, as said below
- video_flag: int32 [2, 16], P('bucket'), may hold values from 0 to 1, as said below
- ada_weight: bfloat16 [1152, 10368], P(None, ('frame', 'seq')), may hold values from -0.1875 to 0.1875
- text_kv_weight: bfloat16 [4096, 2304], P(None, ('frame', 'seq')), may hold values from -0.09375 to 0.09375
- qkv_weight: bfloat16 [1152, 3456], P(('frame', 'seq')), may hold values from -0.1875 to 0.1875
- proj_weight: bfloat16 [1152, 1152], P(('frame', 'seq')), may hold values from -0.75 to 0.75
- cross_q_weight: bfloat16 [1152, 1152], P(('frame', 'seq')), may hold values from -0.125 to 0.125
- cross_proj_weight: bfloat16 [1152, 1152], P(('frame', 'seq')), may hold values from -0.5 to 0.5
- up_weight: bfloat16 [1152, 4608], P(('frame', 'seq')), may hold values from -0.1875 to 0.1875
- down_weight: bfloat16 [4608, 1152], P(('frame', 'seq')), may hold values from -0.09375 to 0.09375
- temporal_qkv_weight: bfloat16 [1152, 3456], P(('frame', 'seq')), may hold values from -0.1875 to 0.1875
- temporal_proj_weight: bfloat16 [1152, 1152], P(('frame', 'seq')), may hold values from -0.25 to 0.25
- cotangent: bfloat16 [2, 16, 1024, 1152], P('bucket', 'frame', 'seq'), may hold values from -6 to 6
Outputs:
- result: bfloat16 [2, 16, 1024, 1152], P('bucket', 'frame', 'seq')
- latent_grad: float32 [2, 16, 1024, 1152], P('bucket', 'frame', 'seq')
- ada_grad: float32 [1152, 10368], P(None, ('frame', 'seq'))
- text_kv_grad: float32 [4096, 2304], P(None, ('frame', 'seq'))
- qkv_grad: float32 [1152, 3456], P(('frame', 'seq'))
- proj_grad: float32 [1152, 1152], P(('frame', 'seq'))
- cross_q_grad: float32 [1152, 1152], P(('frame', 'seq'))
- cross_proj_grad: float32 [1152, 1152], P(('frame', 'seq'))
- up_grad: float32 [1152, 4608], P(('frame', 'seq'))
- down_grad: float32 [4608, 1152], P(('frame', 'seq'))
- temporal_qkv_grad: float32 [1152, 3456], P(('frame', 'seq'))
- temporal_proj_grad: float32 [1152, 1152], P(('frame', 'seq'))
Inputs may be any that keep to these rules, and one draw needn't show every extreme that they name: `clip_ids`: in each bucket, clip ids start at 0 and rise by one from clip to clip along the frames; a video is 8 consecutive frames sharing one id, an image is one frame with an id of its own; half of a bucket's frames belong to videos. `video_flag`: 1 exactly on the frames of videos (clips of 8 frames). `text_len`: some bucket uses all 128 caption tokens.
All inputs are finite; a program needn't handle non-finite values.
Results may differ from a plain program's by a relative error of at most 0.025.
Values may be sent and summed in bfloat16 or wider, within the bound.
No kernel may reach another device: no remote copies, remote signals or barrier semaphores. Data moves between devices by JAX's collectives and lax.ppermute only.
A program may use at most 512 MiB of HBM per device.

v0:
```python
import math

import jax
import jax.numpy as jnp
from jax import lax
from jax.sharding import PartitionSpec as P

HEADS = 16


epsilon = 1e-06
highest = lax.Precision.HIGHEST
masked_fill = -1e30


def extended(array, sides, width):
    for axis, dim in sides:
        devices, length = (lax.axis_size(axis), array.shape[dim])
        up = [(i, (i + 1) % devices) for i in range(devices - 1)]
        down = [(j, i) for i, j in up]
        last = lax.slice_in_dim(array, length - width, length, axis=dim)
        initial = lax.slice_in_dim(array, 0, width, axis=dim)
        before = lax.ppermute(last, axis, up)
        after = lax.ppermute(initial, axis, down)
        array = jnp.concatenate([before, array, after], axis=dim)
    return array


def product(left, right):
    return jnp.dot(left, right, preferred_element_type=jnp.float32)


def product_left(left, right):
    return lax.dot_general(
        left, right, (((0,), (0,)), ((), ())), preferred_element_type=jnp.float32
    )


def product_right(left, right):
    return lax.dot_general(
        left, right, (((1,), (1,)), ((), ())), preferred_element_type=jnp.float32
    )


def normalize(values):
    centred = values - jnp.mean(values, axis=-1, keepdims=True)
    reciprocal = lax.rsqrt(jnp.mean(centred * centred, axis=-1, keepdims=True) + epsilon)
    return (centred * reciprocal, reciprocal)


def normalize_back(upstream, normed, reciprocal):
    return reciprocal * (
        upstream
        - jnp.mean(upstream, axis=-1, keepdims=True)
        - normed * jnp.mean(upstream * normed, axis=-1, keepdims=True)
    )


def block_width():
    return 256


def gelu_tanh(values):
    return jax.nn.gelu(values, approximate=True)


def spatial_forward(query_heads, key_rows, value_rows):
    frame_count, row_count, head_count, head_size = query_heads.shape
    score_scale = 1.0 / math.sqrt(head_size)
    initial = (
        jnp.full((frame_count, row_count, head_count), masked_fill, jnp.float32),
        jnp.zeros((frame_count, row_count, head_count), jnp.float32),
        jnp.zeros((frame_count, row_count, head_count, head_size), jnp.float32),
        jnp.zeros((frame_count, row_count, head_count, head_size), jnp.float32),
    )

    def absorb(carried, pieces, anchor):
        key_piece, value_piece = pieces
        piece_rows = key_piece.shape[1]
        block_rows = block_width()
        running, normaliser, accumulated, exact_sum = carried
        for offset in range(0, piece_rows, block_rows):
            key_block = key_piece[:, offset : offset + block_rows].reshape(
                frame_count, block_rows, head_count, head_size
            )
            value_block = value_piece[:, offset : offset + block_rows].reshape(
                frame_count, block_rows, head_count, head_size
            )
            scores = (
                jnp.einsum(
                    "fqhe,fkhe->fqhk", query_heads, key_block, preferred_element_type=jnp.float32
                )
                * score_scale
            )
            highest_now = jnp.maximum(running, jnp.max(scores, axis=-1))
            factor = jnp.exp(running - highest_now)
            weights = jnp.exp(scores - highest_now[..., None])
            normaliser = normaliser * factor + jnp.sum(weights, axis=-1)
            accumulated = accumulated * factor[..., None] + jnp.einsum(
                "fqhk,fkhe->fqhe",
                weights.astype(jnp.bfloat16),
                value_block,
                preferred_element_type=jnp.float32,
            )
            exact_sum = exact_sum * factor[..., None] + jnp.einsum(
                "fqhk,fkhe->fqhe", weights, value_block.astype(jnp.float32), precision=highest
            )
            running = highest_now
        return (running, normaliser, accumulated, exact_sum)

    running, normaliser, accumulated, exact_sum = absorb(
        initial,
        (
            lax.all_gather(key_rows, "seq", axis=1, tiled=True),
            lax.all_gather(value_rows, "seq", axis=1, tiled=True),
        ),
        jnp.int32(0),
    )
    return (
        accumulated / normaliser[..., None],
        exact_sum / normaliser[..., None],
        running + jnp.log(normaliser),
    )


def spatial_backward(query_heads, key_rows, value_rows, log_total, grad_heads, delta_rows):
    frame_count, row_count, head_count, head_size = query_heads.shape
    score_scale = 1.0 / math.sqrt(head_size)
    model_width = key_rows.shape[2]
    full_rows = key_rows.shape[1] * lax.axis_size("seq")
    initial = (
        jnp.zeros(query_heads.shape, jnp.float32),
        jnp.zeros((frame_count, full_rows, model_width), jnp.float32),
        jnp.zeros((frame_count, full_rows, model_width), jnp.float32),
    )

    def absorb(carried, pieces, anchor):
        key_piece, value_piece = pieces
        piece_rows = key_piece.shape[1]
        block_rows = block_width()
        query_grad, key_grad, value_grad = carried
        for offset in range(0, piece_rows, block_rows):
            key_block = key_piece[:, offset : offset + block_rows].reshape(
                frame_count, block_rows, head_count, head_size
            )
            value_block = value_piece[:, offset : offset + block_rows].reshape(
                frame_count, block_rows, head_count, head_size
            )
            scores = (
                jnp.einsum(
                    "fqhe,fkhe->fqhk", query_heads, key_block, preferred_element_type=jnp.float32
                )
                * score_scale
            )
            prob_rows = jnp.exp(scores - log_total[..., None])
            value_part = jnp.einsum(
                "fqhk,fqhe->fkhe",
                prob_rows.astype(jnp.bfloat16),
                grad_heads,
                preferred_element_type=jnp.float32,
            )
            prob_grad = jnp.einsum(
                "fqhe,fkhe->fqhk", grad_heads, value_block, preferred_element_type=jnp.float32
            )
            score_grad = (prob_rows * (prob_grad - delta_rows[..., None])).astype(jnp.bfloat16)
            query_grad = (
                query_grad
                + jnp.einsum(
                    "fqhk,fkhe->fqhe", score_grad, key_block, preferred_element_type=jnp.float32
                )
                * score_scale
            )
            key_part = (
                jnp.einsum(
                    "fqhk,fqhe->fkhe", score_grad, query_heads, preferred_element_type=jnp.float32
                )
                * score_scale
            )
            row_start = anchor + offset
            key_grad = lax.dynamic_update_slice_in_dim(
                key_grad,
                lax.dynamic_slice_in_dim(key_grad, row_start, block_rows, 1)
                + key_part.reshape(frame_count, block_rows, model_width),
                row_start,
                1,
            )
            value_grad = lax.dynamic_update_slice_in_dim(
                value_grad,
                lax.dynamic_slice_in_dim(value_grad, row_start, block_rows, 1)
                + value_part.reshape(frame_count, block_rows, model_width),
                row_start,
                1,
            )
        return (query_grad, key_grad, value_grad)

    query_grad, key_grad, value_grad = absorb(
        initial,
        (
            lax.all_gather(key_rows, "seq", axis=1, tiled=True),
            lax.all_gather(value_rows, "seq", axis=1, tiled=True),
        ),
        jnp.int32(0),
    )
    key_grad, value_grad = (
        lax.psum_scatter(
            key_grad.astype(jnp.bfloat16), "seq", scatter_dimension=1, tiled=True
        ).astype(jnp.float32),
        lax.psum_scatter(
            value_grad.astype(jnp.bfloat16), "seq", scatter_dimension=1, tiled=True
        ).astype(jnp.float32),
    )
    return (query_grad, key_grad, value_grad)


def per_device(
    latent,
    condition,
    text,
    text_len,
    clip_ids,
    video_flag,
    ada_weight,
    text_kv_weight,
    qkv_weight,
    proj_weight,
    cross_q_weight,
    cross_proj_weight,
    up_weight,
    down_weight,
    temporal_qkv_weight,
    temporal_proj_weight,
    cotangent,
):
    frame_count, row_count, model_width = (latent.shape[1], latent.shape[2], latent.shape[3])
    head_count = HEADS
    head_size = model_width // head_count
    score_scale = 1.0 / math.sqrt(head_size)
    total_rows = frame_count * row_count
    silu_cond = jax.nn.silu(condition.astype(jnp.float32))
    mod_part = jnp.dot(silu_cond, ada_weight.astype(jnp.float32), precision=highest)
    text_part = product(text[0], text_kv_weight)
    mod_full, text_full = (
        lax.all_gather(mod_part, ("frame", "seq"), axis=1, tiled=True),
        lax.all_gather(text_part, ("frame", "seq"), axis=1, tiled=True),
    )
    modulation = mod_full.reshape(9, model_width)
    text_kv = text_full.astype(jnp.bfloat16)
    text_count = text_kv.shape[0]
    key_text = text_kv[:, :model_width].reshape(text_count, head_count, head_size)
    value_text = text_kv[:, model_width:].reshape(text_count, head_count, head_size)
    (
        qkv_full,
        proj_full,
        cross_q_full,
        cross_proj_full,
        up_full,
        down_full,
        tqkv_full,
        tproj_full,
    ) = (
        lax.all_gather(qkv_weight, ("frame", "seq"), axis=0, tiled=True),
        lax.all_gather(proj_weight, ("frame", "seq"), axis=0, tiled=True),
        lax.all_gather(cross_q_weight, ("frame", "seq"), axis=0, tiled=True),
        lax.all_gather(cross_proj_weight, ("frame", "seq"), axis=0, tiled=True),
        lax.all_gather(up_weight, ("frame", "seq"), axis=0, tiled=True),
        lax.all_gather(down_weight, ("frame", "seq"), axis=0, tiled=True),
        lax.all_gather(temporal_qkv_weight, ("frame", "seq"), axis=0, tiled=True),
        lax.all_gather(temporal_proj_weight, ("frame", "seq"), axis=0, tiled=True),
    )
    inputs = latent[0].reshape(total_rows, model_width).astype(jnp.float32)
    normed_a, recip_a = normalize(inputs)
    hidden_a = (normed_a * (1.0 + modulation[1]) + modulation[0]).astype(jnp.bfloat16)
    qkv_rows = product(hidden_a, qkv_full).astype(jnp.bfloat16)
    query_heads = qkv_rows[:, :model_width].reshape(frame_count, row_count, head_count, head_size)
    key_rows = qkv_rows[:, model_width : 2 * model_width].reshape(
        frame_count, row_count, model_width
    )
    value_rows = qkv_rows[:, 2 * model_width :].reshape(frame_count, row_count, model_width)
    attended, attended_exact, log_total = spatial_forward(query_heads, key_rows, value_rows)
    attended_low = attended.reshape(total_rows, model_width).astype(jnp.bfloat16)
    branch_a = product(attended_low, proj_full)
    after_a = inputs + modulation[2] * branch_a
    after_low = after_a.astype(jnp.bfloat16)
    cross_query = (
        product(after_low, cross_q_full)
        .astype(jnp.bfloat16)
        .reshape(total_rows, head_count, head_size)
    )
    live_keys = jnp.arange(text_count) < text_len[0]
    cross_scores = (
        jnp.einsum("rhe,khe->rhk", cross_query, key_text, preferred_element_type=jnp.float32)
        * score_scale
    )
    cross_probs = jax.nn.softmax(jnp.where(live_keys, cross_scores, masked_fill), axis=-1)
    cross_low = cross_probs.astype(jnp.bfloat16)
    cross_out = (
        jnp.einsum("rhk,khe->rhe", cross_low, value_text, preferred_element_type=jnp.float32)
        .reshape(total_rows, model_width)
        .astype(jnp.bfloat16)
    )
    after_c = after_a + product(cross_out, cross_proj_full)
    normed_m, recip_m = normalize(after_c)
    hidden_m = (normed_m * (1.0 + modulation[4]) + modulation[3]).astype(jnp.bfloat16)
    upward = product(hidden_m, up_full)
    activated = gelu_tanh(upward).astype(jnp.bfloat16)
    branch_m = product(activated, down_full)
    after_m = after_c + modulation[5] * branch_m
    normed_t, recip_t = normalize(after_m)
    hidden_t = (normed_t * (1.0 + modulation[7]) + modulation[6]).astype(jnp.bfloat16)
    temporal_rows = product(hidden_t, tqkv_full).astype(jnp.bfloat16)
    temporal_query = (
        temporal_rows[:, :model_width]
        .astype(jnp.float32)
        .reshape(frame_count, row_count, head_count, head_size)
    )
    key_value = temporal_rows[:, model_width:].reshape(frame_count, row_count, 2 * model_width)
    padded = extended(key_value, (("frame", 0),), 1)
    first_frame = lax.axis_index("frame") * frame_count
    clips_ext = jnp.concatenate(
        [jnp.full((1,), -1, jnp.int32), clip_ids[0], jnp.full((1,), -1, jnp.int32)]
    )
    clips_local = lax.dynamic_slice_in_dim(clips_ext, first_frame, frame_count + 2)
    prev_live = clips_local[:-2] == clips_local[1:-1]
    next_live = clips_local[2:] == clips_local[1:-1]
    flag_local = lax.dynamic_slice_in_dim(video_flag[0], first_frame, frame_count).astype(
        jnp.float32
    )
    neighbour_sets = (padded[:-2], padded[1:-1], padded[2:])
    key_sets = [
        member[..., :model_width]
        .astype(jnp.float32)
        .reshape(frame_count, row_count, head_count, head_size)
        for member in neighbour_sets
    ]
    value_sets = [
        member[..., model_width:]
        .astype(jnp.float32)
        .reshape(frame_count, row_count, head_count, head_size)
        for member in neighbour_sets
    ]
    score_prev = jnp.where(
        prev_live[:, None, None],
        jnp.sum(temporal_query * key_sets[0], axis=-1) * score_scale,
        masked_fill,
    )
    score_self = jnp.sum(temporal_query * key_sets[1], axis=-1) * score_scale
    score_next = jnp.where(
        next_live[:, None, None],
        jnp.sum(temporal_query * key_sets[2], axis=-1) * score_scale,
        masked_fill,
    )
    temporal_probs = jax.nn.softmax(
        jnp.stack([score_prev, score_self, score_next], axis=-1), axis=-1
    )
    mixed = (
        temporal_probs[..., 0:1] * value_sets[0]
        + temporal_probs[..., 1:2] * value_sets[1]
        + temporal_probs[..., 2:3] * value_sets[2]
    )
    mixed_low = mixed.reshape(total_rows, model_width).astype(jnp.bfloat16)
    branch_t = product(mixed_low, tproj_full)
    flag_rows = jnp.repeat(flag_local, row_count)[:, None]
    result_rows = after_m + flag_rows * modulation[8] * branch_t
    result = result_rows.astype(jnp.bfloat16).reshape(latent.shape)
    result_grad = cotangent[0].reshape(total_rows, model_width).astype(jnp.float32)
    gate_t_grad = jnp.sum(flag_rows * branch_t * result_grad, axis=0)
    branch_t_grad = (flag_rows * modulation[8] * result_grad).astype(jnp.bfloat16)
    temporal_proj_grad = product_left(mixed_low, branch_t_grad)
    mixed_grad = product_right(branch_t_grad, tproj_full).reshape(
        frame_count, row_count, head_count, head_size
    )
    prob_grads = jnp.stack(
        [
            jnp.sum(mixed_grad * value_sets[0], axis=-1),
            jnp.sum(mixed_grad * value_sets[1], axis=-1),
            jnp.sum(mixed_grad * value_sets[2], axis=-1),
        ],
        axis=-1,
    )
    score_grads = temporal_probs * (
        prob_grads - jnp.sum(temporal_probs * prob_grads, axis=-1, keepdims=True)
    )
    tquery_grad = (
        score_grads[..., 0:1] * key_sets[0]
        + score_grads[..., 1:2] * key_sets[1]
        + score_grads[..., 2:3] * key_sets[2]
    ) * score_scale
    pair_grads = [
        jnp.concatenate(
            [
                (score_grads[..., index : index + 1] * temporal_query * score_scale).reshape(
                    frame_count, row_count, model_width
                ),
                (temporal_probs[..., index : index + 1] * mixed_grad).reshape(
                    frame_count, row_count, model_width
                ),
            ],
            axis=-1,
        )
        for index in range(3)
    ]
    padded_grad = jnp.zeros((frame_count + 2, row_count, 2 * model_width), jnp.float32)
    padded_grad = (
        padded_grad.at[:-2].add(pair_grads[0]).at[1:-1].add(pair_grads[1]).at[2:].add(pair_grads[2])
    )
    outgoing = jnp.stack([padded_grad[0], padded_grad[-1]])
    incoming = extended(outgoing.astype(jnp.bfloat16), (("frame", 0),), 1).astype(outgoing.dtype)
    own_grad = padded_grad[1:-1].at[0].add(incoming[0]).at[-1].add(incoming[3])
    temporal_grad = jnp.concatenate(
        [
            tquery_grad.reshape(total_rows, model_width),
            own_grad.reshape(total_rows, 2 * model_width),
        ],
        axis=1,
    ).astype(jnp.bfloat16)
    temporal_qkv_grad = product_left(hidden_t, temporal_grad)
    hidden_t_grad = product_right(temporal_grad, tqkv_full)
    grad_m = result_grad + normalize_back(hidden_t_grad * (1.0 + modulation[7]), normed_t, recip_t)
    gate_m_grad = jnp.sum(branch_m * grad_m, axis=0)
    branch_m_grad = (modulation[5] * grad_m).astype(jnp.bfloat16)
    down_grad = product_left(activated, branch_m_grad)
    activated_grad = product_right(branch_m_grad, down_full)
    gelu_value, gelu_back = jax.vjp(gelu_tanh, upward)
    upward_grad = gelu_back(activated_grad)[0].astype(jnp.bfloat16)
    up_grad = product_left(hidden_m, upward_grad)
    hidden_m_grad = product_right(upward_grad, up_full)
    grad_c = grad_m + normalize_back(hidden_m_grad * (1.0 + modulation[4]), normed_m, recip_m)
    cross_branch_grad = grad_c.astype(jnp.bfloat16)
    cross_proj_grad = product_left(cross_out, cross_branch_grad)
    cross_out_grad = (
        product_right(cross_branch_grad, cross_proj_full)
        .astype(jnp.bfloat16)
        .reshape(total_rows, head_count, head_size)
    )
    value_text_grad = jnp.einsum(
        "rhk,rhe->khe", cross_low, cross_out_grad, preferred_element_type=jnp.float32
    )
    cross_prob_grad = jnp.einsum(
        "rhe,khe->rhk", cross_out_grad, value_text, preferred_element_type=jnp.float32
    )
    cross_score_grad = (
        cross_probs
        * (cross_prob_grad - jnp.sum(cross_probs * cross_prob_grad, axis=-1, keepdims=True))
    ).astype(jnp.bfloat16)
    cross_query_grad = (
        (
            jnp.einsum(
                "rhk,khe->rhe", cross_score_grad, key_text, preferred_element_type=jnp.float32
            )
            * score_scale
        )
        .reshape(total_rows, model_width)
        .astype(jnp.bfloat16)
    )
    key_text_grad = (
        jnp.einsum(
            "rhk,rhe->khe", cross_score_grad, cross_query, preferred_element_type=jnp.float32
        )
        * score_scale
    )
    cross_q_grad = product_left(after_low, cross_query_grad)
    grad_a = grad_c + product_right(cross_query_grad, cross_q_full)
    gate_a_grad = jnp.sum(branch_a * grad_a, axis=0)
    branch_a_grad = (modulation[2] * grad_a).astype(jnp.bfloat16)
    proj_grad = product_left(attended_low, branch_a_grad)
    attended_grad = (
        product_right(branch_a_grad, proj_full)
        .astype(jnp.bfloat16)
        .reshape(frame_count, row_count, head_count, head_size)
    )
    delta_rows = jnp.sum(attended_grad.astype(jnp.float32) * attended_exact, axis=-1)
    query_grad, key_grad, value_grad = spatial_backward(
        query_heads, key_rows, value_rows, log_total, attended_grad, delta_rows
    )
    qkv_rows_grad = jnp.concatenate(
        [
            query_grad.reshape(total_rows, model_width),
            key_grad.reshape(total_rows, model_width),
            value_grad.reshape(total_rows, model_width),
        ],
        axis=1,
    ).astype(jnp.bfloat16)
    qkv_grad = product_left(hidden_a, qkv_rows_grad)
    hidden_a_grad = product_right(qkv_rows_grad, qkv_full)
    input_grad = grad_a + normalize_back(hidden_a_grad * (1.0 + modulation[1]), normed_a, recip_a)
    latent_grad = input_grad.reshape(latent.shape)
    mod_grad = jnp.stack(
        [
            jnp.sum(hidden_a_grad, axis=0),
            jnp.sum(hidden_a_grad * normed_a, axis=0),
            gate_a_grad,
            jnp.sum(hidden_m_grad, axis=0),
            jnp.sum(hidden_m_grad * normed_m, axis=0),
            gate_m_grad,
            jnp.sum(hidden_t_grad, axis=0),
            jnp.sum(hidden_t_grad * normed_t, axis=0),
            gate_t_grad,
        ]
    ).reshape(1, 9 * model_width)
    text_grad = jnp.concatenate(
        [
            key_text_grad.reshape(text_count, model_width),
            value_text_grad.reshape(text_count, model_width),
        ],
        axis=1,
    )
    mod_slice, text_slice = (
        lax.psum_scatter(mod_grad, ("frame", "seq"), scatter_dimension=1, tiled=True),
        lax.psum_scatter(text_grad, ("frame", "seq"), scatter_dimension=1, tiled=True),
    )
    ada_grad = jnp.dot(silu_cond.T, mod_slice, precision=highest)
    text_kv_grad = product_left(text[0], text_slice.astype(jnp.bfloat16))
    shard_set = (
        lax.psum_scatter(qkv_grad, ("frame", "seq"), scatter_dimension=0, tiled=True),
        lax.psum_scatter(proj_grad, ("frame", "seq"), scatter_dimension=0, tiled=True),
        lax.psum_scatter(cross_q_grad, ("frame", "seq"), scatter_dimension=0, tiled=True),
        lax.psum_scatter(cross_proj_grad, ("frame", "seq"), scatter_dimension=0, tiled=True),
        lax.psum_scatter(up_grad, ("frame", "seq"), scatter_dimension=0, tiled=True),
        lax.psum_scatter(down_grad, ("frame", "seq"), scatter_dimension=0, tiled=True),
        lax.psum_scatter(temporal_qkv_grad, ("frame", "seq"), scatter_dimension=0, tiled=True),
        lax.psum_scatter(temporal_proj_grad, ("frame", "seq"), scatter_dimension=0, tiled=True),
    )
    summed = (
        lax.psum(ada_grad.astype(jnp.bfloat16), "bucket").astype(jnp.float32),
        lax.psum(text_kv_grad.astype(jnp.bfloat16), "bucket").astype(jnp.float32),
        lax.psum(shard_set[0].astype(jnp.bfloat16), "bucket").astype(jnp.float32),
        lax.psum(shard_set[1].astype(jnp.bfloat16), "bucket").astype(jnp.float32),
        lax.psum(shard_set[2].astype(jnp.bfloat16), "bucket").astype(jnp.float32),
        lax.psum(shard_set[3].astype(jnp.bfloat16), "bucket").astype(jnp.float32),
        lax.psum(shard_set[4].astype(jnp.bfloat16), "bucket").astype(jnp.float32),
        lax.psum(shard_set[5].astype(jnp.bfloat16), "bucket").astype(jnp.float32),
        lax.psum(shard_set[6].astype(jnp.bfloat16), "bucket").astype(jnp.float32),
        lax.psum(shard_set[7].astype(jnp.bfloat16), "bucket").astype(jnp.float32),
    )
    return (
        result,
        latent_grad,
        summed[0],
        summed[1],
        summed[2],
        summed[3],
        summed[4],
        summed[5],
        summed[6],
        summed[7],
        summed[8],
        summed[9],
    )


def solution(mesh):
    return jax.shard_map(
        per_device,
        mesh=mesh,
        in_specs=(
            P("bucket", "frame", "seq", None),
            P("bucket", None),
            P("bucket", None, None),
            P("bucket"),
            P("bucket", None),
            P("bucket", None),
            P(None, ("frame", "seq")),
            P(None, ("frame", "seq")),
            P(("frame", "seq"), None),
            P(("frame", "seq"), None),
            P(("frame", "seq"), None),
            P(("frame", "seq"), None),
            P(("frame", "seq"), None),
            P(("frame", "seq"), None),
            P(("frame", "seq"), None),
            P(("frame", "seq"), None),
            P("bucket", "frame", "seq", None),
        ),
        out_specs=(
            P("bucket", "frame", "seq", None),
            P("bucket", "frame", "seq", None),
            P(None, ("frame", "seq")),
            P(None, ("frame", "seq")),
            P(("frame", "seq"), None),
            P(("frame", "seq"), None),
            P(("frame", "seq"), None),
            P(("frame", "seq"), None),
            P(("frame", "seq"), None),
            P(("frame", "seq"), None),
            P(("frame", "seq"), None),
            P(("frame", "seq"), None),
        ),
        check_vma=False,
    )
```

profile of v0, /device:TPU:0, one launch (start us, length us, event | category | flops | bytes accessed | tf_op | source)
XLA Modules:
  0.0 3550.1 jit_solution(16646050555658453682)
XLA Ops:
  12.3 81.0 %all-reduce.3 = f32[10368]{0:T(1024)S(1)} all-reduce(f32[10368]{0:T(1024)S(1)} %dynamic-update-slice.15), channel_id=2, replica_groups=mesh['bucket'=2,'frame'=8,'seq'=2] {'frame','seq'}, use_global_device_ids=true, to_apply=%add.3 | all-reduce | flops 10368 | bytes 82944
  101.0 22.1 all-gather.12.cloned.1.call-done
  145.0 44.5 %all_gather.43 = bf16[128,2304]{0,1:T(8,128)(2,1)S(1)} all-gather(bf16[128,144]{0,1:T(8,128)(2,1)S(1)} %fusion.161), channel_id=1, replica_groups=mesh['bucket'=2,'frame'=8,'seq'=2] {'frame','seq'}, dimensions={1}, use_global_device_ids=true | all-gather | bytes 626688 | tf_op jit(solution)/shard_map/all_gather | solution.py:244
  382.4 25.5 all-gather.20.cloned.1.call-done
  433.7 39.4 %all-gather.22.cloned.1.call-done = bf16[1152,1152]{1,0:T(8,128)(2,1)} async-done(((bf16[72,1152]{1,0:T(8,128)(2,1)}), bf16[1152,1152]{1,0:T(8,128)(2,1)}) %all-gather.22.cloned.1.call-update) | async-done | bytes 2654224 | tf_op jit(solution)/shard_map/all_gather | solution.py:264
  484.0 123.3 %all-gather.24.cloned.1.call-done = bf16[1152,4608]{1,0:T(8,128)(2,1)} async-done(((bf16[72,4608]{1,0:T(8,128)(2,1)}), bf16[1152,4608]{1,0:T(8,128)(2,1)}) %all-gather.24.cloned.1.call-update) | async-done | bytes 10616848 | tf_op jit(solution)/shard_map/all_gather | solution.py:265
  607.2 20.9 fusion.201
  628.2 112.8 %all-gather.26.cloned.1.call-done = bf16[4608,1152]{1,0:T(8,128)(2,1)} async-done(((bf16[288,1152]{1,0:T(8,128)(2,1)}), bf16[4608,1152]{1,0:T(8,128)(2,1)}) %all-gather.26.cloned.1.call-update) | async-done | bytes 10616848 | tf_op jit(solution)/shard_map/all_gather | solution.py:266
  741.0 25.9 fusion.204
  769.9 80.6 %all-gather.28.cloned.1.call-done = bf16[1152,3456]{1,0:T(8,128)(2,1)} async-done(((bf16[72,3456]{1,0:T(8,128)(2,1)}), bf16[1152,3456]{1,0:T(8,128)(2,1)}) %all-gather.28.cloned.1.call-update) | async-done | bytes 7962640 | tf_op jit(solution)/shard_map/all_gather | solution.py:267
  927.0 55.0 %collective-permute-done = bf16[1,512,2304]{2,1,0:T(8,128)(2,1)} collective-permute-done((bf16[1,512,2304]{2,1,0:T(8,128)(2,1)}, bf16[1,512,2304]{2,1,0:T(8,128)(2,1)}, u32[]{:S(2)}, u32[]{:S(2)}) %collective-permute-start) | collective-permute-done | bytes 2359328 | tf_op jit(solution)/shard_map/ppermute | solution.py:23
  998.3 16.9 fusion.125
  1242.1 17.4 multiply_reduce_fusion
  1259.5 23.0 fusion.103
  1282.6 29.1 fusion.7
  1311.7 21.3 multiply_reduce_fusion.2
  1391.0 16.7 fusion.126
  1616.9 16.3 fusion.128
  1685.3 19.7 fusion.200
  1705.7 24.6 fusion.163
  1731.3 26.1 reduce-scatter.29.cloned.1.call-done
  1759.8 144.5 %reduce-scatter.45.cloned.1.call-done = f32[72,1152]{1,0:T(8,128)} async-done(((f32[1152,1152]{1,0:T(8,128)}), f32[72,1152]{1,0:T(8,128)}) %reduce-scatter.45.cloned.1.call-update) | async-done | bytes 331792
  1906.0 17.6 fusion.122
  1931.7 75.3 %all-reduce.4 = f32[1,10368]{1,0:T(1,128)S(1)} all-reduce(f32[1,10368]{1,0:T(1,128)S(1)} %bitcast.624), channel_id=5, replica_groups=mesh['bucket'=2,'frame'=8,'seq'=2] {'frame','seq'}, use_global_device_ids=true, to_apply=%region_43.44.clone | all-reduce | flops 10368 | bytes 82944
  2008.4 42.9 %reduce-scatter.39.cloned.1.call-done = f32[72,1152]{1,0:T(8,128)} async-done(((f32[1152,1152]{1,0:T(8,128)}), f32[72,1152]{1,0:T(8,128)}) %reduce-scatter.39.cloned.1.call-update) | async-done | bytes 331792
  2052.9 144.7 %reduce-scatter.41.cloned.1.call-done = f32[72,1152]{1,0:T(8,128)} async-done(((f32[1152,1152]{1,0:T(8,128)}), f32[72,1152]{1,0:T(8,128)}) %reduce-scatter.41.cloned.1.call-update) | async-done | bytes 331792
  2199.3 145.1 %reduce-scatter.37.cloned.1.call-done = f32[72,1152]{1,0:T(8,128)} async-done(((f32[1152,1152]{1,0:T(8,128)}), f32[72,1152]{1,0:T(8,128)}) %reduce-scatter.37.cloned.1.call-update) | async-done | bytes 331792
  2346.1 255.1 %reduce-scatter.43.cloned.1.call-done = f32[72,3456]{1,0:T(8,128)} async-done(((f32[1152,3456]{1,0:T(8,128)}), f32[72,3456]{1,0:T(8,128)}) %reduce-scatter.43.cloned.1.call-update) | async-done | bytes 995344
  2603.3 255.6 %reduce-scatter.35.cloned.1.call-done = f32[72,3456]{1,0:T(8,128)} async-done(((f32[1152,3456]{1,0:T(8,128)}), f32[72,3456]{1,0:T(8,128)}) %reduce-scatter.35.cloned.1.call-update) | async-done | bytes 995344
  2860.9 315.7 %reduce-scatter.31.cloned.1.call-done = f32[72,4608]{1,0:T(8,128)} async-done(((f32[1152,4608]{1,0:T(8,128)}), f32[72,4608]{1,0:T(8,128)}) %reduce-scatter.31.cloned.1.call-update) | async-done | bytes 1327120 | tf_op jit(solution)/shard_map/reduce_scatter | solution.py:518
  3178.8 315.2 %reduce-scatter.33.cloned.1.call-done = f32[288,1152]{1,0:T(8,128)} async-done(((f32[4608,1152]{1,0:T(8,128)}), f32[288,1152]{1,0:T(8,128)}) %reduce-scatter.33.cloned.1.call-update) | async-done | bytes 1327120 | tf_op jit(solution)/shard_map/reduce_scatter | solution.py:519
  3496.3 34.4 all-reduce.14.cloned.1.call-done
  (591 shorter events, 943.3 us)
Async XLA Ops:
  7.2 115.9 %all-gather.12.cloned.1.call-start = ((), (), s32[]{:S(2)}) async-start(), calls=%async_computation.11 | async-start | bytes 8460288 | tf_op jit(solution)/shard_map/all_gather | solution.py:261
  7.9 204.3 %all-gather.14.cloned.1.call-start = ((), (), s32[]{:S(2)}) async-start(), calls=%async_computation.12 | async-start | bytes 7077888 | tf_op jit(solution)/shard_map/all_gather | solution.py:114
  98.7 272.4 %copy-start.109 = (f32[1152]{0:T(1024)}, f32[1152]{0:T(1024)S(1)}, u32[]{:S(2)}) copy-start(f32[1152]{0:T(1024)S(1)} %get-tuple-element.98) | copy-start | bytes 13828
  139.1 136.6 %all-gather.16.cloned.1.call-start = ((), (), s32[]{:S(2)}) async-start(), calls=%async_computation.13 | async-start | bytes 7077888 | tf_op jit(solution)/shard_map/all_gather | solution.py:115
  139.8 231.2 %all-gather.18.cloned.1.call-start = ((), (), s32[]{:S(2)}) async-start(), calls=%async_computation.14 | async-start | bytes 2820096 | tf_op jit(solution)/shard_map/all_gather | solution.py:262
  140.4 267.5 %all-gather.20.cloned.1.call-start = ((), (), s32[]{:S(2)}) async-start(), calls=%async_computation.15 | async-start | bytes 2820096 | tf_op jit(solution)/shard_map/all_gather | solution.py:263
  141.0 332.2 %all-gather.22.cloned.1.call-start = ((), (), s32[]{:S(2)}) async-start(), calls=%async_computation.16 | async-start | bytes 2820096 | tf_op jit(solution)/shard_map/all_gather | solution.py:264
  141.5 465.7 %all-gather.24.cloned.1.call-start = ((), (), s32[]{:S(2)}) async-start(), calls=%async_computation.17 | async-start | bytes 11280384 | tf_op jit(solution)/shard_map/all_gather | solution.py:265
  142.3 598.7 %all-gather.26.cloned.1.call-start = ((), (), s32[]{:S(2)}) async-start(), calls=%async_computation.18 | async-start | bytes 11280384 | tf_op jit(solution)/shard_map/all_gather | solution.py:266
  143.0 707.5 %all-gather.28.cloned.1.call-start = ((), (), s32[]{:S(2)}) async-start(), calls=%async_computation.19 | async-start | bytes 8460288 | tf_op jit(solution)/shard_map/all_gather | solution.py:267
  143.8 871.8 %all-gather.30.cloned.1.call-start = ((), (), s32[]{:S(2)}) async-start(), calls=%async_computation.20 | async-start | bytes 2820096 | tf_op jit(solution)/shard_map/all_gather | solution.py:268
  144.4 1516.0 %reduce-scatter.25.cloned.1.call-start = ((), (), s32[]{:S(2)}) async-start(), calls=%async_computation.21 | async-start | bytes 7077888 | tf_op jit(solution)/shard_map/reduce_scatter | solution.py:205
  189.6 230.1 %copy-start.48 = (bf16[128,1152]{0,1:T(8,128)(2,1)}, bf16[128,1152]{0,1:T(8,128)(2,1)S(1)}, u32[]{:S(2)}) copy-start(bf16[128,1152]{0,1:T(8,128)(2,1)S(1)} %get-tuple-element.159) | copy-start | bytes 884740
  189.6 238.5 %copy-start.58 = (bf16[128,1152]{0,1:T(8,128)(2,1)}, bf16[128,1152]{0,1:T(8,128)(2,1)S(1)}, u32[]{:S(2)}) copy-start(bf16[128,1152]{0,1:T(8,128)(2,1)S(1)} %get-tuple-element.160) | copy-start | bytes 884740
  866.9 115.0 %collective-permute-start = (bf16[1,512,2304]{2,1,0:T(8,128)(2,1)}, bf16[1,512,2304]{2,1,0:T(8,128)(2,1)}, u32[]{:S(2)}, u32[]{:S(2)}) collective-permute-start(bf16[1,512,2304]{2,1,0:T(8,128)(2,1)} %get-tuple-element.132), channel_id=1, source_target_pairs={{0,2},{2,4},{4,6},{6,8},{8,10},{10,12},{12,14},{1,3},{3,5},{5,7},{... | collective-permute-start | bytes 7077896 | tf_op jit(solution)/shard_map/ppermute | solution.py:23
  871.8 114.5 %collective-permute-start.1 = (bf16[1,512,2304]{2,1,0:T(8,128)(2,1)}, bf16[1,512,2304]{2,1,0:T(8,128)(2,1)}, u32[]{:S(2)}, u32[]{:S(2)}) collective-permute-start(bf16[1,512,2304]{2,1,0:T(8,128)(2,1)} %get-tuple-element.131), channel_id=1, source_target_pairs={{2,0},{4,2},{6,4},{8,6},{10,8},{12,10},{14,12},{3,1},{5,3},{7,5},{... | collective-permute-start | bytes 7077896 | tf_op jit(solution)/shard_map/ppermute | solution.py:24
  1075.0 144.2 %collective-permute-start.2 = (bf16[1,512,2304]{1,2,0:T(8,128)(2,1)}, bf16[1,512,2304]{1,2,0:T(8,128)(2,1)}, u32[]{:S(2)}, u32[]{:S(2)}) collective-permute-start(bf16[1,512,2304]{1,2,0:T(8,128)(2,1)} %slice.437), channel_id=1, source_target_pairs={{0,2},{2,4},{4,6},{6,8},{8,10},{10,12},{12,14},{1,3},{3,5},{5,7},{... | collective-permute-start | bytes 7077896 | tf_op jit(solution)/shard_map/ppermute | solution.py:23
  1084.8 134.4 %collective-permute-start.3 = (bf16[1,512,2304]{1,2,0:T(8,128)(2,1)}, bf16[1,512,2304]{1,2,0:T(8,128)(2,1)}, u32[]{:S(2)}, u32[]{:S(2)}) collective-permute-start(bf16[1,512,2304]{1,2,0:T(8,128)(2,1)} %slice.436), channel_id=1, source_target_pairs={{2,0},{4,2},{6,4},{8,6},{10,8},{12,10},{14,12},{3,1},{5,3},{7,5},{... | collective-permute-start | bytes 7077896 | tf_op jit(solution)/shard_map/ppermute | solution.py:24
  1502.0 162.9 %reduce-scatter.27.cloned.1.call-start = ((), (), s32[]{:S(2)}) async-start(), calls=%async_computation.22 | async-start | bytes 7077888 | tf_op jit(solution)/shard_map/reduce_scatter | solution.py:208
  1568.4 189.1 %reduce-scatter.29.cloned.1.call-start = ((), (), s32[]{:S(2)}) async-start(), calls=%async_computation.23 | async-start | bytes 1253376 | tf_op jit(solution)/shard_map/reduce_scatter | solution.py:509
  1579.6 324.7 %reduce-scatter.45.cloned.1.call-start = ((), (), s32[]{:S(2)}) async-start(), calls=%async_computation.31 | async-start | bytes 5640192
  1589.5 461.8 %reduce-scatter.39.cloned.1.call-start = ((), (), s32[]{:S(2)}) async-start(), calls=%async_computation.28 | async-start | bytes 5640192
  1597.7 600.0 %reduce-scatter.41.cloned.1.call-start = ((), (), s32[]{:S(2)}) async-start(), calls=%async_computation.29 | async-start | bytes 5640192
  1606.9 737.6 %reduce-scatter.37.cloned.1.call-start = ((), (), s32[]{:S(2)}) async-start(), calls=%async_computation.27 | async-start | bytes 5640192
  1616.2 985.0 %reduce-scatter.43.cloned.1.call-start = ((), (), s32[]{:S(2)}) async-start(), calls=%async_computation.30 | async-start | bytes 16920576
  1633.2 1225.6 %reduce-scatter.35.cloned.1.call-start = ((), (), s32[]{:S(2)}) async-start(), calls=%async_computation.26 | async-start | bytes 16920576
  1684.6 1492.0 %reduce-scatter.31.cloned.1.call-start = ((), (), s32[]{:S(2)}) async-start(), calls=%async_computation.24 | async-start | bytes 22560768 | tf_op jit(solution)/shard_map/reduce_scatter | solution.py:518
  1705.0 1789.1 %reduce-scatter.33.cloned.1.call-start = ((), (), s32[]{:S(2)}) async-start(), calls=%async_computation.25 | async-start | bytes 22560768 | tf_op jit(solution)/shard_map/reduce_scatter | solution.py:519
  1730.4 175.6 %copy-start.65 = (f32[1152]{0:T(1024)S(1)}, f32[1152]{0:T(1024)}, u32[]{:S(2)}) copy-start(f32[1152]{0:T(1024)} %copy-done.64) | copy-start | bytes 13828
  1730.4 175.6 %copy-start.83 = (f32[1,4,2,128]{3,1,2,0:T(4,128)S(1)}, f32[1,4,2,128]{3,1,2,0:T(4,128)}, u32[]{:S(2)}) copy-start(f32[1,4,2,128]{3,1,2,0:T(4,128)} %copy-done.82) | copy-start | bytes 12292
  1730.4 175.6 %copy-start.85 = (f32[1,4,2,128]{3,1,2,0:T(4,128)S(1)}, f32[1,4,2,128]{3,1,2,0:T(4,128)}, u32[]{:S(2)}) copy-start(f32[1,4,2,128]{3,1,2,0:T(4,128)} %copy-done.84) | copy-start | bytes 12292
  1730.4 1800.3 %all-reduce.14.cloned.1.call-start = ((), (), s32[]{:S(2)}) async-start(), calls=%async_computation.32 | async-start | bytes 11317248 | tf_op jit(solution)/shard_map/psum | solution.py:524
  (141 other events, 2610.6 us)
Sparse Core Ops, SparseCore 0:
  10.7 112.3 all-gather.11
  139.2 72.0 all-gather.13
  213.4 62.2 all-gather.15
  278.2 64.2 all-gather.17
  345.0 62.7 all-gather.19
  410.4 62.7 all-gather.21
  476.0 131.2 all-gather.23
  610.0 130.9 all-gather.25
  743.7 106.8 all-gather.27
  853.1 118.1 all-gather.29
  1502.1 58.5 reduce-scatter.24
  1568.5 58.5 reduce-scatter.26
  1632.4 124.9 reduce-scatter.28
  1762.6 141.7 reduce-scatter.44
  1909.5 141.7 reduce-scatter.38
  2056.4 141.2 reduce-scatter.40
  2202.8 141.5 reduce-scatter.36
  2350.1 251.0 reduce-scatter.42
  2607.0 251.7 reduce-scatter.34
  2864.7 311.8 reduce-scatter.30
  3182.6 311.3 reduce-scatter.32
  3499.0 31.6 all-reduce.13
where the time goes:
time: 3560 us; the launch traced here: 3550 us
  waiting for transfers between devices  2160 us (61%)
  matrix products  647 us (18%)
  local copies, waits for them, and re-layouts  308 us (9%)
  other arithmetic  203 us (6%)
  blocking collectives  201 us (6%)
    unnamed x28, waiting for transfers between devices  994 us
    reduce_scatter x1, waiting for transfers between devices, per_device(): lax.psum_scatter(up_grad, ('frame', 'seq'), scatter_dimension=0, tiled=True)  316 us
    reduce_scatter x1, waiting for transfers between devices, per_device(): lax.psum_scatter(down_grad, ('frame', 'seq'), scatter_dimension=0, tiled=...  315 us
    unnamed x2, blocking collectives  156 us
    dot_general x9, matrix products, product(): return jnp.dot(left, right, preferred_element_type=jnp.float32)  124 us
    all_gather x1, waiting for transfers between devices, per_device(): lax.all_gather(up_weight, ('frame', 'seq'), axis=0, tiled=True)  123 us
    all_gather x1, waiting for transfers between devices, per_device(): lax.all_gather(down_weight, ('frame', 'seq'), axis=0, tiled=True)  113 us
    dot_general x8, matrix products, product_right(): lax.dot_general(left, right, (((1,), (1,)), ((), ())), preferred_element_...  112 us
  transfers between devices with their start and end apart: 26, of which 18 were waited for; matrix products, arithmetic and copies ran while one was open for 22% of the time, Pallas kernels for 0%

commit v1 on v0

--- a/solution.py
+++ b/solution.py
@@ -53,6 +53,31 @@
         upstream
         - jnp.mean(upstream, axis=-1, keepdims=True)
         - normed * jnp.mean(upstream * normed, axis=-1, keepdims=True)
+    )
+
+
+def gather_halves(is_first, lower, upper):
+    return lax.all_gather(
+        jnp.where(is_first, lower, upper), ("bucket", "frame", "seq"), axis=0, tiled=True
+    )
+
+
+def scatter_halves(lower, upper):
+    stacked = jnp.concatenate(
+        [
+            jnp.concatenate([part.astype(jnp.bfloat16) for part in lower], axis=1),
+            jnp.concatenate([part.astype(jnp.bfloat16) for part in upper], axis=1),
+        ],
+        axis=0,
+    )
+    return lax.psum_scatter(stacked, ("bucket", "frame", "seq"), scatter_dimension=0, tiled=True)
+
+
+def whole_halves(is_first, own):
+    other = lax.ppermute(own, "bucket", [(0, 1), (1, 0)])
+    return (
+        jnp.where(is_first, own, other).astype(jnp.float32),
+        jnp.where(is_first, other, own).astype(jnp.float32),
     )
 
 
@@ -248,25 +273,51 @@
     text_count = text_kv.shape[0]
     key_text = text_kv[:, :model_width].reshape(text_count, head_count, head_size)
     value_text = text_kv[:, model_width:].reshape(text_count, head_count, head_size)
-    (
-        qkv_full,
-        proj_full,
-        cross_q_full,
-        cross_proj_full,
-        up_full,
-        down_full,
-        tqkv_full,
-        tproj_full,
-    ) = (
-        lax.all_gather(qkv_weight, ("frame", "seq"), axis=0, tiled=True),
-        lax.all_gather(proj_weight, ("frame", "seq"), axis=0, tiled=True),
-        lax.all_gather(cross_q_weight, ("frame", "seq"), axis=0, tiled=True),
-        lax.all_gather(cross_proj_weight, ("frame", "seq"), axis=0, tiled=True),
-        lax.all_gather(up_weight, ("frame", "seq"), axis=0, tiled=True),
-        lax.all_gather(down_weight, ("frame", "seq"), axis=0, tiled=True),
-        lax.all_gather(temporal_qkv_weight, ("frame", "seq"), axis=0, tiled=True),
-        lax.all_gather(temporal_proj_weight, ("frame", "seq"), axis=0, tiled=True),
-    )
+    is_first = lax.axis_index("bucket") == 0
+    ff_width = up_weight.shape[1]
+    shard_rows = up_weight.shape[0]
+    shards = lax.axis_size(("frame", "seq"))
+    ff_blocks = ff_width // model_width
+    up_mixed = (
+        up_weight.reshape(shard_rows, shards, ff_blocks, shard_rows)
+        .transpose(0, 2, 1, 3)
+        .reshape(shard_rows, ff_width)
+    )
+    down_wide = (
+        down_weight.reshape(ff_blocks, shard_rows, model_width)
+        .transpose(1, 0, 2)
+        .reshape(shard_rows, ff_width)
+    )
+    half_ff = ff_width // 2
+    gathered_a = gather_halves(
+        is_first,
+        qkv_weight,
+        jnp.concatenate([proj_weight, cross_q_weight, cross_proj_weight], axis=1),
+    )
+    gathered_b = gather_halves(
+        is_first,
+        jnp.concatenate([up_mixed[:, :half_ff], down_wide[:, :half_ff]], axis=1),
+        jnp.concatenate([up_mixed[:, half_ff:], down_wide[:, half_ff:]], axis=1),
+    )
+    gathered_c = gather_halves(
+        is_first,
+        temporal_qkv_weight[:, : 2 * model_width],
+        jnp.concatenate([temporal_qkv_weight[:, 2 * model_width :], temporal_proj_weight], axis=1),
+    )
+    qkv_full = gathered_a[:model_width]
+    proj_full = gathered_a[model_width:, :model_width]
+    cross_q_full = gathered_a[model_width:, model_width : 2 * model_width]
+    cross_proj_full = gathered_a[model_width:, 2 * model_width :]
+    up_halves = (gathered_b[:model_width, :half_ff], gathered_b[model_width:, :half_ff])
+    down_parts = [
+        gathered_b[
+            model_width * (index * 2 // ff_blocks) :, half_ff:
+        ][:model_width, model_width * (index % (ff_blocks // 2)) :][:, :model_width]
+        for index in range(ff_blocks)
+    ]
+    tqk_full = gathered_c[:model_width]
+    tv_full = gathered_c[model_width:, :model_width]
+    tproj_full = gathered_c[model_width:, model_width:]
     inputs = latent[0].reshape(total_rows, model_width).astype(jnp.float32)
     normed_a, recip_a = normalize(inputs)
     hidden_a = (normed_a * (1.0 + modulation[1]) + modulation[0]).astype(jnp.bfloat16)
@@ -301,13 +352,25 @@
     after_c = after_a + product(cross_out, cross_proj_full)
     normed_m, recip_m = normalize(after_c)
     hidden_m = (normed_m * (1.0 + modulation[4]) + modulation[3]).astype(jnp.bfloat16)
-    upward = product(hidden_m, up_full)
-    activated = gelu_tanh(upward).astype(jnp.bfloat16)
-    branch_m = product(activated, down_full)
+    upward_halves = [product(hidden_m, part) for part in up_halves]
+    activated_halves = [gelu_tanh(part).astype(jnp.bfloat16) for part in upward_halves]
+    activated_parts = [
+        activated_halves[index * 2 // ff_blocks][
+            :, model_width * (index % (ff_blocks // 2)) :
+        ][:, :model_width]
+        for index in range(ff_blocks)
+    ]
+    branch_m = sum(product(left, right) for left, right in zip(activated_parts, down_parts))
     after_m = after_c + modulation[5] * branch_m
     normed_t, recip_t = normalize(after_m)
     hidden_t = (normed_t * (1.0 + modulation[7]) + modulation[6]).astype(jnp.bfloat16)
-    temporal_rows = product(hidden_t, tqkv_full).astype(jnp.bfloat16)
+    temporal_rows = jnp.concatenate(
+        [
+            product(hidden_t, tqk_full).astype(jnp.bfloat16),
+            product(hidden_t, tv_full).astype(jnp.bfloat16),
+        ],
+        axis=1,
+    )
     temporal_query = (
         temporal_rows[:, :model_width]
         .astype(jnp.float32)
@@ -413,17 +476,34 @@
         ],
         axis=1,
     ).astype(jnp.bfloat16)
-    temporal_qkv_grad = product_left(hidden_t, temporal_grad)
-    hidden_t_grad = product_right(temporal_grad, tqkv_full)
+    tqk_grad = product_left(hidden_t, temporal_grad[:, : 2 * model_width])
+    tv_grad = product_left(hidden_t, temporal_grad[:, 2 * model_width :])
+    scattered_c = scatter_halves([tqk_grad], [tv_grad, temporal_proj_grad])
+    hidden_t_grad = product_right(temporal_grad[:, : 2 * model_width], tqk_full) + product_right(
+        temporal_grad[:, 2 * model_width :], tv_full
+    )
     grad_m = result_grad + normalize_back(hidden_t_grad * (1.0 + modulation[7]), normed_t, recip_t)
     gate_m_grad = jnp.sum(branch_m * grad_m, axis=0)
     branch_m_grad = (modulation[5] * grad_m).astype(jnp.bfloat16)
-    down_grad = product_left(activated, branch_m_grad)
-    activated_grad = product_right(branch_m_grad, down_full)
-    gelu_value, gelu_back = jax.vjp(gelu_tanh, upward)
-    upward_grad = gelu_back(activated_grad)[0].astype(jnp.bfloat16)
-    up_grad = product_left(hidden_m, upward_grad)
-    hidden_m_grad = product_right(upward_grad, up_full)
+    down_grads = [product_left(part, branch_m_grad) for part in activated_parts]
+    upward_grads = []
+    for index in range(2):
+        activated_grad = jnp.concatenate(
+            [
+                product_right(branch_m_grad, part)
+                for part in down_parts[index * ff_blocks // 2 : (index + 1) * ff_blocks // 2]
+            ],
+            axis=1,
+        )
+        gelu_back = jax.vjp(gelu_tanh, upward_halves[index])[1]
+        upward_grads.append(gelu_back(activated_grad)[0].astype(jnp.bfloat16))
+    up_grads = [product_left(hidden_m, part) for part in upward_grads]
+    scattered_b = scatter_halves(
+        [up_grads[0]] + down_grads[: ff_blocks // 2], [up_grads[1]] + down_grads[ff_blocks // 2 :]
+    )
+    hidden_m_grad = product_right(upward_grads[0], up_halves[0]) + product_right(
+        upward_grads[1], up_halves[1]
+    )
     grad_c = grad_m + normalize_back(hidden_m_grad * (1.0 + modulation[4]), normed_m, recip_m)
     cross_branch_grad = grad_c.astype(jnp.bfloat16)
     cross_proj_grad = product_left(cross_out, cross_branch_grad)
@@ -508,43 +588,45 @@
         lax.psum_scatter(mod_grad, ("frame", "seq"), scatter_dimension=1, tiled=True),
         lax.psum_scatter(text_grad, ("frame", "seq"), scatter_dimension=1, tiled=True),
     )
-    ada_grad = jnp.dot(silu_cond.T, mod_slice, precision=highest)
-    text_kv_grad = product_left(text[0], text_slice.astype(jnp.bfloat16))
-    shard_set = (
-        lax.psum_scatter(qkv_grad, ("frame", "seq"), scatter_dimension=0, tiled=True),
-        lax.psum_scatter(proj_grad, ("frame", "seq"), scatter_dimension=0, tiled=True),
-        lax.psum_scatter(cross_q_grad, ("frame", "seq"), scatter_dimension=0, tiled=True),
-        lax.psum_scatter(cross_proj_grad, ("frame", "seq"), scatter_dimension=0, tiled=True),
-        lax.psum_scatter(up_grad, ("frame", "seq"), scatter_dimension=0, tiled=True),
-        lax.psum_scatter(down_grad, ("frame", "seq"), scatter_dimension=0, tiled=True),
-        lax.psum_scatter(temporal_qkv_grad, ("frame", "seq"), scatter_dimension=0, tiled=True),
-        lax.psum_scatter(temporal_proj_grad, ("frame", "seq"), scatter_dimension=0, tiled=True),
-    )
-    summed = (
-        lax.psum(ada_grad.astype(jnp.bfloat16), "bucket").astype(jnp.float32),
-        lax.psum(text_kv_grad.astype(jnp.bfloat16), "bucket").astype(jnp.float32),
-        lax.psum(shard_set[0].astype(jnp.bfloat16), "bucket").astype(jnp.float32),
-        lax.psum(shard_set[1].astype(jnp.bfloat16), "bucket").astype(jnp.float32),
-        lax.psum(shard_set[2].astype(jnp.bfloat16), "bucket").astype(jnp.float32),
-        lax.psum(shard_set[3].astype(jnp.bfloat16), "bucket").astype(jnp.float32),
-        lax.psum(shard_set[4].astype(jnp.bfloat16), "bucket").astype(jnp.float32),
-        lax.psum(shard_set[5].astype(jnp.bfloat16), "bucket").astype(jnp.float32),
-        lax.psum(shard_set[6].astype(jnp.bfloat16), "bucket").astype(jnp.float32),
-        lax.psum(shard_set[7].astype(jnp.bfloat16), "bucket").astype(jnp.float32),
+    swap = [(0, 1), (1, 0)]
+    silu_pair = jnp.concatenate([silu_cond, lax.ppermute(silu_cond, "bucket", swap)], axis=0)
+    mod_pair = jnp.concatenate([mod_slice, lax.ppermute(mod_slice, "bucket", swap)], axis=0)
+    ada_grad = lax.dot_general(
+        silu_pair, mod_pair, (((0,), (0,)), ((), ())), precision=highest
+    )
+    text_low = text_slice.astype(jnp.bfloat16)
+    text_pair = jnp.concatenate([text[0], lax.ppermute(text[0], "bucket", swap)], axis=0)
+    slice_pair = jnp.concatenate([text_low, lax.ppermute(text_low, "bucket", swap)], axis=0)
+    text_kv_grad = product_left(text_pair, slice_pair)
+    scattered_a = scatter_halves([qkv_grad], [proj_grad, cross_q_grad, cross_proj_grad])
+    lower_a, upper_a = whole_halves(is_first, scattered_a)
+    lower_b, upper_b = whole_halves(is_first, scattered_b)
+    lower_c, upper_c = whole_halves(is_first, scattered_c)
+    up_shard = (
+        jnp.concatenate([lower_b[:, :half_ff], upper_b[:, :half_ff]], axis=1)
+        .reshape(shard_rows, ff_blocks, shards, shard_rows)
+        .transpose(0, 2, 1, 3)
+        .reshape(shard_rows, ff_width)
+    )
+    down_shard = (
+        jnp.concatenate([lower_b[:, half_ff:], upper_b[:, half_ff:]], axis=1)
+        .reshape(shard_rows, ff_blocks, model_width)
+        .transpose(1, 0, 2)
+        .reshape(ff_blocks * shard_rows, model_width)
     )
     return (
         result,
         latent_grad,
-        summed[0],
-        summed[1],
-        summed[2],
-        summed[3],
-        summed[4],
-        summed[5],
-        summed[6],
-        summed[7],
-        summed[8],
-        summed[9],
+        ada_grad,
+        text_kv_grad,
+        lower_a,
+        upper_a[:, :model_width],
+        upper_a[:, model_width : 2 * model_width],
+        upper_a[:, 2 * model_width :],
+        up_shard,
+        down_shard,
+        jnp.concatenate([lower_c, upper_c[:, :model_width]], axis=1),
+        upper_c[:, model_width:],
     )
 
 

time: 3560 us -> 2110 us (0.59)
  waiting for transfers between devices: 2160 us -> 594 us
  other arithmetic: 203 us -> 308 us
    unnamed x28 -> x12, waiting for transfers between devices: 994 us -> 180 us
    reduce_scatter x2, waiting for transfers between devices: 631 us -> 239 us  [scatter_halves(): lax.psum_scatter(stacked, ('bucket', 'frame', 'seq'), scatter_dimension=0...]
    all_gather x8 -> x3, waiting for transfers between devices: 404 us -> 36.3 us  [gather_halves(): lax.all_gather(jnp.where(is_first, lower, upper), ('bucket', 'frame', 'se...]
    concatenate x0 -> x7, other arithmetic: none -> 86 us  [the longest x3 81.4 us: scatter_halves(): jnp.concatenate([jnp.concatenate([part.astype(jnp.bfloat16) for part in l...]
    all_gather x1, waiting for transfers between devices: 0.01 us -> 42.6 us  [spatial_forward(): lax.all_gather(key_rows, 'seq', axis=1, tiled=True)]
    all_gather x1, waiting for transfers between devices: 14.4 us -> 52.2 us  [spatial_forward(): lax.all_gather(value_rows, 'seq', axis=1, tiled=True)]
    dot_general x9 -> x14, matrix products: 109 us -> 85.7 us  [product_left(): lax.dot_general(left, right, (((0,), (0,)), ((), ())), preferred_element_...]
    dot_general x9 -> x14, matrix products: 124 us -> 136 us  [product(): return jnp.dot(left, right, preferred_element_type=jnp.float32)]
  transfers between devices with their start and end apart: 26 -> 22, of which waited for: 18 -> 9; matrix products, arithmetic and copies ran while one was open for 22% -> 37% of each run, Pallas kernels for 0% -> 0%
where the time goes in v1:
time: 2110 us; the launch traced here: 2100 us
  matrix products  624 us (30%)
  waiting for transfers between devices  594 us (28%)
  local copies, waits for them, and re-layouts  336 us (16%)
  other arithmetic  308 us (15%)
  blocking collectives  203 us (10%)
    reduce_scatter x2, waiting for transfers between devices, scatter_halves(): lax.psum_scatter(stacked, ('bucket', 'frame', 'seq'), scatter_dimension=0...  239 us
    unnamed x12, waiting for transfers between devices  180 us
    unnamed x2, blocking collectives  157 us
    dot_general x14, matrix products, product(): return jnp.dot(left, right, preferred_element_type=jnp.float32)  136 us
    dot_general x13, matrix products, product_right(): lax.dot_general(left, right, (((1,), (1,)), ((), ())), preferred_element_...  108 us
    dot_general x14, matrix products, product_left(): lax.dot_general(left, right, (((0,), (0,)), ((), ())), preferred_element_...  85.7 us
    concatenate x3, other arithmetic, scatter_halves(): jnp.concatenate([jnp.concatenate([part.astype(jnp.bfloat16) for part in l...  81.4 us
    dot_general x4, matrix products, absorb(): jnp.einsum('fqhk,fkhe->fqhe', weights, value_block.astype(jnp.float32), p...  55.1 us
  transfers between devices with their start and end apart: 22, of which 9 were waited for; matrix products, arithmetic and copies ran while one was open for 37% of the time, Pallas kernels for 0%

profile of v1, /device:TPU:0, one launch (start us, length us, event | category | flops | bytes accessed | tf_op | source)
XLA Modules:
  0.0 2099.2 jit_solution(6159284359968061599)
XLA Ops:
  16.7 81.9 %all-reduce.3 = f32[10368]{0:T(1024)S(1)} all-reduce(f32[10368]{0:T(1024)S(1)} %dynamic-update-slice.15), channel_id=2, replica_groups=mesh['bucket'=2,'frame'=8,'seq'=2] {'frame','seq'}, use_global_device_ids=true, to_apply=%add.3 | all-reduce | flops 10368 | bytes 82944
  106.4 19.3 all-gather.7.cloned.1.call-done
  125.7 12.8 convolution_convert_fusion.13
  154.7 46.1 %all_gather.27 = bf16[128,2304]{0,1:T(8,128)(2,1)S(1)} all-gather(bf16[128,144]{0,1:T(8,128)(2,1)S(1)} %fusion.248), channel_id=1, replica_groups=mesh['bucket'=2,'frame'=8,'seq'=2] {'frame','seq'}, dimensions={1}, use_global_device_ids=true | all-gather | bytes 626688 | tf_op jit(solution)/shard_map/all_gather | solution.py:269
  204.7 17.0 all-gather.15.cloned.1.call-done
  242.0 42.6 %all-gather.9.cloned.1.call-done = bf16[2,1024,1152]{2,1,0:T(8,128)(2,1)} async-done(((bf16[2,512,1152]{2,1,0:T(8,128)(2,1)}), bf16[2,1024,1152]{2,1,0:T(8,128)(2,1)}) %all-gather.9.cloned.1.call-update) | async-done | bytes 4718608 | tf_op jit(solution)/shard_map/all_gather | solution.py:139
  296.5 52.2 %all-gather.11.cloned.1.call-done = bf16[2,1024,1152]{2,1,0:T(8,128)(2,1)} async-done(((bf16[2,512,1152]{2,1,0:T(8,128)(2,1)}), bf16[2,1024,1152]{2,1,0:T(8,128)(2,1)}) %all-gather.11.cloned.1.call-update) | async-done | bytes 4718608 | tf_op jit(solution)/shard_map/all_gather | solution.py:140
  402.5 12.7 fusion.31
  420.6 14.0 fusion.54
  445.8 12.4 fusion.116
  508.8 12.6 fusion.25
  521.4 12.7 multiply_convert_fusion.1
  548.4 12.4 multiply_convert_fusion
  612.9 12.9 fusion.29
  668.6 42.3 %collective-permute-done = bf16[1,512,2304]{2,1,0:T(8,128)(2,1)} collective-permute-done((bf16[1,512,2304]{2,1,0:T(8,128)(2,1)}, bf16[1,512,2304]{2,1,0:T(8,128)(2,1)}, u32[]{:S(2)}, u32[]{:S(2)}) %collective-permute-start) | collective-permute-done | bytes 2359328 | tf_op jit(solution)/shard_map/ppermute | solution.py:23
  728.6 40.2 %fusion.136 = (f32[2,512,16]{1,0,2:T(2,128)S(1)}, f32[2,512,16]{1,0,2:T(2,128)S(1)}, f32[2,512,16]{1,0,2:T(2,128)S(1)}) fusion(f32[2,512,16,72]{1,0,3,2:T(2,128)} %reshape.725, f32[2,512,16,72]{1,3,2,0:T(8,128)} %bitcast.537, f32[2,512,16,72]{1,3,2,0:T(8,128)} %bitcast.535, f32[2,512,16,72]{1,3,2,0:T(8,128)} %bitcast.536), kind=kLoop, calls=%fused_computation.204 | loop fusion | flops 7028736 | bytes 19070976 | tf_op jit(solution)/shard_map/reduce_sum | solution.py:406
  790.2 13.0 select_maximum_fusion
  829.9 12.6 fusion.21
  920.1 12.2 multiply_convert_fusion.6
  1004.8 22.2 %fusion.114 = (f32[1152]{0:T(1024)}, bf16[1024,1152]{1,0:T(8,128)(2,1)}, f32[1152]{0:T(1024)}, f32[1024,1152]{1,0:T(8,128)}) fusion(bf16[1,2,512,1152]{3,2,1,0:T(8,128)(2,1)} %param.43, f32[1024]{0:T(1024)S(1)} %bitcast.671, f32[1024,1152]{1,0:T(8,128)} %copy-done.8, f32[1152]{0:T(1024)S(1)} %copy-done.79, f32[1024,1152]{1,0:T(8,128)} %get-tuple-element.204, ...), kind=kOutput, calls=%fused_computation.171 | convolution fusion | flops 2746218496 | bytes 54597632 | tf_op jit(solution)/shard_map/dot_general | solution.py:30
  1079.2 12.1 multiply_reduce_fusion.2
  1148.9 16.9 fusion.137
  1260.2 11.7 fusion.60
  1355.5 28.1 %maximum_maximum_fusion.2 = bf16[2304,2304]{1,0:T(8,128)(2,1)} fusion(bf16[1152,1152]{1,0:T(8,128)(2,1)S(1)} %copy-done.50, bf16[1152,1152]{1,0:T(8,128)(2,1)S(1)} %convolution_convert_fusion.5, bf16[1152,2304]{1,0:T(8,128)(2,1)S(1)} %convolution_convert_fusion.1), kind=kLoop, calls=%fused_computation.61 | loop fusion | flops 31850496 | bytes 21233664 | tf_op jit(solution)/shard_map/concatenate | solution.py:66
  1422.7 34.9 %maximum_maximum_fusion = bf16[2304,4608]{1,0:T(8,128)(2,1)} fusion(bf16[1152,1152]{1,0:T(8,128)(2,1)} %convolution_convert_fusion.6, bf16[1152,1152]{1,0:T(8,128)(2,1)} %convolution_convert_fusion.7, bf16[1152,2304]{1,0:T(8,128)(2,1)} %convolution_convert_fusion.2, bf16[1152,1152]{1,0:T(8,128)(2,1)} %convolution_convert_fusion.8, ...), kind=kLoop, calls=%fused_computation.1 | loop fusion | flops 127401984 | bytes 42467328 | tf_op jit(solution)/shard_map/concatenate | solution.py:66
  1507.6 12.2 convolution_convert_fusion
  1519.8 18.4 maximum_maximum_fusion.1
  1541.9 18.4 fusion.133
  1568.8 75.5 %all-reduce.4 = f32[1,10368]{1,0:T(1,128)S(1)} all-reduce(f32[1,10368]{1,0:T(1,128)S(1)} %bitcast.664), channel_id=5, replica_groups=mesh['bucket'=2,'frame'=8,'seq'=2] {'frame','seq'}, use_global_device_ids=true, to_apply=%region_43.44.clone | all-reduce | flops 10368 | bytes 82944
  1644.4 20.0 reduce-scatter.18.cloned.1.call-done
  1670.9 219.3 %reduce-scatter.16.cloned.1.call-done = bf16[72,4608]{1,0:T(8,128)(2,1)} async-done(((bf16[2304,4608]{1,0:T(8,128)(2,1)}), bf16[72,4608]{1,0:T(8,128)(2,1)}) %reduce-scatter.16.cloned.1.call-update) | async-done | bytes 663568 | tf_op jit(solution)/shard_map/reduce_scatter | solution.py:73
  1896.6 179.6 %reduce-scatter.20.cloned.1.call-done = bf16[72,3456]{1,0:T(8,128)(2,1)} async-done(((bf16[2304,3456]{1,0:T(8,128)(2,1)}), bf16[72,3456]{1,0:T(8,128)(2,1)}) %reduce-scatter.20.cloned.1.call-update) | async-done | bytes 497680
  (657 shorter events, 929.2 us)
Async XLA Ops:
  7.2 118.5 %all-gather.7.cloned.1.call-start = ((), (), s32[]{:S(2)}) async-start(), calls=%async_computation.6 | async-start | bytes 16422912 | tf_op jit(solution)/shard_map/all_gather | solution.py:60
  9.5 212.3 %all-gather.15.cloned.1.call-start = ((), (), s32[]{:S(2)}) async-start(), calls=%async_computation.10 | async-start | bytes 10948608 | tf_op jit(solution)/shard_map/all_gather | solution.py:60
  12.4 272.3 %all-gather.9.cloned.1.call-start = ((), (), s32[]{:S(2)}) async-start(), calls=%async_computation.7 | async-start | bytes 7077888 | tf_op jit(solution)/shard_map/all_gather | solution.py:139
  104.0 96.7 %copy-start.78 = (f32[1152]{0:T(1024)}, f32[1152]{0:T(1024)S(1)}, u32[]{:S(2)}) copy-start(f32[1152]{0:T(1024)S(1)} %get-tuple-element.90) | copy-start | bytes 13828
  104.1 359.0 %copy-start.111 = (f32[1152]{0:T(1024)}, f32[1152]{0:T(1024)S(1)}, u32[]{:S(2)}) copy-start(f32[1152]{0:T(1024)S(1)} %get-tuple-element.98) | copy-start | bytes 13828
  104.1 400.9 %copy-start.74 = (f32[1152]{0:T(1024)}, f32[1152]{0:T(1024)S(1)}, u32[]{:S(2)}) copy-start(f32[1152]{0:T(1024)S(1)} %get-tuple-element.94) | copy-start | bytes 13828
  141.7 207.0 %all-gather.11.cloned.1.call-start = ((), (), s32[]{:S(2)}) async-start(), calls=%async_computation.8 | async-start | bytes 7077888 | tf_op jit(solution)/shard_map/all_gather | solution.py:140
  142.3 379.1 %all-gather.13.cloned.1.call-start = ((), (), s32[]{:S(2)}) async-start(), calls=%async_computation.9 | async-start | bytes 21897216 | tf_op jit(solution)/shard_map/all_gather | solution.py:60
  150.6 1348.4 %reduce-scatter.10.cloned.1.call-start = ((), (), s32[]{:S(2)}) async-start(), calls=%async_computation.11 | async-start | bytes 7077888 | tf_op jit(solution)/shard_map/reduce_scatter | solution.py:230
  200.8 283.4 %copy-start.63 = (bf16[128,1152]{0,1:T(8,128)(2,1)}, bf16[128,1152]{0,1:T(8,128)(2,1)S(1)}, u32[]{:S(2)}) copy-start(bf16[128,1152]{0,1:T(8,128)(2,1)S(1)} %get-tuple-element.168) | copy-start | bytes 884740
  200.8 292.0 %copy-start.72 = (bf16[128,1152]{0,1:T(8,128)(2,1)}, bf16[128,1152]{0,1:T(8,128)(2,1)S(1)}, u32[]{:S(2)}) copy-start(bf16[128,1152]{0,1:T(8,128)(2,1)S(1)} %get-tuple-element.169) | copy-start | bytes 884740
  353.5 155.2 %copy-start.16 = (bf16[2,256,1152]{1,2,0:T(8,128)(2,1)}, bf16[2,256,1152]{1,2,0:T(8,128)(2,1)S(1)}, u32[]{:S(2)}) copy-start(bf16[2,256,1152]{1,2,0:T(8,128)(2,1)S(1)} %copy.440) | copy-start | bytes 3538948
  355.5 257.3 %copy-start.18 = (bf16[2,256,1152]{1,2,0:T(8,128)(2,1)}, bf16[2,256,1152]{1,2,0:T(8,128)(2,1)S(1)}, u32[]{:S(2)}) copy-start(bf16[2,256,1152]{1,2,0:T(8,128)(2,1)S(1)} %copy.444) | copy-start | bytes 3538948
  391.0 54.7 %copy-start.68 = (f32[2,512,16]{1,2,0:T(8,128)}, f32[2,512,16]{1,2,0:T(8,128)S(1)}, u32[]{:S(2)}) copy-start(f32[2,512,16]{1,2,0:T(8,128)S(1)} %get-tuple-element.180) | copy-start | bytes 196612
  606.6 104.4 %collective-permute-start = (bf16[1,512,2304]{2,1,0:T(8,128)(2,1)}, bf16[1,512,2304]{2,1,0:T(8,128)(2,1)}, u32[]{:S(2)}, u32[]{:S(2)}) collective-permute-start(bf16[1,512,2304]{2,1,0:T(8,128)(2,1)} %get-tuple-element.122), channel_id=1, source_target_pairs={{0,2},{2,4},{4,6},{6,8},{8,10},{10,12},{12,14},{1,3},{3,5},{5,7},{... | collective-permute-start | bytes 7077896 | tf_op jit(solution)/shard_map/ppermute | solution.py:23
  611.6 103.7 %collective-permute-start.1 = (bf16[1,512,2304]{2,1,0:T(8,128)(2,1)}, bf16[1,512,2304]{2,1,0:T(8,128)(2,1)}, u32[]{:S(2)}, u32[]{:S(2)}) collective-permute-start(bf16[1,512,2304]{2,1,0:T(8,128)(2,1)} %get-tuple-element.121), channel_id=1, source_target_pairs={{2,0},{4,2},{6,4},{8,6},{10,8},{12,10},{14,12},{3,1},{5,3},{7,5},{... | collective-permute-start | bytes 7077896 | tf_op jit(solution)/shard_map/ppermute | solution.py:24
  728.6 55.0 %copy-start.6 = (f32[2,512,1152]{1,2,0:T(8,128)}, f32[2,512,1152]{1,2,0:T(8,128)S(1)}, u32[]{:S(2)}) copy-start(f32[2,512,1152]{1,2,0:T(8,128)S(1)} %get-tuple-element.118) | copy-start | bytes 14155780
  728.6 55.0 %copy-start.7 = (f32[2,512,1152]{1,2,0:T(8,128)}, f32[2,512,1152]{1,2,0:T(8,128)S(1)}, u32[]{:S(2)}) copy-start(f32[2,512,1152]{1,2,0:T(8,128)S(1)} %get-tuple-element.139) | copy-start | bytes 14155780
  818.8 144.1 %collective-permute-start.2 = (bf16[1,512,2304]{1,2,0:T(8,128)(2,1)}, bf16[1,512,2304]{1,2,0:T(8,128)(2,1)}, u32[]{:S(2)}, u32[]{:S(2)}) collective-permute-start(bf16[1,512,2304]{1,2,0:T(8,128)(2,1)} %slice.703), channel_id=1, source_target_pairs={{0,2},{2,4},{4,6},{6,8},{8,10},{10,12},{12,14},{1,3},{3,5},{5,7},{... | collective-permute-start | bytes 7077896 | tf_op jit(solution)/shard_map/ppermute | solution.py:23
  828.6 134.3 %collective-permute-start.3 = (bf16[1,512,2304]{1,2,0:T(8,128)(2,1)}, bf16[1,512,2304]{1,2,0:T(8,128)(2,1)}, u32[]{:S(2)}, u32[]{:S(2)}) collective-permute-start(bf16[1,512,2304]{1,2,0:T(8,128)(2,1)} %slice.702), channel_id=1, source_target_pairs={{2,0},{4,2},{6,4},{8,6},{10,8},{12,10},{14,12},{3,1},{5,3},{7,5},{... | collective-permute-start | bytes 7077896 | tf_op jit(solution)/shard_map/ppermute | solution.py:24
  1260.1 243.2 %reduce-scatter.12.cloned.1.call-start = ((), (), s32[]{:S(2)}) async-start(), calls=%async_computation.12 | async-start | bytes 7077888 | tf_op jit(solution)/shard_map/reduce_scatter | solution.py:233
  1326.4 214.5 %reduce-scatter.14.cloned.1.call-start = ((), (), s32[]{:S(2)}) async-start(), calls=%async_computation.13 | async-start | bytes 1253376 | tf_op jit(solution)/shard_map/reduce_scatter | solution.py:589
  1340.9 323.6 %reduce-scatter.18.cloned.1.call-start = ((), (), s32[]{:S(2)}) async-start(), calls=%async_computation.15 | async-start | bytes 10948608 | tf_op jit(solution)/shard_map/reduce_scatter | solution.py:73
  1383.5 506.7 %reduce-scatter.16.cloned.1.call-start = ((), (), s32[]{:S(2)}) async-start(), calls=%async_computation.14 | async-start | bytes 21897216 | tf_op jit(solution)/shard_map/reduce_scatter | solution.py:73
  1457.7 618.5 %reduce-scatter.20.cloned.1.call-start = ((), (), s32[]{:S(2)}) async-start(), calls=%async_computation.16 | async-start | bytes 16422912
  1539.6 124.9 %collective-permute-start.6 = (bf16[128,4096]{1,0:T(8,128)(2,1)S(1)}, bf16[128,4096]{1,0:T(8,128)(2,1)S(1)}, u32[]{:S(2)}, u32[]{:S(2)}) collective-permute-start(bf16[128,4096]{1,0:T(8,128)(2,1)S(1)} %bitcast.631), channel_id=1, source_target_pairs={{0,16},{16,0},{1,17},{17,1},{2,18},{18,2},{3,19},{19,3},{4,20},{20... | collective-permute-start | bytes 3145736 | tf_op jit(solution)/shard_map/ppermute | solution.py:598
  1539.6 126.8 %collective-permute-start.4 = (f32[1,1152]{1,0:T(1,128)S(1)}, f32[1,1152]{1,0:T(1,128)S(1)}, u32[]{:S(2)}, u32[]{:S(2)}) collective-permute-start(f32[1,1152]{1,0:T(1,128)S(1)} %divide_multiply_fusion), channel_id=1, source_target_pairs={{0,16},{16,0},{1,17},{17,1},{2,18},{18,2},{3,19},{19,3},{4,20},{20... | collective-permute-start | bytes 13832 | tf_op jit(solution)/shard_map/ppermute | solution.py:592
  1541.9 122.6 %collective-permute-start.7 = (bf16[128,144]{0,1:T(8,128)(2,1)S(1)}, bf16[128,144]{0,1:T(8,128)(2,1)S(1)}, u32[]{:S(2)}, u32[]{:S(2)}) collective-permute-start(bf16[128,144]{0,1:T(8,128)(2,1)S(1)} %convert_element_type.352), channel_id=1, source_target_pairs={{0,16},{16,0},{1,17},{17,1},{2,18},{18,2},{3,19},{19,3},{4,20},{20... | collective-permute-start | bytes 110600 | tf_op jit(solution)/shard_map/ppermute | solution.py:599
  1644.4 22.0 %collective-permute-start.5 = (f32[1,648]{1,0:T(1,128)S(1)}, f32[1,648]{1,0:T(1,128)S(1)}, u32[]{:S(2)}, u32[]{:S(2)}) collective-permute-start(f32[1,648]{1,0:T(1,128)S(1)} %constant_dynamic-slice_fusion.1), channel_id=1, source_target_pairs={{0,16},{16,0},{1,17},{17,1},{2,18},{18,2},{3,19},{19,3},{4,20},{20... | collective-permute-start | bytes 7784 | tf_op jit(solution)/shard_map/ppermute | solution.py:593
  1664.5 6.3 collective-permute-start.10
  1890.2 2.3 collective-permute-start.9
  2076.2 14.0 collective-permute-start.8
  (159 other events, 1796.5 us)
Sparse Core Ops, SparseCore 0:
  11.4 114.2 all-gather.6
  129.2 92.5 all-gather.14
  223.3 61.2 all-gather.8
  286.0 62.6 all-gather.10
  352.0 135.0 all-gather.12
  1260.3 59.1 reduce-scatter.9
  1326.6 59.0 reduce-scatter.11
  1391.0 124.9 reduce-scatter.13
  1522.1 142.2 reduce-scatter.17
  1670.7 219.4 reduce-scatter.15
  1896.7 179.4 reduce-scatter.19

commit v2 on v1

v2 whole, which is shorter than its diff:
```python
import math

import jax
import jax.numpy as jnp
from jax import lax
from jax.experimental import pallas as pl
from jax.experimental.pallas import tpu as pltpu
from jax.sharding import PartitionSpec as P

HEADS = 16


epsilon = 1e-06
highest = lax.Precision.HIGHEST
masked_fill = -1e30
vmem_limit = 48 * 1024 * 1024


def product(left, right):
    return jnp.dot(left, right, preferred_element_type=jnp.float32)


def contract(left, right, left_dim, right_dim):
    return lax.dot_general(
        left, right, (((left_dim,), (right_dim,)), ((), ())), preferred_element_type=jnp.float32
    )


def call(body, grid, in_specs, out_specs, out_shape, name):
    return pl.pallas_call(
        body,
        grid=grid,
        in_specs=in_specs,
        out_specs=out_specs,
        out_shape=out_shape,
        name=name,
        compiler_params=pltpu.CompilerParams(vmem_limit_bytes=vmem_limit),
    )


def spatial_forward(query, key_value, frame_count):
    model_width, total_rows = query.shape
    head_size = model_width // HEADS
    rows = total_rows // frame_count
    keys = key_value.shape[1] // frame_count
    scale = 1.0 / math.sqrt(head_size)

    def body(q_ref, k_ref, v_ref, out_ref, lse_ref):
        scores = contract(k_ref[...], q_ref[...], 0, 0) * scale
        top = jnp.max(scores, axis=0, keepdims=True)
        weights = jnp.exp(scores - top)
        total = jnp.sum(weights, axis=0, keepdims=True)
        out = product(v_ref[...], weights.astype(jnp.bfloat16))
        out_ref[...] = (out / total).astype(jnp.bfloat16)
        lse_ref[0] = top + jnp.log(total)

    return call(
        body,
        (frame_count, HEADS),
        [
            pl.BlockSpec((head_size, rows), lambda f, h: (h, f)),
            pl.BlockSpec((head_size, keys), lambda f, h: (h, f)),
            pl.BlockSpec((head_size, keys), lambda f, h: (HEADS + h, f)),
        ],
        [
            pl.BlockSpec((head_size, rows), lambda f, h: (h, f)),
            pl.BlockSpec((1, 1, rows), lambda f, h: (f * HEADS + h, 0, 0)),
        ],
        [
            jax.ShapeDtypeStruct(query.shape, jnp.bfloat16),
            jax.ShapeDtypeStruct((frame_count * HEADS, 1, rows), jnp.float32),
        ],
        "spatial_forward",
    )(query, key_value, key_value)


def spatial_backward(query, key_value, log_total, upstream, frame_count, frame):
    model_width, total_rows = query.shape
    head_size = model_width // HEADS
    rows = total_rows // frame_count
    keys = key_value.shape[1] // frame_count
    scale = 1.0 / math.sqrt(head_size)

    def body(q_ref, k_ref, v_ref, lse_ref, up_ref, dq_ref, dkv_ref):
        query_head, key_head, up_head = (q_ref[...], k_ref[...], up_ref[...])
        probs = jnp.exp(contract(key_head, query_head, 0, 0) * scale - lse_ref[0])
        dkv_ref[1] = contract(up_head, probs.astype(jnp.bfloat16), 1, 1).astype(jnp.bfloat16)
        prob_grad = contract(v_ref[...], up_head, 0, 0)
        delta = jnp.sum(probs * prob_grad, axis=0, keepdims=True)
        score_grad = (probs * (prob_grad - delta)).astype(jnp.bfloat16)
        dq_ref[...] = (product(key_head, score_grad) * scale).astype(jnp.bfloat16)
        dkv_ref[0] = (contract(query_head, score_grad, 1, 1) * scale).astype(jnp.bfloat16)

    query_grad, pair_grad = call(
        body,
        (HEADS,),
        [
            pl.BlockSpec((head_size, rows), lambda h: (h, frame)),
            pl.BlockSpec((head_size, keys), lambda h: (h, frame)),
            pl.BlockSpec((head_size, keys), lambda h: (HEADS + h, frame)),
            pl.BlockSpec((1, 1, rows), lambda h: (frame * HEADS + h, 0, 0)),
            pl.BlockSpec((head_size, rows), lambda h: (h, frame)),
        ],
        [
            pl.BlockSpec((head_size, rows), lambda h: (h, 0)),
            pl.BlockSpec((2, head_size, keys), lambda h: (0, h, 0)),
        ],
        [
            jax.ShapeDtypeStruct((model_width, rows), jnp.bfloat16),
            jax.ShapeDtypeStruct((2, model_width, keys), jnp.bfloat16),
        ],
        "spatial_backward",
    )(query, key_value, key_value, log_total, upstream)
    return (query_grad, pair_grad.reshape(2 * model_width, keys))


def cross_probs_of(length_ref, q_ref, k_ref, scale):
    scores = contract(k_ref[...], q_ref[...], 0, 0) * scale
    live = lax.broadcasted_iota(jnp.int32, scores.shape, 0) < length_ref[0]
    scores = jnp.where(live, scores, masked_fill)
    weights = jnp.exp(scores - jnp.max(scores, axis=0, keepdims=True))
    return weights / jnp.sum(weights, axis=0, keepdims=True)


def cross_forward(length, query, text_pair):
    model_width, total_rows = query.shape
    head_size = model_width // HEADS
    keys = text_pair.shape[1]
    scale = 1.0 / math.sqrt(head_size)

    def body(length_ref, q_ref, k_ref, v_ref, out_ref):
        probs = cross_probs_of(length_ref, q_ref, k_ref, scale)
        out_ref[...] = product(v_ref[...], probs.astype(jnp.bfloat16)).astype(jnp.bfloat16)

    return call(
        body,
        (HEADS,),
        [
            pl.BlockSpec(memory_space=pltpu.SMEM),
            pl.BlockSpec((head_size, total_rows), lambda h: (h, 0)),
            pl.BlockSpec((head_size, keys), lambda h: (h, 0)),
            pl.BlockSpec((head_size, keys), lambda h: (HEADS + h, 0)),
        ],
        pl.BlockSpec((head_size, total_rows), lambda h: (h, 0)),
        jax.ShapeDtypeStruct(query.shape, jnp.bfloat16),
        "cross_forward",
    )(length, query, text_pair, text_pair)


def cross_backward(length, query, text_pair, upstream):
    model_width, total_rows = query.shape
    head_size = model_width // HEADS
    keys = text_pair.shape[1]
    scale = 1.0 / math.sqrt(head_size)

    def body(length_ref, q_ref, k_ref, v_ref, up_ref, dq_ref, dkv_ref):
        up_head = up_ref[...]
        probs = cross_probs_of(length_ref, q_ref, k_ref, scale)
        prob_grad = contract(v_ref[...], up_head, 0, 0)
        delta = jnp.sum(probs * prob_grad, axis=0, keepdims=True)
        score_grad = (probs * (prob_grad - delta)).astype(jnp.bfloat16)
        dq_ref[...] = (product(k_ref[...], score_grad) * scale).astype(jnp.bfloat16)
        dkv_ref[0] = contract(q_ref[...], score_grad, 1, 1) * scale
        dkv_ref[1] = contract(up_head, probs.astype(jnp.bfloat16), 1, 1)

    query_grad, pair_grad = call(
        body,
        (HEADS,),
        [
            pl.BlockSpec(memory_space=pltpu.SMEM),
            pl.BlockSpec((head_size, total_rows), lambda h: (h, 0)),
            pl.BlockSpec((head_size, keys), lambda h: (h, 0)),
            pl.BlockSpec((head_size, keys), lambda h: (HEADS + h, 0)),
            pl.BlockSpec((head_size, total_rows), lambda h: (h, 0)),
        ],
        [
            pl.BlockSpec((head_size, total_rows), lambda h: (h, 0)),
            pl.BlockSpec((2, head_size, keys), lambda h: (0, h, 0)),
        ],
        [
            jax.ShapeDtypeStruct(query.shape, jnp.bfloat16),
            jax.ShapeDtypeStruct((2, model_width, keys), jnp.float32),
        ],
        "cross_backward",
    )(length, query, text_pair, text_pair, upstream)
    return (query_grad, pair_grad.reshape(text_pair.shape))


def temporal_probs_of(live_ref, query_frame, key_frames, frame, scale):
    scores = []
    for index in range(3):
        score = jnp.sum(query_frame * key_frames[index], axis=0, keepdims=True) * scale
        if index != 1:
            score = jnp.where(live_ref[frame, index // 2] != 0, score, masked_fill)
        scores.append(score)
    top = jnp.maximum(jnp.maximum(scores[0], scores[1]), scores[2])
    weights = [jnp.exp(score - top) for score in scores]
    inverse = 1.0 / (weights[0] + weights[1] + weights[2])
    return [weight * inverse for weight in weights]


def temporal_forward(live, query, key_value, frame_count):
    model_width, total_rows = query.shape
    head_size = model_width // HEADS
    rows = total_rows // frame_count
    extended_rows = key_value.shape[1]
    scale = 1.0 / math.sqrt(head_size)

    def body(live_ref, q_ref, k_ref, v_ref, out_ref):
        for frame in range(frame_count):
            query_frame = q_ref[:, frame * rows : (frame + 1) * rows].astype(jnp.float32)
            spans = [slice((frame + j) * rows, (frame + j + 1) * rows) for j in range(3)]
            key_frames = [k_ref[:, span].astype(jnp.float32) for span in spans]
            probs = temporal_probs_of(live_ref, query_frame, key_frames, frame, scale)
            mixed = sum(
                prob * v_ref[:, span].astype(jnp.float32) for prob, span in zip(probs, spans)
            )
            out_ref[:, frame * rows : (frame + 1) * rows] = mixed.astype(jnp.bfloat16)

    return call(
        body,
        (HEADS,),
        [
            pl.BlockSpec(memory_space=pltpu.SMEM),
            pl.BlockSpec((head_size, total_rows), lambda h: (h, 0)),
            pl.BlockSpec((head_size, extended_rows), lambda h: (h, 0)),
            pl.BlockSpec((head_size, extended_rows), lambda h: (HEADS + h, 0)),
        ],
        pl.BlockSpec((head_size, total_rows), lambda h: (h, 0)),
        jax.ShapeDtypeStruct(query.shape, jnp.bfloat16),
        "temporal_forward",
    )(live, query, key_value, key_value)


def temporal_backward(live, query, key_value, upstream, frame_count):
    model_width, total_rows = query.shape
    head_size = model_width // HEADS
    rows = total_rows // frame_count
    extended_rows = key_value.shape[1]
    scale = 1.0 / math.sqrt(head_size)

    def body(live_ref, q_ref, k_ref, v_ref, up_ref, dq_ref, dkv_ref):
        key_sums = [None] * (frame_count + 2)
        value_sums = [None] * (frame_count + 2)
        for frame in range(frame_count):
            own = slice(frame * rows, (frame + 1) * rows)
            query_frame = q_ref[:, own].astype(jnp.float32)
            up_frame = up_ref[:, own]
            spans = [slice((frame + j) * rows, (frame + j + 1) * rows) for j in range(3)]
            key_frames = [k_ref[:, span].astype(jnp.float32) for span in spans]
            probs = temporal_probs_of(live_ref, query_frame, key_frames, frame, scale)
            prob_grads = [
                jnp.sum(up_frame * v_ref[:, span].astype(jnp.float32), axis=0, keepdims=True)
                for span in spans
            ]
            delta = sum(prob * grad for prob, grad in zip(probs, prob_grads))
            score_grads = [
                prob * (grad - delta) * scale for prob, grad in zip(probs, prob_grads)
            ]
            dq_ref[:, own] = sum(
                grad * key_frame for grad, key_frame in zip(score_grads, key_frames)
            ).astype(jnp.bfloat16)
            for j in range(3):
                key_part = score_grads[j] * query_frame
                value_part = probs[j] * up_frame
                at = frame + j
                key_sums[at] = key_part if key_sums[at] is None else key_sums[at] + key_part
                value_sums[at] = (
                    value_part if value_sums[at] is None else value_sums[at] + value_part
                )
        for at in range(frame_count + 2):
            dkv_ref[0, :, at * rows : (at + 1) * rows] = key_sums[at].astype(jnp.bfloat16)
            dkv_ref[1, :, at * rows : (at + 1) * rows] = value_sums[at].astype(jnp.bfloat16)

    query_grad, pair_grad = call(
        body,
        (HEADS,),
        [
            pl.BlockSpec(memory_space=pltpu.SMEM),
            pl.BlockSpec((head_size, total_rows), lambda h: (h, 0)),
            pl.BlockSpec((head_size, extended_rows), lambda h: (h, 0)),
            pl.BlockSpec((head_size, extended_rows), lambda h: (HEADS + h, 0)),
            pl.BlockSpec((head_size, total_rows), lambda h: (h, 0)),
        ],
        [
            pl.BlockSpec((head_size, total_rows), lambda h: (h, 0)),
            pl.BlockSpec((2, head_size, extended_rows), lambda h: (0, h, 0)),
        ],
        [
            jax.ShapeDtypeStruct(query.shape, jnp.bfloat16),
            jax.ShapeDtypeStruct((2, model_width, extended_rows), jnp.bfloat16),
        ],
        "temporal_backward",
    )(live, query, key_value, key_value, upstream)
    return (query_grad, pair_grad.reshape(key_value.shape))


def normalize(values):
    centred = values - jnp.mean(values, axis=-1, keepdims=True)
    reciprocal = lax.rsqrt(jnp.mean(centred * centred, axis=-1, keepdims=True) + epsilon)
    return (centred * reciprocal, reciprocal)


def normalize_back(upstream, normed, reciprocal):
    return reciprocal * (
        upstream
        - jnp.mean(upstream, axis=-1, keepdims=True)
        - normed * jnp.mean(upstream * normed, axis=-1, keepdims=True)
    )


def gelu_tanh(values):
    return jax.nn.gelu(values, approximate=True)


def gather_halves(is_first, lower, upper):
    return lax.all_gather(
        jnp.where(is_first, lower, upper), ("bucket", "frame", "seq"), axis=0, tiled=True
    )


def tree_bits():
    return [
        (axis, step)
        for axis in ("frame", "seq")
        for step in reversed(range(lax.axis_size(axis).bit_length() - 1))
    ]


def tree_order(turn):
    bits = tree_bits()
    last = bits[0]
    first = [bit for bit in bits[::-1] if bit != last]
    turn = turn % len(first)
    return first[turn:] + first[:turn] + [last]


def my_bit(bit):
    return (lax.axis_index(bit[0]) >> bit[1]) & 1


def across(value, bit):
    axis, step = bit
    return lax.ppermute(
        value, axis, [(i, i ^ (1 << step)) for i in range(lax.axis_size(axis))]
    )


def gather_tree(value):
    for bit in tree_bits()[::-1]:
        other = across(value, bit)
        mine = my_bit(bit) == 0
        value = jnp.concatenate(
            [jnp.where(mine, value, other), jnp.where(mine, other, value)], axis=0
        )
    return value


class Chain:
    def __init__(self, is_first, pair, turn):
        self.order = tree_order(turn)
        self.dims = tree_bits()
        self.is_first = is_first
        self.received = None
        if len(pair) == 2:
            lower, upper = pair
            self.kept = jnp.where(is_first, lower, upper)
            self.received = swapped(jnp.where(is_first, upper, lower))
        else:
            self.kept = pair[0]

    def advance(self):
        value = self.kept
        if self.received is not None:
            value = (
                value.astype(jnp.float32) + self.received.astype(jnp.float32)
            ).astype(value.dtype)
        if self.dims and value.ndim == 2:
            count = 1 << len(self.dims)
            value = value.reshape(
                (2,) * len(self.dims) + (value.shape[0] // count, value.shape[1])
            )
        if self.order:
            bit = self.order.pop(0)
            dim = self.dims.index(bit)
            self.dims.remove(bit)
            index = my_bit(bit)
            self.received = across(
                lax.dynamic_index_in_dim(value, 1 - index, dim, keepdims=False), bit
            )
            self.kept = lax.dynamic_index_in_dim(value, index, dim, keepdims=False)
        else:
            self.kept = value
            self.received = None

    def finish(self):
        while self.received is not None or self.order:
            self.advance()
        return self.kept


def tick(main, chains):
    main, received = lax.optimization_barrier((main, [chain.received for chain in chains]))
    for chain, value in zip(chains, received):
        chain.received = value
        chain.advance()
    return main


def both_of(chain):
    own = chain.finish()
    other = swapped(own)
    return (
        jnp.where(chain.is_first, own, other).astype(jnp.float32),
        jnp.where(chain.is_first, other, own).astype(jnp.float32),
    )


def low(value):
    return value.astype(jnp.bfloat16)


def swapped(value):
    return lax.ppermute(value, "bucket", [(0, 1), (1, 0)])


def per_device(
    latent,
    condition,
    text,
    text_len,
    clip_ids,
    video_flag,
    ada_weight,
    text_kv_weight,
    qkv_weight,
    proj_weight,
    cross_q_weight,
    cross_proj_weight,
    up_weight,
    down_weight,
    temporal_qkv_weight,
    temporal_proj_weight,
    cotangent,
):
    frame_count, row_count, width = (latent.shape[1], latent.shape[2], latent.shape[3])
    total_rows = frame_count * row_count
    seq_size = lax.axis_size("seq")
    frame_size = lax.axis_size("frame")
    shards = seq_size * frame_size
    is_first = lax.axis_index("bucket") == 0
    ff_width = up_weight.shape[1]
    shard_rows = up_weight.shape[0]
    ff_blocks = ff_width // width
    half_ff = ff_width // 2

    shifts = [
        [((i + s) % seq_size, i) for i in range(seq_size)] for s in range(1, seq_size)
    ]
    latent_rest = [lax.ppermute(latent[0], "seq", shift) for shift in shifts]

    gathered_a = gather_halves(
        is_first,
        qkv_weight,
        jnp.concatenate([proj_weight, cross_q_weight, cross_proj_weight], axis=1),
    )
    up_mixed = (
        up_weight.reshape(shard_rows, shards, ff_blocks, shard_rows)
        .transpose(0, 2, 1, 3)
        .reshape(shard_rows, ff_width)
    )
    down_wide = (
        down_weight.reshape(ff_blocks, shard_rows, width)
        .transpose(1, 0, 2)
        .reshape(shard_rows, ff_width)
    )
    gathered_b = gather_halves(
        is_first,
        jnp.concatenate([up_mixed[:, :half_ff], down_wide[:, :half_ff]], axis=1),
        jnp.concatenate([up_mixed[:, half_ff:], down_wide[:, half_ff:]], axis=1),
    )

    silu_cond = jax.nn.silu(condition.astype(jnp.float32))
    mod_part = jnp.dot(silu_cond, ada_weight.astype(jnp.float32), precision=highest)
    modulation = gather_tree(mod_part).reshape(9, width)
    text_part = contract(text_kv_weight, text[0], 0, 1).astype(jnp.bfloat16)
    text_pair = gather_tree(text_part)

    inputs = latent[0].reshape(total_rows, width).astype(jnp.float32)
    normed_a, recip_a = normalize(inputs)
    hidden_a = (normed_a * (1.0 + modulation[1]) + modulation[0]).astype(jnp.bfloat16)
    normed_rest = [
        normalize(rest.reshape(total_rows, width).astype(jnp.float32))[0] for rest in latent_rest
    ]
    hidden_rest = [
        (normed * (1.0 + modulation[1]) + modulation[0]).astype(jnp.bfloat16)
        for normed in normed_rest
    ]
    hidden_all = jnp.concatenate(
        [part.reshape(frame_count, row_count, width) for part in [hidden_a] + hidden_rest], axis=1
    ).reshape(frame_count * seq_size * row_count, width)
    query_full = gathered_a[:width, :width]
    pair_full = gathered_a[:width, width:]
    proj_full = gathered_a[width:, :width]
    cross_q_full = gathered_a[width:, width : 2 * width]
    cross_proj_full = gathered_a[width:, 2 * width :]
    query = contract(query_full, hidden_a, 0, 1).astype(jnp.bfloat16)
    key_value = contract(pair_full, hidden_all, 0, 1).astype(jnp.bfloat16)
    attended, log_total = spatial_forward(query, key_value, frame_count)
    branch_a = contract(attended, proj_full, 0, 0)
    after_a = inputs + modulation[2] * branch_a
    after_low = after_a.astype(jnp.bfloat16)
    cross_query = contract(cross_q_full, after_low, 0, 1).astype(jnp.bfloat16)
    cross_out = cross_forward(text_len, cross_query, text_pair)
    after_c = after_a + contract(cross_out, cross_proj_full, 0, 0)
    normed_m, recip_m = normalize(after_c)
    hidden_m = (normed_m * (1.0 + modulation[4]) + modulation[3]).astype(jnp.bfloat16)

    temporal_lower, temporal_upper = lax.optimization_barrier(
        (
            jnp.concatenate([temporal_qkv_weight[:, :width], temporal_proj_weight], axis=1),
            temporal_qkv_weight[:, width:],
            query,
        )
    )[:2]
    gathered_c = gather_halves(is_first, temporal_lower, temporal_upper)
    up_halves = (gathered_b[:width, :half_ff], gathered_b[width:, :half_ff])
    per_half = ff_blocks // 2
    down_halves = (gathered_b[:width, half_ff:], gathered_b[width:, half_ff:])
    down_parts = [
        down_halves[index // per_half][
            :, width * (index % per_half) : width * (index % per_half + 1)
        ]
        for index in range(ff_blocks)
    ]
    tquery_full = gathered_c[:width, :width]
    tproj_full = gathered_c[:width, width:]
    tpair_full = gathered_c[width:]

    upward_halves = [product(hidden_m, part) for part in up_halves]
    activated_halves = [gelu_tanh(part).astype(jnp.bfloat16) for part in upward_halves]
    activated_parts = [
        activated_halves[index // per_half][
            :, width * (index % per_half) : width * (index % per_half + 1)
        ]
        for index in range(ff_blocks)
    ]
    branch_m = sum(product(left, right) for left, right in zip(activated_parts, down_parts))
    after_m = after_c + modulation[5] * branch_m
    normed_t, recip_t = normalize(after_m)
    hidden_t = (normed_t * (1.0 + modulation[7]) + modulation[6]).astype(jnp.bfloat16)
    ahead = [(i, i + 1) for i in range(frame_size - 1)]
    back = [(i + 1, i) for i in range(frame_size - 1)]
    hidden_prev = lax.ppermute(hidden_t[total_rows - row_count :], "frame", ahead)
    hidden_next = lax.ppermute(hidden_t[:row_count], "frame", back)
    hidden_ext = jnp.concatenate([hidden_prev, hidden_t, hidden_next], axis=0)
    tquery = contract(tquery_full, hidden_t, 0, 1).astype(jnp.bfloat16)
    tpair = contract(tpair_full, hidden_ext, 0, 1).astype(jnp.bfloat16)
    first_frame = lax.axis_index("frame") * frame_count
    clips_ext = jnp.concatenate(
        [jnp.full((1,), -1, jnp.int32), clip_ids[0], jnp.full((1,), -1, jnp.int32)]
    )
    clips_local = lax.dynamic_slice_in_dim(clips_ext, first_frame, frame_count + 2)
    live = jnp.stack(
        [clips_local[:-2] == clips_local[1:-1], clips_local[2:] == clips_local[1:-1]], axis=1
    ).astype(jnp.int32)
    flag_local = lax.dynamic_slice_in_dim(video_flag[0], first_frame, frame_count).astype(
        jnp.float32
    )
    mixed = temporal_forward(live, tquery, tpair, frame_count)
    branch_t = contract(mixed, tproj_full, 0, 0)
    flag_rows = jnp.repeat(flag_local, row_count)[:, None]
    result_rows = after_m + flag_rows * modulation[8] * branch_t
    result = result_rows.astype(jnp.bfloat16).reshape(latent.shape)

    result_grad = cotangent[0].reshape(total_rows, width).astype(jnp.float32)
    gate_t_grad = jnp.sum(flag_rows * branch_t * result_grad, axis=0)
    branch_t_grad = (flag_rows * modulation[8] * result_grad).astype(jnp.bfloat16)
    mixed_grad = contract(tproj_full, branch_t_grad, 1, 1)
    tquery_grad, tpair_grad = temporal_backward(live, tquery, tpair, mixed_grad, frame_count)
    ext_grad = contract(tpair_grad, tpair_full, 0, 1)
    to_prev = lax.ppermute(low(ext_grad[:row_count]), "frame", back)
    to_next = lax.ppermute(low(ext_grad[-row_count:]), "frame", ahead)
    tpair_weight_grad = low(contract(hidden_ext, tpair_grad, 0, 1))
    tquery_weight_grad = low(contract(hidden_t, tquery_grad, 0, 1))
    tproj_weight_grad = low(contract(mixed, branch_t_grad, 1, 0))
    hidden_t_grad = ext_grad[row_count:-row_count] + contract(tquery_grad, tquery_full, 0, 1)
    hidden_t_grad = jnp.concatenate(
        [
            hidden_t_grad[:row_count] + to_next.astype(jnp.float32),
            hidden_t_grad[row_count : total_rows - row_count],
            hidden_t_grad[total_rows - row_count :] + to_prev.astype(jnp.float32),
        ],
        axis=0,
    )
    hidden_t_grad, tpair_weight_grad, tquery_weight_grad, tproj_weight_grad = (
        lax.optimization_barrier(
            (hidden_t_grad, tpair_weight_grad, tquery_weight_grad, tproj_weight_grad)
        )
    )
    chain_tqk = Chain(is_first, (tquery_weight_grad, tpair_weight_grad[:, :width]), 0)
    chain_tpv = Chain(is_first, (tproj_weight_grad, tpair_weight_grad[:, width:]), 1)
    chains_t = [chain_tqk, chain_tpv]
    grad_m = result_grad + normalize_back(hidden_t_grad * (1.0 + modulation[7]), normed_t, recip_t)
    gate_m_grad = jnp.sum(branch_m * grad_m, axis=0)
    branch_m_grad = low(modulation[5] * grad_m)
    upward_grads = []
    for index in range(2):
        activated_grad = jnp.concatenate(
            [
                contract(branch_m_grad, part, 1, 1)
                for part in down_parts[index * per_half : (index + 1) * per_half]
            ],
            axis=1,
        )
        if index == 0:
            activated_grad = tick(activated_grad, chains_t)
        gelu_back = jax.vjp(gelu_tanh, upward_halves[index])[1]
        upward_grads.append(low(gelu_back(activated_grad)[0]))
    hidden_m_grad = contract(upward_grads[0], up_halves[0], 1, 1) + contract(
        upward_grads[1], up_halves[1], 1, 1
    )
    hidden_m_grad = tick(hidden_m_grad, chains_t)
    up_grads = [low(contract(hidden_m, part, 0, 0)) for part in upward_grads]
    down_grads = [low(contract(part, branch_m_grad, 0, 0)) for part in activated_parts]
    hidden_m_grad, up_grads, down_grads = lax.optimization_barrier(
        (hidden_m_grad, up_grads, down_grads)
    )
    chains_m = [
        Chain(
            is_first,
            (
                up_grads[0][:, width * index : width * (index + 1)],
                up_grads[1][:, width * index : width * (index + 1)],
            ),
            index,
        )
        for index in range(per_half)
    ] + [
        Chain(is_first, (down_grads[index], down_grads[per_half + index]), per_half + index)
        for index in range(per_half)
    ]
    hidden_m_grad = tick(hidden_m_grad, chains_t)
    grad_c = grad_m + normalize_back(hidden_m_grad * (1.0 + modulation[4]), normed_m, recip_m)
    cross_branch_grad = low(grad_c)
    cross_out_grad = low(contract(cross_proj_full, cross_branch_grad, 1, 1))
    cross_out_grad = tick(cross_out_grad, chains_t + chains_m)
    cross_query_grad, text_grad = cross_backward(text_len, cross_query, text_pair, cross_out_grad)
    chain_text = Chain(is_first, (low(text_grad),), 1)
    chain_text.advance()
    grad_a = grad_c + contract(cross_query_grad, cross_q_full, 0, 1)
    gate_a_grad = jnp.sum(branch_a * grad_a, axis=0)
    branch_a_grad = low(modulation[2] * grad_a)
    attended_grad = low(contract(proj_full, branch_a_grad, 1, 1))
    attended_grad = tick(attended_grad, chains_t + [chain_text])
    proj_grad = low(contract(attended, branch_a_grad, 1, 0))
    cross_q_grad = low(contract(after_low, cross_query_grad, 0, 1))
    cross_proj_grad = low(contract(cross_out, cross_branch_grad, 1, 0))
    attended_grad, proj_grad, cross_q_grad, cross_proj_grad = lax.optimization_barrier(
        (attended_grad, proj_grad, cross_q_grad, cross_proj_grad)
    )
    chain_pq = Chain(is_first, (proj_grad, cross_q_grad), 2)
    attended_grad = tick(attended_grad, chains_m + [chain_text])
    query_grads, pair_grads = ([], [])
    for frame in range(frame_count):
        query_grad, pair_grad = spatial_backward(
            query, key_value, log_total, attended_grad, frame_count, frame
        )
        query_grads.append(query_grad)
        pair_grads.append(pair_grad)
        if frame == 0:
            query_grads[0], attended_grad = tick(
                (query_grads[0], attended_grad), chains_m + [chain_pq, chain_text]
            )
    query_grad = jnp.concatenate(query_grads, axis=1)
    pair_grad = jnp.concatenate(pair_grads, axis=1)
    pair_grad = tick(pair_grad, chains_m + [chain_pq, chain_text])
    all_grad = contract(pair_grad, pair_full, 0, 1).reshape(
        frame_count, seq_size, row_count, width
    )
    rest_grad = [
        lax.ppermute(
            low(all_grad[:, s + 1]), "seq", [(j, i) for i, j in shifts[s]]
        )
        for s in range(seq_size - 1)
    ]
    pair_weight_grad = low(contract(hidden_all, pair_grad, 0, 1))
    chain_vp = Chain(is_first, (pair_weight_grad[:, width:], cross_proj_grad), 1)
    query_weight_grad = low(contract(hidden_a, query_grad, 0, 1))
    chain_qk = Chain(is_first, (query_weight_grad, pair_weight_grad[:, :width]), 2)
    own_grad = all_grad[:, 0].reshape(total_rows, width) + contract(query_grad, query_full, 0, 1)
    shift_a_grad = jnp.sum(own_grad, axis=0)
    scale_a_grad = jnp.sum(own_grad * normed_a, axis=0)
    for s in range(seq_size - 1):
        rest_rows = all_grad[:, s + 1].reshape(total_rows, width)
        shift_a_grad = shift_a_grad + jnp.sum(rest_rows, axis=0)
        scale_a_grad = scale_a_grad + jnp.sum(rest_rows * normed_rest[s], axis=0)
    hidden_a_grad = sum([rest.astype(jnp.float32).reshape(total_rows, width) for rest in rest_grad], own_grad)
    input_grad = grad_a + normalize_back(hidden_a_grad * (1.0 + modulation[1]), normed_a, recip_a)
    latent_grad = input_grad.reshape(latent.shape)
    mod_grad = jnp.stack(
        [
            shift_a_grad,
            scale_a_grad,
            gate_a_grad,
            jnp.sum(hidden_m_grad, axis=0),
            jnp.sum(hidden_m_grad * normed_m, axis=0),
            gate_m_grad,
            jnp.sum(hidden_t_grad, axis=0),
            jnp.sum(hidden_t_grad * normed_t, axis=0),
            gate_t_grad,
        ]
    ).reshape(shards, 9 * width // shards)
    mod_slice = Chain(is_first, (mod_grad,), 0).finish()
    text_low = chain_text.finish()
    silu_pair = jnp.concatenate([silu_cond, swapped(silu_cond)], axis=0)
    mod_pair = jnp.concatenate([mod_slice, swapped(mod_slice)], axis=0)
    ada_grad = lax.dot_general(
        silu_pair, mod_pair, (((0,), (0,)), ((), ())), precision=highest
    )
    text_both = jnp.concatenate([text[0], swapped(text[0])], axis=0)
    slice_both = jnp.concatenate([text_low, swapped(text_low)], axis=1)
    text_kv_grad = contract(text_both, slice_both, 0, 1)
    query_shard, key_shard = both_of(chain_qk)
    value_shard, cross_proj_shard = both_of(chain_vp)
    proj_shard, cross_q_shard = both_of(chain_pq)
    tquery_shard, tkey_shard = both_of(chain_tqk)
    tproj_shard, tvalue_shard = both_of(chain_tpv)
    ff_shards = [both_of(chain) for chain in chains_m]
    up_shard = (
        jnp.concatenate(
            [pair[side] for side in range(2) for pair in ff_shards[:per_half]], axis=1
        )
        .reshape(shard_rows, ff_blocks, shards, shard_rows)
        .transpose(0, 2, 1, 3)
        .reshape(shard_rows, ff_width)
    )
    down_shard = jnp.concatenate(
        [pair[side] for side in range(2) for pair in ff_shards[per_half:]], axis=0
    )
    return (
        result,
        latent_grad,
        ada_grad,
        text_kv_grad,
        jnp.concatenate([query_shard, key_shard, value_shard], axis=1),
        proj_shard,
        cross_q_shard,
        cross_proj_shard,
        up_shard,
        down_shard,
        jnp.concatenate([tquery_shard, tkey_shard, tvalue_shard], axis=1),
        tproj_shard,
    )


def solution(mesh):
    return jax.shard_map(
        per_device,
        mesh=mesh,
        in_specs=(
            P("bucket", "frame", "seq", None),
            P("bucket", None),
            P("bucket", None, None),
            P("bucket"),
            P("bucket", None),
            P("bucket", None),
            P(None, ("frame", "seq")),
            P(None, ("frame", "seq")),
            P(("frame", "seq"), None),
            P(("frame", "seq"), None),
            P(("frame", "seq"), None),
            P(("frame", "seq"), None),
            P(("frame", "seq"), None),
            P(("frame", "seq"), None),
            P(("frame", "seq"), None),
            P(("frame", "seq"), None),
            P("bucket", "frame", "seq", None),
        ),
        out_specs=(
            P("bucket", "frame", "seq", None),
            P("bucket", "frame", "seq", None),
            P(None, ("frame", "seq")),
            P(None, ("frame", "seq")),
            P(("frame", "seq"), None),
            P(("frame", "seq"), None),
            P(("frame", "seq"), None),
            P(("frame", "seq"), None),
            P(("frame", "seq"), None),
            P(("frame", "seq"), None),
            P(("frame", "seq"), None),
            P(("frame", "seq"), None),
        ),
        check_vma=False,
    )
```

time: 2110 us -> 1230 us (0.58)
  local copies, waits for them, and re-layouts: 336 us -> 70.1 us
  matrix products: 624 us -> 378 us
  waiting for transfers between devices: 594 us -> 370 us
  blocking collectives: 203 us -> 0 us
  other arithmetic: 308 us -> 146 us
  Pallas kernels: 0 us -> 157 us
  starting transfers between devices: 15.7 us -> 82.5 us
    reduce_scatter x5 -> x0, waiting for transfers between devices: 239 us -> none  [the longest x2 239 us: scatter_halves(): lax.psum_scatter(stacked, ('bucket', 'frame', 'seq'), scatter_dimension=0...]
    unnamed x12 -> x3, waiting for transfers between devices: 180 us -> 0.05 us
    ppermute x11 -> x80, waiting for transfers between devices: 42.9 us -> 222 us  [the longest x52 158 us: across(): lax.ppermute(value, axis, [(i, i ^ 1 << step) for i in range(lax.axis_siz...]
    dot_general x60 -> x38, matrix products: 473 us -> 312 us  [contract(): lax.dot_general(left, right, (((left_dim,), (right_dim,)), ((), ())), pre...]
    unnamed x2 -> x0, blocking collectives: 157 us -> none
    pallas_call x0 -> x7, Pallas kernels: none -> 157 us  [the longest x2 68.2 us: spatial_backward(): call(body, (HEADS,), [pl.BlockSpec((head_size, rows), lambda h: (h, frame...]
    reshape x27 -> x5, local copies, waits for them, and re-layouts: 134 us -> 12.4 us  [the longest x3 11 us: per_device(): up_shard = jnp.concatenate([pair[side] for side in range(2) for pair in f...]
    all_gather x3, waiting for transfers between devices: 36.3 us -> 148 us  [gather_halves(): lax.all_gather(jnp.where(is_first, lower, upper), ('bucket', 'frame', 'se...]
  transfers between devices with their start and end apart: 22 -> 83, of which waited for: 9 -> 35; matrix products, arithmetic and copies ran while one was open for 37% -> 38% of each run, Pallas kernels for 0% -> 11%
where the time goes in v2:
time: 1230 us; the launch traced here: 1220 us
  matrix products  378 us (31%)
  waiting for transfers between devices  370 us (30%)
  Pallas kernels  157 us (13%)
  other arithmetic  146 us (12%)
  starting transfers between devices  82.5 us (7%)
  local copies, waits for them, and re-layouts  70.1 us (6%)
  between operations  17.4 us (1%)
    dot_general x38, matrix products, contract(): lax.dot_general(left, right, (((left_dim,), (right_dim,)), ((), ())), pre...  312 us
    ppermute x52, waiting for transfers between devices, across(): lax.ppermute(value, axis, [(i, i ^ 1 << step) for i in range(lax.axis_siz...  158 us
    all_gather x3, waiting for transfers between devices, gather_halves(): lax.all_gather(jnp.where(is_first, lower, upper), ('bucket', 'frame', 'se...  148 us
    pallas_call x2, Pallas kernels, spatial_backward(): call(body, (HEADS,), [pl.BlockSpec((head_size, rows), lambda h: (h, frame...  68.2 us
    ppermute x52, starting transfers between devices, across(): lax.ppermute(value, axis, [(i, i ^ 1 << step) for i in range(lax.axis_siz...  65.8 us
    dot_general x6, matrix products, product(): return jnp.dot(left, right, preferred_element_type=jnp.float32)  59.4 us
    convert_element_type x45, other arithmetic, advance(): value = (value.astype(jnp.float32) + self.received.astype(jnp.float32)).a...  53.5 us
    pallas_call x1, Pallas kernels, spatial_forward(): call(body, (frame_count, HEADS), [pl.BlockSpec((head_size, rows), lambda...  37.4 us
  transfers between devices with their start and end apart: 83, of which 35 were waited for; matrix products, arithmetic and copies ran while one was open for 38% of the time, Pallas kernels for 11%

profile of v2, /device:TPU:0, one launch (start us, length us, event | category | flops | bytes accessed | tf_op | source)
XLA Modules:
  0.0 1221.1 jit_solution(790486059705969899)
XLA Ops:
  46.2 97.4 %all-gather.4.cloned.1.call-done = bf16[2304,3456]{1,0:T(8,128)(2,1)} async-done(((bf16[72,3456]{1,0:T(8,128)(2,1)}), bf16[2304,3456]{1,0:T(8,128)(2,1)}) %all-gather.4.cloned.1.call-update) | async-done | bytes 15925264 | tf_op jit(solution)/shard_map/all_gather | solution.py:317
  156.4 11.4 collective-permute-done.7
  168.5 18.4 %collective-permute-done.8 = bf16[1152,128]{1,0:T(8,128)(2,1)S(1)} collective-permute-done((bf16[1152,128]{1,0:T(8,128)(2,1)S(1)}, bf16[1152,128]{1,0:T(8,128)(2,1)S(1)}, u32[]{:S(2)}, u32[]{:S(2)}) %collective-permute-start.8) | collective-permute-done | bytes 294944 | tf_op jit(solution)/shard_map/ppermute | solution.py:344
  198.3 17.2 %convolution_convert_fusion.3.k_ref.v_ref = bf16[2304,2048]{1,0:T(8,128)(2,1)} fusion(bf16[2048,1152]{1,0:T(8,128)(2,1)S(1)} %bitcast.443, bf16[2304,3456]{1,0:T(8,128)(2,1)} %all-gather.4.cloned.1.call-done), kind=kOutput, calls=%fused_computation.7 | convolution fusion | flops 10876354560 | bytes 19464192 | tf_op jit(solution)/shard_map/dot_general | solution.py:24
  215.5 37.4 %spatial_forward.1 = (bf16[1152,1024]{1,0:T(8,128)(2,1)S(1)}, f32[32,1,512]{2,1,0:T(1,128)S(1)}) custom-call(bf16[1152,1024]{1,0:T(8,128)(2,1)S(1)} %convolution_convert_fusion.20.q_ref, bf16[2304,2048]{1,0:T(8,128)(2,1)} %convolution_convert_fusion.3.k_ref.v_ref, bf16[2304,2048]{1,0:T(8,128)(2,1)} %convolution_convert_fusion.3.k_ref.v_ref), custom_call_target="tpu_custom_call" | custom-call | tf_op jit(solution)/shard_map/spatial_forward/pallas_call | solution.py:57
  291.7 12.6 %multiply_convert_fusion.1 = (bf16[1024,2304]{1,0:T(8,128)(2,1)S(1)}, f32[1024,2304]{1,0:T(8,128)}) fusion(bf16[1024,1152]{1,0:T(8,128)(2,1)} %add_convert_fusion.10, bf16[2304,4608]{1,0:T(8,128)(2,1)} %all-gather.6.cloned.1.call-done), kind=kOutput, calls=%fused_computation.28 | convolution fusion | flops 5457051648 | bytes 21823488 | tf_op jit(solution)/shard_map/dot_general | solution.py:20
  318.4 12.5 %multiply_convert_fusion = (bf16[1024,2304]{1,0:T(8,128)(2,1)S(1)}, f32[1024,2304]{1,0:T(8,128)}) fusion(bf16[1024,1152]{1,0:T(8,128)(2,1)S(1)} %copy-done.57, bf16[2304,4608]{1,0:T(8,128)(2,1)} %all-gather.6.cloned.1.call-done), kind=kOutput, calls=%fused_computation.27 | convolution fusion | flops 5457051648 | bytes 21823488 | tf_op jit(solution)/shard_map/dot_general | solution.py:20
  339.6 11.6 fusion.181
  365.2 45.9 %all-gather.8.cloned.1.call-done = bf16[2304,2304]{1,0:T(8,128)(2,1)} async-done(((bf16[72,2304]{1,0:T(8,128)(2,1)}), bf16[2304,2304]{1,0:T(8,128)(2,1)}) %all-gather.8.cloned.1.call-update) | async-done | bytes 10616848 | tf_op jit(solution)/shard_map/all_gather | solution.py:317
  417.0 17.5 %convolution_convert_fusion.2.k_ref.v_ref = bf16[2304,2048]{1,0:T(8,128)(2,1)} fusion(bf16[2304,2304]{1,0:T(8,128)(2,1)} %all-gather.8.cloned.1.call-done, bf16[512,1152]{1,0:T(8,128)(2,1)} %collective-permute-done.10, bf16[1024,1152]{1,0:T(8,128)(2,1)S(1)} %copy-done.28, bf16[512,1152]{1,0:T(8,128)(2,1)} %collective-permute-done.9), kind=kOutput, calls=%fused_computation.6 | convolution fusion | flops 10890510336 | bytes 19464192 | tf_op jit(solution)/shard_map/dot_general | solution.py:24
  434.5 10.9 temporal_forward.1
  456.6 16.6 %temporal_backward.1 = (bf16[1152,1024]{1,0:T(8,128)(2,1)S(1)}, bf16[2,1152,2048]{2,1,0:T(8,128)(2,1)}) custom-call(s32[2,2]{1,0:T(2,128)S(1)} %add_convert_fusion.12.live_ref, bf16[1152,1024]{1,0:T(8,128)(2,1)S(1)} %convolution_convert_fusion.18.q_ref, bf16[2304,2048]{1,0:T(8,128)(2,1)} %convolution_convert_fusion.2.k_ref.v_ref, ...), custom_call_target="tpu_custom_call" | custom-call | tf_op jit(solution)/shard_map/temporal_backward/pallas_call | solution.py:275
  473.2 19.0 %fusion.187 = (bf16[2048,1152]{1,0:T(8,128)(2,1)S(1)}, f32[2048,1152]{1,0:T(8,128)}) fusion(bf16[2304,2048]{1,0:T(8,128)(2,1)} %bitcast.471, bf16[2304,2304]{1,0:T(8,128)(2,1)} %all-gather.8.cloned.1.call-done), kind=kOutput, calls=%fused_computation.473 | convolution fusion | flops 10873995264 | bytes 28901376 | tf_op jit(solution)/shard_map/dot_general | solution.py:24
  495.6 14.5 %convolution_convert_fusion.5 = bf16[1152,2304]{1,0:T(8,128)(2,1)S(1)} fusion(bf16[2304,2048]{1,0:T(8,128)(2,1)} %bitcast.472, bf16[512,1152]{1,0:T(8,128)(2,1)} %collective-permute-done.10, bf16[1024,1152]{1,0:T(8,128)(2,1)S(1)} %copy-done.29, bf16[512,1152]{1,0:T(8,128)(2,1)} %collective-permute-done.9), kind=kOutput, calls=%fused_computation.9 | convolution fusion | flops 10888445952 | bytes 19464192 | tf_op jit(solution)/shard_map/dot_general | solution.py:24
  521.2 23.8 %collective-permute-done.11 = bf16[512,1152]{1,0:T(8,128)(2,1)S(1)} collective-permute-done((bf16[512,1152]{1,0:T(8,128)(2,1)S(1)}, bf16[512,1152]{1,0:T(8,128)(2,1)S(1)}, u32[]{:S(2)}, u32[]{:S(2)}) %collective-permute-start.11) | collective-permute-done | bytes 1179680 | tf_op jit(solution)/shard_map/ppermute | solution.py:583
  552.5 11.8 fusion.26
  606.3 9.9 fusion.85
  623.2 10.6 fusion.45
  651.5 9.1 convolution_convert_fusion
  693.2 10.8 fusion.56
  704.1 14.8 %collective-permute-done.16 = bf16[2,2,2,72,1152]{4,3,0,2,1:T(8,128)(2,1)} collective-permute-done((bf16[2,2,2,72,1152]{4,3,0,2,1:T(8,128)(2,1)}, bf16[2,2,2,72,1152]{4,3,0,2,1:T(8,128)(2,1)}, u32[]{:S(2)}, u32[]{:S(2)}) %collective-permute-start.16) | collective-permute-done | bytes 1327136 | tf_op jit(solution)/shard_map/ppermute | solution.py:344
  780.3 15.4 %cross_backward.1 = (bf16[1152,1024]{1,0:T(8,128)(2,1)S(1)}, f32[2,1152,128]{2,1,0:T(8,128)S(1)}) custom-call(s32[1]{0:T(128)S(6)} %copy.140.length_ref, bf16[1152,1024]{1,0:T(8,128)(2,1)} %copy-done.4, bf16[2304,128]{1,0:T(8,128)(2,1)S(1)} %copy-done.3, bf16[2304,128]{1,0:T(8,128)(2,1)S(1)} %copy-done.3, bf16[1152,1024]{1,0:T(8,128)(2,1)} %convolution_convert_fusion.17.up_ref), custom_call_target="tpu_custom_call" | custom-call | tf_op jit(solution)/shard_map/cross_backward/pallas_call | solution.py:166
  848.7 16.1 %collective-permute-done.29 = bf16[2,2,2,72,1152]{4,3,0,2,1:T(8,128)(2,1)S(1)} collective-permute-done((bf16[2,2,2,72,1152]{4,3,0,2,1:T(8,128)(2,1)S(1)}, bf16[2,2,2,72,1152]{4,3,0,2,1:T(8,128)(2,1)S(1)}, u32[]{:S(2)}, u32[]{:S(2)}) %collective-permute-start.29) | collective-permute-done | bytes 1327136 | tf_op jit(solution)/shard_map/ppermute | solution.py:344
  878.8 34.1 %spatial_backward.2 = (bf16[1152,512]{1,0:T(8,128)(2,1)S(1)}, bf16[2,1152,1024]{2,1,0:T(8,128)(2,1)}) custom-call(bf16[1152,1024]{1,0:T(8,128)(2,1)S(1)} %convolution_convert_fusion.20.q_ref, bf16[2304,2048]{1,0:T(8,128)(2,1)} %convolution_convert_fusion.3.k_ref.v_ref, bf16[2304,2048]{1,0:T(8,128)(2,1)} %convolution_convert_fusion.3.k_ref.v_ref, ...), custom_call_target="tpu_custom_call" | custom-call | tf_op jit(solution)/shard_map/spatial_backward/pallas_call | solution.py:94
  930.1 34.1 %spatial_backward.3 = (bf16[1152,512]{1,0:T(8,128)(2,1)S(1)}, bf16[2,1152,1024]{2,1,0:T(8,128)(2,1)}) custom-call(bf16[1152,1024]{1,0:T(8,128)(2,1)S(1)} %convolution_convert_fusion.20.q_ref, bf16[2304,2048]{1,0:T(8,128)(2,1)} %convolution_convert_fusion.3.k_ref.v_ref, bf16[2304,2048]{1,0:T(8,128)(2,1)} %convolution_convert_fusion.3.k_ref.v_ref, ...), custom_call_target="tpu_custom_call" | custom-call | tf_op jit(solution)/shard_map/spatial_backward/pallas_call | solution.py:94
  989.3 13.1 %convolution_convert_fusion.4 = bf16[1152,2304]{1,0:T(8,128)(2,1)S(1)} fusion(bf16[2048,1152]{1,0:T(8,128)(2,1)} %bitcast.444, bf16[2304,2048]{1,0:T(8,128)(2,1)S(1)} %pad_maximum_fusion.2), kind=kOutput, calls=%fused_computation.8 | convolution fusion | flops 10874290176 | bytes 19464192 | tf_op jit(solution)/shard_map/dot_general | solution.py:24
  1004.7 9.7 broadcast_select_fusion.1
  1014.4 16.8 %fusion.53 = f32[2048,1152]{1,0:T(8,128)S(1)} fusion(bf16[2304,2048]{1,0:T(8,128)(2,1)} %copy-done.26, bf16[2304,3456]{1,0:T(8,128)(2,1)} %all-gather.4.cloned.1.call-done), kind=kOutput, calls=%fused_computation.120 | convolution fusion | flops 10871635968 | bytes 24182784 | tf_op jit(solution)/shard_map/dot_general | solution.py:24
  1072.7 35.9 %collective-permute-done.45 = bf16[2,512,1152]{2,1,0:T(8,128)(2,1)} collective-permute-done((bf16[2,512,1152]{2,1,0:T(8,128)(2,1)}, bf16[2,512,1152]{2,1,0:T(8,128)(2,1)}, u32[]{:S(2)}, u32[]{:S(2)}) %collective-permute-start.45) | collective-permute-done | bytes 2359328 | tf_op jit(solution)/shard_map/ppermute | solution.py:682
  1108.6 9.8 fusion.41
  1153.8 16.6 %collective-permute-done.55 = bf16[2,2,2,72,1152]{4,3,0,1,2:T(8,128)(2,1)S(1)} collective-permute-done((bf16[2,2,2,72,1152]{4,3,0,1,2:T(8,128)(2,1)S(1)}, bf16[2,2,2,72,1152]{4,3,0,1,2:T(8,128)(2,1)S(1)}, u32[]{:S(2)}, u32[]{:S(2)}) %collective-permute-start.55) | collective-permute-done | bytes 1327136 | tf_op jit(solution)/shard_map/ppermute | solution.py:344
  1182.9 11.4 collective-permute-done.62
  (687 shorter events, 557.3 us)
Async XLA Ops:
  7.2 136.4 %all-gather.4.cloned.1.call-start = ((), (), s32[]{:S(2)}) async-start(), calls=%async_computation | async-start | bytes 16422912 | tf_op jit(solution)/shard_map/all_gather | solution.py:317
  9.5 282.3 %all-gather.6.cloned.1.call-start = ((), (), s32[]{:S(2)}) async-start(), calls=%async_computation.1 | async-start | bytes 21897216 | tf_op jit(solution)/shard_map/all_gather | solution.py:317
  22.0 389.1 %all-gather.8.cloned.1.call-start = ((), (), s32[]{:S(2)}) async-start(), calls=%async_computation.2 | async-start | bytes 10948608 | tf_op jit(solution)/shard_map/all_gather | solution.py:317
  26.6 160.6 %collective-permute-start.4 = (bf16[2,512,1152]{2,1,0:T(8,128)(2,1)}, bf16[2,512,1152]{2,1,0:T(8,128)(2,1)}, u32[]{:S(2)}, u32[]{:S(2)}) collective-permute-start(bf16[2,512,1152]{2,1,0:T(8,128)(2,1)} %bitcast.416), channel_id=1, source_target_pairs={{1,0},{0,1},{3,2},{2,3},{5,4},{4,5},{7,6},{6,7},{9,8},{8,9},{11,10... | collective-permute-start | bytes 7077896 | tf_op jit(solution)/shard_map/ppermute | solution.py:460
  28.9 121.4 %collective-permute-start.5 = (bf16[144,128]{1,0:T(8,128)(2,1)S(1)}, bf16[144,128]{1,0:T(8,128)(2,1)S(1)}, u32[]{:S(2)}, u32[]{:S(2)}) collective-permute-start(bf16[144,128]{1,0:T(8,128)(2,1)S(1)} %convolution_convert_fusion.21), channel_id=1, source_target_pairs={{0,1},{1,0},{2,3},{3,2},{4,5},{5,4},{6,7},{7,6},{8,9},{9,8},{10,11... | collective-permute-start | bytes 110600 | tf_op jit(solution)/shard_map/ppermute | solution.py:344
  355.7 61.3 %collective-permute-start.10 = (bf16[512,1152]{1,0:T(8,128)(2,1)}, bf16[512,1152]{1,0:T(8,128)(2,1)}, u32[]{:S(2)}, u32[]{:S(2)}) collective-permute-start(bf16[512,1152]{1,0:T(8,128)(2,1)} %get-tuple-element.218), channel_id=1, source_target_pairs={{2,0},{4,2},{6,4},{8,6},{10,8},{12,10},{14,12},{3,1},{5,3},{7,5},{... | collective-permute-start | bytes 3538952 | tf_op jit(solution)/shard_map/ppermute | solution.py:555
  357.1 59.9 %collective-permute-start.9 = (bf16[512,1152]{1,0:T(8,128)(2,1)}, bf16[512,1152]{1,0:T(8,128)(2,1)}, u32[]{:S(2)}, u32[]{:S(2)}) collective-permute-start(bf16[512,1152]{1,0:T(8,128)(2,1)} %get-tuple-element.217), channel_id=1, source_target_pairs={{0,2},{2,4},{4,6},{6,8},{8,10},{10,12},{12,14},{1,3},{3,5},{5,7},{... | collective-permute-start | bytes 3538952 | tf_op jit(solution)/shard_map/ppermute | solution.py:554
  492.4 52.6 %collective-permute-start.11 = (bf16[512,1152]{1,0:T(8,128)(2,1)S(1)}, bf16[512,1152]{1,0:T(8,128)(2,1)S(1)}, u32[]{:S(2)}, u32[]{:S(2)}) collective-permute-start(bf16[512,1152]{1,0:T(8,128)(2,1)S(1)} %get-tuple-element.197), channel_id=1, source_target_pairs={{0,2},{2,4},{4,6},{6,8},{8,10},{10,12},{12,14},{1,3},{3,5},{5,7},{... | collective-permute-start | bytes 3538952 | tf_op jit(solution)/shard_map/ppermute | solution.py:583
  494.3 50.7 %collective-permute-start.12 = (bf16[512,1152]{1,0:T(8,128)(2,1)S(1)}, bf16[512,1152]{1,0:T(8,128)(2,1)}, u32[]{:S(2)}, u32[]{:S(2)}) collective-permute-start(bf16[512,1152]{1,0:T(8,128)(2,1)S(1)} %get-tuple-element.198), channel_id=1, source_target_pairs={{2,0},{4,2},{6,4},{8,6},{10,8},{12,10},{14,12},{3,1},{5,3},{7,5},{... | collective-permute-start | bytes 3538952 | tf_op jit(solution)/shard_map/ppermute | solution.py:582
  587.4 73.2 %collective-permute-start.13 = (bf16[1152,1152]{1,0:T(8,128)(2,1)}, bf16[1152,1152]{1,0:T(8,128)(2,1)}, u32[]{:S(2)}, u32[]{:S(2)}) collective-permute-start(bf16[1152,1152]{1,0:T(8,128)(2,1)} %get-tuple-element.188), channel_id=1, source_target_pairs={{0,16},{16,0},{1,17},{17,1},{2,18},{18,2},{3,19},{19,3},{4,20},{20... | collective-permute-start | bytes 7962632 | tf_op jit(solution)/shard_map/ppermute | solution.py:424
  587.4 73.2 %collective-permute-start.14 = (bf16[1152,1152]{1,0:T(8,128)(2,1)}, bf16[1152,1152]{1,0:T(8,128)(2,1)}, u32[]{:S(2)}, u32[]{:S(2)}) collective-permute-start(bf16[1152,1152]{1,0:T(8,128)(2,1)} %get-tuple-element.187), channel_id=1, source_target_pairs={{0,16},{16,0},{1,17},{17,1},{2,18},{18,2},{3,19},{19,3},{4,20},{20... | collective-permute-start | bytes 7962632 | tf_op jit(solution)/shard_map/ppermute | solution.py:424
  726.3 49.2 %collective-permute-start.24 = (bf16[1152,1152]{1,0:T(8,128)(2,1)}, bf16[1152,1152]{1,0:T(8,128)(2,1)}, u32[]{:S(2)}, u32[]{:S(2)}) collective-permute-start(bf16[1152,1152]{1,0:T(8,128)(2,1)} %broadcast_select_fusion.3), channel_id=1, source_target_pairs={{0,16},{16,0},{1,17},{17,1},{2,18},{18,2},{3,19},{19,3},{4,20},{20... | collective-permute-start | bytes 7962632 | tf_op jit(solution)/shard_map/ppermute | solution.py:424
  728.3 47.2 %collective-permute-start.23 = (bf16[1152,1152]{1,0:T(8,128)(2,1)}, bf16[1152,1152]{1,0:T(8,128)(2,1)}, u32[]{:S(2)}, u32[]{:S(2)}) collective-permute-start(bf16[1152,1152]{1,0:T(8,128)(2,1)} %broadcast_select_fusion.4), channel_id=1, source_target_pairs={{0,16},{16,0},{1,17},{17,1},{2,18},{18,2},{3,19},{19,3},{4,20},{20... | collective-permute-start | bytes 7962632 | tf_op jit(solution)/shard_map/ppermute | solution.py:424
  776.5 60.3 %collective-permute-start.26 = (bf16[72,1152]{1,0:T(8,128)(2,1)}, bf16[72,1152]{1,0:T(8,128)(2,1)S(1)}, u32[]{:S(2)}, u32[]{:S(2)}) collective-permute-start(bf16[72,1152]{1,0:T(8,128)(2,1)} %dynamic-slice_bitcast_fusion.26), channel_id=1, source_target_pairs={{0,8},{2,10},{4,12},{6,14},{8,0},{10,2},{12,4},{14,6},{1,9},{3,11}... | collective-permute-start | bytes 497672 | tf_op jit(solution)/shard_map/ppermute | solution.py:344
  778.4 58.7 %collective-permute-start.25 = (bf16[72,1152]{1,0:T(8,128)(2,1)}, bf16[72,1152]{1,0:T(8,128)(2,1)}, u32[]{:S(2)}, u32[]{:S(2)}) collective-permute-start(bf16[72,1152]{1,0:T(8,128)(2,1)} %dynamic-slice_bitcast_fusion.27), channel_id=1, source_target_pairs={{0,8},{2,10},{4,12},{6,14},{8,0},{10,2},{12,4},{14,6},{1,9},{3,11}... | collective-permute-start | bytes 497672 | tf_op jit(solution)/shard_map/ppermute | solution.py:344
  796.5 41.3 %collective-permute-start.27 = (bf16[2,2,2,144,128]{4,3,2,1,0:T(8,128)(2,1)}, bf16[2,2,2,144,128]{4,3,2,1,0:T(8,128)(2,1)}, u32[]{:S(2)}, u32[]{:S(2)}) collective-permute-start(bf16[2,2,2,144,128]{4,3,2,1,0:T(8,128)(2,1)} %dynamic-slice_bitcast_fusion.18), channel_id=1, source_target_pairs={{0,2},{2,0},{4,6},{6,4},{8,10},{10,8},{12,14},{14,12},{1,3},{3,1},... | collective-permute-start | bytes 884744 | tf_op jit(solution)/shard_map/ppermute | solution.py:344
  809.9 38.2 %collective-permute-start.31 = (bf16[2,2,2,72,1152]{4,3,0,1,2:T(8,128)(2,1)}, bf16[2,2,2,72,1152]{4,3,0,1,2:T(8,128)(2,1)}, u32[]{:S(2)}, u32[]{:S(2)}) collective-permute-start(bf16[2,2,2,72,1152]{4,3,0,1,2:T(8,128)(2,1)} %bitcast.403), channel_id=1, source_target_pairs={{0,1},{1,0},{2,3},{3,2},{4,5},{5,4},{6,7},{7,6},{8,9},{9,8},{10,11... | collective-permute-start | bytes 3981320 | tf_op jit(solution)/shard_map/ppermute | solution.py:344
  848.2 64.8 %collective-permute-start.37 = (bf16[1152,1152]{1,0:T(8,128)(2,1)}, bf16[1152,1152]{1,0:T(8,128)(2,1)}, u32[]{:S(2)}, u32[]{:S(2)}) collective-permute-start(bf16[1152,1152]{1,0:T(8,128)(2,1)} %broadcast_select_fusion.2), channel_id=1, source_target_pairs={{0,16},{16,0},{1,17},{17,1},{2,18},{18,2},{3,19},{19,3},{4,20},{20... | collective-permute-start | bytes 7962632 | tf_op jit(solution)/shard_map/ppermute | solution.py:424
  868.8 44.1 %collective-permute-start.36 = (bf16[2,2,72,1152]{3,2,0,1:T(8,128)(2,1)S(1)}, bf16[2,2,72,1152]{3,2,0,1:T(8,128)(2,1)}, u32[]{:S(2)}, u32[]{:S(2)}) collective-permute-start(bf16[2,2,72,1152]{3,2,0,1:T(8,128)(2,1)S(1)} %dynamic-slice_bitcast_fusion.3), channel_id=1, source_target_pairs={{0,2},{2,0},{4,6},{6,4},{8,10},{10,8},{12,14},{14,12},{1,3},{3,1},... | collective-permute-start | bytes 1990664 | tf_op jit(solution)/shard_map/ppermute | solution.py:344
  872.6 40.4 %collective-permute-start.35 = (bf16[2,2,72,1152]{3,2,0,1:T(8,128)(2,1)}, bf16[2,2,72,1152]{3,2,0,1:T(8,128)(2,1)}, u32[]{:S(2)}, u32[]{:S(2)}) collective-permute-start(bf16[2,2,72,1152]{3,2,0,1:T(8,128)(2,1)} %dynamic-slice_bitcast_fusion.4), channel_id=1, source_target_pairs={{0,1},{1,0},{2,3},{3,2},{4,5},{5,4},{6,7},{7,6},{8,9},{9,8},{10,11... | collective-permute-start | bytes 1990664 | tf_op jit(solution)/shard_map/ppermute | solution.py:344
  913.0 58.7 %collective-permute-start.44 = (bf16[144,128]{1,0:T(8,128)(2,1)S(1)}, bf16[144,128]{1,0:T(8,128)(2,1)S(1)}, u32[]{:S(2)}, u32[]{:S(2)}) collective-permute-start(bf16[144,128]{1,0:T(8,128)(2,1)S(1)} %dynamic-slice_bitcast_fusion.30), channel_id=1, source_target_pairs={{0,8},{2,10},{4,12},{6,14},{8,0},{10,2},{12,4},{14,6},{1,9},{3,11}... | collective-permute-start | bytes 110600 | tf_op jit(solution)/shard_map/ppermute | solution.py:344
  920.0 59.0 %collective-permute-start.43 = (bf16[2,2,2,72,1152]{4,3,0,1,2:T(8,128)(2,1)}, bf16[2,2,2,72,1152]{4,3,0,1,2:T(8,128)(2,1)}, u32[]{:S(2)}, u32[]{:S(2)}) collective-permute-start(bf16[2,2,2,72,1152]{4,3,0,1,2:T(8,128)(2,1)} %bitcast.402), channel_id=1, source_target_pairs={{0,4},{2,6},{4,0},{6,2},{8,12},{10,14},{12,8},{14,10},{1,5},{3,7},... | collective-permute-start | bytes 3981320 | tf_op jit(solution)/shard_map/ppermute | solution.py:344
  922.8 50.0 %collective-permute-start.42 = (bf16[2,72,1152]{2,1,0:T(8,128)(2,1)}, bf16[2,72,1152]{2,1,0:T(8,128)(2,1)}, u32[]{:S(2)}, u32[]{:S(2)}) collective-permute-start(bf16[2,72,1152]{2,1,0:T(8,128)(2,1)} %dynamic-slice_bitcast_fusion.12), channel_id=1, source_target_pairs={{0,4},{2,6},{4,0},{6,2},{8,12},{10,14},{12,8},{14,10},{1,5},{3,7},... | collective-permute-start | bytes 995336 | tf_op jit(solution)/shard_map/ppermute | solution.py:344
  926.4 46.5 %collective-permute-start.41 = (bf16[2,72,1152]{2,1,0:T(8,128)(2,1)}, bf16[2,72,1152]{2,1,0:T(8,128)(2,1)}, u32[]{:S(2)}, u32[]{:S(2)}) collective-permute-start(bf16[2,72,1152]{2,1,0:T(8,128)(2,1)} %dynamic-slice_bitcast_fusion.13), channel_id=1, source_target_pairs={{0,2},{2,0},{4,6},{6,4},{8,10},{10,8},{12,14},{14,12},{1,3},{3,1},... | collective-permute-start | bytes 995336 | tf_op jit(solution)/shard_map/ppermute | solution.py:344
  929.7 43.7 %collective-permute-start.40 = (bf16[2,72,1152]{2,1,0:T(8,128)(2,1)}, bf16[2,72,1152]{2,1,0:T(8,128)(2,1)}, u32[]{:S(2)}, u32[]{:S(2)}) collective-permute-start(bf16[2,72,1152]{2,1,0:T(8,128)(2,1)} %dynamic-slice_bitcast_fusion.14), channel_id=1, source_target_pairs={{0,1},{1,0},{2,3},{3,2},{4,5},{5,4},{6,7},{7,6},{8,9},{9,8},{10,11... | collective-permute-start | bytes 995336 | tf_op jit(solution)/shard_map/ppermute | solution.py:344
  972.8 64.9 %collective-permute-start.52 = (bf16[128,4096]{1,0:T(8,128)(2,1)}, bf16[128,4096]{1,0:T(8,128)(2,1)}, u32[]{:S(2)}, u32[]{:S(2)}) collective-permute-start(bf16[128,4096]{1,0:T(8,128)(2,1)} %bitcast.3), channel_id=1, source_target_pairs={{0,16},{16,0},{1,17},{17,1},{2,18},{18,2},{3,19},{19,3},{4,20},{20... | collective-permute-start | bytes 3145736 | tf_op jit(solution)/shard_map/ppermute | solution.py:424
  972.9 175.7 %collective-permute-start.46 = (f32[1,1152]{1,0:T(1,128)S(1)}, f32[1,1152]{1,0:T(1,128)}, u32[]{:S(2)}, u32[]{:S(2)}) collective-permute-start(f32[1,1152]{1,0:T(1,128)S(1)} %copy-done.86), channel_id=1, source_target_pairs={{0,16},{16,0},{1,17},{17,1},{2,18},{18,2},{3,19},{19,3},{4,20},{20... | collective-permute-start | bytes 13832 | tf_op jit(solution)/shard_map/ppermute | solution.py:424
  980.8 63.3 %collective-permute-start.74 = (bf16[72,1152]{1,0:T(8,128)(2,1)}, bf16[72,1152]{1,0:T(8,128)(2,1)}, u32[]{:S(2)}, u32[]{:S(2)}) collective-permute-start(bf16[72,1152]{1,0:T(8,128)(2,1)} %dynamic-slice_bitcast_fusion.20), channel_id=1, source_target_pairs={{0,8},{2,10},{4,12},{6,14},{8,0},{10,2},{12,4},{14,6},{1,9},{3,11}... | collective-permute-start | bytes 497672 | tf_op jit(solution)/shard_map/ppermute | solution.py:344
  983.8 62.9 %collective-permute-start.76 = (bf16[72,1152]{1,0:T(8,128)(2,1)}, bf16[72,1152]{1,0:T(8,128)(2,1)}, u32[]{:S(2)}, u32[]{:S(2)}) collective-permute-start(bf16[72,1152]{1,0:T(8,128)(2,1)} %dynamic-slice_bitcast_fusion.19), channel_id=1, source_target_pairs={{0,8},{2,10},{4,12},{6,14},{8,0},{10,2},{12,4},{14,6},{1,9},{3,11}... | collective-permute-start | bytes 497672 | tf_op jit(solution)/shard_map/ppermute | solution.py:344
  1046.7 91.3 %collective-permute-start.54 = (bf16[1152,1152]{1,0:T(8,128)(2,1)}, bf16[1152,1152]{1,0:T(8,128)(2,1)}, u32[]{:S(2)}, u32[]{:S(2)}) collective-permute-start(bf16[1152,1152]{1,0:T(8,128)(2,1)} %get-tuple-element.183), channel_id=1, source_target_pairs={{0,16},{16,0},{1,17},{17,1},{2,18},{18,2},{3,19},{19,3},{4,20},{20... | collective-permute-start | bytes 7962632 | tf_op jit(solution)/shard_map/ppermute | solution.py:424
  1049.6 59.0 %collective-permute-start.45 = (bf16[2,512,1152]{2,1,0:T(8,128)(2,1)}, bf16[2,512,1152]{2,1,0:T(8,128)(2,1)}, u32[]{:S(2)}, u32[]{:S(2)}) collective-permute-start(bf16[2,512,1152]{2,1,0:T(8,128)(2,1)} %fusion.71), channel_id=1, source_target_pairs={{0,1},{1,0},{2,3},{3,2},{4,5},{5,4},{6,7},{7,6},{8,9},{9,8},{10,11... | collective-permute-start | bytes 7077896 | tf_op jit(solution)/shard_map/ppermute | solution.py:682
  1068.5 69.5 %collective-permute-start.60 = (bf16[1152,1152]{1,0:T(8,128)(2,1)}, bf16[1152,1152]{1,0:T(8,128)(2,1)}, u32[]{:S(2)}, u32[]{:S(2)}) collective-permute-start(bf16[1152,1152]{1,0:T(8,128)(2,1)} %get-tuple-element.184), channel_id=1, source_target_pairs={{0,16},{16,0},{1,17},{17,1},{2,18},{18,2},{3,19},{19,3},{4,20},{20... | collective-permute-start | bytes 7962632 | tf_op jit(solution)/shard_map/ppermute | solution.py:424
  (182 other events, 3096.5 us)
Sparse Core Ops, SparseCore 0:
  11.4 132.1 all-gather.3
  147.1 144.6 all-gather.5
  295.2 115.8 all-gather.7

commit v3 on v2

--- a/solution.py
+++ b/solution.py
@@ -335,6 +335,11 @@
     return first[turn:] + first[:turn] + [last]
 
 
+def column_halves(value):
+    middle = value.shape[1] // 2
+    return (value[:, :middle], value[:, middle:])
+
+
 def my_bit(bit):
     return (lax.axis_index(bit[0]) >> bit[1]) & 1
 
@@ -476,8 +481,19 @@
     )
     gathered_b = gather_halves(
         is_first,
-        jnp.concatenate([up_mixed[:, :half_ff], down_wide[:, :half_ff]], axis=1),
-        jnp.concatenate([up_mixed[:, half_ff:], down_wide[:, half_ff:]], axis=1),
+        jnp.concatenate(
+            [
+                up_mixed[:, :half_ff],
+                down_wide[:, :half_ff],
+                temporal_qkv_weight[:, :width],
+                temporal_proj_weight,
+            ],
+            axis=1,
+        ),
+        jnp.concatenate(
+            [up_mixed[:, half_ff:], down_wide[:, half_ff:], temporal_qkv_weight[:, width:]],
+            axis=1,
+        ),
     )
 
     silu_cond = jax.nn.silu(condition.astype(jnp.float32))
@@ -499,6 +515,9 @@
     hidden_all = jnp.concatenate(
         [part.reshape(frame_count, row_count, width) for part in [hidden_a] + hidden_rest], axis=1
     ).reshape(frame_count * seq_size * row_count, width)
+    hidden_a, hidden_all, text_pair, gathered_a = lax.optimization_barrier(
+        (hidden_a, hidden_all, text_pair, gathered_a)
+    )
     query_full = gathered_a[:width, :width]
     pair_full = gathered_a[:width, width:]
     proj_full = gathered_a[width:, :width]
@@ -516,26 +535,18 @@
     normed_m, recip_m = normalize(after_c)
     hidden_m = (normed_m * (1.0 + modulation[4]) + modulation[3]).astype(jnp.bfloat16)
 
-    temporal_lower, temporal_upper = lax.optimization_barrier(
-        (
-            jnp.concatenate([temporal_qkv_weight[:, :width], temporal_proj_weight], axis=1),
-            temporal_qkv_weight[:, width:],
-            query,
-        )
-    )[:2]
-    gathered_c = gather_halves(is_first, temporal_lower, temporal_upper)
     up_halves = (gathered_b[:width, :half_ff], gathered_b[width:, :half_ff])
     per_half = ff_blocks // 2
-    down_halves = (gathered_b[:width, half_ff:], gathered_b[width:, half_ff:])
+    down_halves = (gathered_b[:width, half_ff:ff_width], gathered_b[width:, half_ff:ff_width])
     down_parts = [
         down_halves[index // per_half][
             :, width * (index % per_half) : width * (index % per_half + 1)
         ]
         for index in range(ff_blocks)
     ]
-    tquery_full = gathered_c[:width, :width]
-    tproj_full = gathered_c[:width, width:]
-    tpair_full = gathered_c[width:]
+    tquery_full = gathered_b[:width, ff_width : ff_width + width]
+    tproj_full = gathered_b[:width, ff_width + width :]
+    tpair_full = gathered_b[width:, ff_width:]
 
     upward_halves = [product(hidden_m, part) for part in up_halves]
     activated_halves = [gelu_tanh(part).astype(jnp.bfloat16) for part in upward_halves]
@@ -555,7 +566,13 @@
     hidden_next = lax.ppermute(hidden_t[:row_count], "frame", back)
     hidden_ext = jnp.concatenate([hidden_prev, hidden_t, hidden_next], axis=0)
     tquery = contract(tquery_full, hidden_t, 0, 1).astype(jnp.bfloat16)
-    tpair = contract(tpair_full, hidden_ext, 0, 1).astype(jnp.bfloat16)
+    tpair = jnp.concatenate(
+        [
+            low(contract(tpair_full, part, 0, 1))
+            for part in (hidden_prev, hidden_t, hidden_next)
+        ],
+        axis=1,
+    )
     first_frame = lax.axis_index("frame") * frame_count
     clips_ext = jnp.concatenate(
         [jnp.full((1,), -1, jnp.int32), clip_ids[0], jnp.full((1,), -1, jnp.int32)]
@@ -578,13 +595,21 @@
     branch_t_grad = (flag_rows * modulation[8] * result_grad).astype(jnp.bfloat16)
     mixed_grad = contract(tproj_full, branch_t_grad, 1, 1)
     tquery_grad, tpair_grad = temporal_backward(live, tquery, tpair, mixed_grad, frame_count)
-    ext_grad = contract(tpair_grad, tpair_full, 0, 1)
-    to_prev = lax.ppermute(low(ext_grad[:row_count]), "frame", back)
-    to_next = lax.ppermute(low(ext_grad[-row_count:]), "frame", ahead)
+    halo_prev, halo_next, tpair_grad = lax.optimization_barrier(
+        (
+            low(contract(tpair_grad[:, :row_count], tpair_full, 0, 1)),
+            low(contract(tpair_grad[:, -row_count:], tpair_full, 0, 1)),
+            tpair_grad,
+        )
+    )
+    to_prev = lax.ppermute(halo_prev, "frame", back)
+    to_next = lax.ppermute(halo_next, "frame", ahead)
     tpair_weight_grad = low(contract(hidden_ext, tpair_grad, 0, 1))
     tquery_weight_grad = low(contract(hidden_t, tquery_grad, 0, 1))
     tproj_weight_grad = low(contract(mixed, branch_t_grad, 1, 0))
-    hidden_t_grad = ext_grad[row_count:-row_count] + contract(tquery_grad, tquery_full, 0, 1)
+    hidden_t_grad = contract(tpair_grad[:, row_count:-row_count], tpair_full, 0, 1) + contract(
+        tquery_grad, tquery_full, 0, 1
+    )
     hidden_t_grad = jnp.concatenate(
         [
             hidden_t_grad[:row_count] + to_next.astype(jnp.float32),
@@ -660,42 +685,67 @@
         (attended_grad, proj_grad, cross_q_grad, cross_proj_grad)
     )
     chain_pq = Chain(is_first, (proj_grad, cross_q_grad), 2)
+    chain_cp = Chain(is_first, column_halves(cross_proj_grad), 1)
+    chains_c = [chain_pq, chain_cp, chain_text]
     attended_grad = tick(attended_grad, chains_m + [chain_text])
-    query_grads, pair_grads = ([], [])
+    query_grads, pair_grads, rest_grads, rest_received = ([], [], [], [])
     for frame in range(frame_count):
         query_grad, pair_grad = spatial_backward(
             query, key_value, log_total, attended_grad, frame_count, frame
         )
+        rest_sent = contract(pair_grad[:, row_count:], pair_full, 0, 1)
+        rest_low = low(rest_sent)
+        pair_grad, rest_low, attended_grad = lax.optimization_barrier(
+            (pair_grad, rest_low, attended_grad)
+        )
         query_grads.append(query_grad)
         pair_grads.append(pair_grad)
+        rest_grads.append(rest_sent)
+        rest_received.append(
+            [
+                lax.ppermute(
+                    rest_low[s * row_count : (s + 1) * row_count],
+                    "seq",
+                    [(j, i) for i, j in shifts[s]],
+                )
+                for s in range(seq_size - 1)
+            ]
+        )
         if frame == 0:
-            query_grads[0], attended_grad = tick(
-                (query_grads[0], attended_grad), chains_m + [chain_pq, chain_text]
+            attended_grad = tick(attended_grad, chains_m + chains_c)
+        else:
+            query_grads, pair_grads, rest_received[frame - 1] = lax.optimization_barrier(
+                (query_grads, pair_grads, rest_received[frame - 1])
             )
     query_grad = jnp.concatenate(query_grads, axis=1)
     pair_grad = jnp.concatenate(pair_grads, axis=1)
-    pair_grad = tick(pair_grad, chains_m + [chain_pq, chain_text])
-    all_grad = contract(pair_grad, pair_full, 0, 1).reshape(
-        frame_count, seq_size, row_count, width
-    )
-    rest_grad = [
-        lax.ppermute(
-            low(all_grad[:, s + 1]), "seq", [(j, i) for i, j in shifts[s]]
-        )
-        for s in range(seq_size - 1)
+    query_weight_grad = low(contract(hidden_a, query_grad, 0, 1))
+    pair_weight_grad = low(contract(hidden_all, pair_grad, 0, 1))
+    query_grad, pair_grads, query_weight_grad, pair_weight_grad = lax.optimization_barrier(
+        (query_grad, pair_grads, query_weight_grad, pair_weight_grad)
+    )
+    chains_a = [
+        Chain(is_first, column_halves(part), turn)
+        for turn, part in enumerate(
+            (query_weight_grad, pair_weight_grad[:, :width], pair_weight_grad[:, width:])
+        )
     ]
-    pair_weight_grad = low(contract(hidden_all, pair_grad, 0, 1))
-    chain_vp = Chain(is_first, (pair_weight_grad[:, width:], cross_proj_grad), 1)
-    query_weight_grad = low(contract(hidden_a, query_grad, 0, 1))
-    chain_qk = Chain(is_first, (query_weight_grad, pair_weight_grad[:, :width]), 2)
-    own_grad = all_grad[:, 0].reshape(total_rows, width) + contract(query_grad, query_full, 0, 1)
+    query_grad = tick(query_grad, chains_m + chains_c)
+    own_grad = jnp.concatenate(
+        [contract(part[:, :row_count], pair_full, 0, 1) for part in pair_grads], axis=0
+    ) + contract(query_grad, query_full, 0, 1)
+    own_grad, rest_received = tick((own_grad, rest_received), chains_a + chains_c)
     shift_a_grad = jnp.sum(own_grad, axis=0)
     scale_a_grad = jnp.sum(own_grad * normed_a, axis=0)
-    for s in range(seq_size - 1):
-        rest_rows = all_grad[:, s + 1].reshape(total_rows, width)
-        shift_a_grad = shift_a_grad + jnp.sum(rest_rows, axis=0)
-        scale_a_grad = scale_a_grad + jnp.sum(rest_rows * normed_rest[s], axis=0)
-    hidden_a_grad = sum([rest.astype(jnp.float32).reshape(total_rows, width) for rest in rest_grad], own_grad)
+    for frame in range(frame_count):
+        for s in range(seq_size - 1):
+            rest_rows = rest_grads[frame][s * row_count : (s + 1) * row_count]
+            rest_normed = normed_rest[s][frame * row_count : (frame + 1) * row_count]
+            shift_a_grad = shift_a_grad + jnp.sum(rest_rows, axis=0)
+            scale_a_grad = scale_a_grad + jnp.sum(rest_rows * rest_normed, axis=0)
+    hidden_a_grad = own_grad + jnp.concatenate(
+        [sum(part.astype(jnp.float32) for part in parts) for parts in rest_received], axis=0
+    )
     input_grad = grad_a + normalize_back(hidden_a_grad * (1.0 + modulation[1]), normed_a, recip_a)
     latent_grad = input_grad.reshape(latent.shape)
     mod_grad = jnp.stack(
@@ -711,6 +761,7 @@
             gate_t_grad,
         ]
     ).reshape(shards, 9 * width // shards)
+    latent_grad, mod_grad = tick((latent_grad, mod_grad), chains_a)
     mod_slice = Chain(is_first, (mod_grad,), 0).finish()
     text_low = chain_text.finish()
     silu_pair = jnp.concatenate([silu_cond, swapped(silu_cond)], axis=0)
@@ -721,9 +772,9 @@
     text_both = jnp.concatenate([text[0], swapped(text[0])], axis=0)
     slice_both = jnp.concatenate([text_low, swapped(text_low)], axis=1)
     text_kv_grad = contract(text_both, slice_both, 0, 1)
-    query_shard, key_shard = both_of(chain_qk)
-    value_shard, cross_proj_shard = both_of(chain_vp)
     proj_shard, cross_q_shard = both_of(chain_pq)
+    cross_proj_shard = jnp.concatenate(both_of(chain_cp), axis=1)
+    qkv_shard = jnp.concatenate([part for chain in chains_a for part in both_of(chain)], axis=1)
     tquery_shard, tkey_shard = both_of(chain_tqk)
     tproj_shard, tvalue_shard = both_of(chain_tpv)
     ff_shards = [both_of(chain) for chain in chains_m]
@@ -743,7 +794,7 @@
         latent_grad,
         ada_grad,
         text_kv_grad,
-        jnp.concatenate([query_shard, key_shard, value_shard], axis=1),
+        qkv_shard,
         proj_shard,
         cross_q_shard,
         cross_proj_shard,

time: 1230 us -> 1310 us (1.065)
  local copies, waits for them, and re-layouts: 70.1 us -> 101 us
  other arithmetic: 146 us -> 171 us
  matrix products: 378 us -> 398 us
    ppermute x3 -> x4, waiting for transfers between devices: 59.7 us -> 14.2 us  [the longest x1 14.2 us: per_device(): to_next = lax.ppermute(halo_next, 'frame', ahead)]
    ppermute x1, waiting for transfers between devices: 0.01 us -> 27.9 us  [per_device(): lax.ppermute(hidden_t[total_rows - row_count:], 'frame', ahead)]
    all_gather x3 -> x2, waiting for transfers between devices: 148 us -> 127 us  [gather_halves(): lax.all_gather(jnp.where(is_first, lower, upper), ('bucket', 'frame', 'se...]
    ppermute x1, waiting for transfers between devices: 0.01 us -> 21.2 us  [per_device(): latent_rest = [lax.ppermute(latent[0], 'seq', shift) for shift in shifts]]
    dot_general x38 -> x45, matrix products: 312 us -> 330 us  [contract(): lax.dot_general(left, right, (((left_dim,), (right_dim,)), ((), ())), pre...]
    ppermute x52 -> x60, waiting for transfers between devices: 158 us -> 174 us  [across(): lax.ppermute(value, axis, [(i, i ^ 1 << step) for i in range(lax.axis_siz...]
    convert_element_type x45 -> x55, other arithmetic: 53.5 us -> 65.8 us  [advance(): value = (value.astype(jnp.float32) + self.received.astype(jnp.float32)).a...]
    ppermute x52 -> x60, starting transfers between devices: 65.8 us -> 65.9 us  [across(): lax.ppermute(value, axis, [(i, i ^ 1 << step) for i in range(lax.axis_siz...]
  transfers between devices with their start and end apart: 83 -> 95, of which waited for: 35 -> 44; matrix products, arithmetic and copies ran while one was open for 38% -> 36% of each run, Pallas kernels for 11% -> 9%
where the time goes in v3:
time: 1310 us; the launch traced here: 1300 us
  matrix products  398 us (30%)
  waiting for transfers between devices  369 us (28%)
  other arithmetic  171 us (13%)
  Pallas kernels  159 us (12%)
  local copies, waits for them, and re-layouts  101 us (8%)
  starting transfers between devices  84.4 us (6%)
  between operations  18 us (1%)
    dot_general x45, matrix products, contract(): lax.dot_general(left, right, (((left_dim,), (right_dim,)), ((), ())), pre...  330 us
    ppermute x60, waiting for transfers between devices, across(): lax.ppermute(value, axis, [(i, i ^ 1 << step) for i in range(lax.axis_siz...  174 us
    all_gather x2, waiting for transfers between devices, gather_halves(): lax.all_gather(jnp.where(is_first, lower, upper), ('bucket', 'frame', 'se...  127 us
    pallas_call x2, Pallas kernels, spatial_backward(): call(body, (HEADS,), [pl.BlockSpec((head_size, rows), lambda h: (h, frame...  69.3 us
    ppermute x60, starting transfers between devices, across(): lax.ppermute(value, axis, [(i, i ^ 1 << step) for i in range(lax.axis_siz...  65.9 us
    convert_element_type x55, other arithmetic, advance(): value = (value.astype(jnp.float32) + self.received.astype(jnp.float32)).a...  65.8 us
    dot_general x6, matrix products, product(): return jnp.dot(left, right, preferred_element_type=jnp.float32)  62 us
    pallas_call x1, Pallas kernels, spatial_forward(): call(body, (frame_count, HEADS), [pl.BlockSpec((head_size, rows), lambda...  37.4 us
  transfers between devices with their start and end apart: 95, of which 44 were waited for; matrix products, arithmetic and copies ran while one was open for 36% of the time, Pallas kernels for 9%

profile of v3, /device:TPU:0, one launch (start us, length us, event | category | flops | bytes accessed | tf_op | source)
XLA Modules:
  0.0 1299.7 jit_solution(15798431119168807446)
XLA Ops:
  62.4 14.9 %collective-permute-done.8 = bf16[1152,128]{1,0:T(8,128)(2,1)S(1)} collective-permute-done((bf16[1152,128]{1,0:T(8,128)(2,1)S(1)}, bf16[1152,128]{1,0:T(8,128)(2,1)S(1)}, u32[]{:S(2)}, u32[]{:S(2)}) %collective-permute-start.8) | collective-permute-done | bytes 294944 | tf_op jit(solution)/shard_map/ppermute | solution.py:349
  77.4 21.2 %collective-permute-done.4 = bf16[2,512,1152]{2,1,0:T(8,128)(2,1)S(1)} collective-permute-done((bf16[2,512,1152]{2,1,0:T(8,128)(2,1)}, bf16[2,512,1152]{2,1,0:T(8,128)(2,1)S(1)}, u32[]{:S(2)}, u32[]{:S(2)}) %collective-permute-start.4) | collective-permute-done | bytes 2359328 | tf_op jit(solution)/shard_map/ppermute | solution.py:465
  108.5 35.1 %all-gather.3.cloned.1.call-done = bf16[2304,3456]{1,0:T(8,128)(2,1)} async-done(((bf16[72,3456]{1,0:T(8,128)(2,1)}), bf16[2304,3456]{1,0:T(8,128)(2,1)}) %all-gather.3.cloned.1.call-update) | async-done | bytes 15925264 | tf_op jit(solution)/shard_map/all_gather | solution.py:317
  149.5 18.0 %convolution_convert_fusion.2.k_ref.v_ref = bf16[2304,2048]{1,0:T(8,128)(2,1)} fusion(bf16[2048,1152]{1,0:T(8,128)(2,1)S(1)} %bitcast.471, bf16[2304,3456]{1,0:T(8,128)(2,1)} %all-gather.3.cloned.1.call-done), kind=kOutput, calls=%fused_computation.6 | convolution fusion | flops 10876354560 | bytes 19464192 | tf_op jit(solution)/shard_map/dot_general | solution.py:24
  167.5 37.4 %spatial_forward.1 = (bf16[1152,1024]{1,0:T(8,128)(2,1)S(1)}, f32[32,1,512]{2,1,0:T(1,128)S(1)}) custom-call(bf16[1152,1024]{1,0:T(8,128)(2,1)S(1)} %convolution_convert_fusion.22.q_ref, bf16[2304,2048]{1,0:T(8,128)(2,1)} %convolution_convert_fusion.2.k_ref.v_ref, bf16[2304,2048]{1,0:T(8,128)(2,1)} %convolution_convert_fusion.2.k_ref.v_ref), custom_call_target="tpu_custom_call" | custom-call | tf_op jit(solution)/shard_map/spatial_forward/pallas_call | solution.py:57
  204.9 9.1 fusion.54
  240.0 91.5 %all-gather.5.cloned.1.call-done = bf16[2304,6912]{1,0:T(8,128)(2,1)} async-done(((bf16[72,6912]{1,0:T(8,128)(2,1)}), bf16[2304,6912]{1,0:T(8,128)(2,1)}) %all-gather.5.cloned.1.call-update) | async-done | bytes 31850512 | tf_op jit(solution)/shard_map/all_gather | solution.py:317
  331.5 12.3 multiply_convert_fusion.1
  359.4 12.6 multiply_convert_fusion
  380.6 12.9 fusion.209
  399.9 9.4 convolution_convert_fusion.15
  421.5 27.9 %collective-permute-done.9 = bf16[512,1152]{1,0:T(8,128)(2,1)S(1)} collective-permute-done((bf16[512,1152]{1,0:T(8,128)(2,1)S(1)}, bf16[512,1152]{1,0:T(8,128)(2,1)S(1)}, u32[]{:S(2)}, u32[]{:S(2)}) %collective-permute-start.9) | collective-permute-done | bytes 1179680 | tf_op jit(solution)/shard_map/ppermute | solution.py:565
  466.9 10.7 temporal_forward.1
  481.0 17.1 %temporal_backward.1 = (bf16[1152,1024]{1,0:T(8,128)(2,1)S(1)}, bf16[2,1152,2048]{2,1,0:T(8,128)(2,1)}) custom-call(s32[2,2]{1,0:T(2,128)S(1)} %add_convert_fusion.15.live_ref, bf16[1152,1024]{1,0:T(8,128)(2,1)S(1)} %convolution_convert_fusion.20.q_ref, bf16[2304,2048]{1,0:T(8,128)(2,1)} %pad_maximum_fusion.k_ref.v_ref, ...), custom_call_target="tpu_custom_call" | custom-call | tf_op jit(solution)/shard_map/temporal_backward/pallas_call | solution.py:275
  519.1 15.1 %convolution_convert_fusion.4 = bf16[1152,2304]{1,0:T(8,128)(2,1)} fusion(bf16[2304,2048]{1,0:T(8,128)(2,1)} %bitcast.502, bf16[512,1152]{1,0:T(8,128)(2,1)S(1)} %copy-done.139, bf16[1024,1152]{1,0:T(8,128)(2,1)S(1)} %copy-done.32, bf16[512,1152]{1,0:T(8,128)(2,1)S(1)} %copy-done.137), kind=kOutput, calls=%fused_computation.8 | convolution fusion | flops 10888445952 | bytes 19464192 | tf_op jit(solution)/shard_map/dot_general | solution.py:24
  534.2 9.9 fusion.41
  553.8 14.2 %collective-permute-done.11 = bf16[512,1152]{1,0:T(8,128)(2,1)S(1)} collective-permute-done((bf16[512,1152]{1,0:T(8,128)(2,1)}, bf16[512,1152]{1,0:T(8,128)(2,1)S(1)}, u32[]{:S(2)}, u32[]{:S(2)}) %collective-permute-start.11) | collective-permute-done | bytes 1179680 | tf_op jit(solution)/shard_map/ppermute | solution.py:606
  571.5 10.7 fusion.20
  624.3 9.9 fusion.92
  641.1 10.6 fusion.43
  707.5 11.0 fusion.51
  718.5 15.5 %collective-permute-done.16 = bf16[2,2,2,72,1152]{4,3,0,2,1:T(8,128)(2,1)} collective-permute-done((bf16[2,2,2,72,1152]{4,3,0,2,1:T(8,128)(2,1)}, bf16[2,2,2,72,1152]{4,3,0,2,1:T(8,128)(2,1)}, u32[]{:S(2)}, u32[]{:S(2)}) %collective-permute-start.16) | collective-permute-done | bytes 1327136 | tf_op jit(solution)/shard_map/ppermute | solution.py:349
  750.5 10.5 collective-permute-done.18
  784.7 15.6 %cross_backward.1 = (bf16[1152,1024]{1,0:T(8,128)(2,1)S(1)}, f32[2,1152,128]{2,1,0:T(8,128)S(1)}) custom-call(s32[1]{0:T(128)S(6)} %copy.175.length_ref, bf16[1152,1024]{1,0:T(8,128)(2,1)} %copy-done.6, bf16[2304,128]{1,0:T(8,128)(2,1)S(1)} %pad_maximum_fusion.5.k_ref.v_ref, bf16[2304,128]{1,0:T(8,128)(2,1)S(1)} %pad_maximum_fusion.5.k_ref.v_ref, ...), custom_call_target="tpu_custom_call" | custom-call | tf_op jit(solution)/shard_map/cross_backward/pallas_call | solution.py:166
  883.5 15.5 %collective-permute-done.28 = bf16[2,2,2,72,1152]{4,3,0,1,2:T(8,128)(2,1)} collective-permute-done((bf16[2,2,2,72,1152]{4,3,0,1,2:T(8,128)(2,1)}, bf16[2,2,2,72,1152]{4,3,0,1,2:T(8,128)(2,1)}, u32[]{:S(2)}, u32[]{:S(2)}) %collective-permute-start.28) | collective-permute-done | bytes 1327136 | tf_op jit(solution)/shard_map/ppermute | solution.py:349
  911.9 34.3 %spatial_backward.2 = (bf16[1152,512]{1,0:T(8,128)(2,1)S(1)}, bf16[2,1152,1024]{2,1,0:T(8,128)(2,1)}) custom-call(bf16[1152,1024]{1,0:T(8,128)(2,1)S(1)} %copy-done.3, bf16[2304,2048]{1,0:T(8,128)(2,1)} %convolution_convert_fusion.2.k_ref.v_ref, bf16[2304,2048]{1,0:T(8,128)(2,1)} %convolution_convert_fusion.2.k_ref.v_ref, f32[32,1,512]{2,1,0:T(1,128)S(1)} %copy-done.10, ...), custom_call_target="tpu_custom_call" | custom-call | tf_op jit(solution)/shard_map/spatial_backward/pallas_call | solution.py:94
  980.5 35.0 %spatial_backward.3 = (bf16[1152,512]{1,0:T(8,128)(2,1)S(1)}, bf16[2,1152,1024]{2,1,0:T(8,128)(2,1)}) custom-call(bf16[1152,1024]{1,0:T(8,128)(2,1)S(1)} %copy-done.3, bf16[2304,2048]{1,0:T(8,128)(2,1)} %convolution_convert_fusion.2.k_ref.v_ref, bf16[2304,2048]{1,0:T(8,128)(2,1)} %convolution_convert_fusion.2.k_ref.v_ref, f32[32,1,512]{2,1,0:T(1,128)S(1)} %copy-done.11, ...), custom_call_target="tpu_custom_call" | custom-call | tf_op jit(solution)/shard_map/spatial_backward/pallas_call | solution.py:94
  1032.0 13.3 %convolution_convert_fusion.3 = bf16[1152,2304]{1,0:T(8,128)(2,1)S(1)} fusion(bf16[2048,1152]{1,0:T(8,128)(2,1)S(1)} %bitcast.474, bf16[2304,1024]{1,0:T(8,128)(2,1)} %bitcast.510, bf16[2304,1024]{1,0:T(8,128)(2,1)S(1)} %bitcast.507), kind=kOutput, calls=%fused_computation.7 | convolution fusion | flops 10893164544 | bytes 19464192 | tf_op jit(solution)/shard_map/dot_general | solution.py:24
  1045.3 9.1 fusion.57
  1120.9 10.3 collective-permute-done.83
  1131.3 9.3 collective-permute-done.85
  1218.4 9.7 collective-permute-done.78
  (862 shorter events, 692.2 us)
Async XLA Ops:
  7.2 136.4 %all-gather.3.cloned.1.call-start = ((), (), s32[]{:S(2)}) async-start(), calls=%async_computation | async-start | bytes 16422912 | tf_op jit(solution)/shard_map/all_gather | solution.py:317
  9.5 321.9 %all-gather.5.cloned.1.call-start = ((), (), s32[]{:S(2)}) async-start(), calls=%async_computation.1 | async-start | bytes 32845824 | tf_op jit(solution)/shard_map/all_gather | solution.py:317
  26.2 72.4 %collective-permute-start.4 = (bf16[2,512,1152]{2,1,0:T(8,128)(2,1)}, bf16[2,512,1152]{2,1,0:T(8,128)(2,1)S(1)}, u32[]{:S(2)}, u32[]{:S(2)}) collective-permute-start(bf16[2,512,1152]{2,1,0:T(8,128)(2,1)} %bitcast.1), channel_id=1, source_target_pairs={{1,0},{0,1},{3,2},{2,3},{5,4},{4,5},{7,6},{6,7},{9,8},{8,9},{11,10... | collective-permute-start | bytes 7077896 | tf_op jit(solution)/shard_map/ppermute | solution.py:465
  395.2 54.3 %collective-permute-start.9 = (bf16[512,1152]{1,0:T(8,128)(2,1)S(1)}, bf16[512,1152]{1,0:T(8,128)(2,1)S(1)}, u32[]{:S(2)}, u32[]{:S(2)}) collective-permute-start(bf16[512,1152]{1,0:T(8,128)(2,1)S(1)} %get-tuple-element.282), channel_id=1, source_target_pairs={{0,2},{2,4},{4,6},{6,8},{8,10},{10,12},{12,14},{1,3},{3,5},{5,7},{... | collective-permute-start | bytes 3538952 | tf_op jit(solution)/shard_map/ppermute | solution.py:565
  398.6 57.3 %collective-permute-start.10 = (bf16[512,1152]{1,0:T(8,128)(2,1)S(1)}, bf16[512,1152]{1,0:T(8,128)(2,1)S(1)}, u32[]{:S(2)}, u32[]{:S(2)}) collective-permute-start(bf16[512,1152]{1,0:T(8,128)(2,1)S(1)} %get-tuple-element.283), channel_id=1, source_target_pairs={{2,0},{4,2},{6,4},{8,6},{10,8},{12,10},{14,12},{3,1},{5,3},{7,5},{... | collective-permute-start | bytes 3538952 | tf_op jit(solution)/shard_map/ppermute | solution.py:566
  513.3 54.7 %collective-permute-start.11 = (bf16[512,1152]{1,0:T(8,128)(2,1)}, bf16[512,1152]{1,0:T(8,128)(2,1)S(1)}, u32[]{:S(2)}, u32[]{:S(2)}) collective-permute-start(bf16[512,1152]{1,0:T(8,128)(2,1)} %convolution_convert_fusion.23), channel_id=1, source_target_pairs={{0,2},{2,4},{4,6},{6,8},{8,10},{10,12},{12,14},{1,3},{3,5},{5,7},{... | collective-permute-start | bytes 3538952 | tf_op jit(solution)/shard_map/ppermute | solution.py:606
  517.7 50.3 %collective-permute-start.12 = (bf16[512,1152]{1,0:T(8,128)(2,1)}, bf16[512,1152]{1,0:T(8,128)(2,1)S(1)}, u32[]{:S(2)}, u32[]{:S(2)}) collective-permute-start(bf16[512,1152]{1,0:T(8,128)(2,1)} %convolution_convert_fusion.24), channel_id=1, source_target_pairs={{2,0},{4,2},{6,4},{8,6},{10,8},{12,10},{14,12},{3,1},{5,3},{7,5},{... | collective-permute-start | bytes 3538952 | tf_op jit(solution)/shard_map/ppermute | solution.py:605
  605.8 72.8 %collective-permute-start.13 = (bf16[1152,1152]{1,0:T(8,128)(2,1)}, bf16[1152,1152]{1,0:T(8,128)(2,1)}, u32[]{:S(2)}, u32[]{:S(2)}) collective-permute-start(bf16[1152,1152]{1,0:T(8,128)(2,1)} %get-tuple-element.258), channel_id=1, source_target_pairs={{0,16},{16,0},{1,17},{17,1},{2,18},{18,2},{3,19},{19,3},{4,20},{20... | collective-permute-start | bytes 7962632 | tf_op jit(solution)/shard_map/ppermute | solution.py:429
  605.8 72.8 %collective-permute-start.14 = (bf16[1152,1152]{1,0:T(8,128)(2,1)}, bf16[1152,1152]{1,0:T(8,128)(2,1)}, u32[]{:S(2)}, u32[]{:S(2)}) collective-permute-start(bf16[1152,1152]{1,0:T(8,128)(2,1)} %get-tuple-element.257), channel_id=1, source_target_pairs={{0,16},{16,0},{1,17},{17,1},{2,18},{18,2},{3,19},{19,3},{4,20},{20... | collective-permute-start | bytes 7962632 | tf_op jit(solution)/shard_map/ppermute | solution.py:429
  739.8 43.4 %collective-permute-start.24 = (bf16[1152,1152]{1,0:T(8,128)(2,1)}, bf16[1152,1152]{1,0:T(8,128)(2,1)}, u32[]{:S(2)}, u32[]{:S(2)}) collective-permute-start(bf16[1152,1152]{1,0:T(8,128)(2,1)} %broadcast_select_fusion.1), channel_id=1, source_target_pairs={{0,16},{16,0},{1,17},{17,1},{2,18},{18,2},{3,19},{19,3},{4,20},{20... | collective-permute-start | bytes 7962632 | tf_op jit(solution)/shard_map/ppermute | solution.py:429
  741.8 41.4 %collective-permute-start.23 = (bf16[1152,1152]{1,0:T(8,128)(2,1)}, bf16[1152,1152]{1,0:T(8,128)(2,1)}, u32[]{:S(2)}, u32[]{:S(2)}) collective-permute-start(bf16[1152,1152]{1,0:T(8,128)(2,1)} %broadcast_select_fusion.2), channel_id=1, source_target_pairs={{0,16},{16,0},{1,17},{17,1},{2,18},{18,2},{3,19},{19,3},{4,20},{20... | collective-permute-start | bytes 7962632 | tf_op jit(solution)/shard_map/ppermute | solution.py:429
  856.8 42.2 %collective-permute-start.28 = (bf16[2,2,2,72,1152]{4,3,0,1,2:T(8,128)(2,1)}, bf16[2,2,2,72,1152]{4,3,0,1,2:T(8,128)(2,1)}, u32[]{:S(2)}, u32[]{:S(2)}) collective-permute-start(bf16[2,2,2,72,1152]{4,3,0,1,2:T(8,128)(2,1)} %bitcast.430), channel_id=1, source_target_pairs={{0,1},{1,0},{2,3},{3,2},{4,5},{5,4},{6,7},{7,6},{8,9},{9,8},{10,11... | collective-permute-start | bytes 3981320 | tf_op jit(solution)/shard_map/ppermute | solution.py:349
  877.0 81.9 %collective-permute-start.37 = (bf16[1152,1152]{1,0:T(8,128)(2,1)S(1)}, bf16[1152,1152]{1,0:T(8,128)(2,1)S(1)}, u32[]{:S(2)}, u32[]{:S(2)}) collective-permute-start(bf16[1152,1152]{1,0:T(8,128)(2,1)S(1)} %copy-done.67), channel_id=1, source_target_pairs={{0,16},{16,0},{1,17},{17,1},{2,18},{18,2},{3,19},{19,3},{4,20},{20... | collective-permute-start | bytes 7962632 | tf_op jit(solution)/shard_map/ppermute | solution.py:429
  877.0 70.5 %collective-permute-start.38 = (bf16[1152,576]{0,1:T(8,128)(2,1)}, bf16[1152,576]{0,1:T(8,128)(2,1)S(1)}, u32[]{:S(2)}, u32[]{:S(2)}) collective-permute-start(bf16[1152,576]{0,1:T(8,128)(2,1)} %copy.78), channel_id=1, source_target_pairs={{0,16},{16,0},{1,17},{17,1},{2,18},{18,2},{3,19},{19,3},{4,20},{20... | collective-permute-start | bytes 3981320 | tf_op jit(solution)/shard_map/ppermute | solution.py:429
  899.7 46.4 %collective-permute-start.39 = (bf16[2,144,128]{2,1,0:T(8,128)(2,1)}, bf16[2,144,128]{2,1,0:T(8,128)(2,1)S(1)}, u32[]{:S(2)}, u32[]{:S(2)}) collective-permute-start(bf16[2,144,128]{2,1,0:T(8,128)(2,1)} %dynamic-slice_bitcast_fusion.35), channel_id=1, source_target_pairs={{0,1},{1,0},{2,3},{3,2},{4,5},{5,4},{6,7},{7,6},{8,9},{9,8},{10,11... | collective-permute-start | bytes 221192 | tf_op jit(solution)/shard_map/ppermute | solution.py:349
  903.0 53.9 %collective-permute-start.36 = (bf16[2,2,72,1152]{3,2,0,1:T(8,128)(2,1)S(1)}, bf16[2,2,72,1152]{3,2,0,1:T(8,128)(2,1)}, u32[]{:S(2)}, u32[]{:S(2)}) collective-permute-start(bf16[2,2,72,1152]{3,2,0,1:T(8,128)(2,1)S(1)} %dynamic-slice_bitcast_fusion.1), channel_id=1, source_target_pairs={{0,2},{2,0},{4,6},{6,4},{8,10},{10,8},{12,14},{14,12},{1,3},{3,1},... | collective-permute-start | bytes 1990664 | tf_op jit(solution)/shard_map/ppermute | solution.py:349
  905.9 52.4 %collective-permute-start.35 = (bf16[2,2,72,1152]{3,2,0,1:T(8,128)(2,1)S(1)}, bf16[2,2,72,1152]{3,2,0,1:T(8,128)(2,1)}, u32[]{:S(2)}, u32[]{:S(2)}) collective-permute-start(bf16[2,2,72,1152]{3,2,0,1:T(8,128)(2,1)S(1)} %dynamic-slice_bitcast_fusion.2), channel_id=1, source_target_pairs={{0,1},{1,0},{2,3},{3,2},{4,5},{5,4},{6,7},{7,6},{8,9},{9,8},{10,11... | collective-permute-start | bytes 1990664 | tf_op jit(solution)/shard_map/ppermute | solution.py:349
  956.9 69.7 %collective-permute-start.40 = (bf16[512,1152]{1,0:T(8,128)(2,1)}, bf16[512,1152]{1,0:T(8,128)(2,1)}, u32[]{:S(2)}, u32[]{:S(2)}) collective-permute-start(bf16[512,1152]{1,0:T(8,128)(2,1)} %get-tuple-element.174), channel_id=1, source_target_pairs={{0,1},{1,0},{2,3},{3,2},{4,5},{5,4},{6,7},{7,6},{8,9},{9,8},{10,11... | collective-permute-start | bytes 3538952 | tf_op jit(solution)/shard_map/ppermute | solution.py:706
  961.3 110.8 %collective-permute-start.47 = (bf16[144,128]{1,0:T(8,128)(2,1)}, bf16[144,128]{1,0:T(8,128)(2,1)}, u32[]{:S(2)}, u32[]{:S(2)}) collective-permute-start(bf16[144,128]{1,0:T(8,128)(2,1)} %dynamic-slice_bitcast_fusion.36), channel_id=1, source_target_pairs={{0,8},{2,10},{4,12},{6,14},{8,0},{10,2},{12,4},{14,6},{1,9},{3,11}... | collective-permute-start | bytes 110600 | tf_op jit(solution)/shard_map/ppermute | solution.py:349
  970.9 110.1 %collective-permute-start.46 = (bf16[2,2,2,72,576]{4,3,0,2,1:T(8,128)(2,1)}, bf16[2,2,2,72,576]{4,3,0,2,1:T(8,128)(2,1)}, u32[]{:S(2)}, u32[]{:S(2)}) collective-permute-start(bf16[2,2,2,72,576]{4,3,0,2,1:T(8,128)(2,1)} %bitcast.437), channel_id=1, source_target_pairs={{0,2},{2,0},{4,6},{6,4},{8,10},{10,8},{12,14},{14,12},{1,3},{3,1},... | collective-permute-start | bytes 1990664 | tf_op jit(solution)/shard_map/ppermute | solution.py:349
  975.7 105.8 %collective-permute-start.45 = (bf16[2,2,2,72,1152]{4,3,0,1,2:T(8,128)(2,1)}, bf16[2,2,2,72,1152]{4,3,0,1,2:T(8,128)(2,1)}, u32[]{:S(2)}, u32[]{:S(2)}) collective-permute-start(bf16[2,2,2,72,1152]{4,3,0,1,2:T(8,128)(2,1)} %bitcast.426), channel_id=1, source_target_pairs={{0,4},{2,6},{4,0},{6,2},{8,12},{10,14},{12,8},{14,10},{1,5},{3,7},... | collective-permute-start | bytes 3981320 | tf_op jit(solution)/shard_map/ppermute | solution.py:349
  979.7 93.8 %collective-permute-start.44 = (bf16[2,72,1152]{2,1,0:T(8,128)(2,1)}, bf16[2,72,1152]{2,1,0:T(8,128)(2,1)}, u32[]{:S(2)}, u32[]{:S(2)}) collective-permute-start(bf16[2,72,1152]{2,1,0:T(8,128)(2,1)} %dynamic-slice_bitcast_fusion.12), channel_id=1, source_target_pairs={{0,4},{2,6},{4,0},{6,2},{8,12},{10,14},{12,8},{14,10},{1,5},{3,7},... | collective-permute-start | bytes 995336 | tf_op jit(solution)/shard_map/ppermute | solution.py:349
  1026.5 52.1 %collective-permute-start.43 = (bf16[2,72,1152]{2,1,0:T(8,128)(2,1)}, bf16[2,72,1152]{2,1,0:T(8,128)(2,1)}, u32[]{:S(2)}, u32[]{:S(2)}) collective-permute-start(bf16[2,72,1152]{2,1,0:T(8,128)(2,1)} %dynamic-slice_bitcast_fusion.13), channel_id=1, source_target_pairs={{0,2},{2,0},{4,6},{6,4},{8,10},{10,8},{12,14},{14,12},{1,3},{3,1},... | collective-permute-start | bytes 995336 | tf_op jit(solution)/shard_map/ppermute | solution.py:349
  1079.5 84.7 %collective-permute-start.50 = (bf16[1152,576]{0,1:T(8,128)(2,1)}, bf16[1152,576]{0,1:T(8,128)(2,1)}, u32[]{:S(2)}, u32[]{:S(2)}) collective-permute-start(bf16[1152,576]{0,1:T(8,128)(2,1)} %copy.83), channel_id=1, source_target_pairs={{0,16},{16,0},{1,17},{17,1},{2,18},{18,2},{3,19},{19,3},{4,20},{20... | collective-permute-start | bytes 3981320 | tf_op jit(solution)/shard_map/ppermute | solution.py:429
  1080.9 83.3 %collective-permute-start.51 = (bf16[1152,576]{0,1:T(8,128)(2,1)}, bf16[1152,576]{0,1:T(8,128)(2,1)}, u32[]{:S(2)}, u32[]{:S(2)}) collective-permute-start(bf16[1152,576]{0,1:T(8,128)(2,1)} %copy.84), channel_id=1, source_target_pairs={{0,16},{16,0},{1,17},{17,1},{2,18},{18,2},{3,19},{19,3},{4,20},{20... | collective-permute-start | bytes 3981320 | tf_op jit(solution)/shard_map/ppermute | solution.py:429
  1080.9 83.3 %collective-permute-start.49 = (bf16[1152,576]{0,1:T(8,128)(2,1)}, bf16[1152,576]{0,1:T(8,128)(2,1)}, u32[]{:S(2)}, u32[]{:S(2)}) collective-permute-start(bf16[1152,576]{0,1:T(8,128)(2,1)} %copy.82), channel_id=1, source_target_pairs={{0,16},{16,0},{1,17},{17,1},{2,18},{18,2},{3,19},{19,3},{4,20},{20... | collective-permute-start | bytes 3981320 | tf_op jit(solution)/shard_map/ppermute | solution.py:429
  1100.4 45.5 %collective-permute-start.48 = (bf16[512,1152]{1,0:T(8,128)(2,1)S(1)}, bf16[512,1152]{1,0:T(8,128)(2,1)}, u32[]{:S(2)}, u32[]{:S(2)}) collective-permute-start(bf16[512,1152]{1,0:T(8,128)(2,1)S(1)} %copy-done.135), channel_id=1, source_target_pairs={{0,1},{1,0},{2,3},{3,2},{4,5},{5,4},{6,7},{7,6},{8,9},{9,8},{10,11... | collective-permute-start | bytes 3538952 | tf_op jit(solution)/shard_map/ppermute | solution.py:706
  1164.2 97.5 %collective-permute-start.57 = (f32[1,1152]{1,0:T(1,128)S(1)}, f32[1,1152]{1,0:T(1,128)S(1)}, u32[]{:S(2)}, u32[]{:S(2)}) collective-permute-start(f32[1,1152]{1,0:T(1,128)S(1)} %copy-done.122), channel_id=1, source_target_pairs={{0,16},{16,0},{1,17},{17,1},{2,18},{18,2},{3,19},{19,3},{4,20},{20... | collective-permute-start | bytes 13832 | tf_op jit(solution)/shard_map/ppermute | solution.py:429
  1166.1 40.6 %collective-permute-start.80 = (bf16[2,72,576]{2,1,0:T(8,128)(2,1)}, bf16[2,72,576]{2,1,0:T(8,128)(2,1)}, u32[]{:S(2)}, u32[]{:S(2)}) collective-permute-start(bf16[2,72,576]{2,1,0:T(8,128)(2,1)} %dynamic-slice_bitcast_fusion.19), channel_id=1, source_target_pairs={{0,1},{1,0},{2,3},{3,2},{4,5},{5,4},{6,7},{7,6},{8,9},{9,8},{10,11... | collective-permute-start | bytes 497672 | tf_op jit(solution)/shard_map/ppermute | solution.py:349
  1169.9 46.0 %collective-permute-start.77 = (bf16[2,72,1152]{2,1,0:T(8,128)(2,1)}, bf16[2,72,1152]{2,1,0:T(8,128)(2,1)}, u32[]{:S(2)}, u32[]{:S(2)}) collective-permute-start(bf16[2,72,1152]{2,1,0:T(8,128)(2,1)} %dynamic-slice_bitcast_fusion.11), channel_id=1, source_target_pairs={{0,2},{2,0},{4,6},{6,4},{8,10},{10,8},{12,14},{14,12},{1,3},{3,1},... | collective-permute-start | bytes 995336 | tf_op jit(solution)/shard_map/ppermute | solution.py:349
  1184.3 44.0 %collective-permute-start.56 = (bf16[2,2,2,72,576]{4,3,0,1,2:T(8,128)(2,1)}, bf16[2,2,2,72,576]{4,3,0,1,2:T(8,128)(2,1)}, u32[]{:S(2)}, u32[]{:S(2)}) collective-permute-start(bf16[2,2,2,72,576]{4,3,0,1,2:T(8,128)(2,1)} %bitcast.434), channel_id=1, source_target_pairs={{0,4},{2,6},{4,0},{6,2},{8,12},{10,14},{12,8},{14,10},{1,5},{3,7},... | collective-permute-start | bytes 1990664 | tf_op jit(solution)/shard_map/ppermute | solution.py:349
  1186.9 41.4 %collective-permute-start.55 = (bf16[2,2,2,72,576]{4,3,0,2,1:T(8,128)(2,1)}, bf16[2,2,2,72,576]{4,3,0,2,1:T(8,128)(2,1)}, u32[]{:S(2)}, u32[]{:S(2)}) collective-permute-start(bf16[2,2,2,72,576]{4,3,0,2,1:T(8,128)(2,1)} %bitcast.435), channel_id=1, source_target_pairs={{0,2},{2,0},{4,6},{6,4},{8,10},{10,8},{12,14},{14,12},{1,3},{3,1},... | collective-permute-start | bytes 1990664 | tf_op jit(solution)/shard_map/ppermute | solution.py:349
  (248 other events, 3108.8 us)
Sparse Core Ops, SparseCore 0:
  11.4 132.1 all-gather.2
  147.1 184.3 all-gather.4

commit v4 on v3

--- a/solution.py
+++ b/solution.py
@@ -335,9 +335,36 @@
     return first[turn:] + first[:turn] + [last]
 
 
-def column_halves(value):
-    middle = value.shape[1] // 2
-    return (value[:, :middle], value[:, middle:])
+def blank(shape):
+    return pl.pallas_call(
+        lambda out_ref: None,
+        out_specs=pl.BlockSpec(memory_space=pl.ANY),
+        out_shape=jax.ShapeDtypeStruct(shape, jnp.bfloat16),
+        name="blank",
+    )()
+
+
+def stack_halves(lower, upper):
+    depth = lower[0].shape[0]
+    stacked = blank((2 * depth, sum(part.shape[1] for part in lower)))
+    for index, parts in enumerate((lower, upper)):
+        column = 0
+        for part in parts:
+            stacked = lax.dynamic_update_slice(stacked, low(part), (index * depth, column))
+            column += part.shape[1]
+    return stacked
+
+
+def scatter_halves(stacked):
+    return lax.psum_scatter(stacked, ("bucket", "frame", "seq"), scatter_dimension=0, tiled=True)
+
+
+def whole_halves(is_first, own):
+    other = swapped(own)
+    return (
+        jnp.where(is_first, own, other).astype(jnp.float32),
+        jnp.where(is_first, other, own).astype(jnp.float32),
+    )
 
 
 def my_bit(bit):
@@ -404,21 +431,30 @@
         return self.kept
 
 
+def finish_together(chains):
+    for chain in chains:
+        while len(chain.order) > 1:
+            chain.advance()
+    first = chains[0]
+    parts = [
+        low(chain.kept.astype(jnp.float32) + chain.received.astype(jnp.float32))
+        for chain in chains
+    ]
+    bit = first.order[0]
+    index = my_bit(bit)
+    kept = [lax.dynamic_index_in_dim(part, index, 0, keepdims=False) for part in parts]
+    sent = [lax.dynamic_index_in_dim(part, 1 - index, 0, keepdims=False) for part in parts]
+    received = across(jnp.concatenate(sent, axis=1), bit)
+    own = jnp.concatenate(kept, axis=1).astype(jnp.float32) + received.astype(jnp.float32)
+    return whole_halves(first.is_first, low(own))
+
+
 def tick(main, chains):
     main, received = lax.optimization_barrier((main, [chain.received for chain in chains]))
     for chain, value in zip(chains, received):
         chain.received = value
         chain.advance()
     return main
-
-
-def both_of(chain):
-    own = chain.finish()
-    other = swapped(own)
-    return (
-        jnp.where(chain.is_first, own, other).astype(jnp.float32),
-        jnp.where(chain.is_first, other, own).astype(jnp.float32),
-    )
 
 
 def low(value):
@@ -481,19 +517,8 @@
     )
     gathered_b = gather_halves(
         is_first,
-        jnp.concatenate(
-            [
-                up_mixed[:, :half_ff],
-                down_wide[:, :half_ff],
-                temporal_qkv_weight[:, :width],
-                temporal_proj_weight,
-            ],
-            axis=1,
-        ),
-        jnp.concatenate(
-            [up_mixed[:, half_ff:], down_wide[:, half_ff:], temporal_qkv_weight[:, width:]],
-            axis=1,
-        ),
+        jnp.concatenate([up_mixed[:, :half_ff], down_wide[:, :half_ff]], axis=1),
+        jnp.concatenate([up_mixed[:, half_ff:], down_wide[:, half_ff:]], axis=1),
     )
 
     silu_cond = jax.nn.silu(condition.astype(jnp.float32))
@@ -535,6 +560,14 @@
     normed_m, recip_m = normalize(after_c)
     hidden_m = (normed_m * (1.0 + modulation[4]) + modulation[3]).astype(jnp.bfloat16)
 
+    temporal_lower, temporal_upper = lax.optimization_barrier(
+        (
+            jnp.concatenate([temporal_qkv_weight[:, :width], temporal_proj_weight], axis=1),
+            temporal_qkv_weight[:, width:],
+            query,
+        )
+    )[:2]
+    gathered_c = gather_halves(is_first, temporal_lower, temporal_upper)
     up_halves = (gathered_b[:width, :half_ff], gathered_b[width:, :half_ff])
     per_half = ff_blocks // 2
     down_halves = (gathered_b[:width, half_ff:ff_width], gathered_b[width:, half_ff:ff_width])
@@ -544,9 +577,9 @@
         ]
         for index in range(ff_blocks)
     ]
-    tquery_full = gathered_b[:width, ff_width : ff_width + width]
-    tproj_full = gathered_b[:width, ff_width + width :]
-    tpair_full = gathered_b[width:, ff_width:]
+    tquery_full = gathered_c[:width, :width]
+    tproj_full = gathered_c[:width, width:]
+    tpair_full = gathered_c[width:]
 
     upward_halves = [product(hidden_m, part) for part in up_halves]
     activated_halves = [gelu_tanh(part).astype(jnp.bfloat16) for part in upward_halves]
@@ -566,13 +599,7 @@
     hidden_next = lax.ppermute(hidden_t[:row_count], "frame", back)
     hidden_ext = jnp.concatenate([hidden_prev, hidden_t, hidden_next], axis=0)
     tquery = contract(tquery_full, hidden_t, 0, 1).astype(jnp.bfloat16)
-    tpair = jnp.concatenate(
-        [
-            low(contract(tpair_full, part, 0, 1))
-            for part in (hidden_prev, hidden_t, hidden_next)
-        ],
-        axis=1,
-    )
+    tpair = low(contract(tpair_full, hidden_ext, 0, 1))
     first_frame = lax.axis_index("frame") * frame_count
     clips_ext = jnp.concatenate(
         [jnp.full((1,), -1, jnp.int32), clip_ids[0], jnp.full((1,), -1, jnp.int32)]
@@ -604,9 +631,10 @@
     )
     to_prev = lax.ppermute(halo_prev, "frame", back)
     to_next = lax.ppermute(halo_next, "frame", ahead)
-    tpair_weight_grad = low(contract(hidden_ext, tpair_grad, 0, 1))
-    tquery_weight_grad = low(contract(hidden_t, tquery_grad, 0, 1))
-    tproj_weight_grad = low(contract(mixed, branch_t_grad, 1, 0))
+    stacked_c = stack_halves(
+        [contract(hidden_t, tquery_grad, 0, 1), contract(mixed, branch_t_grad, 1, 0)],
+        [contract(hidden_ext, tpair_grad, 0, 1)],
+    )
     hidden_t_grad = contract(tpair_grad[:, row_count:-row_count], tpair_full, 0, 1) + contract(
         tquery_grad, tquery_full, 0, 1
     )
@@ -618,14 +646,8 @@
         ],
         axis=0,
     )
-    hidden_t_grad, tpair_weight_grad, tquery_weight_grad, tproj_weight_grad = (
-        lax.optimization_barrier(
-            (hidden_t_grad, tpair_weight_grad, tquery_weight_grad, tproj_weight_grad)
-        )
-    )
-    chain_tqk = Chain(is_first, (tquery_weight_grad, tpair_weight_grad[:, :width]), 0)
-    chain_tpv = Chain(is_first, (tproj_weight_grad, tpair_weight_grad[:, width:]), 1)
-    chains_t = [chain_tqk, chain_tpv]
+    hidden_t_grad, stacked_c = lax.optimization_barrier((hidden_t_grad, stacked_c))
+    scattered_c = scatter_halves(stacked_c)
     grad_m = result_grad + normalize_back(hidden_t_grad * (1.0 + modulation[7]), normed_t, recip_t)
     gate_m_grad = jnp.sum(branch_m * grad_m, axis=0)
     branch_m_grad = low(modulation[5] * grad_m)
@@ -638,38 +660,20 @@
             ],
             axis=1,
         )
-        if index == 0:
-            activated_grad = tick(activated_grad, chains_t)
         gelu_back = jax.vjp(gelu_tanh, upward_halves[index])[1]
         upward_grads.append(low(gelu_back(activated_grad)[0]))
     hidden_m_grad = contract(upward_grads[0], up_halves[0], 1, 1) + contract(
         upward_grads[1], up_halves[1], 1, 1
     )
-    hidden_m_grad = tick(hidden_m_grad, chains_t)
-    up_grads = [low(contract(hidden_m, part, 0, 0)) for part in upward_grads]
-    down_grads = [low(contract(part, branch_m_grad, 0, 0)) for part in activated_parts]
-    hidden_m_grad, up_grads, down_grads = lax.optimization_barrier(
-        (hidden_m_grad, up_grads, down_grads)
-    )
-    chains_m = [
-        Chain(
-            is_first,
-            (
-                up_grads[0][:, width * index : width * (index + 1)],
-                up_grads[1][:, width * index : width * (index + 1)],
-            ),
-            index,
-        )
-        for index in range(per_half)
-    ] + [
-        Chain(is_first, (down_grads[index], down_grads[per_half + index]), per_half + index)
-        for index in range(per_half)
-    ]
-    hidden_m_grad = tick(hidden_m_grad, chains_t)
+    up_grads = [contract(hidden_m, part, 0, 0) for part in upward_grads]
+    down_grads = [contract(part, branch_m_grad, 0, 0) for part in activated_parts]
+    stacked_b = stack_halves(
+        [up_grads[0]] + down_grads[:per_half], [up_grads[1]] + down_grads[per_half:]
+    )
+    hidden_m_grad, stacked_b = lax.optimization_barrier((hidden_m_grad, stacked_b))
     grad_c = grad_m + normalize_back(hidden_m_grad * (1.0 + modulation[4]), normed_m, recip_m)
     cross_branch_grad = low(grad_c)
     cross_out_grad = low(contract(cross_proj_full, cross_branch_grad, 1, 1))
-    cross_out_grad = tick(cross_out_grad, chains_t + chains_m)
     cross_query_grad, text_grad = cross_backward(text_len, cross_query, text_pair, cross_out_grad)
     chain_text = Chain(is_first, (low(text_grad),), 1)
     chain_text.advance()
@@ -677,17 +681,17 @@
     gate_a_grad = jnp.sum(branch_a * grad_a, axis=0)
     branch_a_grad = low(modulation[2] * grad_a)
     attended_grad = low(contract(proj_full, branch_a_grad, 1, 1))
-    attended_grad = tick(attended_grad, chains_t + [chain_text])
+    attended_grad, scattered_c, stacked_b = lax.optimization_barrier(
+        (attended_grad, scattered_c, stacked_b)
+    )
+    scattered_b = scatter_halves(stacked_b)
+    attended_grad = tick(attended_grad, [chain_text])
     proj_grad = low(contract(attended, branch_a_grad, 1, 0))
     cross_q_grad = low(contract(after_low, cross_query_grad, 0, 1))
     cross_proj_grad = low(contract(cross_out, cross_branch_grad, 1, 0))
     attended_grad, proj_grad, cross_q_grad, cross_proj_grad = lax.optimization_barrier(
         (attended_grad, proj_grad, cross_q_grad, cross_proj_grad)
     )
-    chain_pq = Chain(is_first, (proj_grad, cross_q_grad), 2)
-    chain_cp = Chain(is_first, column_halves(cross_proj_grad), 1)
-    chains_c = [chain_pq, chain_cp, chain_text]
-    attended_grad = tick(attended_grad, chains_m + [chain_text])
     query_grads, pair_grads, rest_grads, rest_received = ([], [], [], [])
     for frame in range(frame_count):
         query_grad, pair_grad = spatial_backward(
@@ -712,7 +716,7 @@
             ]
         )
         if frame == 0:
-            attended_grad = tick(attended_grad, chains_m + chains_c)
+            attended_grad = tick(attended_grad, [chain_text])
         else:
             query_grads, pair_grads, rest_received[frame - 1] = lax.optimization_barrier(
                 (query_grads, pair_grads, rest_received[frame - 1])
@@ -725,16 +729,20 @@
         (query_grad, pair_grads, query_weight_grad, pair_weight_grad)
     )
     chains_a = [
-        Chain(is_first, column_halves(part), turn)
-        for turn, part in enumerate(
-            (query_weight_grad, pair_weight_grad[:, :width], pair_weight_grad[:, width:])
+        Chain(is_first, pair, turn)
+        for turn, pair in enumerate(
+            (
+                (pair_weight_grad[:, width:], cross_proj_grad),
+                (query_weight_grad, proj_grad),
+                (pair_weight_grad[:, :width], cross_q_grad),
+            )
         )
     ]
-    query_grad = tick(query_grad, chains_m + chains_c)
-    own_grad = jnp.concatenate(
+    pair_own = jnp.concatenate(
         [contract(part[:, :row_count], pair_full, 0, 1) for part in pair_grads], axis=0
-    ) + contract(query_grad, query_full, 0, 1)
-    own_grad, rest_received = tick((own_grad, rest_received), chains_a + chains_c)
+    )
+    pair_own = tick(pair_own, chains_a + [chain_text])
+    own_grad = pair_own + contract(query_grad, query_full, 0, 1)
     shift_a_grad = jnp.sum(own_grad, axis=0)
     scale_a_grad = jnp.sum(own_grad * normed_a, axis=0)
     for frame in range(frame_count):
@@ -743,6 +751,9 @@
             rest_normed = normed_rest[s][frame * row_count : (frame + 1) * row_count]
             shift_a_grad = shift_a_grad + jnp.sum(rest_rows, axis=0)
             scale_a_grad = scale_a_grad + jnp.sum(rest_rows * rest_normed, axis=0)
+    shift_a_grad, scale_a_grad, rest_received = lax.optimization_barrier(
+        (shift_a_grad, scale_a_grad, rest_received)
+    )
     hidden_a_grad = own_grad + jnp.concatenate(
         [sum(part.astype(jnp.float32) for part in parts) for parts in rest_received], axis=0
     )
@@ -772,36 +783,36 @@
     text_both = jnp.concatenate([text[0], swapped(text[0])], axis=0)
     slice_both = jnp.concatenate([text_low, swapped(text_low)], axis=1)
     text_kv_grad = contract(text_both, slice_both, 0, 1)
-    proj_shard, cross_q_shard = both_of(chain_pq)
-    cross_proj_shard = jnp.concatenate(both_of(chain_cp), axis=1)
-    qkv_shard = jnp.concatenate([part for chain in chains_a for part in both_of(chain)], axis=1)
-    tquery_shard, tkey_shard = both_of(chain_tqk)
-    tproj_shard, tvalue_shard = both_of(chain_tpv)
-    ff_shards = [both_of(chain) for chain in chains_m]
+    lower_a, upper_a = finish_together(chains_a)
+    lower_b, upper_b = whole_halves(is_first, scattered_b)
+    lower_c, upper_c = whole_halves(is_first, scattered_c)
     up_shard = (
-        jnp.concatenate(
-            [pair[side] for side in range(2) for pair in ff_shards[:per_half]], axis=1
-        )
+        jnp.concatenate([lower_b[:, :half_ff], upper_b[:, :half_ff]], axis=1)
         .reshape(shard_rows, ff_blocks, shards, shard_rows)
         .transpose(0, 2, 1, 3)
         .reshape(shard_rows, ff_width)
     )
     down_shard = jnp.concatenate(
-        [pair[side] for side in range(2) for pair in ff_shards[per_half:]], axis=0
+        [
+            half[:, half_ff + width * index : half_ff + width * (index + 1)]
+            for half in (lower_b, upper_b)
+            for index in range(per_half)
+        ],
+        axis=0,
     )
     return (
         result,
         latent_grad,
         ada_grad,
         text_kv_grad,
-        qkv_shard,
-        proj_shard,
-        cross_q_shard,
-        cross_proj_shard,
+        jnp.concatenate([lower_a[:, width : 2 * width], lower_a[:, 2 * width :], lower_a[:, :width]], axis=1),
+        upper_a[:, width : 2 * width],
+        upper_a[:, 2 * width :],
+        upper_a[:, :width],
         up_shard,
         down_shard,
-        jnp.concatenate([tquery_shard, tkey_shard, tvalue_shard], axis=1),
-        tproj_shard,
+        jnp.concatenate([lower_c[:, :width], upper_c], axis=1),
+        lower_c[:, width:],
     )
 
 

time: 1310 us -> 1060 us (0.81)
  waiting for transfers between devices: 369 us -> 288 us
  other arithmetic: 171 us -> 97 us
  local copies, waits for them, and re-layouts: 101 us -> 49.1 us
  starting transfers between devices: 84.4 us -> 56.1 us
    convert_element_type x55 -> x12, other arithmetic: 65.8 us -> 16.4 us  [advance(): value = (value.astype(jnp.float32) + self.received.astype(jnp.float32)).a...]
    ppermute x60 -> x26, waiting for transfers between devices: 174 us -> 126 us  [across(): lax.ppermute(value, axis, [(i, i ^ 1 << step) for i in range(lax.axis_siz...]
    ppermute x1, waiting for transfers between devices: 27.9 us -> 0.01 us  [per_device(): lax.ppermute(hidden_t[total_rows - row_count:], 'frame', ahead)]
    ppermute x60 -> x26, starting transfers between devices: 65.9 us -> 38 us  [across(): lax.ppermute(value, axis, [(i, i ^ 1 << step) for i in range(lax.axis_siz...]
    dynamic_slice x22 -> x0, local copies, waits for them, and re-layouts: 24.2 us -> none  [the longest x11 12.2 us: advance(): lax.dynamic_index_in_dim(value, 1 - index, dim, keepdims=False)]
    all_gather x2 -> x3, waiting for transfers between devices: 127 us -> 108 us  [gather_halves(): lax.all_gather(jnp.where(is_first, lower, upper), ('bucket', 'frame', 'se...]
    ppermute x2, waiting for transfers between devices: 0.01 us -> 18.7 us  [per_device(): lax.ppermute(rest_low[s * row_count:(s + 1) * row_count], 'seq', [(j, i)...]
    concatenate x6 -> x7, other arithmetic: 17.8 us -> 3.65 us  [the longest x1 1.15 us: per_device(): jnp.concatenate([half[:, half_ff + width * index:half_ff + width * (index...]
  transfers between devices with their start and end apart: 95 -> 48, of which waited for: 44 -> 21; matrix products, arithmetic and copies ran while one was open for 36% -> 48% of each run, Pallas kernels for 9% -> 15%
where the time goes in v4:
time: 1060 us; the launch traced here: 1050 us
  matrix products  387 us (37%)
  waiting for transfers between devices  288 us (27%)
  Pallas kernels  158 us (15%)
  other arithmetic  97 us (9%)
  starting transfers between devices  56.1 us (5%)
  local copies, waits for them, and re-layouts  49.1 us (5%)
  between operations  16.8 us (2%)
    dot_general x43, matrix products, contract(): lax.dot_general(left, right, (((left_dim,), (right_dim,)), ((), ())), pre...  321 us
    ppermute x26, waiting for transfers between devices, across(): lax.ppermute(value, axis, [(i, i ^ 1 << step) for i in range(lax.axis_siz...  126 us
    all_gather x3, waiting for transfers between devices, gather_halves(): lax.all_gather(jnp.where(is_first, lower, upper), ('bucket', 'frame', 'se...  108 us
    pallas_call x2, Pallas kernels, spatial_backward(): call(body, (HEADS,), [pl.BlockSpec((head_size, rows), lambda h: (h, frame...  68.9 us
    dot_general x6, matrix products, product(): return jnp.dot(left, right, preferred_element_type=jnp.float32)  60.3 us
    ppermute x26, starting transfers between devices, across(): lax.ppermute(value, axis, [(i, i ^ 1 << step) for i in range(lax.axis_siz...  38 us
    pallas_call x1, Pallas kernels, spatial_forward(): call(body, (frame_count, HEADS), [pl.BlockSpec((head_size, rows), lambda...  37.5 us
    ppermute x1, waiting for transfers between devices, per_device(): latent_rest = [lax.ppermute(latent[0], 'seq', shift) for shift in shifts]  28.4 us
  transfers between devices with their start and end apart: 48, of which 21 were waited for; matrix products, arithmetic and copies ran while one was open for 48% of the time, Pallas kernels for 15%

profile of v4, /device:TPU:0, one launch (start us, length us, event | category | flops | bytes accessed | tf_op | source)
XLA Modules:
  0.0 1051.9 jit_solution(12389242763953762356)
XLA Ops:
  50.8 8.4 collective-permute-done.7
  61.8 13.6 %collective-permute-done.8 = bf16[1152,128]{1,0:T(8,128)(2,1)S(1)} collective-permute-done((bf16[1152,128]{1,0:T(8,128)(2,1)S(1)}, bf16[1152,128]{1,0:T(8,128)(2,1)S(1)}, u32[]{:S(2)}, u32[]{:S(2)}) %collective-permute-start.8) | collective-permute-done | bytes 294944 | tf_op jit(solution)/shard_map/ppermute | solution.py:376
  75.5 28.4 %collective-permute-done.4 = bf16[2,512,1152]{2,1,0:T(8,128)(2,1)} collective-permute-done((bf16[2,512,1152]{2,1,0:T(8,128)(2,1)}, bf16[2,512,1152]{2,1,0:T(8,128)(2,1)}, u32[]{:S(2)}, u32[]{:S(2)}) %collective-permute-start.4) | collective-permute-done | bytes 2359328 | tf_op jit(solution)/shard_map/ppermute | solution.py:501
  114.3 31.2 %all-gather.4.cloned.1.call-done = bf16[2304,3456]{1,0:T(8,128)(2,1)} async-done(((bf16[72,3456]{1,0:T(8,128)(2,1)}), bf16[2304,3456]{1,0:T(8,128)(2,1)}) %all-gather.4.cloned.1.call-update) | async-done | bytes 15925264 | tf_op jit(solution)/shard_map/all_gather | solution.py:317
  158.3 18.3 %convolution_convert_fusion.3.k_ref.v_ref = bf16[2304,2048]{1,0:T(8,128)(2,1)} fusion(bf16[2048,1152]{1,0:T(8,128)(2,1)} %bitcast.246, bf16[2304,3456]{1,0:T(8,128)(2,1)} %all-gather.4.cloned.1.call-done), kind=kOutput, calls=%fused_computation.9 | convolution fusion | flops 10876354560 | bytes 19464192 | tf_op jit(solution)/shard_map/dot_general | solution.py:24
  176.6 37.5 %spatial_forward.1 = (bf16[1152,1024]{1,0:T(8,128)(2,1)S(1)}, f32[32,1,512]{2,1,0:T(1,128)S(1)}) custom-call(bf16[1152,1024]{1,0:T(8,128)(2,1)S(1)} %convolution_convert_fusion.20.q_ref, bf16[2304,2048]{1,0:T(8,128)(2,1)} %convolution_convert_fusion.3.k_ref.v_ref, bf16[2304,2048]{1,0:T(8,128)(2,1)} %convolution_convert_fusion.3.k_ref.v_ref), custom_call_target="tpu_custom_call" | custom-call | tf_op jit(solution)/shard_map/spatial_forward/pallas_call | solution.py:57
  214.1 9.0 fusion.70
  229.3 8.5 cross_forward.1
  249.7 33.7 %all-gather.6.cloned.1.call-done = bf16[2304,4608]{1,0:T(8,128)(2,1)} async-done(((bf16[72,4608]{1,0:T(8,128)(2,1)}), bf16[2304,4608]{1,0:T(8,128)(2,1)}) %all-gather.6.cloned.1.call-update) | async-done | bytes 21233680 | tf_op jit(solution)/shard_map/all_gather | solution.py:317
  283.4 12.7 %multiply_convert_fusion.1 = (bf16[1024,2304]{1,0:T(8,128)(2,1)S(1)}, f32[1024,2304]{1,0:T(8,128)}) fusion(bf16[1024,1152]{1,0:T(8,128)(2,1)} %add_convert_fusion.4, bf16[2304,4608]{1,0:T(8,128)(2,1)} %all-gather.6.cloned.1.call-done), kind=kOutput, calls=%fused_computation.33 | convolution fusion | flops 5457051648 | bytes 21823488 | tf_op jit(solution)/shard_map/dot_general | solution.py:20
  310.1 13.0 %multiply_convert_fusion = (bf16[1024,2304]{1,0:T(8,128)(2,1)S(1)}, f32[1024,2304]{1,0:T(8,128)}) fusion(bf16[1024,1152]{1,0:T(8,128)(2,1)S(1)} %copy-done.39, bf16[2304,4608]{1,0:T(8,128)(2,1)} %all-gather.6.cloned.1.call-done), kind=kOutput, calls=%fused_computation.32 | convolution fusion | flops 5457051648 | bytes 21823488 | tf_op jit(solution)/shard_map/dot_general | solution.py:20
  323.1 8.5 fusion.102
  331.7 12.1 %fusion.180 = (f32[1024]{0:T(1024)S(1)}, f32[1024,1152]{1,0:T(8,128)S(1)}, f32[1024,1152]{1,0:T(8,128)}) fusion(f32[1024,1152]{1,0:T(8,128)S(1)} %bitcast.228, f32[1152]{0:T(1024)S(1)} %get-tuple-element.159, bf16[2304,4608]{1,0:T(8,128)(2,1)} %all-gather.6.cloned.1.call-done, bf16[1024,2304]{1,0:T(8,128)(2,1)} %copy-done.42, f32[1024,1152]{1,0:T(8,128)} %fusion.102, ...), kind=kOutput, calls=%fused_computation.369 | convolution fusion | flops 2724985856 | bytes 33333760 | tf_op jit(solution)/shard_map/dot_general | solution.py:20
  359.5 43.0 %all-gather.8.cloned.1.call-done = bf16[2304,2304]{1,0:T(8,128)(2,1)} async-done(((bf16[72,2304]{1,0:T(8,128)(2,1)}), bf16[2304,2304]{1,0:T(8,128)(2,1)}) %all-gather.8.cloned.1.call-update) | async-done | bytes 10616848 | tf_op jit(solution)/shard_map/all_gather | solution.py:317
  408.4 17.4 %convolution_convert_fusion.2.k_ref.v_ref = bf16[2304,2048]{1,0:T(8,128)(2,1)} fusion(bf16[2304,2304]{1,0:T(8,128)(2,1)} %all-gather.8.cloned.1.call-done, bf16[512,1152]{1,0:T(8,128)(2,1)} %collective-permute-done.10, bf16[1024,1152]{1,0:T(8,128)(2,1)S(1)} %copy-done.26, bf16[512,1152]{1,0:T(8,128)(2,1)} %collective-permute-done.9), kind=kOutput, calls=%fused_computation.8 | convolution fusion | flops 10890510336 | bytes 19464192 | tf_op jit(solution)/shard_map/dot_general | solution.py:24
  425.7 10.9 %temporal_forward.1 = bf16[1152,1024]{1,0:T(8,128)(2,1)S(1)} custom-call(s32[2,2]{1,0:T(2,128)S(1)} %add_convert_fusion.8.live_ref, bf16[1152,1024]{1,0:T(8,128)(2,1)S(1)} %convolution_convert_fusion.18.q_ref, bf16[2304,2048]{1,0:T(8,128)(2,1)} %convolution_convert_fusion.2.k_ref.v_ref, bf16[2304,2048]{1,0:T(8,128)(2,1)} %convolution_convert_fusion.2.k_ref.v_ref), custom_call_target="tpu_custom_call" | custom-call | tf_op jit(solution)/shard_map/temporal_forward/pallas_call | solution.py:220
  444.2 16.8 %temporal_backward.1 = (bf16[1152,1024]{1,0:T(8,128)(2,1)S(1)}, bf16[2,1152,2048]{2,1,0:T(8,128)(2,1)}) custom-call(s32[2,2]{1,0:T(2,128)S(1)} %add_convert_fusion.8.live_ref, bf16[1152,1024]{1,0:T(8,128)(2,1)S(1)} %convolution_convert_fusion.18.q_ref, bf16[2304,2048]{1,0:T(8,128)(2,1)} %convolution_convert_fusion.2.k_ref.v_ref, ...), custom_call_target="tpu_custom_call" | custom-call | tf_op jit(solution)/shard_map/temporal_backward/pallas_call | solution.py:275
  491.0 15.7 %fusion.2 = bf16[2304,2304]{1,0:T(8,128)(2,1)} fusion(bf16[2304,2304]{1,0:T(8,128)(2,1)} %fusion.24, bf16[2304,2048]{1,0:T(8,128)(2,1)} %bitcast.276, bf16[512,1152]{1,0:T(8,128)(2,1)} %collective-permute-done.10, bf16[1024,1152]{1,0:T(8,128)(2,1)S(1)} %copy-done.26, bf16[512,1152]{1,0:T(8,128)(2,1)} %collective-permute-done.9), kind=kOutput, calls=%fused_computation.12 | convolution fusion | flops 10888445952 | bytes 19464192 | tf_op jit(solution)/shard_map/dot_general | solution.py:24
  506.7 10.1 fusion.45
  535.4 10.2 fusion.29
  626.4 10.0 fusion.47
  636.4 10.0 fusion.55
  656.9 15.4 %cross_backward.1 = (bf16[1152,1024]{1,0:T(8,128)(2,1)S(1)}, f32[2,1152,128]{2,1,0:T(8,128)S(1)}) custom-call(s32[1]{0:T(128)S(6)} %copy.52.length_ref, bf16[1152,1024]{1,0:T(8,128)(2,1)} %copy-done.3, bf16[2304,128]{1,0:T(8,128)(2,1)S(1)} %pad_maximum_fusion.12.k_ref.v_ref, bf16[2304,128]{1,0:T(8,128)(2,1)S(1)} %pad_maximum_fusion.12.k_ref.v_ref, ...), custom_call_target="tpu_custom_call" | custom-call | tf_op jit(solution)/shard_map/cross_backward/pallas_call | solution.py:166
  708.8 34.1 %spatial_backward.2 = (bf16[1152,512]{1,0:T(8,128)(2,1)S(1)}, bf16[2,1152,1024]{2,1,0:T(8,128)(2,1)}) custom-call(bf16[1152,1024]{1,0:T(8,128)(2,1)S(1)} %convolution_convert_fusion.20.q_ref, bf16[2304,2048]{1,0:T(8,128)(2,1)} %convolution_convert_fusion.3.k_ref.v_ref, bf16[2304,2048]{1,0:T(8,128)(2,1)} %convolution_convert_fusion.3.k_ref.v_ref, ...), custom_call_target="tpu_custom_call" | custom-call | tf_op jit(solution)/shard_map/spatial_backward/pallas_call | solution.py:94
  742.9 8.6 fusion.189
  753.7 34.8 %spatial_backward.3 = (bf16[1152,512]{1,0:T(8,128)(2,1)S(1)}, bf16[2,1152,1024]{2,1,0:T(8,128)(2,1)}) custom-call(bf16[1152,1024]{1,0:T(8,128)(2,1)S(1)} %convolution_convert_fusion.20.q_ref, bf16[2304,2048]{1,0:T(8,128)(2,1)} %convolution_convert_fusion.3.k_ref.v_ref, bf16[2304,2048]{1,0:T(8,128)(2,1)} %convolution_convert_fusion.3.k_ref.v_ref, ...), custom_call_target="tpu_custom_call" | custom-call | tf_op jit(solution)/shard_map/spatial_backward/pallas_call | solution.py:94
  788.6 8.8 fusion.84
  805.2 14.3 %convolution_convert_fusion.4 = bf16[1152,2304]{1,0:T(8,128)(2,1)S(1)} fusion(bf16[2048,1152]{1,0:T(8,128)(2,1)S(1)} %bitcast.249, bf16[2304,1024]{1,0:T(8,128)(2,1)} %bitcast.286, bf16[2304,1024]{1,0:T(8,128)(2,1)S(1)} %bitcast.281), kind=kOutput, calls=%fused_computation.10 | convolution fusion | flops 10893164544 | bytes 19464192 | tf_op jit(solution)/shard_map/dot_general | solution.py:24
  867.6 18.7 %collective-permute-done.20 = bf16[512,1152]{1,0:T(8,128)(2,1)S(1)} collective-permute-done((bf16[512,1152]{1,0:T(8,128)(2,1)S(1)}, bf16[512,1152]{1,0:T(8,128)(2,1)S(1)}, u32[]{:S(2)}, u32[]{:S(2)}) %collective-permute-start.20) | collective-permute-done | bytes 1179680 | tf_op jit(solution)/shard_map/ppermute | solution.py:710
  900.5 22.4 %collective-permute-done.23 = bf16[2,2,2,72,1152]{4,3,2,1,0:T(8,128)(2,1)} collective-permute-done((bf16[2,2,2,72,1152]{4,3,2,1,0:T(8,128)(2,1)}, bf16[2,2,2,72,1152]{4,3,2,1,0:T(8,128)(2,1)}, u32[]{:S(2)}, u32[]{:S(2)}) %collective-permute-start.23) | collective-permute-done | bytes 1327136 | tf_op jit(solution)/shard_map/ppermute | solution.py:376
  944.8 25.7 %collective-permute-done.35 = bf16[2,2,72,1152]{3,2,1,0:T(8,128)(2,1)S(1)} collective-permute-done((bf16[2,2,72,1152]{3,2,1,0:T(8,128)(2,1)S(1)}, bf16[2,2,72,1152]{3,2,1,0:T(8,128)(2,1)S(1)}, u32[]{:S(2)}, u32[]{:S(2)}) %collective-permute-start.35) | collective-permute-done | bytes 663584 | tf_op jit(solution)/shard_map/ppermute | solution.py:376
  999.5 19.0 %collective-permute-done.39 = bf16[72,3456]{1,0:T(8,128)(2,1)S(1)} collective-permute-done((bf16[72,3456]{1,0:T(8,128)(2,1)S(1)}, bf16[72,3456]{1,0:T(8,128)(2,1)S(1)}, u32[]{:S(2)}, u32[]{:S(2)}) %collective-permute-start.39) | collective-permute-done | bytes 497696 | tf_op jit(solution)/shard_map/ppermute | solution.py:376
  (502 shorter events, 454.3 us)
Async XLA Ops:
  7.2 138.2 %all-gather.4.cloned.1.call-start = ((), (), s32[]{:S(2)}) async-start(), calls=%async_computation.2 | async-start | bytes 16422912 | tf_op jit(solution)/shard_map/all_gather | solution.py:317
  9.5 273.9 %all-gather.6.cloned.1.call-start = ((), (), s32[]{:S(2)}) async-start(), calls=%async_computation.3 | async-start | bytes 21897216 | tf_op jit(solution)/shard_map/all_gather | solution.py:317
  22.2 380.3 %all-gather.8.cloned.1.call-start = ((), (), s32[]{:S(2)}) async-start(), calls=%async_computation.4 | async-start | bytes 10948608 | tf_op jit(solution)/shard_map/all_gather | solution.py:317
  24.7 18.3 %collective-permute-start.5 = (bf16[144,128]{1,0:T(8,128)(2,1)S(1)}, bf16[144,128]{1,0:T(8,128)(2,1)S(1)}, u32[]{:S(2)}, u32[]{:S(2)}) collective-permute-start(bf16[144,128]{1,0:T(8,128)(2,1)S(1)} %convolution_convert_fusion.21), channel_id=1, source_target_pairs={{0,1},{1,0},{2,3},{3,2},{4,5},{5,4},{6,7},{7,6},{8,9},{9,8},{10,11... | collective-permute-start | bytes 110600 | tf_op jit(solution)/shard_map/ppermute | solution.py:376
  29.0 74.9 %collective-permute-start.4 = (bf16[2,512,1152]{2,1,0:T(8,128)(2,1)}, bf16[2,512,1152]{2,1,0:T(8,128)(2,1)}, u32[]{:S(2)}, u32[]{:S(2)}) collective-permute-start(bf16[2,512,1152]{2,1,0:T(8,128)(2,1)} %bitcast.231), channel_id=1, source_target_pairs={{1,0},{0,1},{3,2},{2,3},{5,4},{4,5},{7,6},{6,7},{9,8},{8,9},{11,10... | collective-permute-start | bytes 7077896 | tf_op jit(solution)/shard_map/ppermute | solution.py:501
  152.0 549.9 %reduce-scatter.3.cloned.1.call-start = ((), (), s32[]{:S(2)}) async-start(), calls=%async_computation.5 | async-start | bytes 10948608 | tf_op jit(solution)/shard_map/reduce_scatter | solution.py:359
  152.1 867.2 %collective-permute-start.30 = (bf16[128,4096]{1,0:T(8,128)(2,1)}, bf16[128,4096]{1,0:T(8,128)(2,1)}, u32[]{:S(2)}, u32[]{:S(2)}) collective-permute-start(bf16[128,4096]{1,0:T(8,128)(2,1)} %bitcast.253), channel_id=1, source_target_pairs={{0,16},{16,0},{1,17},{17,1},{2,18},{18,2},{3,19},{19,3},{4,20},{20... | collective-permute-start | bytes 3145736 | tf_op jit(solution)/shard_map/ppermute | solution.py:465
  348.1 60.2 %collective-permute-start.10 = (bf16[512,1152]{1,0:T(8,128)(2,1)}, bf16[512,1152]{1,0:T(8,128)(2,1)}, u32[]{:S(2)}, u32[]{:S(2)}) collective-permute-start(bf16[512,1152]{1,0:T(8,128)(2,1)} %get-tuple-element.184), channel_id=1, source_target_pairs={{2,0},{4,2},{6,4},{8,6},{10,8},{12,10},{14,12},{3,1},{5,3},{7,5},{... | collective-permute-start | bytes 3538952 | tf_op jit(solution)/shard_map/ppermute | solution.py:599
  349.4 58.9 %collective-permute-start.9 = (bf16[512,1152]{1,0:T(8,128)(2,1)}, bf16[512,1152]{1,0:T(8,128)(2,1)}, u32[]{:S(2)}, u32[]{:S(2)}) collective-permute-start(bf16[512,1152]{1,0:T(8,128)(2,1)} %get-tuple-element.183), channel_id=1, source_target_pairs={{0,2},{2,4},{4,6},{6,8},{8,10},{10,12},{12,14},{1,3},{3,5},{5,7},{... | collective-permute-start | bytes 3538952 | tf_op jit(solution)/shard_map/ppermute | solution.py:598
  476.9 52.8 %collective-permute-start.11 = (bf16[512,1152]{1,0:T(8,128)(2,1)}, bf16[512,1152]{1,0:T(8,128)(2,1)}, u32[]{:S(2)}, u32[]{:S(2)}) collective-permute-start(bf16[512,1152]{1,0:T(8,128)(2,1)} %fusion.67), channel_id=1, source_target_pairs={{0,2},{2,4},{4,6},{6,8},{8,10},{10,12},{12,14},{1,3},{3,5},{5,7},{... | collective-permute-start | bytes 3538952 | tf_op jit(solution)/shard_map/ppermute | solution.py:633
  479.7 49.9 %collective-permute-start.12 = (bf16[512,1152]{1,0:T(8,128)(2,1)}, bf16[512,1152]{1,0:T(8,128)(2,1)}, u32[]{:S(2)}, u32[]{:S(2)}) collective-permute-start(bf16[512,1152]{1,0:T(8,128)(2,1)} %fusion.64), channel_id=1, source_target_pairs={{2,0},{4,2},{6,4},{8,6},{10,8},{12,10},{14,12},{3,1},{5,3},{7,5},{... | collective-permute-start | bytes 3538952 | tf_op jit(solution)/shard_map/ppermute | solution.py:632
  549.6 477.5 %reduce-scatter.5.cloned.1.call-start = ((), (), s32[]{:S(2)}) async-start(), calls=%async_computation.6 | async-start | bytes 21897216 | tf_op jit(solution)/shard_map/reduce_scatter | solution.py:359
  673.1 28.9 %collective-permute-start.13 = (bf16[2,2,2,144,128]{4,3,2,1,0:T(8,128)(2,1)}, bf16[2,2,2,144,128]{4,3,2,1,0:T(8,128)(2,1)}, u32[]{:S(2)}, u32[]{:S(2)}) collective-permute-start(bf16[2,2,2,144,128]{4,3,2,1,0:T(8,128)(2,1)} %dynamic-slice_bitcast_fusion.9), channel_id=1, source_target_pairs={{0,2},{2,0},{4,6},{6,4},{8,10},{10,8},{12,14},{14,12},{1,3},{3,1},... | collective-permute-start | bytes 884744 | tf_op jit(solution)/shard_map/ppermute | solution.py:376
  701.9 95.4 %collective-permute-start.42 = (bf16[72,2304]{1,0:T(8,128)(2,1)}, bf16[72,2304]{1,0:T(8,128)(2,1)S(1)}, u32[]{:S(2)}, u32[]{:S(2)}) collective-permute-start(bf16[72,2304]{1,0:T(8,128)(2,1)} %reduce-scatter.3.cloned.1.call-done), channel_id=1, source_target_pairs={{0,16},{16,0},{1,17},{17,1},{2,18},{18,2},{3,19},{19,3},{4,20},{20... | collective-permute-start | bytes 995336 | tf_op jit(solution)/shard_map/ppermute | solution.py:465
  703.1 50.0 %collective-permute-start.14 = (bf16[2,2,144,128]{3,2,1,0:T(8,128)(2,1)S(1)}, bf16[2,2,144,128]{3,2,1,0:T(8,128)(2,1)S(1)}, u32[]{:S(2)}, u32[]{:S(2)}) collective-permute-start(bf16[2,2,144,128]{3,2,1,0:T(8,128)(2,1)S(1)} %dynamic-slice_bitcast_fusion.16), channel_id=1, source_target_pairs={{0,4},{2,6},{4,0},{6,2},{8,12},{10,14},{12,8},{14,10},{1,5},{3,7},... | collective-permute-start | bytes 442376 | tf_op jit(solution)/shard_map/ppermute | solution.py:376
  751.5 47.8 %collective-permute-start.15 = (bf16[512,1152]{1,0:T(8,128)(2,1)S(1)}, bf16[512,1152]{1,0:T(8,128)(2,1)S(1)}, u32[]{:S(2)}, u32[]{:S(2)}) collective-permute-start(bf16[512,1152]{1,0:T(8,128)(2,1)S(1)} %get-tuple-element.106), channel_id=1, source_target_pairs={{0,1},{1,0},{2,3},{3,2},{4,5},{5,4},{6,7},{7,6},{8,9},{9,8},{10,11... | collective-permute-start | bytes 3538952 | tf_op jit(solution)/shard_map/ppermute | solution.py:710
  753.2 94.4 %collective-permute-start.19 = (bf16[2,144,128]{2,1,0:T(8,128)(2,1)S(1)}, bf16[2,144,128]{2,1,0:T(8,128)(2,1)S(1)}, u32[]{:S(2)}, u32[]{:S(2)}) collective-permute-start(bf16[2,144,128]{2,1,0:T(8,128)(2,1)S(1)} %dynamic-slice_bitcast_fusion.17), channel_id=1, source_target_pairs={{0,1},{1,0},{2,3},{3,2},{4,5},{5,4},{6,7},{7,6},{8,9},{9,8},{10,11... | collective-permute-start | bytes 221192 | tf_op jit(solution)/shard_map/ppermute | solution.py:376
  821.4 26.5 %collective-permute-start.17 = (bf16[1152,1152]{1,0:T(8,128)(2,1)}, bf16[1152,1152]{1,0:T(8,128)(2,1)}, u32[]{:S(2)}, u32[]{:S(2)}) collective-permute-start(bf16[1152,1152]{1,0:T(8,128)(2,1)} %broadcast_select_fusion.1), channel_id=1, source_target_pairs={{0,16},{16,0},{1,17},{17,1},{2,18},{18,2},{3,19},{19,3},{4,20},{20... | collective-permute-start | bytes 7962632 | tf_op jit(solution)/shard_map/ppermute | solution.py:465
  826.2 23.3 %collective-permute-start.16 = (bf16[1152,1152]{1,0:T(8,128)(2,1)}, bf16[1152,1152]{1,0:T(8,128)(2,1)S(1)}, u32[]{:S(2)}, u32[]{:S(2)}) collective-permute-start(bf16[1152,1152]{1,0:T(8,128)(2,1)} %get-tuple-element.173), channel_id=1, source_target_pairs={{0,16},{16,0},{1,17},{17,1},{2,18},{18,2},{3,19},{19,3},{4,20},{20... | collective-permute-start | bytes 7962632 | tf_op jit(solution)/shard_map/ppermute | solution.py:465
  826.2 23.3 %collective-permute-start.18 = (bf16[1152,1152]{1,0:T(8,128)(2,1)}, bf16[1152,1152]{1,0:T(8,128)(2,1)}, u32[]{:S(2)}, u32[]{:S(2)}) collective-permute-start(bf16[1152,1152]{1,0:T(8,128)(2,1)} %get-tuple-element.172), channel_id=1, source_target_pairs={{0,16},{16,0},{1,17},{17,1},{2,18},{18,2},{3,19},{19,3},{4,20},{20... | collective-permute-start | bytes 7962632 | tf_op jit(solution)/shard_map/ppermute | solution.py:465
  847.9 174.5 %collective-permute-start.24 = (f32[1,1152]{1,0:T(1,128)S(1)}, f32[1,1152]{1,0:T(1,128)S(1)}, u32[]{:S(2)}, u32[]{:S(2)}) collective-permute-start(f32[1,1152]{1,0:T(1,128)S(1)} %copy-done.64), channel_id=1, source_target_pairs={{0,16},{16,0},{1,17},{17,1},{2,18},{18,2},{3,19},{19,3},{4,20},{20... | collective-permute-start | bytes 13832 | tf_op jit(solution)/shard_map/ppermute | solution.py:465
  848.5 37.7 %collective-permute-start.20 = (bf16[512,1152]{1,0:T(8,128)(2,1)S(1)}, bf16[512,1152]{1,0:T(8,128)(2,1)S(1)}, u32[]{:S(2)}, u32[]{:S(2)}) collective-permute-start(bf16[512,1152]{1,0:T(8,128)(2,1)S(1)} %copy-done.69), channel_id=1, source_target_pairs={{0,1},{1,0},{2,3},{3,2},{4,5},{5,4},{6,7},{7,6},{8,9},{9,8},{10,11... | collective-permute-start | bytes 3538952 | tf_op jit(solution)/shard_map/ppermute | solution.py:710
  856.4 42.3 %collective-permute-start.22 = (bf16[2,2,2,72,1152]{4,3,2,1,0:T(8,128)(2,1)}, bf16[2,2,2,72,1152]{4,3,2,1,0:T(8,128)(2,1)}, u32[]{:S(2)}, u32[]{:S(2)}) collective-permute-start(bf16[2,2,2,72,1152]{4,3,2,1,0:T(8,128)(2,1)} %dynamic-slice_bitcast_fusion.1), channel_id=1, source_target_pairs={{0,2},{2,0},{4,6},{6,4},{8,10},{10,8},{12,14},{14,12},{1,3},{3,1},... | collective-permute-start | bytes 3981320 | tf_op jit(solution)/shard_map/ppermute | solution.py:376
  863.0 59.9 %collective-permute-start.23 = (bf16[2,2,2,72,1152]{4,3,2,1,0:T(8,128)(2,1)}, bf16[2,2,2,72,1152]{4,3,2,1,0:T(8,128)(2,1)}, u32[]{:S(2)}, u32[]{:S(2)}) collective-permute-start(bf16[2,2,2,72,1152]{4,3,2,1,0:T(8,128)(2,1)} %dynamic-slice_bitcast_fusion), channel_id=1, source_target_pairs={{0,4},{2,6},{4,0},{6,2},{8,12},{10,14},{12,8},{14,10},{1,5},{3,7},... | collective-permute-start | bytes 3981320 | tf_op jit(solution)/shard_map/ppermute | solution.py:376
  886.3 36.6 %collective-permute-start.21 = (bf16[2,2,2,72,1152]{4,3,2,1,0:T(8,128)(2,1)}, bf16[2,2,2,72,1152]{4,3,2,1,0:T(8,128)(2,1)}, u32[]{:S(2)}, u32[]{:S(2)}) collective-permute-start(bf16[2,2,2,72,1152]{4,3,2,1,0:T(8,128)(2,1)} %dynamic-slice_bitcast_fusion.2), channel_id=1, source_target_pairs={{0,1},{1,0},{2,3},{3,2},{4,5},{5,4},{6,7},{7,6},{8,9},{9,8},{10,11... | collective-permute-start | bytes 3981320 | tf_op jit(solution)/shard_map/ppermute | solution.py:376
  898.7 100.4 %collective-permute-start.31 = (bf16[144,128]{1,0:T(8,128)(2,1)}, bf16[144,128]{1,0:T(8,128)(2,1)S(1)}, u32[]{:S(2)}, u32[]{:S(2)}) collective-permute-start(bf16[144,128]{1,0:T(8,128)(2,1)} %dynamic-slice_bitcast_fusion.18), channel_id=1, source_target_pairs={{0,8},{2,10},{4,12},{6,14},{8,0},{10,2},{12,4},{14,6},{1,9},{3,11}... | collective-permute-start | bytes 110600 | tf_op jit(solution)/shard_map/ppermute | solution.py:376
  941.8 28.7 %collective-permute-start.35 = (bf16[2,2,72,1152]{3,2,1,0:T(8,128)(2,1)S(1)}, bf16[2,2,72,1152]{3,2,1,0:T(8,128)(2,1)S(1)}, u32[]{:S(2)}, u32[]{:S(2)}) collective-permute-start(bf16[2,2,72,1152]{3,2,1,0:T(8,128)(2,1)S(1)} %dynamic-slice_bitcast_fusion.4), channel_id=1, source_target_pairs={{0,4},{2,6},{4,0},{6,2},{8,12},{10,14},{12,8},{14,10},{1,5},{3,7},... | collective-permute-start | bytes 1990664 | tf_op jit(solution)/shard_map/ppermute | solution.py:376
  942.5 28.5 %collective-permute-start.37 = (bf16[2,2,72,1152]{3,2,1,0:T(8,128)(2,1)S(1)}, bf16[2,2,72,1152]{3,2,1,0:T(8,128)(2,1)S(1)}, u32[]{:S(2)}, u32[]{:S(2)}) collective-permute-start(bf16[2,2,72,1152]{3,2,1,0:T(8,128)(2,1)S(1)} %dynamic-slice_bitcast_fusion.3), channel_id=1, source_target_pairs={{0,1},{1,0},{2,3},{3,2},{4,5},{5,4},{6,7},{7,6},{8,9},{9,8},{10,11... | collective-permute-start | bytes 1990664 | tf_op jit(solution)/shard_map/ppermute | solution.py:376
  970.4 28.7 %collective-permute-start.27 = (f32[2,1,648]{2,1,0:T(1,128)S(1)}, f32[2,1,648]{2,1,0:T(1,128)S(1)}, u32[]{:S(2)}, u32[]{:S(2)}) collective-permute-start(f32[2,1,648]{2,1,0:T(1,128)S(1)} %fusion.155), channel_id=1, source_target_pairs={{0,4},{2,6},{4,0},{6,2},{8,12},{10,14},{12,8},{14,10},{1,5},{3,7},... | collective-permute-start | bytes 15560 | tf_op jit(solution)/shard_map/ppermute | solution.py:376
  996.3 22.2 %collective-permute-start.39 = (bf16[72,3456]{1,0:T(8,128)(2,1)S(1)}, bf16[72,3456]{1,0:T(8,128)(2,1)S(1)}, u32[]{:S(2)}, u32[]{:S(2)}) collective-permute-start(bf16[72,3456]{1,0:T(8,128)(2,1)S(1)} %pad_maximum_fusion.13), channel_id=1, source_target_pairs={{0,8},{2,10},{4,12},{6,14},{8,0},{10,2},{12,4},{14,6},{1,9},{3,11}... | collective-permute-start | bytes 1493000 | tf_op jit(solution)/shard_map/ppermute | solution.py:376
  999.1 20.3 %collective-permute-start.32 = (bf16[144,128]{1,0:T(8,128)(2,1)S(1)}, bf16[144,128]{1,0:T(8,128)(2,1)S(1)}, u32[]{:S(2)}, u32[]{:S(2)}) collective-permute-start(bf16[144,128]{1,0:T(8,128)(2,1)S(1)} %fusion.148), channel_id=1, source_target_pairs={{0,16},{16,0},{1,17},{17,1},{2,18},{18,2},{3,19},{19,3},{4,20},{20... | collective-permute-start | bytes 110600 | tf_op jit(solution)/shard_map/ppermute | solution.py:465
  999.2 19.5 %collective-permute-start.28 = (f32[1,648]{1,0:T(1,128)S(1)}, f32[1,648]{1,0:T(1,128)S(1)}, u32[]{:S(2)}, u32[]{:S(2)}) collective-permute-start(f32[1,648]{1,0:T(1,128)S(1)} %fusion.166), channel_id=1, source_target_pairs={{0,8},{2,10},{4,12},{6,14},{8,0},{10,2},{12,4},{14,6},{1,9},{3,11}... | collective-permute-start | bytes 7784 | tf_op jit(solution)/shard_map/ppermute | solution.py:376
  (117 other events, 1771.8 us)
Sparse Core Ops, SparseCore 0:
  11.4 133.9 all-gather.3
  148.9 134.4 all-gather.5
  286.9 115.5 all-gather.7
  549.8 146.8 reduce-scatter.2
  702.9 264.5 reduce-scatter.4

commit v5 on v4

--- a/solution.py
+++ b/solution.py
@@ -431,22 +431,29 @@
         return self.kept
 
 
-def finish_together(chains):
-    for chain in chains:
-        while len(chain.order) > 1:
-            chain.advance()
-    first = chains[0]
+def merged(chains):
     parts = [
         low(chain.kept.astype(jnp.float32) + chain.received.astype(jnp.float32))
         for chain in chains
     ]
-    bit = first.order[0]
+    last = Chain(chains[0].is_first, (None,), 0)
+    last.order = []
+    last.dims = []
+    bit = chains[0].order[0]
     index = my_bit(bit)
-    kept = [lax.dynamic_index_in_dim(part, index, 0, keepdims=False) for part in parts]
+    last.kept = jnp.concatenate(
+        [lax.dynamic_index_in_dim(part, index, 0, keepdims=False) for part in parts], axis=1
+    )
     sent = [lax.dynamic_index_in_dim(part, 1 - index, 0, keepdims=False) for part in parts]
-    received = across(jnp.concatenate(sent, axis=1), bit)
-    own = jnp.concatenate(kept, axis=1).astype(jnp.float32) + received.astype(jnp.float32)
-    return whole_halves(first.is_first, low(own))
+    last.received = across(jnp.concatenate(sent, axis=1), bit)
+    return last
+
+
+def together(main, chains):
+    main, received = lax.optimization_barrier((main, [chain.received for chain in chains]))
+    for chain, value in zip(chains, received):
+        chain.received = value
+    return main
 
 
 def tick(main, chains):
@@ -638,6 +645,8 @@
     hidden_t_grad = contract(tpair_grad[:, row_count:-row_count], tpair_full, 0, 1) + contract(
         tquery_grad, tquery_full, 0, 1
     )
+    hidden_t_grad, stacked_c = lax.optimization_barrier((hidden_t_grad, stacked_c))
+    scattered_c = scatter_halves(stacked_c)
     hidden_t_grad = jnp.concatenate(
         [
             hidden_t_grad[:row_count] + to_next.astype(jnp.float32),
@@ -646,8 +655,6 @@
         ],
         axis=0,
     )
-    hidden_t_grad, stacked_c = lax.optimization_barrier((hidden_t_grad, stacked_c))
-    scattered_c = scatter_halves(stacked_c)
     grad_m = result_grad + normalize_back(hidden_t_grad * (1.0 + modulation[7]), normed_t, recip_t)
     gate_m_grad = jnp.sum(branch_m * grad_m, axis=0)
     branch_m_grad = low(modulation[5] * grad_m)
@@ -751,14 +758,6 @@
             rest_normed = normed_rest[s][frame * row_count : (frame + 1) * row_count]
             shift_a_grad = shift_a_grad + jnp.sum(rest_rows, axis=0)
             scale_a_grad = scale_a_grad + jnp.sum(rest_rows * rest_normed, axis=0)
-    shift_a_grad, scale_a_grad, rest_received = lax.optimization_barrier(
-        (shift_a_grad, scale_a_grad, rest_received)
-    )
-    hidden_a_grad = own_grad + jnp.concatenate(
-        [sum(part.astype(jnp.float32) for part in parts) for parts in rest_received], axis=0
-    )
-    input_grad = grad_a + normalize_back(hidden_a_grad * (1.0 + modulation[1]), normed_a, recip_a)
-    latent_grad = input_grad.reshape(latent.shape)
     mod_grad = jnp.stack(
         [
             shift_a_grad,
@@ -772,18 +771,25 @@
             gate_t_grad,
         ]
     ).reshape(shards, 9 * width // shards)
-    latent_grad, mod_grad = tick((latent_grad, mod_grad), chains_a)
-    mod_slice = Chain(is_first, (mod_grad,), 0).finish()
-    text_low = chain_text.finish()
-    silu_pair = jnp.concatenate([silu_cond, swapped(silu_cond)], axis=0)
-    mod_pair = jnp.concatenate([mod_slice, swapped(mod_slice)], axis=0)
-    ada_grad = lax.dot_general(
-        silu_pair, mod_pair, (((0,), (0,)), ((), ())), precision=highest
-    )
-    text_both = jnp.concatenate([text[0], swapped(text[0])], axis=0)
-    slice_both = jnp.concatenate([text_low, swapped(text_low)], axis=1)
-    text_kv_grad = contract(text_both, slice_both, 0, 1)
-    lower_a, upper_a = finish_together(chains_a)
+    own_grad, mod_grad, rest_received = together(
+        (own_grad, mod_grad, rest_received), chains_a + [chain_text]
+    )
+    for chain in chains_a + [chain_text]:
+        chain.advance()
+    chain_mod = Chain(is_first, (mod_grad,), 0)
+    chain_mod.advance()
+    hidden_a_grad = own_grad + jnp.concatenate(
+        [sum(part.astype(jnp.float32) for part in parts) for parts in rest_received], axis=0
+    )
+    input_grad = grad_a + normalize_back(hidden_a_grad * (1.0 + modulation[1]), normed_a, recip_a)
+    latent_grad = input_grad.reshape(latent.shape)
+    latent_grad = together(latent_grad, chains_a + [chain_mod])
+    while len(chains_a[0].order) > 1:
+        for chain in chains_a + [chain_mod]:
+            chain.advance()
+        latent_grad = together(latent_grad, chains_a + [chain_mod])
+    chain_last = merged(chains_a)
+    chain_mod.advance()
     lower_b, upper_b = whole_halves(is_first, scattered_b)
     lower_c, upper_c = whole_halves(is_first, scattered_c)
     up_shard = (
@@ -800,6 +806,23 @@
         ],
         axis=0,
     )
+    latent_grad = together(latent_grad, [chain_last, chain_mod])
+    mod_slice = chain_mod.finish()
+    own_a = chain_last.finish()
+    other_a, up_shard, down_shard = lax.optimization_barrier(
+        (swapped(own_a), up_shard, down_shard)
+    )
+    lower_a = jnp.where(is_first, own_a, other_a).astype(jnp.float32)
+    upper_a = jnp.where(is_first, other_a, own_a).astype(jnp.float32)
+    text_low = chain_text.finish()
+    silu_pair = jnp.concatenate([silu_cond, swapped(silu_cond)], axis=0)
+    mod_pair = jnp.concatenate([mod_slice, swapped(mod_slice)], axis=0)
+    ada_grad = lax.dot_general(
+        silu_pair, mod_pair, (((0,), (0,)), ((), ())), precision=highest
+    )
+    text_both = jnp.concatenate([text[0], swapped(text[0])], axis=0)
+    slice_both = jnp.concatenate([text_low, swapped(text_low)], axis=1)
+    text_kv_grad = contract(text_both, slice_both, 0, 1)
     return (
         result,
         latent_grad,

time: 1060 us -> 1050 us (level)
  waiting for transfers between devices: 288 us -> 241 us
  local copies, waits for them, and re-layouts: 49.1 us -> 62.2 us
  other arithmetic: 97 us -> 109 us
    ppermute x26, waiting for transfers between devices: 126 us -> 103 us  [across(): lax.ppermute(value, axis, [(i, i ^ 1 << step) for i in range(lax.axis_siz...]
    all_gather x3, waiting for transfers between devices: 108 us -> 89 us  [gather_halves(): lax.all_gather(jnp.where(is_first, lower, upper), ('bucket', 'frame', 'se...]
    ppermute x2, waiting for transfers between devices: 18.7 us -> 0.01 us  [per_device(): lax.ppermute(rest_low[s * row_count:(s + 1) * row_count], 'seq', [(j, i)...]
    ppermute x1, waiting for transfers between devices: 0.01 us -> 14.5 us  [per_device(): lax.ppermute(hidden_t[total_rows - row_count:], 'frame', ahead)]
  transfers between devices with their start and end apart: 48 -> 48, of which waited for: 21 -> 22; matrix products, arithmetic and copies ran while one was open for 48% -> 48% of each run, Pallas kernels for 15% -> 13%
where the time goes in v5:
time: 1050 us; the launch traced here: 1040 us
  matrix products  392 us (37%)
  waiting for transfers between devices  241 us (23%)
  Pallas kernels  158 us (15%)
  other arithmetic  109 us (10%)
  local copies, waits for them, and re-layouts  62.2 us (6%)
  starting transfers between devices  58.4 us (6%)
  between operations  17.1 us (2%)
    dot_general x43, matrix products, contract(): lax.dot_general(left, right, (((left_dim,), (right_dim,)), ((), ())), pre...  326 us
    ppermute x26, waiting for transfers between devices, across(): lax.ppermute(value, axis, [(i, i ^ 1 << step) for i in range(lax.axis_siz...  103 us
    all_gather x3, waiting for transfers between devices, gather_halves(): lax.all_gather(jnp.where(is_first, lower, upper), ('bucket', 'frame', 'se...  89 us
    pallas_call x2, Pallas kernels, spatial_backward(): call(body, (HEADS,), [pl.BlockSpec((head_size, rows), lambda h: (h, frame...  69.4 us
    dot_general x6, matrix products, product(): return jnp.dot(left, right, preferred_element_type=jnp.float32)  60.3 us
    ppermute x26, starting transfers between devices, across(): lax.ppermute(value, axis, [(i, i ^ 1 << step) for i in range(lax.axis_siz...  38.1 us
    pallas_call x1, Pallas kernels, spatial_forward(): call(body, (frame_count, HEADS), [pl.BlockSpec((head_size, rows), lambda...  37.5 us
    ppermute x1, waiting for transfers between devices, per_device(): latent_rest = [lax.ppermute(latent[0], 'seq', shift) for shift in shifts]  28 us
  transfers between devices with their start and end apart: 48, of which 22 were waited for; matrix products, arithmetic and copies ran while one was open for 48% of the time, Pallas kernels for 13%

profile of v5, /device:TPU:0, one launch (start us, length us, event | category | flops | bytes accessed | tf_op | source)
XLA Modules:
  0.0 1038.1 jit_solution(14756382246345325275)
XLA Ops:
  50.4 8.8 collective-permute-done.7
  62.1 13.1 %collective-permute-done.8 = bf16[1152,128]{1,0:T(8,128)(2,1)S(1)} collective-permute-done((bf16[1152,128]{1,0:T(8,128)(2,1)S(1)}, bf16[1152,128]{1,0:T(8,128)(2,1)S(1)}, u32[]{:S(2)}, u32[]{:S(2)}) %collective-permute-start.8) | collective-permute-done | bytes 294944 | tf_op jit(solution)/shard_map/ppermute | solution.py:376
  75.4 28.0 %collective-permute-done.4 = bf16[2,512,1152]{2,1,0:T(8,128)(2,1)} collective-permute-done((bf16[2,512,1152]{2,1,0:T(8,128)(2,1)}, bf16[2,512,1152]{2,1,0:T(8,128)(2,1)}, u32[]{:S(2)}, u32[]{:S(2)}) %collective-permute-start.4) | collective-permute-done | bytes 2359328 | tf_op jit(solution)/shard_map/ppermute | solution.py:508
  113.7 31.5 %all-gather.4.cloned.1.call-done = bf16[2304,3456]{1,0:T(8,128)(2,1)} async-done(((bf16[72,3456]{1,0:T(8,128)(2,1)}), bf16[2304,3456]{1,0:T(8,128)(2,1)}) %all-gather.4.cloned.1.call-update) | async-done | bytes 15925264 | tf_op jit(solution)/shard_map/all_gather | solution.py:317
  158.2 18.1 %convolution_convert_fusion.3.k_ref.v_ref = bf16[2304,2048]{1,0:T(8,128)(2,1)} fusion(bf16[2048,1152]{1,0:T(8,128)(2,1)} %bitcast.249, bf16[2304,3456]{1,0:T(8,128)(2,1)} %all-gather.4.cloned.1.call-done), kind=kOutput, calls=%fused_computation.9 | convolution fusion | flops 10876354560 | bytes 19464192 | tf_op jit(solution)/shard_map/dot_general | solution.py:24
  176.3 37.5 %spatial_forward.1 = (bf16[1152,1024]{1,0:T(8,128)(2,1)S(1)}, f32[32,1,512]{2,1,0:T(1,128)S(1)}) custom-call(bf16[1152,1024]{1,0:T(8,128)(2,1)S(1)} %convolution_convert_fusion.20.q_ref, bf16[2304,2048]{1,0:T(8,128)(2,1)} %convolution_convert_fusion.3.k_ref.v_ref, bf16[2304,2048]{1,0:T(8,128)(2,1)} %convolution_convert_fusion.3.k_ref.v_ref), custom_call_target="tpu_custom_call" | custom-call | tf_op jit(solution)/shard_map/spatial_forward/pallas_call | solution.py:57
  213.9 8.9 fusion.70
  229.0 8.5 cross_forward.1
  249.4 33.7 %all-gather.6.cloned.1.call-done = bf16[2304,4608]{1,0:T(8,128)(2,1)} async-done(((bf16[72,4608]{1,0:T(8,128)(2,1)}), bf16[2304,4608]{1,0:T(8,128)(2,1)}) %all-gather.6.cloned.1.call-update) | async-done | bytes 21233680 | tf_op jit(solution)/shard_map/all_gather | solution.py:317
  283.1 12.7 %multiply_convert_fusion.1 = (bf16[1024,2304]{1,0:T(8,128)(2,1)S(1)}, f32[1024,2304]{1,0:T(8,128)}) fusion(bf16[1024,1152]{1,0:T(8,128)(2,1)} %add_convert_fusion.4, bf16[2304,4608]{1,0:T(8,128)(2,1)} %all-gather.6.cloned.1.call-done), kind=kOutput, calls=%fused_computation.33 | convolution fusion | flops 5457051648 | bytes 21823488 | tf_op jit(solution)/shard_map/dot_general | solution.py:20
  309.8 12.9 %multiply_convert_fusion = (bf16[1024,2304]{1,0:T(8,128)(2,1)S(1)}, f32[1024,2304]{1,0:T(8,128)}) fusion(bf16[1024,1152]{1,0:T(8,128)(2,1)S(1)} %copy-done.51, bf16[2304,4608]{1,0:T(8,128)(2,1)} %all-gather.6.cloned.1.call-done), kind=kOutput, calls=%fused_computation.32 | convolution fusion | flops 5457051648 | bytes 21823488 | tf_op jit(solution)/shard_map/dot_general | solution.py:20
  322.6 8.5 fusion.102
  331.2 12.2 %fusion.182 = (f32[1024]{0:T(1024)S(1)}, f32[1024,1152]{1,0:T(8,128)S(1)}, f32[1024,1152]{1,0:T(8,128)}) fusion(f32[1024,1152]{1,0:T(8,128)S(1)} %bitcast.228, f32[1152]{0:T(1024)S(1)} %get-tuple-element.188, bf16[2304,4608]{1,0:T(8,128)(2,1)} %all-gather.6.cloned.1.call-done, bf16[1024,2304]{1,0:T(8,128)(2,1)} %copy-done.56, f32[1024,1152]{1,0:T(8,128)} %fusion.102, ...), kind=kOutput, calls=%fused_computation.371 | convolution fusion | flops 2724985856 | bytes 33333760 | tf_op jit(solution)/shard_map/dot_general | solution.py:20
  361.0 23.9 %all-gather.8.cloned.1.call-done = bf16[2304,2304]{1,0:T(8,128)(2,1)} async-done(((bf16[72,2304]{1,0:T(8,128)(2,1)}), bf16[2304,2304]{1,0:T(8,128)(2,1)}) %all-gather.8.cloned.1.call-update) | async-done | bytes 10616848 | tf_op jit(solution)/shard_map/all_gather | solution.py:317
  390.8 14.5 %collective-permute-done.9 = bf16[512,1152]{1,0:T(8,128)(2,1)} collective-permute-done((bf16[512,1152]{1,0:T(8,128)(2,1)}, bf16[512,1152]{1,0:T(8,128)(2,1)}, u32[]{:S(2)}, u32[]{:S(2)}) %collective-permute-start.9) | collective-permute-done | bytes 1179680 | tf_op jit(solution)/shard_map/ppermute | solution.py:605
  405.3 17.3 %convolution_convert_fusion.2.k_ref.v_ref = bf16[2304,2048]{1,0:T(8,128)(2,1)} fusion(bf16[2304,2304]{1,0:T(8,128)(2,1)} %all-gather.8.cloned.1.call-done, bf16[512,1152]{1,0:T(8,128)(2,1)} %collective-permute-done.10, bf16[1024,1152]{1,0:T(8,128)(2,1)S(1)} %copy-done.30, bf16[512,1152]{1,0:T(8,128)(2,1)} %collective-permute-done.9), kind=kOutput, calls=%fused_computation.8 | convolution fusion | flops 10890510336 | bytes 19464192 | tf_op jit(solution)/shard_map/dot_general | solution.py:24
  422.6 10.9 %temporal_forward.1 = bf16[1152,1024]{1,0:T(8,128)(2,1)S(1)} custom-call(s32[2,2]{1,0:T(2,128)S(1)} %add_convert_fusion.8.live_ref, bf16[1152,1024]{1,0:T(8,128)(2,1)S(1)} %convolution_convert_fusion.18.q_ref, bf16[2304,2048]{1,0:T(8,128)(2,1)} %convolution_convert_fusion.2.k_ref.v_ref, bf16[2304,2048]{1,0:T(8,128)(2,1)} %convolution_convert_fusion.2.k_ref.v_ref), custom_call_target="tpu_custom_call" | custom-call | tf_op jit(solution)/shard_map/temporal_forward/pallas_call | solution.py:220
  441.1 16.8 %temporal_backward.1 = (bf16[1152,1024]{1,0:T(8,128)(2,1)S(1)}, bf16[2,1152,2048]{2,1,0:T(8,128)(2,1)}) custom-call(s32[2,2]{1,0:T(2,128)S(1)} %add_convert_fusion.8.live_ref, bf16[1152,1024]{1,0:T(8,128)(2,1)S(1)} %convolution_convert_fusion.18.q_ref, bf16[2304,2048]{1,0:T(8,128)(2,1)} %convolution_convert_fusion.2.k_ref.v_ref, ...), custom_call_target="tpu_custom_call" | custom-call | tf_op jit(solution)/shard_map/temporal_backward/pallas_call | solution.py:275
  457.9 8.4 fusion.67
  490.1 15.7 %fusion.2 = bf16[2304,2304]{1,0:T(8,128)(2,1)} fusion(bf16[2304,2304]{1,0:T(8,128)(2,1)} %fusion.24, bf16[2304,2048]{1,0:T(8,128)(2,1)} %bitcast.278, bf16[512,1152]{1,0:T(8,128)(2,1)} %collective-permute-done.10, bf16[1024,1152]{1,0:T(8,128)(2,1)S(1)} %copy-done.30, bf16[512,1152]{1,0:T(8,128)(2,1)} %collective-permute-done.9), kind=kOutput, calls=%fused_computation.12 | convolution fusion | flops 10888445952 | bytes 19464192 | tf_op jit(solution)/shard_map/dot_general | solution.py:24
  505.8 9.9 fusion.45
  538.8 11.8 %fusion.29 = (f32[1152]{0:T(1024)S(1)}, bf16[1024,1152]{1,0:T(8,128)(2,1)}, f32[1152]{0:T(1024)S(1)}, f32[1024,1152]{1,0:T(8,128)S(1)}) fusion(bf16[1,2,512,1152]{3,2,1,0:T(8,128)(2,1)S(1)} %copy-done.49, f32[1024]{0:T(1024)S(1)} %bitcast.275, f32[1024,1152]{1,0:T(8,128)} %copy-done.17, f32[1152]{0:T(1024)S(1)} %copy-done.80, ...), kind=kOutput, calls=%fused_computation.60 | convolution fusion | flops 2740320256 | bytes 28645376 | tf_op jit(solution)/shard_map/dot_general | solution.py:24
  632.0 9.9 fusion.47
  641.9 9.8 fusion.55
  662.1 15.4 %cross_backward.1 = (bf16[1152,1024]{1,0:T(8,128)(2,1)S(1)}, f32[2,1152,128]{2,1,0:T(8,128)S(1)}) custom-call(s32[1]{0:T(128)S(6)} %copy.52.length_ref, bf16[1152,1024]{1,0:T(8,128)(2,1)} %copy-done.3, bf16[2304,128]{1,0:T(8,128)(2,1)S(1)} %pad_maximum_fusion.12.k_ref.v_ref, bf16[2304,128]{1,0:T(8,128)(2,1)S(1)} %pad_maximum_fusion.12.k_ref.v_ref, ...), custom_call_target="tpu_custom_call" | custom-call | tf_op jit(solution)/shard_map/cross_backward/pallas_call | solution.py:166
  715.6 34.1 %spatial_backward.2 = (bf16[1152,512]{1,0:T(8,128)(2,1)S(1)}, bf16[2,1152,1024]{2,1,0:T(8,128)(2,1)}) custom-call(bf16[1152,1024]{1,0:T(8,128)(2,1)S(1)} %convolution_convert_fusion.20.q_ref, bf16[2304,2048]{1,0:T(8,128)(2,1)} %convolution_convert_fusion.3.k_ref.v_ref, bf16[2304,2048]{1,0:T(8,128)(2,1)} %convolution_convert_fusion.3.k_ref.v_ref, ...), custom_call_target="tpu_custom_call" | custom-call | tf_op jit(solution)/shard_map/spatial_backward/pallas_call | solution.py:94
  749.7 8.9 fusion.191
  761.4 35.3 %spatial_backward.3 = (bf16[1152,512]{1,0:T(8,128)(2,1)S(1)}, bf16[2,1152,1024]{2,1,0:T(8,128)(2,1)}) custom-call(bf16[1152,1024]{1,0:T(8,128)(2,1)S(1)} %convolution_convert_fusion.20.q_ref, bf16[2304,2048]{1,0:T(8,128)(2,1)} %convolution_convert_fusion.3.k_ref.v_ref, bf16[2304,2048]{1,0:T(8,128)(2,1)} %convolution_convert_fusion.3.k_ref.v_ref, ...), custom_call_target="tpu_custom_call" | custom-call | tf_op jit(solution)/shard_map/spatial_backward/pallas_call | solution.py:94
  796.7 9.4 fusion.84
  815.7 14.5 %convolution_convert_fusion.4 = bf16[1152,2304]{1,0:T(8,128)(2,1)S(1)} fusion(bf16[2048,1152]{1,0:T(8,128)(2,1)S(1)} %bitcast.252, bf16[2304,1024]{1,0:T(8,128)(2,1)} %bitcast.286, bf16[2304,1024]{1,0:T(8,128)(2,1)S(1)} %bitcast.284), kind=kOutput, calls=%fused_computation.10 | convolution fusion | flops 10893164544 | bytes 19464192 | tf_op jit(solution)/shard_map/dot_general | solution.py:24
  888.3 39.8 %collective-permute-done.24 = bf16[144,128]{1,0:T(8,128)(2,1)} collective-permute-done((bf16[144,128]{1,0:T(8,128)(2,1)}, bf16[144,128]{1,0:T(8,128)(2,1)}, u32[]{:S(2)}, u32[]{:S(2)}) %collective-permute-start.24) | collective-permute-done | bytes 36896 | tf_op jit(solution)/shard_map/ppermute | solution.py:376
  992.1 10.2 collective-permute-done.33
  (550 shorter events, 470.1 us)
Async XLA Ops:
  7.2 138.0 %all-gather.4.cloned.1.call-start = ((), (), s32[]{:S(2)}) async-start(), calls=%async_computation.2 | async-start | bytes 16422912 | tf_op jit(solution)/shard_map/all_gather | solution.py:317
  9.5 273.6 %all-gather.6.cloned.1.call-start = ((), (), s32[]{:S(2)}) async-start(), calls=%async_computation.3 | async-start | bytes 21897216 | tf_op jit(solution)/shard_map/all_gather | solution.py:317
  22.2 362.7 %all-gather.8.cloned.1.call-start = ((), (), s32[]{:S(2)}) async-start(), calls=%async_computation.4 | async-start | bytes 10948608 | tf_op jit(solution)/shard_map/all_gather | solution.py:317
  24.4 18.2 %collective-permute-start.5 = (bf16[144,128]{1,0:T(8,128)(2,1)S(1)}, bf16[144,128]{1,0:T(8,128)(2,1)S(1)}, u32[]{:S(2)}, u32[]{:S(2)}) collective-permute-start(bf16[144,128]{1,0:T(8,128)(2,1)S(1)} %convolution_convert_fusion.21), channel_id=1, source_target_pairs={{0,1},{1,0},{2,3},{3,2},{4,5},{5,4},{6,7},{7,6},{8,9},{9,8},{10,11... | collective-permute-start | bytes 110600 | tf_op jit(solution)/shard_map/ppermute | solution.py:376
  28.7 74.7 %collective-permute-start.4 = (bf16[2,512,1152]{2,1,0:T(8,128)(2,1)}, bf16[2,512,1152]{2,1,0:T(8,128)(2,1)}, u32[]{:S(2)}, u32[]{:S(2)}) collective-permute-start(bf16[2,512,1152]{2,1,0:T(8,128)(2,1)} %bitcast.231), channel_id=1, source_target_pairs={{1,0},{0,1},{3,2},{2,3},{5,4},{4,5},{7,6},{6,7},{9,8},{8,9},{11,10... | collective-permute-start | bytes 7077896 | tf_op jit(solution)/shard_map/ppermute | solution.py:508
  59.3 15.9 %collective-permute-start.8 = (bf16[1152,128]{1,0:T(8,128)(2,1)S(1)}, bf16[1152,128]{1,0:T(8,128)(2,1)S(1)}, u32[]{:S(2)}, u32[]{:S(2)}) collective-permute-start(bf16[1152,128]{1,0:T(8,128)(2,1)S(1)} %pad_maximum_fusion.15), channel_id=1, source_target_pairs={{0,8},{2,10},{4,12},{6,14},{8,0},{10,2},{12,4},{14,6},{1,9},{3,11}... | collective-permute-start | bytes 884744 | tf_op jit(solution)/shard_map/ppermute | solution.py:376
  151.8 559.5 %reduce-scatter.3.cloned.1.call-start = ((), (), s32[]{:S(2)}) async-start(), calls=%async_computation.5 | async-start | bytes 10948608 | tf_op jit(solution)/shard_map/reduce_scatter | solution.py:359
  349.4 41.4 %collective-permute-start.10 = (bf16[512,1152]{1,0:T(8,128)(2,1)}, bf16[512,1152]{1,0:T(8,128)(2,1)}, u32[]{:S(2)}, u32[]{:S(2)}) collective-permute-start(bf16[512,1152]{1,0:T(8,128)(2,1)} %get-tuple-element.215), channel_id=1, source_target_pairs={{2,0},{4,2},{6,4},{8,6},{10,8},{12,10},{14,12},{3,1},{5,3},{7,5},{... | collective-permute-start | bytes 3538952 | tf_op jit(solution)/shard_map/ppermute | solution.py:606
  350.7 54.6 %collective-permute-start.9 = (bf16[512,1152]{1,0:T(8,128)(2,1)}, bf16[512,1152]{1,0:T(8,128)(2,1)}, u32[]{:S(2)}, u32[]{:S(2)}) collective-permute-start(bf16[512,1152]{1,0:T(8,128)(2,1)} %get-tuple-element.214), channel_id=1, source_target_pairs={{0,2},{2,4},{4,6},{6,8},{8,10},{10,12},{12,14},{1,3},{3,5},{5,7},{... | collective-permute-start | bytes 3538952 | tf_op jit(solution)/shard_map/ppermute | solution.py:605
  473.8 54.8 %collective-permute-start.11 = (bf16[512,1152]{1,0:T(8,128)(2,1)}, bf16[512,1152]{1,0:T(8,128)(2,1)}, u32[]{:S(2)}, u32[]{:S(2)}) collective-permute-start(bf16[512,1152]{1,0:T(8,128)(2,1)} %fusion.67), channel_id=1, source_target_pairs={{0,2},{2,4},{4,6},{6,8},{8,10},{10,12},{12,14},{1,3},{3,5},{5,7},{... | collective-permute-start | bytes 3538952 | tf_op jit(solution)/shard_map/ppermute | solution.py:640
  479.2 49.4 %collective-permute-start.12 = (bf16[512,1152]{1,0:T(8,128)(2,1)}, bf16[512,1152]{1,0:T(8,128)(2,1)}, u32[]{:S(2)}, u32[]{:S(2)}) collective-permute-start(bf16[512,1152]{1,0:T(8,128)(2,1)} %fusion.64), channel_id=1, source_target_pairs={{2,0},{4,2},{6,4},{8,6},{10,8},{12,10},{14,12},{3,1},{5,3},{7,5},{... | collective-permute-start | bytes 3538952 | tf_op jit(solution)/shard_map/ppermute | solution.py:639
  522.9 484.0 %reduce-scatter.5.cloned.1.call-start = ((), (), s32[]{:S(2)}) async-start(), calls=%async_computation.6 | async-start | bytes 21897216 | tf_op jit(solution)/shard_map/reduce_scatter | solution.py:359
  678.3 33.0 %collective-permute-start.13 = (bf16[2,2,2,144,128]{4,3,2,1,0:T(8,128)(2,1)}, bf16[2,2,2,144,128]{4,3,2,1,0:T(8,128)(2,1)S(1)}, u32[]{:S(2)}, u32[]{:S(2)}) collective-permute-start(bf16[2,2,2,144,128]{4,3,2,1,0:T(8,128)(2,1)} %dynamic-slice_bitcast_fusion.9), channel_id=1, source_target_pairs={{0,2},{2,0},{4,6},{6,4},{8,10},{10,8},{12,14},{14,12},{1,3},{3,1},... | collective-permute-start | bytes 884744 | tf_op jit(solution)/shard_map/ppermute | solution.py:376
  711.3 95.5 %collective-permute-start.42 = (bf16[72,2304]{1,0:T(8,128)(2,1)}, bf16[72,2304]{1,0:T(8,128)(2,1)}, u32[]{:S(2)}, u32[]{:S(2)}) collective-permute-start(bf16[72,2304]{1,0:T(8,128)(2,1)} %reduce-scatter.3.cloned.1.call-done), channel_id=1, source_target_pairs={{0,16},{16,0},{1,17},{17,1},{2,18},{18,2},{3,19},{19,3},{4,20},{20... | collective-permute-start | bytes 995336 | tf_op jit(solution)/shard_map/ppermute | solution.py:472
  711.5 48.6 %collective-permute-start.14 = (bf16[2,2,144,128]{3,2,1,0:T(8,128)(2,1)S(1)}, bf16[2,2,144,128]{3,2,1,0:T(8,128)(2,1)S(1)}, u32[]{:S(2)}, u32[]{:S(2)}) collective-permute-start(bf16[2,2,144,128]{3,2,1,0:T(8,128)(2,1)S(1)} %dynamic-slice_bitcast_fusion.16), channel_id=1, source_target_pairs={{0,4},{2,6},{4,0},{6,2},{8,12},{10,14},{12,8},{14,10},{1,5},{3,7},... | collective-permute-start | bytes 442376 | tf_op jit(solution)/shard_map/ppermute | solution.py:376
  758.6 51.1 %collective-permute-start.15 = (bf16[512,1152]{1,0:T(8,128)(2,1)}, bf16[512,1152]{1,0:T(8,128)(2,1)S(1)}, u32[]{:S(2)}, u32[]{:S(2)}) collective-permute-start(bf16[512,1152]{1,0:T(8,128)(2,1)} %get-tuple-element.121), channel_id=1, source_target_pairs={{0,1},{1,0},{2,3},{3,2},{4,5},{5,4},{6,7},{7,6},{8,9},{9,8},{10,11... | collective-permute-start | bytes 3538952 | tf_op jit(solution)/shard_map/ppermute | solution.py:717
  760.8 98.4 %collective-permute-start.19 = (bf16[2,144,128]{2,1,0:T(8,128)(2,1)}, bf16[2,144,128]{2,1,0:T(8,128)(2,1)}, u32[]{:S(2)}, u32[]{:S(2)}) collective-permute-start(bf16[2,144,128]{2,1,0:T(8,128)(2,1)} %dynamic-slice_bitcast_fusion.17), channel_id=1, source_target_pairs={{0,1},{1,0},{2,3},{3,2},{4,5},{5,4},{6,7},{7,6},{8,9},{9,8},{10,11... | collective-permute-start | bytes 221192 | tf_op jit(solution)/shard_map/ppermute | solution.py:376
  806.1 82.1 %collective-permute-start.20 = (bf16[512,1152]{1,0:T(8,128)(2,1)}, bf16[512,1152]{1,0:T(8,128)(2,1)S(1)}, u32[]{:S(2)}, u32[]{:S(2)}) collective-permute-start(bf16[512,1152]{1,0:T(8,128)(2,1)} %get-tuple-element.137), channel_id=1, source_target_pairs={{0,1},{1,0},{2,3},{3,2},{4,5},{5,4},{6,7},{7,6},{8,9},{9,8},{10,11... | collective-permute-start | bytes 3538952 | tf_op jit(solution)/shard_map/ppermute | solution.py:717
  832.0 27.2 %collective-permute-start.17 = (bf16[1152,1152]{1,0:T(8,128)(2,1)}, bf16[1152,1152]{1,0:T(8,128)(2,1)}, u32[]{:S(2)}, u32[]{:S(2)}) collective-permute-start(bf16[1152,1152]{1,0:T(8,128)(2,1)} %broadcast_select_fusion.1), channel_id=1, source_target_pairs={{0,16},{16,0},{1,17},{17,1},{2,18},{18,2},{3,19},{19,3},{4,20},{20... | collective-permute-start | bytes 7962632 | tf_op jit(solution)/shard_map/ppermute | solution.py:472
  836.7 22.5 %collective-permute-start.16 = (bf16[1152,1152]{1,0:T(8,128)(2,1)}, bf16[1152,1152]{1,0:T(8,128)(2,1)S(1)}, u32[]{:S(2)}, u32[]{:S(2)}) collective-permute-start(bf16[1152,1152]{1,0:T(8,128)(2,1)} %get-tuple-element.206), channel_id=1, source_target_pairs={{0,16},{16,0},{1,17},{17,1},{2,18},{18,2},{3,19},{19,3},{4,20},{20... | collective-permute-start | bytes 7962632 | tf_op jit(solution)/shard_map/ppermute | solution.py:472
  836.7 24.0 %collective-permute-start.18 = (bf16[1152,1152]{1,0:T(8,128)(2,1)}, bf16[1152,1152]{1,0:T(8,128)(2,1)}, u32[]{:S(2)}, u32[]{:S(2)}) collective-permute-start(bf16[1152,1152]{1,0:T(8,128)(2,1)} %get-tuple-element.205), channel_id=1, source_target_pairs={{0,16},{16,0},{1,17},{17,1},{2,18},{18,2},{3,19},{19,3},{4,20},{20... | collective-permute-start | bytes 7962632 | tf_op jit(solution)/shard_map/ppermute | solution.py:472
  865.8 62.3 %collective-permute-start.22 = (bf16[2,2,2,72,1152]{4,3,2,1,0:T(8,128)(2,1)}, bf16[2,2,2,72,1152]{4,3,2,1,0:T(8,128)(2,1)}, u32[]{:S(2)}, u32[]{:S(2)}) collective-permute-start(bf16[2,2,2,72,1152]{4,3,2,1,0:T(8,128)(2,1)} %dynamic-slice_bitcast_fusion.1), channel_id=1, source_target_pairs={{0,2},{2,0},{4,6},{6,4},{8,10},{10,8},{12,14},{14,12},{1,3},{3,1},... | collective-permute-start | bytes 3981320 | tf_op jit(solution)/shard_map/ppermute | solution.py:376
  873.3 60.4 %collective-permute-start.23 = (bf16[2,2,2,72,1152]{4,3,2,1,0:T(8,128)(2,1)}, bf16[2,2,2,72,1152]{4,3,2,1,0:T(8,128)(2,1)}, u32[]{:S(2)}, u32[]{:S(2)}) collective-permute-start(bf16[2,2,2,72,1152]{4,3,2,1,0:T(8,128)(2,1)} %dynamic-slice_bitcast_fusion), channel_id=1, source_target_pairs={{0,4},{2,6},{4,0},{6,2},{8,12},{10,14},{12,8},{14,10},{1,5},{3,7},... | collective-permute-start | bytes 3981320 | tf_op jit(solution)/shard_map/ppermute | solution.py:376
  874.5 59.2 %collective-permute-start.21 = (bf16[2,2,2,72,1152]{4,3,2,1,0:T(8,128)(2,1)}, bf16[2,2,2,72,1152]{4,3,2,1,0:T(8,128)(2,1)}, u32[]{:S(2)}, u32[]{:S(2)}) collective-permute-start(bf16[2,2,2,72,1152]{4,3,2,1,0:T(8,128)(2,1)} %dynamic-slice_bitcast_fusion.2), channel_id=1, source_target_pairs={{0,1},{1,0},{2,3},{3,2},{4,5},{5,4},{6,7},{7,6},{8,9},{9,8},{10,11... | collective-permute-start | bytes 3981320 | tf_op jit(solution)/shard_map/ppermute | solution.py:376
  877.1 51.0 %collective-permute-start.24 = (bf16[144,128]{1,0:T(8,128)(2,1)}, bf16[144,128]{1,0:T(8,128)(2,1)}, u32[]{:S(2)}, u32[]{:S(2)}) collective-permute-start(bf16[144,128]{1,0:T(8,128)(2,1)} %dynamic-slice_bitcast_fusion.18), channel_id=1, source_target_pairs={{0,8},{2,10},{4,12},{6,14},{8,0},{10,2},{12,4},{14,6},{1,9},{3,11}... | collective-permute-start | bytes 110600 | tf_op jit(solution)/shard_map/ppermute | solution.py:376
  888.2 114.1 %collective-permute-start.38 = (bf16[128,4096]{1,0:T(8,128)(2,1)}, bf16[128,4096]{1,0:T(8,128)(2,1)}, u32[]{:S(2)}, u32[]{:S(2)}) collective-permute-start(bf16[128,4096]{1,0:T(8,128)(2,1)} %bitcast.255), channel_id=1, source_target_pairs={{0,16},{16,0},{1,17},{17,1},{2,18},{18,2},{3,19},{19,3},{4,20},{20... | collective-permute-start | bytes 3145736 | tf_op jit(solution)/shard_map/ppermute | solution.py:472
  937.2 22.0 %collective-permute-start.27 = (bf16[2,2,72,1152]{3,2,1,0:T(8,128)(2,1)}, bf16[2,2,72,1152]{3,2,1,0:T(8,128)(2,1)}, u32[]{:S(2)}, u32[]{:S(2)}) collective-permute-start(bf16[2,2,72,1152]{3,2,1,0:T(8,128)(2,1)} %dynamic-slice_bitcast_fusion.3), channel_id=1, source_target_pairs={{0,1},{1,0},{2,3},{3,2},{4,5},{5,4},{6,7},{7,6},{8,9},{9,8},{10,11... | collective-permute-start | bytes 1990664 | tf_op jit(solution)/shard_map/ppermute | solution.py:376
  940.7 25.5 %collective-permute-start.26 = (bf16[2,2,72,1152]{3,2,1,0:T(8,128)(2,1)}, bf16[2,2,72,1152]{3,2,1,0:T(8,128)(2,1)}, u32[]{:S(2)}, u32[]{:S(2)}) collective-permute-start(bf16[2,2,72,1152]{3,2,1,0:T(8,128)(2,1)} %dynamic-slice_bitcast_fusion.4), channel_id=1, source_target_pairs={{0,4},{2,6},{4,0},{6,2},{8,12},{10,14},{12,8},{14,10},{1,5},{3,7},... | collective-permute-start | bytes 1990664 | tf_op jit(solution)/shard_map/ppermute | solution.py:376
  944.3 21.9 %collective-permute-start.25 = (bf16[2,2,72,1152]{3,2,1,0:T(8,128)(2,1)}, bf16[2,2,72,1152]{3,2,1,0:T(8,128)(2,1)}, u32[]{:S(2)}, u32[]{:S(2)}) collective-permute-start(bf16[2,2,72,1152]{3,2,1,0:T(8,128)(2,1)} %dynamic-slice_bitcast_fusion.5), channel_id=1, source_target_pairs={{0,2},{2,0},{4,6},{6,4},{8,10},{10,8},{12,14},{14,12},{1,3},{3,1},... | collective-permute-start | bytes 1990664 | tf_op jit(solution)/shard_map/ppermute | solution.py:376
  975.3 32.4 %collective-permute-start.35 = (f32[1,1152]{1,0:T(1,128)S(1)}, f32[1,1152]{1,0:T(1,128)S(1)}, u32[]{:S(2)}, u32[]{:S(2)}) collective-permute-start(f32[1,1152]{1,0:T(1,128)S(1)} %copy-done.85), channel_id=1, source_target_pairs={{0,16},{16,0},{1,17},{17,1},{2,18},{18,2},{3,19},{19,3},{4,20},{20... | collective-permute-start | bytes 13832 | tf_op jit(solution)/shard_map/ppermute | solution.py:472
  980.3 21.9 %collective-permute-start.33 = (bf16[72,3456]{1,0:T(8,128)(2,1)S(1)}, bf16[72,3456]{1,0:T(8,128)(2,1)S(1)}, u32[]{:S(2)}, u32[]{:S(2)}) collective-permute-start(bf16[72,3456]{1,0:T(8,128)(2,1)S(1)} %pad_maximum_fusion.13), channel_id=1, source_target_pairs={{0,8},{2,10},{4,12},{6,14},{8,0},{10,2},{12,4},{14,6},{1,9},{3,11}... | collective-permute-start | bytes 1493000 | tf_op jit(solution)/shard_map/ppermute | solution.py:376
  1007.5 20.4 %collective-permute-start.40 = (bf16[72,3456]{1,0:T(8,128)(2,1)S(1)}, bf16[72,3456]{1,0:T(8,128)(2,1)}, u32[]{:S(2)}, u32[]{:S(2)}) collective-permute-start(bf16[72,3456]{1,0:T(8,128)(2,1)S(1)} %add_convert_fusion.7), channel_id=1, source_target_pairs={{0,16},{16,0},{1,17},{17,1},{2,18},{18,2},{3,19},{19,3},{4,20},{20... | collective-permute-start | bytes 1493000 | tf_op jit(solution)/shard_map/ppermute | solution.py:472
  (141 other events, 2047.5 us)
Sparse Core Ops, SparseCore 0:
  11.4 133.7 all-gather.3
  148.6 134.3 all-gather.5
  286.5 98.2 all-gather.7
  523.0 144.2 reduce-scatter.2
  711.5 260.7 reduce-scatter.4

commit v6 on v5

--- a/solution.py
+++ b/solution.py
@@ -43,16 +43,17 @@
     head_size = model_width // HEADS
     rows = total_rows // frame_count
     keys = key_value.shape[1] // frame_count
-    scale = 1.0 / math.sqrt(head_size)
-
-    def body(q_ref, k_ref, v_ref, out_ref, lse_ref):
-        scores = contract(k_ref[...], q_ref[...], 0, 0) * scale
-        top = jnp.max(scores, axis=0, keepdims=True)
-        weights = jnp.exp(scores - top)
+    scale = math.log2(math.e) / math.sqrt(head_size)
+
+    def body(q_ref, k_ref, v_ref, out_ref, exact_ref, lse_ref):
+        scores = contract(k_ref[...], q_ref[...], 0, 0)
+        top = jnp.max(scores, axis=0, keepdims=True) * scale
+        weights = jnp.exp2(scores * scale - top)
         total = jnp.sum(weights, axis=0, keepdims=True)
-        out = product(v_ref[...], weights.astype(jnp.bfloat16))
-        out_ref[...] = (out / total).astype(jnp.bfloat16)
-        lse_ref[0] = top + jnp.log(total)
+        out = product(v_ref[...], weights.astype(jnp.bfloat16)) / total
+        out_ref[...] = out.astype(jnp.bfloat16)
+        exact_ref[...] = out
+        lse_ref[0] = top + jnp.log2(total)
 
     return call(
         body,
@@ -64,29 +65,32 @@
         ],
         [
             pl.BlockSpec((head_size, rows), lambda f, h: (h, f)),
+            pl.BlockSpec((head_size, rows), lambda f, h: (h, f)),
             pl.BlockSpec((1, 1, rows), lambda f, h: (f * HEADS + h, 0, 0)),
         ],
         [
             jax.ShapeDtypeStruct(query.shape, jnp.bfloat16),
+            jax.ShapeDtypeStruct(query.shape, jnp.float32),
             jax.ShapeDtypeStruct((frame_count * HEADS, 1, rows), jnp.float32),
         ],
         "spatial_forward",
     )(query, key_value, key_value)
 
 
-def spatial_backward(query, key_value, log_total, upstream, frame_count, frame):
+def spatial_backward(query, key_value, log_total, exact, upstream, frame_count, frame):
     model_width, total_rows = query.shape
     head_size = model_width // HEADS
     rows = total_rows // frame_count
     keys = key_value.shape[1] // frame_count
     scale = 1.0 / math.sqrt(head_size)
-
-    def body(q_ref, k_ref, v_ref, lse_ref, up_ref, dq_ref, dkv_ref):
+    scale_two = math.log2(math.e) * scale
+
+    def body(q_ref, k_ref, v_ref, lse_ref, exact_ref, up_ref, dq_ref, dkv_ref):
         query_head, key_head, up_head = (q_ref[...], k_ref[...], up_ref[...])
-        probs = jnp.exp(contract(key_head, query_head, 0, 0) * scale - lse_ref[0])
+        probs = jnp.exp2(contract(key_head, query_head, 0, 0) * scale_two - lse_ref[0])
         dkv_ref[1] = contract(up_head, probs.astype(jnp.bfloat16), 1, 1).astype(jnp.bfloat16)
         prob_grad = contract(v_ref[...], up_head, 0, 0)
-        delta = jnp.sum(probs * prob_grad, axis=0, keepdims=True)
+        delta = jnp.sum(up_head.astype(jnp.float32) * exact_ref[...], axis=0, keepdims=True)
         score_grad = (probs * (prob_grad - delta)).astype(jnp.bfloat16)
         dq_ref[...] = (product(key_head, score_grad) * scale).astype(jnp.bfloat16)
         dkv_ref[0] = (contract(query_head, score_grad, 1, 1) * scale).astype(jnp.bfloat16)
@@ -100,6 +104,7 @@
             pl.BlockSpec((head_size, keys), lambda h: (HEADS + h, frame)),
             pl.BlockSpec((1, 1, rows), lambda h: (frame * HEADS + h, 0, 0)),
             pl.BlockSpec((head_size, rows), lambda h: (h, frame)),
+            pl.BlockSpec((head_size, rows), lambda h: (h, frame)),
         ],
         [
             pl.BlockSpec((head_size, rows), lambda h: (h, 0)),
@@ -110,7 +115,7 @@
             jax.ShapeDtypeStruct((2, model_width, keys), jnp.bfloat16),
         ],
         "spatial_backward",
-    )(query, key_value, key_value, log_total, upstream)
+    )(query, key_value, key_value, log_total, exact, upstream)
     return (query_grad, pair_grad.reshape(2 * model_width, keys))
 
 
@@ -344,14 +349,9 @@
     )()
 
 
-def stack_halves(lower, upper):
-    depth = lower[0].shape[0]
-    stacked = blank((2 * depth, sum(part.shape[1] for part in lower)))
-    for index, parts in enumerate((lower, upper)):
-        column = 0
-        for part in parts:
-            stacked = lax.dynamic_update_slice(stacked, low(part), (index * depth, column))
-            column += part.shape[1]
+def placed(stacked, parts):
+    for part, row, column in parts:
+        stacked = lax.dynamic_update_slice(stacked, low(part), (row, column))
     return stacked
 
 
@@ -557,7 +557,7 @@
     cross_proj_full = gathered_a[width:, 2 * width :]
     query = contract(query_full, hidden_a, 0, 1).astype(jnp.bfloat16)
     key_value = contract(pair_full, hidden_all, 0, 1).astype(jnp.bfloat16)
-    attended, log_total = spatial_forward(query, key_value, frame_count)
+    attended, attended_exact, log_total = spatial_forward(query, key_value, frame_count)
     branch_a = contract(attended, proj_full, 0, 0)
     after_a = inputs + modulation[2] * branch_a
     after_low = after_a.astype(jnp.bfloat16)
@@ -638,15 +638,18 @@
     )
     to_prev = lax.ppermute(halo_prev, "frame", back)
     to_next = lax.ppermute(halo_next, "frame", ahead)
-    stacked_c = stack_halves(
-        [contract(hidden_t, tquery_grad, 0, 1), contract(mixed, branch_t_grad, 1, 0)],
-        [contract(hidden_ext, tpair_grad, 0, 1)],
+    stacked = placed(
+        blank((2 * width, ff_width + 2 * width)),
+        [
+            (contract(hidden_t, tquery_grad, 0, 1), 0, ff_width),
+            (contract(mixed, branch_t_grad, 1, 0), 0, ff_width + width),
+            (contract(hidden_ext, tpair_grad, 0, 1), width, ff_width),
+        ],
     )
     hidden_t_grad = contract(tpair_grad[:, row_count:-row_count], tpair_full, 0, 1) + contract(
         tquery_grad, tquery_full, 0, 1
     )
-    hidden_t_grad, stacked_c = lax.optimization_barrier((hidden_t_grad, stacked_c))
-    scattered_c = scatter_halves(stacked_c)
+    hidden_t_grad, stacked = lax.optimization_barrier((hidden_t_grad, stacked))
     hidden_t_grad = jnp.concatenate(
         [
             hidden_t_grad[:row_count] + to_next.astype(jnp.float32),
@@ -674,10 +677,20 @@
     )
     up_grads = [contract(hidden_m, part, 0, 0) for part in upward_grads]
     down_grads = [contract(part, branch_m_grad, 0, 0) for part in activated_parts]
-    stacked_b = stack_halves(
-        [up_grads[0]] + down_grads[:per_half], [up_grads[1]] + down_grads[per_half:]
-    )
-    hidden_m_grad, stacked_b = lax.optimization_barrier((hidden_m_grad, stacked_b))
+    stacked = placed(
+        stacked,
+        [(up_grads[side], side * width, 0) for side in range(2)]
+        + [
+            (
+                down_grads[index],
+                index // per_half * width,
+                half_ff + index % per_half * width,
+            )
+            for index in range(ff_blocks)
+        ],
+    )
+    hidden_m_grad, stacked = lax.optimization_barrier((hidden_m_grad, stacked))
+    scattered = scatter_halves(stacked)
     grad_c = grad_m + normalize_back(hidden_m_grad * (1.0 + modulation[4]), normed_m, recip_m)
     cross_branch_grad = low(grad_c)
     cross_out_grad = low(contract(cross_proj_full, cross_branch_grad, 1, 1))
@@ -688,10 +701,6 @@
     gate_a_grad = jnp.sum(branch_a * grad_a, axis=0)
     branch_a_grad = low(modulation[2] * grad_a)
     attended_grad = low(contract(proj_full, branch_a_grad, 1, 1))
-    attended_grad, scattered_c, stacked_b = lax.optimization_barrier(
-        (attended_grad, scattered_c, stacked_b)
-    )
-    scattered_b = scatter_halves(stacked_b)
     attended_grad = tick(attended_grad, [chain_text])
     proj_grad = low(contract(attended, branch_a_grad, 1, 0))
     cross_q_grad = low(contract(after_low, cross_query_grad, 0, 1))
@@ -702,7 +711,7 @@
     query_grads, pair_grads, rest_grads, rest_received = ([], [], [], [])
     for frame in range(frame_count):
         query_grad, pair_grad = spatial_backward(
-            query, key_value, log_total, attended_grad, frame_count, frame
+            query, key_value, log_total, attended_exact, attended_grad, frame_count, frame
         )
         rest_sent = contract(pair_grad[:, row_count:], pair_full, 0, 1)
         rest_low = low(rest_sent)
@@ -790,8 +799,7 @@
         latent_grad = together(latent_grad, chains_a + [chain_mod])
     chain_last = merged(chains_a)
     chain_mod.advance()
-    lower_b, upper_b = whole_halves(is_first, scattered_b)
-    lower_c, upper_c = whole_halves(is_first, scattered_c)
+    lower_b, upper_b = whole_halves(is_first, scattered)
     up_shard = (
         jnp.concatenate([lower_b[:, :half_ff], upper_b[:, :half_ff]], axis=1)
         .reshape(shard_rows, ff_blocks, shards, shard_rows)
@@ -834,8 +842,10 @@
         upper_a[:, :width],
         up_shard,
         down_shard,
-        jnp.concatenate([lower_c[:, :width], upper_c], axis=1),
-        lower_c[:, width:],
+        jnp.concatenate(
+            [lower_b[:, ff_width : ff_width + width], upper_b[:, ff_width:]], axis=1
+        ),
+        lower_b[:, ff_width + width :],
     )
 
 

time: 1050 us -> 1050 us (level)
  waiting for transfers between devices: 241 us -> 280 us
  Pallas kernels: 158 us -> 144 us
    ppermute x26, waiting for transfers between devices: 103 us -> 130 us  [across(): lax.ppermute(value, axis, [(i, i ^ 1 << step) for i in range(lax.axis_siz...]
    all_gather x3, waiting for transfers between devices: 89 us -> 111 us  [gather_halves(): lax.all_gather(jnp.where(is_first, lower, upper), ('bucket', 'frame', 'se...]
    pallas_call x2, Pallas kernels: 69.4 us -> 52.8 us  [spatial_backward(): call(body, (HEADS,), [pl.BlockSpec((head_size, rows), lambda h: (h, frame...]
    ppermute x1, waiting for transfers between devices: 14.5 us -> 0.01 us  [per_device(): lax.ppermute(hidden_t[total_rows - row_count:], 'frame', ahead)]
  transfers between devices with their start and end apart: 48 -> 46, of which waited for: 22 -> 22; matrix products, arithmetic and copies ran while one was open for 48% -> 37% of each run, Pallas kernels for 13% -> 11%
where the time goes in v6:
time: 1050 us
  matrix products  388 us (37%)
  waiting for transfers between devices  280 us (27%)
  Pallas kernels  144 us (14%)
  other arithmetic  107 us (10%)
  local copies, waits for them, and re-layouts  60.2 us (6%)
  starting transfers between devices  50.2 us (5%)
  between operations  16.8 us (2%)
    dot_general x43, matrix products, contract(): lax.dot_general(left, right, (((left_dim,), (right_dim,)), ((), ())), pre...  322 us
    ppermute x26, waiting for transfers between devices, across(): lax.ppermute(value, axis, [(i, i ^ 1 << step) for i in range(lax.axis_siz...  130 us
    all_gather x3, waiting for transfers between devices, gather_halves(): lax.all_gather(jnp.where(is_first, lower, upper), ('bucket', 'frame', 'se...  111 us
    dot_general x6, matrix products, product(): return jnp.dot(left, right, preferred_element_type=jnp.float32)  60.4 us
    pallas_call x2, Pallas kernels, spatial_backward(): call(body, (HEADS,), [pl.BlockSpec((head_size, rows), lambda h: (h, frame...  52.8 us
    pallas_call x1, Pallas kernels, spatial_forward(): call(body, (frame_count, HEADS), [pl.BlockSpec((head_size, rows), lambda...  39.6 us
    ppermute x26, starting transfers between devices, across(): lax.ppermute(value, axis, [(i, i ^ 1 << step) for i in range(lax.axis_siz...  32.6 us
    ppermute x1, waiting for transfers between devices, per_device(): latent_rest = [lax.ppermute(latent[0], 'seq', shift) for shift in shifts]  28.4 us
  transfers between devices with their start and end apart: 46, of which 22 were waited for; matrix products, arithmetic and copies ran while one was open for 37% of the time, Pallas kernels for 11%

profile of v6, /device:TPU:0, one launch (start us, length us, event | category | flops | bytes accessed | tf_op | source)
XLA Modules:
  0.0 1046.8 jit_solution(9473268765075046966)
XLA Ops:
  50.8 8.5 collective-permute-done.7
  61.8 13.6 %collective-permute-done.8 = bf16[1152,128]{1,0:T(8,128)(2,1)S(1)} collective-permute-done((bf16[1152,128]{1,0:T(8,128)(2,1)S(1)}, bf16[1152,128]{1,0:T(8,128)(2,1)S(1)}, u32[]{:S(2)}, u32[]{:S(2)}) %collective-permute-start.8) | collective-permute-done | bytes 294944 | tf_op jit(solution)/shard_map/ppermute | solution.py:376
  75.5 28.4 %collective-permute-done.4 = bf16[2,512,1152]{2,1,0:T(8,128)(2,1)} collective-permute-done((bf16[2,512,1152]{2,1,0:T(8,128)(2,1)}, bf16[2,512,1152]{2,1,0:T(8,128)(2,1)}, u32[]{:S(2)}, u32[]{:S(2)}) %collective-permute-start.4) | collective-permute-done | bytes 2359328 | tf_op jit(solution)/shard_map/ppermute | solution.py:508
  115.4 30.0 %all-gather.4.cloned.1.call-done = bf16[2304,3456]{1,0:T(8,128)(2,1)} async-done(((bf16[72,3456]{1,0:T(8,128)(2,1)}), bf16[2304,3456]{1,0:T(8,128)(2,1)}) %all-gather.4.cloned.1.call-update) | async-done | bytes 15925264 | tf_op jit(solution)/shard_map/all_gather | solution.py:322
  153.6 18.4 %convolution_convert_fusion.3.k_ref.v_ref = bf16[2304,2048]{1,0:T(8,128)(2,1)} fusion(bf16[2048,1152]{1,0:T(8,128)(2,1)} %bitcast.253, bf16[2304,3456]{1,0:T(8,128)(2,1)} %all-gather.4.cloned.1.call-done), kind=kOutput, calls=%fused_computation.9 | convolution fusion | flops 10876354560 | bytes 19464192 | tf_op jit(solution)/shard_map/dot_general | solution.py:24
  172.1 39.6 %spatial_forward.1 = (bf16[1152,1024]{1,0:T(8,128)(2,1)S(1)}, f32[1152,1024]{1,0:T(8,128)}, f32[32,1,512]{2,1,0:T(1,128)S(1)}) custom-call(bf16[1152,1024]{1,0:T(8,128)(2,1)S(1)} %convolution_convert_fusion.20.q_ref, bf16[2304,2048]{1,0:T(8,128)(2,1)} %convolution_convert_fusion.3.k_ref.v_ref, bf16[2304,2048]{1,0:T(8,128)(2,1)} %convolution_convert_fusion.3.k_ref.v_ref), custom_call_target="tpu_custom_call" | custom-call | tf_op jit(solution)/shard_map/spatial_forward/pallas_call | solution.py:58
  211.7 9.5 fusion.70
  227.7 8.5 cross_forward.1
  248.0 35.4 %all-gather.6.cloned.1.call-done = bf16[2304,4608]{1,0:T(8,128)(2,1)} async-done(((bf16[72,4608]{1,0:T(8,128)(2,1)}), bf16[2304,4608]{1,0:T(8,128)(2,1)}) %all-gather.6.cloned.1.call-update) | async-done | bytes 21233680 | tf_op jit(solution)/shard_map/all_gather | solution.py:322
  283.4 12.7 %multiply_convert_fusion.1 = (bf16[1024,2304]{1,0:T(8,128)(2,1)S(1)}, f32[1024,2304]{1,0:T(8,128)}) fusion(bf16[1024,1152]{1,0:T(8,128)(2,1)} %add_convert_fusion.4, bf16[2304,4608]{1,0:T(8,128)(2,1)} %all-gather.6.cloned.1.call-done), kind=kOutput, calls=%fused_computation.33 | convolution fusion | flops 5457051648 | bytes 21823488 | tf_op jit(solution)/shard_map/dot_general | solution.py:20
  310.2 13.0 %multiply_convert_fusion = (bf16[1024,2304]{1,0:T(8,128)(2,1)S(1)}, f32[1024,2304]{1,0:T(8,128)}) fusion(bf16[1024,1152]{1,0:T(8,128)(2,1)S(1)} %copy-done.49, bf16[2304,4608]{1,0:T(8,128)(2,1)} %all-gather.6.cloned.1.call-done), kind=kOutput, calls=%fused_computation.32 | convolution fusion | flops 5457051648 | bytes 21823488 | tf_op jit(solution)/shard_map/dot_general | solution.py:20
  323.2 8.5 fusion.102
  331.8 12.1 %fusion.182 = (f32[1024]{0:T(1024)S(1)}, f32[1024,1152]{1,0:T(8,128)S(1)}, f32[1024,1152]{1,0:T(8,128)}) fusion(f32[1024,1152]{1,0:T(8,128)S(1)} %bitcast.228, f32[1152]{0:T(1024)S(1)} %get-tuple-element.184, bf16[2304,4608]{1,0:T(8,128)(2,1)} %all-gather.6.cloned.1.call-done, bf16[1024,2304]{1,0:T(8,128)(2,1)} %copy-done.52, f32[1024,1152]{1,0:T(8,128)} %fusion.102, ...), kind=kOutput, calls=%fused_computation.369 | convolution fusion | flops 2724985856 | bytes 33333760 | tf_op jit(solution)/shard_map/dot_general | solution.py:20
  357.4 45.2 %all-gather.8.cloned.1.call-done = bf16[2304,2304]{1,0:T(8,128)(2,1)} async-done(((bf16[72,2304]{1,0:T(8,128)(2,1)}), bf16[2304,2304]{1,0:T(8,128)(2,1)}) %all-gather.8.cloned.1.call-update) | async-done | bytes 10616848 | tf_op jit(solution)/shard_map/all_gather | solution.py:322
  408.5 17.3 %convolution_convert_fusion.2.k_ref.v_ref = bf16[2304,2048]{1,0:T(8,128)(2,1)} fusion(bf16[2304,2304]{1,0:T(8,128)(2,1)} %all-gather.8.cloned.1.call-done, bf16[512,1152]{1,0:T(8,128)(2,1)} %collective-permute-done.10, bf16[1024,1152]{1,0:T(8,128)(2,1)S(1)} %copy-done.25, bf16[512,1152]{1,0:T(8,128)(2,1)} %collective-permute-done.9), kind=kOutput, calls=%fused_computation.8 | convolution fusion | flops 10890510336 | bytes 19464192 | tf_op jit(solution)/shard_map/dot_general | solution.py:24
  425.8 10.9 %temporal_forward.1 = bf16[1152,1024]{1,0:T(8,128)(2,1)S(1)} custom-call(s32[2,2]{1,0:T(2,128)S(1)} %add_convert_fusion.8.live_ref, bf16[1152,1024]{1,0:T(8,128)(2,1)S(1)} %convolution_convert_fusion.18.q_ref, bf16[2304,2048]{1,0:T(8,128)(2,1)} %convolution_convert_fusion.2.k_ref.v_ref, bf16[2304,2048]{1,0:T(8,128)(2,1)} %convolution_convert_fusion.2.k_ref.v_ref), custom_call_target="tpu_custom_call" | custom-call | tf_op jit(solution)/shard_map/temporal_forward/pallas_call | solution.py:225
  443.4 16.8 %temporal_backward.1 = (bf16[1152,1024]{1,0:T(8,128)(2,1)S(1)}, bf16[2,1152,2048]{2,1,0:T(8,128)(2,1)}) custom-call(s32[2,2]{1,0:T(2,128)S(1)} %add_convert_fusion.8.live_ref, bf16[1152,1024]{1,0:T(8,128)(2,1)S(1)} %convolution_convert_fusion.18.q_ref, bf16[2304,2048]{1,0:T(8,128)(2,1)} %convolution_convert_fusion.2.k_ref.v_ref, ...), custom_call_target="tpu_custom_call" | custom-call | tf_op jit(solution)/shard_map/temporal_backward/pallas_call | solution.py:280
  486.1 15.7 %fusion.2 = bf16[2304,6912]{1,0:T(8,128)(2,1)} fusion(bf16[2304,6912]{1,0:T(8,128)(2,1)} %fusion.24, bf16[2304,2048]{1,0:T(8,128)(2,1)} %bitcast.282, bf16[512,1152]{1,0:T(8,128)(2,1)} %collective-permute-done.10, bf16[1024,1152]{1,0:T(8,128)(2,1)S(1)} %copy-done.25, bf16[512,1152]{1,0:T(8,128)(2,1)} %collective-permute-done.9), kind=kOutput, calls=%fused_computation.12 | convolution fusion | flops 10888445952 | bytes 19464192 | tf_op jit(solution)/shard_map/dot_general | solution.py:24
  501.8 10.0 fusion.45
  517.2 8.5 collective-permute-done.11
  530.2 12.3 %fusion.29 = (f32[1152]{0:T(1024)}, bf16[1024,1152]{1,0:T(8,128)(2,1)}, f32[1152]{0:T(1024)}, f32[1024,1152]{1,0:T(8,128)}) fusion(bf16[1,2,512,1152]{3,2,1,0:T(8,128)(2,1)S(1)} %copy-done.46, f32[1024]{0:T(1024)S(1)} %bitcast.279, f32[1024,1152]{1,0:T(8,128)S(1)} %bitcast.233, f32[1152]{0:T(1024)S(1)} %get-tuple-element.179, ...), kind=kOutput, calls=%fused_computation.60 | convolution fusion | flops 2740320256 | bytes 28645376 | tf_op jit(solution)/shard_map/dot_general | solution.py:24
  617.6 9.7 fusion.47
  627.3 11.2 %fusion.55 = f32[1024,1152]{1,0:T(8,128)} fusion(f32[1024,1152]{1,0:T(8,128)S(1)} %fusion.47, bf16[1024,2304]{1,0:T(8,128)(2,1)} %copy-done.38, bf16[2304,4608]{1,0:T(8,128)(2,1)} %all-gather.6.cloned.1.call-done), kind=kOutput, calls=%fused_computation.117 | convolution fusion | flops 5436997632 | bytes 19464192 | tf_op jit(solution)/shard_map/dot_general | solution.py:24
  659.6 15.9 %cross_backward.1 = (bf16[1152,1024]{1,0:T(8,128)(2,1)S(1)}, f32[2,1152,128]{2,1,0:T(8,128)S(1)}) custom-call(s32[1]{0:T(128)S(6)} %copy.60.length_ref, bf16[1152,1024]{1,0:T(8,128)(2,1)} %copy-done.2, bf16[2304,128]{1,0:T(8,128)(2,1)S(1)} %pad_maximum_fusion.12.k_ref.v_ref, bf16[2304,128]{1,0:T(8,128)(2,1)S(1)} %pad_maximum_fusion.12.k_ref.v_ref, ...), custom_call_target="tpu_custom_call" | custom-call | tf_op jit(solution)/shard_map/cross_backward/pallas_call | solution.py:171
  714.5 26.4 %spatial_backward.2 = (bf16[1152,512]{1,0:T(8,128)(2,1)S(1)}, bf16[2,1152,1024]{2,1,0:T(8,128)(2,1)}) custom-call(bf16[1152,1024]{1,0:T(8,128)(2,1)S(1)} %convolution_convert_fusion.20.q_ref, bf16[2304,2048]{1,0:T(8,128)(2,1)} %convolution_convert_fusion.3.k_ref.v_ref, bf16[2304,2048]{1,0:T(8,128)(2,1)} %convolution_convert_fusion.3.k_ref.v_ref, ...), custom_call_target="tpu_custom_call" | custom-call | tf_op jit(solution)/shard_map/spatial_backward/pallas_call | solution.py:98
  751.0 26.4 %spatial_backward.3 = (bf16[1152,512]{1,0:T(8,128)(2,1)S(1)}, bf16[2,1152,1024]{2,1,0:T(8,128)(2,1)}) custom-call(bf16[1152,1024]{1,0:T(8,128)(2,1)S(1)} %convolution_convert_fusion.20.q_ref, bf16[2304,2048]{1,0:T(8,128)(2,1)} %convolution_convert_fusion.3.k_ref.v_ref, bf16[2304,2048]{1,0:T(8,128)(2,1)} %convolution_convert_fusion.3.k_ref.v_ref, ...), custom_call_target="tpu_custom_call" | custom-call | tf_op jit(solution)/shard_map/spatial_backward/pallas_call | solution.py:98
  777.4 10.1 fusion.84
  794.4 15.1 %convolution_convert_fusion.4 = bf16[1152,2304]{1,0:T(8,128)(2,1)S(1)} fusion(bf16[2048,1152]{1,0:T(8,128)(2,1)S(1)} %bitcast.256, bf16[2304,1024]{1,0:T(8,128)(2,1)} %bitcast.288, bf16[2304,1024]{1,0:T(8,128)(2,1)} %bitcast.285), kind=kOutput, calls=%fused_computation.10 | convolution fusion | flops 10893164544 | bytes 19464192 | tf_op jit(solution)/shard_map/dot_general | solution.py:24
  869.8 29.0 %collective-permute-done.24 = bf16[144,128]{1,0:T(8,128)(2,1)} collective-permute-done((bf16[144,128]{1,0:T(8,128)(2,1)}, bf16[144,128]{1,0:T(8,128)(2,1)}, u32[]{:S(2)}, u32[]{:S(2)}) %collective-permute-start.24) | collective-permute-done | bytes 36896 | tf_op jit(solution)/shard_map/ppermute | solution.py:376
  898.8 18.6 %collective-permute-done.23 = bf16[2,2,2,72,1152]{4,3,2,1,0:T(8,128)(2,1)} collective-permute-done((bf16[2,2,2,72,1152]{4,3,2,1,0:T(8,128)(2,1)}, bf16[2,2,2,72,1152]{4,3,2,1,0:T(8,128)(2,1)}, u32[]{:S(2)}, u32[]{:S(2)}) %collective-permute-start.23) | collective-permute-done | bytes 1327136 | tf_op jit(solution)/shard_map/ppermute | solution.py:376
  969.4 9.2 collective-permute-done.34
  978.5 29.9 %collective-permute-done.33 = bf16[72,3456]{1,0:T(8,128)(2,1)S(1)} collective-permute-done((bf16[72,3456]{1,0:T(8,128)(2,1)S(1)}, bf16[72,3456]{1,0:T(8,128)(2,1)S(1)}, u32[]{:S(2)}, u32[]{:S(2)}) %collective-permute-start.33) | collective-permute-done | bytes 497696 | tf_op jit(solution)/shard_map/ppermute | solution.py:376
  (530 shorter events, 453.7 us)
Async XLA Ops:
  7.2 138.2 %all-gather.4.cloned.1.call-start = ((), (), s32[]{:S(2)}) async-start(), calls=%async_computation.1 | async-start | bytes 16422912 | tf_op jit(solution)/shard_map/all_gather | solution.py:322
  9.5 274.0 %all-gather.6.cloned.1.call-start = ((), (), s32[]{:S(2)}) async-start(), calls=%async_computation.2 | async-start | bytes 21897216 | tf_op jit(solution)/shard_map/all_gather | solution.py:322
  22.2 380.4 %all-gather.8.cloned.1.call-start = ((), (), s32[]{:S(2)}) async-start(), calls=%async_computation.3 | async-start | bytes 10948608 | tf_op jit(solution)/shard_map/all_gather | solution.py:322
  24.7 18.3 %collective-permute-start.5 = (bf16[144,128]{1,0:T(8,128)(2,1)S(1)}, bf16[144,128]{1,0:T(8,128)(2,1)S(1)}, u32[]{:S(2)}, u32[]{:S(2)}) collective-permute-start(bf16[144,128]{1,0:T(8,128)(2,1)S(1)} %convolution_convert_fusion.21), channel_id=1, source_target_pairs={{0,1},{1,0},{2,3},{3,2},{4,5},{5,4},{6,7},{7,6},{8,9},{9,8},{10,11... | collective-permute-start | bytes 110600 | tf_op jit(solution)/shard_map/ppermute | solution.py:376
  29.0 74.9 %collective-permute-start.4 = (bf16[2,512,1152]{2,1,0:T(8,128)(2,1)}, bf16[2,512,1152]{2,1,0:T(8,128)(2,1)}, u32[]{:S(2)}, u32[]{:S(2)}) collective-permute-start(bf16[2,512,1152]{2,1,0:T(8,128)(2,1)} %bitcast.231), channel_id=1, source_target_pairs={{1,0},{0,1},{3,2},{2,3},{5,4},{4,5},{7,6},{6,7},{9,8},{8,9},{11,10... | collective-permute-start | bytes 7077896 | tf_op jit(solution)/shard_map/ppermute | solution.py:508
  59.3 16.0 %collective-permute-start.8 = (bf16[1152,128]{1,0:T(8,128)(2,1)S(1)}, bf16[1152,128]{1,0:T(8,128)(2,1)S(1)}, u32[]{:S(2)}, u32[]{:S(2)}) collective-permute-start(bf16[1152,128]{1,0:T(8,128)(2,1)S(1)} %pad_maximum_fusion.15), channel_id=1, source_target_pairs={{0,8},{2,10},{4,12},{6,14},{8,0},{10,2},{12,4},{14,6},{1,9},{3,11}... | collective-permute-start | bytes 884744 | tf_op jit(solution)/shard_map/ppermute | solution.py:376
  152.0 861.1 %reduce-scatter.4.cloned.1.call-start = ((), (), s32[]{:S(2)}) async-start(), calls=%async_computation.4 | async-start | bytes 32845824
  348.3 60.2 %collective-permute-start.10 = (bf16[512,1152]{1,0:T(8,128)(2,1)}, bf16[512,1152]{1,0:T(8,128)(2,1)}, u32[]{:S(2)}, u32[]{:S(2)}) collective-permute-start(bf16[512,1152]{1,0:T(8,128)(2,1)} %get-tuple-element.211), channel_id=1, source_target_pairs={{2,0},{4,2},{6,4},{8,6},{10,8},{12,10},{14,12},{3,1},{5,3},{7,5},{... | collective-permute-start | bytes 3538952 | tf_op jit(solution)/shard_map/ppermute | solution.py:606
  349.6 58.9 %collective-permute-start.9 = (bf16[512,1152]{1,0:T(8,128)(2,1)}, bf16[512,1152]{1,0:T(8,128)(2,1)}, u32[]{:S(2)}, u32[]{:S(2)}) collective-permute-start(bf16[512,1152]{1,0:T(8,128)(2,1)} %get-tuple-element.210), channel_id=1, source_target_pairs={{0,2},{2,4},{4,6},{6,8},{8,10},{10,12},{12,14},{1,3},{3,5},{5,7},{... | collective-permute-start | bytes 3538952 | tf_op jit(solution)/shard_map/ppermute | solution.py:605
  473.2 52.5 %collective-permute-start.11 = (bf16[512,1152]{1,0:T(8,128)(2,1)S(1)}, bf16[512,1152]{1,0:T(8,128)(2,1)S(1)}, u32[]{:S(2)}, u32[]{:S(2)}) collective-permute-start(bf16[512,1152]{1,0:T(8,128)(2,1)S(1)} %fusion.67), channel_id=1, source_target_pairs={{0,2},{2,4},{4,6},{6,8},{8,10},{10,12},{12,14},{1,3},{3,5},{5,7},{... | collective-permute-start | bytes 3538952 | tf_op jit(solution)/shard_map/ppermute | solution.py:640
  475.0 50.7 %collective-permute-start.12 = (bf16[512,1152]{1,0:T(8,128)(2,1)S(1)}, bf16[512,1152]{1,0:T(8,128)(2,1)S(1)}, u32[]{:S(2)}, u32[]{:S(2)}) collective-permute-start(bf16[512,1152]{1,0:T(8,128)(2,1)S(1)} %fusion.64), channel_id=1, source_target_pairs={{2,0},{4,2},{6,4},{8,6},{10,8},{12,10},{14,12},{3,1},{5,3},{7,5},{... | collective-permute-start | bytes 3538952 | tf_op jit(solution)/shard_map/ppermute | solution.py:639
  675.6 35.9 %collective-permute-start.13 = (bf16[2,2,2,144,128]{4,3,2,1,0:T(8,128)(2,1)S(1)}, bf16[2,2,2,144,128]{4,3,2,1,0:T(8,128)(2,1)S(1)}, u32[]{:S(2)}, u32[]{:S(2)}) collective-permute-start(bf16[2,2,2,144,128]{4,3,2,1,0:T(8,128)(2,1)S(1)} %dynamic-slice_bitcast_fusion.9), channel_id=1, source_target_pairs={{0,2},{2,0},{4,6},{6,4},{8,10},{10,8},{12,14},{14,12},{1,3},{3,1},... | collective-permute-start | bytes 884744 | tf_op jit(solution)/shard_map/ppermute | solution.py:376
  711.6 38.7 %collective-permute-start.14 = (bf16[2,2,144,128]{3,2,1,0:T(8,128)(2,1)S(1)}, bf16[2,2,144,128]{3,2,1,0:T(8,128)(2,1)S(1)}, u32[]{:S(2)}, u32[]{:S(2)}) collective-permute-start(bf16[2,2,144,128]{3,2,1,0:T(8,128)(2,1)S(1)} %dynamic-slice_bitcast_fusion.16), channel_id=1, source_target_pairs={{0,4},{2,6},{4,0},{6,2},{8,12},{10,14},{12,8},{14,10},{1,5},{3,7},... | collective-permute-start | bytes 442376 | tf_op jit(solution)/shard_map/ppermute | solution.py:376
  748.9 41.8 %collective-permute-start.15 = (bf16[512,1152]{1,0:T(8,128)(2,1)S(1)}, bf16[512,1152]{1,0:T(8,128)(2,1)S(1)}, u32[]{:S(2)}, u32[]{:S(2)}) collective-permute-start(bf16[512,1152]{1,0:T(8,128)(2,1)S(1)} %get-tuple-element.118), channel_id=1, source_target_pairs={{0,1},{1,0},{2,3},{3,2},{4,5},{5,4},{6,7},{7,6},{8,9},{9,8},{10,11... | collective-permute-start | bytes 3538952 | tf_op jit(solution)/shard_map/ppermute | solution.py:726
  750.5 89.8 %collective-permute-start.19 = (bf16[2,144,128]{2,1,0:T(8,128)(2,1)S(1)}, bf16[2,144,128]{2,1,0:T(8,128)(2,1)S(1)}, u32[]{:S(2)}, u32[]{:S(2)}) collective-permute-start(bf16[2,144,128]{2,1,0:T(8,128)(2,1)S(1)} %dynamic-slice_bitcast_fusion.17), channel_id=1, source_target_pairs={{0,1},{1,0},{2,3},{3,2},{4,5},{5,4},{6,7},{7,6},{8,9},{9,8},{10,11... | collective-permute-start | bytes 221192 | tf_op jit(solution)/shard_map/ppermute | solution.py:376
  787.5 82.3 %collective-permute-start.20 = (bf16[512,1152]{1,0:T(8,128)(2,1)}, bf16[512,1152]{1,0:T(8,128)(2,1)S(1)}, u32[]{:S(2)}, u32[]{:S(2)}) collective-permute-start(bf16[512,1152]{1,0:T(8,128)(2,1)} %get-tuple-element.134), channel_id=1, source_target_pairs={{0,1},{1,0},{2,3},{3,2},{4,5},{5,4},{6,7},{7,6},{8,9},{9,8},{10,11... | collective-permute-start | bytes 3538952 | tf_op jit(solution)/shard_map/ppermute | solution.py:726
  811.4 28.9 %collective-permute-start.17 = (bf16[1152,1152]{1,0:T(8,128)(2,1)}, bf16[1152,1152]{1,0:T(8,128)(2,1)}, u32[]{:S(2)}, u32[]{:S(2)}) collective-permute-start(bf16[1152,1152]{1,0:T(8,128)(2,1)} %broadcast_select_fusion.1), channel_id=1, source_target_pairs={{0,16},{16,0},{1,17},{17,1},{2,18},{18,2},{3,19},{19,3},{4,20},{20... | collective-permute-start | bytes 7962632 | tf_op jit(solution)/shard_map/ppermute | solution.py:472
  815.5 24.7 %collective-permute-start.16 = (bf16[1152,1152]{1,0:T(8,128)(2,1)}, bf16[1152,1152]{1,0:T(8,128)(2,1)S(1)}, u32[]{:S(2)}, u32[]{:S(2)}) collective-permute-start(bf16[1152,1152]{1,0:T(8,128)(2,1)} %get-tuple-element.202), channel_id=1, source_target_pairs={{0,16},{16,0},{1,17},{17,1},{2,18},{18,2},{3,19},{19,3},{4,20},{20... | collective-permute-start | bytes 7962632 | tf_op jit(solution)/shard_map/ppermute | solution.py:472
  815.6 26.2 %collective-permute-start.18 = (bf16[1152,1152]{1,0:T(8,128)(2,1)}, bf16[1152,1152]{1,0:T(8,128)(2,1)S(1)}, u32[]{:S(2)}, u32[]{:S(2)}) collective-permute-start(bf16[1152,1152]{1,0:T(8,128)(2,1)} %get-tuple-element.201), channel_id=1, source_target_pairs={{0,16},{16,0},{1,17},{17,1},{2,18},{18,2},{3,19},{19,3},{4,20},{20... | collective-permute-start | bytes 7962632 | tf_op jit(solution)/shard_map/ppermute | solution.py:472
  847.9 50.9 %collective-permute-start.22 = (bf16[2,2,2,72,1152]{4,3,2,1,0:T(8,128)(2,1)}, bf16[2,2,2,72,1152]{4,3,2,1,0:T(8,128)(2,1)}, u32[]{:S(2)}, u32[]{:S(2)}) collective-permute-start(bf16[2,2,2,72,1152]{4,3,2,1,0:T(8,128)(2,1)} %dynamic-slice_bitcast_fusion.1), channel_id=1, source_target_pairs={{0,2},{2,0},{4,6},{6,4},{8,10},{10,8},{12,14},{14,12},{1,3},{3,1},... | collective-permute-start | bytes 3981320 | tf_op jit(solution)/shard_map/ppermute | solution.py:376
  856.4 61.0 %collective-permute-start.23 = (bf16[2,2,2,72,1152]{4,3,2,1,0:T(8,128)(2,1)}, bf16[2,2,2,72,1152]{4,3,2,1,0:T(8,128)(2,1)}, u32[]{:S(2)}, u32[]{:S(2)}) collective-permute-start(bf16[2,2,2,72,1152]{4,3,2,1,0:T(8,128)(2,1)} %dynamic-slice_bitcast_fusion), channel_id=1, source_target_pairs={{0,4},{2,6},{4,0},{6,2},{8,12},{10,14},{12,8},{14,10},{1,5},{3,7},... | collective-permute-start | bytes 3981320 | tf_op jit(solution)/shard_map/ppermute | solution.py:376
  857.6 59.8 %collective-permute-start.21 = (bf16[2,2,2,72,1152]{4,3,2,1,0:T(8,128)(2,1)}, bf16[2,2,2,72,1152]{4,3,2,1,0:T(8,128)(2,1)}, u32[]{:S(2)}, u32[]{:S(2)}) collective-permute-start(bf16[2,2,2,72,1152]{4,3,2,1,0:T(8,128)(2,1)} %dynamic-slice_bitcast_fusion.2), channel_id=1, source_target_pairs={{0,1},{1,0},{2,3},{3,2},{4,5},{5,4},{6,7},{7,6},{8,9},{9,8},{10,11... | collective-permute-start | bytes 3981320 | tf_op jit(solution)/shard_map/ppermute | solution.py:376
  859.8 39.0 %collective-permute-start.24 = (bf16[144,128]{1,0:T(8,128)(2,1)}, bf16[144,128]{1,0:T(8,128)(2,1)}, u32[]{:S(2)}, u32[]{:S(2)}) collective-permute-start(bf16[144,128]{1,0:T(8,128)(2,1)} %dynamic-slice_bitcast_fusion.18), channel_id=1, source_target_pairs={{0,8},{2,10},{4,12},{6,14},{8,0},{10,2},{12,4},{14,6},{1,9},{3,11}... | collective-permute-start | bytes 110600 | tf_op jit(solution)/shard_map/ppermute | solution.py:376
  869.8 138.8 %collective-permute-start.38 = (bf16[128,4096]{1,0:T(8,128)(2,1)}, bf16[128,4096]{1,0:T(8,128)(2,1)}, u32[]{:S(2)}, u32[]{:S(2)}) collective-permute-start(bf16[128,4096]{1,0:T(8,128)(2,1)} %bitcast.259), channel_id=1, source_target_pairs={{0,16},{16,0},{1,17},{17,1},{2,18},{18,2},{3,19},{19,3},{4,20},{20... | collective-permute-start | bytes 3145736 | tf_op jit(solution)/shard_map/ppermute | solution.py:472
  920.9 21.8 %collective-permute-start.27 = (bf16[2,2,72,1152]{3,2,1,0:T(8,128)(2,1)}, bf16[2,2,72,1152]{3,2,1,0:T(8,128)(2,1)}, u32[]{:S(2)}, u32[]{:S(2)}) collective-permute-start(bf16[2,2,72,1152]{3,2,1,0:T(8,128)(2,1)} %dynamic-slice_bitcast_fusion.3), channel_id=1, source_target_pairs={{0,1},{1,0},{2,3},{3,2},{4,5},{5,4},{6,7},{7,6},{8,9},{9,8},{10,11... | collective-permute-start | bytes 1990664 | tf_op jit(solution)/shard_map/ppermute | solution.py:376
  925.5 20.3 %collective-permute-start.26 = (bf16[2,2,72,1152]{3,2,1,0:T(8,128)(2,1)}, bf16[2,2,72,1152]{3,2,1,0:T(8,128)(2,1)}, u32[]{:S(2)}, u32[]{:S(2)}) collective-permute-start(bf16[2,2,72,1152]{3,2,1,0:T(8,128)(2,1)} %dynamic-slice_bitcast_fusion.4), channel_id=1, source_target_pairs={{0,4},{2,6},{4,0},{6,2},{8,12},{10,14},{12,8},{14,10},{1,5},{3,7},... | collective-permute-start | bytes 1990664 | tf_op jit(solution)/shard_map/ppermute | solution.py:376
  929.1 18.1 %collective-permute-start.25 = (bf16[2,2,72,1152]{3,2,1,0:T(8,128)(2,1)}, bf16[2,2,72,1152]{3,2,1,0:T(8,128)(2,1)}, u32[]{:S(2)}, u32[]{:S(2)}) collective-permute-start(bf16[2,2,72,1152]{3,2,1,0:T(8,128)(2,1)} %dynamic-slice_bitcast_fusion.5), channel_id=1, source_target_pairs={{0,2},{2,0},{4,6},{6,4},{8,10},{10,8},{12,14},{14,12},{1,3},{3,1},... | collective-permute-start | bytes 1990664 | tf_op jit(solution)/shard_map/ppermute | solution.py:376
  950.1 14.3 %collective-permute-start.31 = (bf16[2,72,1152]{2,1,0:T(8,128)(2,1)}, bf16[2,72,1152]{2,1,0:T(8,128)(2,1)S(1)}, u32[]{:S(2)}, u32[]{:S(2)}) collective-permute-start(bf16[2,72,1152]{2,1,0:T(8,128)(2,1)} %dynamic-slice_bitcast_fusion.6), channel_id=1, source_target_pairs={{0,2},{2,0},{4,6},{6,4},{8,10},{10,8},{12,14},{14,12},{1,3},{3,1},... | collective-permute-start | bytes 995336 | tf_op jit(solution)/shard_map/ppermute | solution.py:376
  957.4 56.5 %collective-permute-start.35 = (f32[1,1152]{1,0:T(1,128)S(1)}, f32[1,1152]{1,0:T(1,128)S(1)}, u32[]{:S(2)}, u32[]{:S(2)}) collective-permute-start(f32[1,1152]{1,0:T(1,128)S(1)} %divide_multiply_fusion), channel_id=1, source_target_pairs={{0,16},{16,0},{1,17},{17,1},{2,18},{18,2},{3,19},{19,3},{4,20},{20... | collective-permute-start | bytes 13832 | tf_op jit(solution)/shard_map/ppermute | solution.py:472
  966.8 41.7 %collective-permute-start.33 = (bf16[72,3456]{1,0:T(8,128)(2,1)S(1)}, bf16[72,3456]{1,0:T(8,128)(2,1)S(1)}, u32[]{:S(2)}, u32[]{:S(2)}) collective-permute-start(bf16[72,3456]{1,0:T(8,128)(2,1)S(1)} %pad_maximum_fusion.13), channel_id=1, source_target_pairs={{0,8},{2,10},{4,12},{6,14},{8,0},{10,2},{12,4},{14,6},{1,9},{3,11}... | collective-permute-start | bytes 1493000 | tf_op jit(solution)/shard_map/ppermute | solution.py:376
  969.3 39.3 %collective-permute-start.39 = (bf16[144,128]{1,0:T(8,128)(2,1)S(1)}, bf16[144,128]{1,0:T(8,128)(2,1)S(1)}, u32[]{:S(2)}, u32[]{:S(2)}) collective-permute-start(bf16[144,128]{1,0:T(8,128)(2,1)S(1)} %fusion.148), channel_id=1, source_target_pairs={{0,16},{16,0},{1,17},{17,1},{2,18},{18,2},{3,19},{19,3},{4,20},{20... | collective-permute-start | bytes 110600 | tf_op jit(solution)/shard_map/ppermute | solution.py:472
  1013.7 22.0 %collective-permute-start.40 = (bf16[72,3456]{1,0:T(8,128)(2,1)S(1)}, bf16[72,3456]{1,0:T(8,128)(2,1)}, u32[]{:S(2)}, u32[]{:S(2)}) collective-permute-start(bf16[72,3456]{1,0:T(8,128)(2,1)S(1)} %add_convert_fusion.7), channel_id=1, source_target_pairs={{0,16},{16,0},{1,17},{17,1},{2,18},{18,2},{3,19},{19,3},{4,20},{20... | collective-permute-start | bytes 1493000 | tf_op jit(solution)/shard_map/ppermute | solution.py:472
  (132 other events, 1741.1 us)
Sparse Core Ops, SparseCore 0:
  11.4 133.9 all-gather.3
  148.9 134.4 all-gather.5
  286.9 115.5 all-gather.7
  638.6 371.9 reduce-scatter.3

commit v7 on v5

--- a/solution.py
+++ b/solution.py
@@ -43,16 +43,17 @@
     head_size = model_width // HEADS
     rows = total_rows // frame_count
     keys = key_value.shape[1] // frame_count
-    scale = 1.0 / math.sqrt(head_size)
-
-    def body(q_ref, k_ref, v_ref, out_ref, lse_ref):
-        scores = contract(k_ref[...], q_ref[...], 0, 0) * scale
-        top = jnp.max(scores, axis=0, keepdims=True)
-        weights = jnp.exp(scores - top)
+    scale = math.log2(math.e) / math.sqrt(head_size)
+
+    def body(q_ref, k_ref, v_ref, out_ref, exact_ref, lse_ref):
+        scores = contract(k_ref[...], q_ref[...], 0, 0)
+        top = jnp.max(scores, axis=0, keepdims=True) * scale
+        weights = jnp.exp2(scores * scale - top)
         total = jnp.sum(weights, axis=0, keepdims=True)
-        out = product(v_ref[...], weights.astype(jnp.bfloat16))
-        out_ref[...] = (out / total).astype(jnp.bfloat16)
-        lse_ref[0] = top + jnp.log(total)
+        out = product(v_ref[...], weights.astype(jnp.bfloat16)) / total
+        out_ref[...] = out.astype(jnp.bfloat16)
+        exact_ref[...] = out
+        lse_ref[0] = top + jnp.log2(total)
 
     return call(
         body,
@@ -64,29 +65,32 @@
         ],
         [
             pl.BlockSpec((head_size, rows), lambda f, h: (h, f)),
+            pl.BlockSpec((head_size, rows), lambda f, h: (h, f)),
             pl.BlockSpec((1, 1, rows), lambda f, h: (f * HEADS + h, 0, 0)),
         ],
         [
             jax.ShapeDtypeStruct(query.shape, jnp.bfloat16),
+            jax.ShapeDtypeStruct(query.shape, jnp.float32),
             jax.ShapeDtypeStruct((frame_count * HEADS, 1, rows), jnp.float32),
         ],
         "spatial_forward",
     )(query, key_value, key_value)
 
 
-def spatial_backward(query, key_value, log_total, upstream, frame_count, frame):
+def spatial_backward(query, key_value, log_total, exact, upstream, frame_count, frame):
     model_width, total_rows = query.shape
     head_size = model_width // HEADS
     rows = total_rows // frame_count
     keys = key_value.shape[1] // frame_count
     scale = 1.0 / math.sqrt(head_size)
-
-    def body(q_ref, k_ref, v_ref, lse_ref, up_ref, dq_ref, dkv_ref):
+    scale_two = math.log2(math.e) * scale
+
+    def body(q_ref, k_ref, v_ref, lse_ref, exact_ref, up_ref, dq_ref, dkv_ref):
         query_head, key_head, up_head = (q_ref[...], k_ref[...], up_ref[...])
-        probs = jnp.exp(contract(key_head, query_head, 0, 0) * scale - lse_ref[0])
+        probs = jnp.exp2(contract(key_head, query_head, 0, 0) * scale_two - lse_ref[0])
         dkv_ref[1] = contract(up_head, probs.astype(jnp.bfloat16), 1, 1).astype(jnp.bfloat16)
         prob_grad = contract(v_ref[...], up_head, 0, 0)
-        delta = jnp.sum(probs * prob_grad, axis=0, keepdims=True)
+        delta = jnp.sum(up_head.astype(jnp.float32) * exact_ref[...], axis=0, keepdims=True)
         score_grad = (probs * (prob_grad - delta)).astype(jnp.bfloat16)
         dq_ref[...] = (product(key_head, score_grad) * scale).astype(jnp.bfloat16)
         dkv_ref[0] = (contract(query_head, score_grad, 1, 1) * scale).astype(jnp.bfloat16)
@@ -100,6 +104,7 @@
             pl.BlockSpec((head_size, keys), lambda h: (HEADS + h, frame)),
             pl.BlockSpec((1, 1, rows), lambda h: (frame * HEADS + h, 0, 0)),
             pl.BlockSpec((head_size, rows), lambda h: (h, frame)),
+            pl.BlockSpec((head_size, rows), lambda h: (h, frame)),
         ],
         [
             pl.BlockSpec((head_size, rows), lambda h: (h, 0)),
@@ -110,7 +115,7 @@
             jax.ShapeDtypeStruct((2, model_width, keys), jnp.bfloat16),
         ],
         "spatial_backward",
-    )(query, key_value, key_value, log_total, upstream)
+    )(query, key_value, key_value, log_total, exact, upstream)
     return (query_grad, pair_grad.reshape(2 * model_width, keys))
 
 
@@ -557,7 +562,7 @@
     cross_proj_full = gathered_a[width:, 2 * width :]
     query = contract(query_full, hidden_a, 0, 1).astype(jnp.bfloat16)
     key_value = contract(pair_full, hidden_all, 0, 1).astype(jnp.bfloat16)
-    attended, log_total = spatial_forward(query, key_value, frame_count)
+    attended, attended_exact, log_total = spatial_forward(query, key_value, frame_count)
     branch_a = contract(attended, proj_full, 0, 0)
     after_a = inputs + modulation[2] * branch_a
     after_low = after_a.astype(jnp.bfloat16)
@@ -702,7 +707,7 @@
     query_grads, pair_grads, rest_grads, rest_received = ([], [], [], [])
     for frame in range(frame_count):
         query_grad, pair_grad = spatial_backward(
-            query, key_value, log_total, attended_grad, frame_count, frame
+            query, key_value, log_total, attended_exact, attended_grad, frame_count, frame
         )
         rest_sent = contract(pair_grad[:, row_count:], pair_full, 0, 1)
         rest_low = low(rest_sent)
@@ -745,11 +750,15 @@
             )
         )
     ]
-    pair_own = jnp.concatenate(
-        [contract(part[:, :row_count], pair_full, 0, 1) for part in pair_grads], axis=0
-    )
-    pair_own = tick(pair_own, chains_a + [chain_text])
-    own_grad = pair_own + contract(query_grad, query_full, 0, 1)
+    pair_own = contract(pair_grads[0][:, :row_count], pair_full, 0, 1)
+    pair_own, query_grad, pair_grads = tick(
+        (pair_own, query_grad, pair_grads), chains_a + [chain_text]
+    )
+    own_grad = jnp.concatenate(
+        [pair_own]
+        + [contract(part[:, :row_count], pair_full, 0, 1) for part in pair_grads[1:]],
+        axis=0,
+    ) + contract(query_grad, query_full, 0, 1)
     shift_a_grad = jnp.sum(own_grad, axis=0)
     scale_a_grad = jnp.sum(own_grad * normed_a, axis=0)
     for frame in range(frame_count):
@@ -771,13 +780,13 @@
             gate_t_grad,
         ]
     ).reshape(shards, 9 * width // shards)
-    own_grad, mod_grad, rest_received = together(
-        (own_grad, mod_grad, rest_received), chains_a + [chain_text]
-    )
-    for chain in chains_a + [chain_text]:
-        chain.advance()
     chain_mod = Chain(is_first, (mod_grad,), 0)
     chain_mod.advance()
+    own_grad, rest_received = together(
+        (own_grad, rest_received), chains_a + [chain_text, chain_mod]
+    )
+    for chain in chains_a + [chain_text, chain_mod]:
+        chain.advance()
     hidden_a_grad = own_grad + jnp.concatenate(
         [sum(part.astype(jnp.float32) for part in parts) for parts in rest_received], axis=0
     )

time: 1050 us -> 1070 us (1.019)
  waiting for transfers between devices: 241 us -> 285 us
  Pallas kernels: 158 us -> 144 us
  other arithmetic: 109 us -> 97.8 us
    reduce_scatter x2, waiting for transfers between devices: 0.02 us -> 31.3 us  [scatter_halves(): lax.psum_scatter(stacked, ('bucket', 'frame', 'seq'), scatter_dimension=0...]
    all_gather x3, waiting for transfers between devices: 89 us -> 108 us  [gather_halves(): lax.all_gather(jnp.where(is_first, lower, upper), ('bucket', 'frame', 'se...]
    pallas_call x2, Pallas kernels: 69.4 us -> 53.1 us  [spatial_backward(): call(body, (HEADS,), [pl.BlockSpec((head_size, rows), lambda h: (h, frame...]
    ppermute x1, waiting for transfers between devices: 14.5 us -> 0.01 us  [per_device(): lax.ppermute(hidden_t[total_rows - row_count:], 'frame', ahead)]
  transfers between devices with their start and end apart: 48 -> 48, of which waited for: 22 -> 20; matrix products, arithmetic and copies ran while one was open for 48% -> 46% of each run, Pallas kernels for 13% -> 11%
where the time goes in v7:
time: 1070 us; the launch traced here: 1060 us
  matrix products  395 us (37%)
  waiting for transfers between devices  285 us (27%)
  Pallas kernels  144 us (13%)
  other arithmetic  97.8 us (9%)
  local copies, waits for them, and re-layouts  59.3 us (6%)
  starting transfers between devices  59.2 us (6%)
  between operations  17 us (2%)
    dot_general x43, matrix products, contract(): lax.dot_general(left, right, (((left_dim,), (right_dim,)), ((), ())), pre...  329 us
    ppermute x26, waiting for transfers between devices, across(): lax.ppermute(value, axis, [(i, i ^ 1 << step) for i in range(lax.axis_siz...  110 us
    all_gather x3, waiting for transfers between devices, gather_halves(): lax.all_gather(jnp.where(is_first, lower, upper), ('bucket', 'frame', 'se...  108 us
    dot_general x6, matrix products, product(): return jnp.dot(left, right, preferred_element_type=jnp.float32)  60.3 us
    pallas_call x2, Pallas kernels, spatial_backward(): call(body, (HEADS,), [pl.BlockSpec((head_size, rows), lambda h: (h, frame...  53.1 us
    pallas_call x1, Pallas kernels, spatial_forward(): call(body, (frame_count, HEADS), [pl.BlockSpec((head_size, rows), lambda...  39.6 us
    ppermute x26, starting transfers between devices, across(): lax.ppermute(value, axis, [(i, i ^ 1 << step) for i in range(lax.axis_siz...  39.4 us
    reduce_scatter x2, waiting for transfers between devices, scatter_halves(): lax.psum_scatter(stacked, ('bucket', 'frame', 'seq'), scatter_dimension=0...  31.3 us
  transfers between devices with their start and end apart: 48, of which 20 were waited for; matrix products, arithmetic and copies ran while one was open for 46% of the time, Pallas kernels for 11%

profile of v7, /device:TPU:0, one launch (start us, length us, event | category | flops | bytes accessed | tf_op | source)
XLA Modules:
  0.0 1058.2 jit_solution(13814093221416834136)
XLA Ops:
  50.4 8.8 collective-permute-done.7
  62.1 13.1 %collective-permute-done.8 = bf16[1152,128]{1,0:T(8,128)(2,1)S(1)} collective-permute-done((bf16[1152,128]{1,0:T(8,128)(2,1)S(1)}, bf16[1152,128]{1,0:T(8,128)(2,1)S(1)}, u32[]{:S(2)}, u32[]{:S(2)}) %collective-permute-start.8) | collective-permute-done | bytes 294944 | tf_op jit(solution)/shard_map/ppermute | solution.py:381
  75.4 28.0 %collective-permute-done.4 = bf16[2,512,1152]{2,1,0:T(8,128)(2,1)} collective-permute-done((bf16[2,512,1152]{2,1,0:T(8,128)(2,1)}, bf16[2,512,1152]{2,1,0:T(8,128)(2,1)}, u32[]{:S(2)}, u32[]{:S(2)}) %collective-permute-start.4) | collective-permute-done | bytes 2359328 | tf_op jit(solution)/shard_map/ppermute | solution.py:513
  113.7 31.5 %all-gather.4.cloned.1.call-done = bf16[2304,3456]{1,0:T(8,128)(2,1)} async-done(((bf16[72,3456]{1,0:T(8,128)(2,1)}), bf16[2304,3456]{1,0:T(8,128)(2,1)}) %all-gather.4.cloned.1.call-update) | async-done | bytes 15925264 | tf_op jit(solution)/shard_map/all_gather | solution.py:322
  153.6 18.5 %convolution_convert_fusion.3.k_ref.v_ref = bf16[2304,2048]{1,0:T(8,128)(2,1)} fusion(bf16[2048,1152]{1,0:T(8,128)(2,1)} %bitcast.251, bf16[2304,3456]{1,0:T(8,128)(2,1)} %all-gather.4.cloned.1.call-done), kind=kOutput, calls=%fused_computation.9 | convolution fusion | flops 10876354560 | bytes 19464192 | tf_op jit(solution)/shard_map/dot_general | solution.py:24
  172.2 39.6 %spatial_forward.1 = (bf16[1152,1024]{1,0:T(8,128)(2,1)S(1)}, f32[1152,1024]{1,0:T(8,128)}, f32[32,1,512]{2,1,0:T(1,128)S(1)}) custom-call(bf16[1152,1024]{1,0:T(8,128)(2,1)S(1)} %convolution_convert_fusion.20.q_ref, bf16[2304,2048]{1,0:T(8,128)(2,1)} %convolution_convert_fusion.3.k_ref.v_ref, bf16[2304,2048]{1,0:T(8,128)(2,1)} %convolution_convert_fusion.3.k_ref.v_ref), custom_call_target="tpu_custom_call" | custom-call | tf_op jit(solution)/shard_map/spatial_forward/pallas_call | solution.py:58
  211.8 10.1 fusion.70
  228.2 8.5 cross_forward.1
  248.4 34.6 %all-gather.6.cloned.1.call-done = bf16[2304,4608]{1,0:T(8,128)(2,1)} async-done(((bf16[72,4608]{1,0:T(8,128)(2,1)}), bf16[2304,4608]{1,0:T(8,128)(2,1)}) %all-gather.6.cloned.1.call-update) | async-done | bytes 21233680 | tf_op jit(solution)/shard_map/all_gather | solution.py:322
  283.0 12.7 %multiply_convert_fusion.1 = (bf16[1024,2304]{1,0:T(8,128)(2,1)S(1)}, f32[1024,2304]{1,0:T(8,128)}) fusion(bf16[1024,1152]{1,0:T(8,128)(2,1)} %add_convert_fusion.4, bf16[2304,4608]{1,0:T(8,128)(2,1)} %all-gather.6.cloned.1.call-done), kind=kOutput, calls=%fused_computation.33 | convolution fusion | flops 5457051648 | bytes 21823488 | tf_op jit(solution)/shard_map/dot_general | solution.py:20
  309.7 12.8 %multiply_convert_fusion = (bf16[1024,2304]{1,0:T(8,128)(2,1)S(1)}, f32[1024,2304]{1,0:T(8,128)}) fusion(bf16[1024,1152]{1,0:T(8,128)(2,1)S(1)} %copy-done.43, bf16[2304,4608]{1,0:T(8,128)(2,1)} %all-gather.6.cloned.1.call-done), kind=kOutput, calls=%fused_computation.32 | convolution fusion | flops 5457051648 | bytes 21823488 | tf_op jit(solution)/shard_map/dot_general | solution.py:20
  322.6 8.5 fusion.102
  331.1 12.3 %fusion.184 = (f32[1024]{0:T(1024)S(1)}, f32[1024,1152]{1,0:T(8,128)S(1)}, f32[1024,1152]{1,0:T(8,128)}) fusion(f32[1024,1152]{1,0:T(8,128)S(1)} %bitcast.228, f32[1152]{0:T(1024)S(1)} %get-tuple-element.194, bf16[2304,4608]{1,0:T(8,128)(2,1)} %all-gather.6.cloned.1.call-done, bf16[1024,2304]{1,0:T(8,128)(2,1)} %copy-done.47, f32[1024,1152]{1,0:T(8,128)} %fusion.102, ...), kind=kOutput, calls=%fused_computation.371 | convolution fusion | flops 2724985856 | bytes 33333760 | tf_op jit(solution)/shard_map/dot_general | solution.py:20
  358.7 41.6 %all-gather.8.cloned.1.call-done = bf16[2304,2304]{1,0:T(8,128)(2,1)} async-done(((bf16[72,2304]{1,0:T(8,128)(2,1)}), bf16[2304,2304]{1,0:T(8,128)(2,1)}) %all-gather.8.cloned.1.call-update) | async-done | bytes 10616848 | tf_op jit(solution)/shard_map/all_gather | solution.py:322
  406.2 17.3 %convolution_convert_fusion.2.k_ref.v_ref = bf16[2304,2048]{1,0:T(8,128)(2,1)} fusion(bf16[2304,2304]{1,0:T(8,128)(2,1)} %all-gather.8.cloned.1.call-done, bf16[512,1152]{1,0:T(8,128)(2,1)} %collective-permute-done.10, bf16[1024,1152]{1,0:T(8,128)(2,1)S(1)} %copy-done.32, bf16[512,1152]{1,0:T(8,128)(2,1)} %collective-permute-done.9), kind=kOutput, calls=%fused_computation.8 | convolution fusion | flops 10890510336 | bytes 19464192 | tf_op jit(solution)/shard_map/dot_general | solution.py:24
  423.5 10.9 %temporal_forward.1 = bf16[1152,1024]{1,0:T(8,128)(2,1)S(1)} custom-call(s32[2,2]{1,0:T(2,128)S(1)} %add_convert_fusion.8.live_ref, bf16[1152,1024]{1,0:T(8,128)(2,1)S(1)} %convolution_convert_fusion.18.q_ref, bf16[2304,2048]{1,0:T(8,128)(2,1)} %convolution_convert_fusion.2.k_ref.v_ref, bf16[2304,2048]{1,0:T(8,128)(2,1)} %convolution_convert_fusion.2.k_ref.v_ref), custom_call_target="tpu_custom_call" | custom-call | tf_op jit(solution)/shard_map/temporal_forward/pallas_call | solution.py:225
  441.9 16.8 %temporal_backward.1 = (bf16[1152,1024]{1,0:T(8,128)(2,1)S(1)}, bf16[2,1152,2048]{2,1,0:T(8,128)(2,1)}) custom-call(s32[2,2]{1,0:T(2,128)S(1)} %add_convert_fusion.8.live_ref, bf16[1152,1024]{1,0:T(8,128)(2,1)S(1)} %convolution_convert_fusion.18.q_ref, bf16[2304,2048]{1,0:T(8,128)(2,1)} %convolution_convert_fusion.2.k_ref.v_ref, ...), custom_call_target="tpu_custom_call" | custom-call | tf_op jit(solution)/shard_map/temporal_backward/pallas_call | solution.py:280
  458.7 8.4 fusion.67
  489.9 15.7 %fusion.2 = bf16[2304,2304]{1,0:T(8,128)(2,1)} fusion(bf16[2304,2304]{1,0:T(8,128)(2,1)} %fusion.24, bf16[2304,2048]{1,0:T(8,128)(2,1)} %bitcast.278, bf16[512,1152]{1,0:T(8,128)(2,1)} %collective-permute-done.10, bf16[1024,1152]{1,0:T(8,128)(2,1)S(1)} %copy-done.32, bf16[512,1152]{1,0:T(8,128)(2,1)} %collective-permute-done.9), kind=kOutput, calls=%fused_computation.12 | convolution fusion | flops 10888445952 | bytes 19464192 | tf_op jit(solution)/shard_map/dot_general | solution.py:24
  505.6 9.9 fusion.45
  538.9 12.4 %fusion.29 = (f32[1152]{0:T(1024)}, bf16[1024,1152]{1,0:T(8,128)(2,1)}, f32[1152]{0:T(1024)}, f32[1024,1152]{1,0:T(8,128)S(1)}) fusion(bf16[1,2,512,1152]{3,2,1,0:T(8,128)(2,1)S(1)} %copy-done.41, f32[1024]{0:T(1024)S(1)} %bitcast.275, f32[1024,1152]{1,0:T(8,128)} %copy-done.21, f32[1152]{0:T(1024)S(1)} %get-tuple-element.189, ...), kind=kOutput, calls=%fused_computation.60 | convolution fusion | flops 2740320256 | bytes 28645376 | tf_op jit(solution)/shard_map/dot_general | solution.py:24
  632.6 9.9 fusion.47
  642.6 9.9 fusion.55
  662.8 15.4 %cross_backward.1 = (bf16[1152,1024]{1,0:T(8,128)(2,1)S(1)}, f32[2,1152,128]{2,1,0:T(8,128)S(1)}) custom-call(s32[1]{0:T(128)S(6)} %copy.52.length_ref, bf16[1152,1024]{1,0:T(8,128)(2,1)} %copy-done.4, bf16[2304,128]{1,0:T(8,128)(2,1)S(1)} %pad_maximum_fusion.11.k_ref.v_ref, bf16[2304,128]{1,0:T(8,128)(2,1)S(1)} %pad_maximum_fusion.11.k_ref.v_ref, ...), custom_call_target="tpu_custom_call" | custom-call | tf_op jit(solution)/shard_map/cross_backward/pallas_call | solution.py:171
  714.3 26.2 %spatial_backward.2 = (bf16[1152,512]{1,0:T(8,128)(2,1)S(1)}, bf16[2,1152,1024]{2,1,0:T(8,128)(2,1)}) custom-call(bf16[1152,1024]{1,0:T(8,128)(2,1)S(1)} %convolution_convert_fusion.20.q_ref, bf16[2304,2048]{1,0:T(8,128)(2,1)} %convolution_convert_fusion.3.k_ref.v_ref, bf16[2304,2048]{1,0:T(8,128)(2,1)} %convolution_convert_fusion.3.k_ref.v_ref, ...), custom_call_target="tpu_custom_call" | custom-call | tf_op jit(solution)/shard_map/spatial_backward/pallas_call | solution.py:98
  757.2 26.9 %spatial_backward.3 = (bf16[1152,512]{1,0:T(8,128)(2,1)S(1)}, bf16[2,1152,1024]{2,1,0:T(8,128)(2,1)}) custom-call(bf16[1152,1024]{1,0:T(8,128)(2,1)S(1)} %convolution_convert_fusion.20.q_ref, bf16[2304,2048]{1,0:T(8,128)(2,1)} %convolution_convert_fusion.3.k_ref.v_ref, bf16[2304,2048]{1,0:T(8,128)(2,1)} %convolution_convert_fusion.3.k_ref.v_ref, ...), custom_call_target="tpu_custom_call" | custom-call | tf_op jit(solution)/shard_map/spatial_backward/pallas_call | solution.py:98
  784.1 9.1 fusion.84
  799.2 14.3 %convolution_convert_fusion.4 = bf16[1152,2304]{1,0:T(8,128)(2,1)S(1)} fusion(bf16[2048,1152]{1,0:T(8,128)(2,1)S(1)} %bitcast.254, bf16[2304,1024]{1,0:T(8,128)(2,1)} %bitcast.281, bf16[2304,1024]{1,0:T(8,128)(2,1)} %bitcast.286), kind=kOutput, calls=%fused_computation.10 | convolution fusion | flops 10893164544 | bytes 19464192 | tf_op jit(solution)/shard_map/dot_general | solution.py:24
  880.7 25.4 %collective-permute-done.25 = f32[2,2,2,1,648]{4,3,2,1,0:T(1,128)S(1)} collective-permute-done((f32[2,2,2,1,648]{4,3,2,1,0:T(1,128)S(1)}, f32[2,2,2,1,648]{4,3,2,1,0:T(1,128)S(1)}, u32[]{:S(2)}, u32[]{:S(2)}) %collective-permute-start.25) | collective-permute-done | bytes 20768 | tf_op jit(solution)/shard_map/ppermute | solution.py:381
  937.4 12.3 %collective-permute-done.33 = f32[2,1,648]{2,1,0:T(1,128)S(1)} collective-permute-done((f32[2,1,648]{2,1,0:T(1,128)S(1)}, f32[2,1,648]{2,1,0:T(1,128)S(1)}, u32[]{:S(2)}, u32[]{:S(2)}) %collective-permute-start.33) | collective-permute-done | bytes 5216 | tf_op jit(solution)/shard_map/ppermute | solution.py:381
  960.0 35.6 %collective-permute-done.35 = f32[1,648]{1,0:T(1,128)S(1)} collective-permute-done((f32[1,648]{1,0:T(1,128)S(1)}, f32[1,648]{1,0:T(1,128)S(1)}, u32[]{:S(2)}, u32[]{:S(2)}) %collective-permute-start.35) | collective-permute-done | bytes 2624 | tf_op jit(solution)/shard_map/ppermute | solution.py:381
  995.7 31.3 %reduce-scatter.5.cloned.1.call-done = bf16[72,4608]{1,0:T(8,128)(2,1)} async-done(((bf16[2304,4608]{1,0:T(8,128)(2,1)}), bf16[72,4608]{1,0:T(8,128)(2,1)}) %reduce-scatter.5.cloned.1.call-update) | async-done | bytes 663568 | tf_op jit(solution)/shard_map/reduce_scatter | solution.py:364
  (537 shorter events, 453.0 us)
Async XLA Ops:
  7.2 138.0 %all-gather.4.cloned.1.call-start = ((), (), s32[]{:S(2)}) async-start(), calls=%async_computation.2 | async-start | bytes 16422912 | tf_op jit(solution)/shard_map/all_gather | solution.py:322
  9.5 273.5 %all-gather.6.cloned.1.call-start = ((), (), s32[]{:S(2)}) async-start(), calls=%async_computation.3 | async-start | bytes 21897216 | tf_op jit(solution)/shard_map/all_gather | solution.py:322
  22.2 378.1 %all-gather.8.cloned.1.call-start = ((), (), s32[]{:S(2)}) async-start(), calls=%async_computation.4 | async-start | bytes 10948608 | tf_op jit(solution)/shard_map/all_gather | solution.py:322
  24.4 18.2 %collective-permute-start.5 = (bf16[144,128]{1,0:T(8,128)(2,1)S(1)}, bf16[144,128]{1,0:T(8,128)(2,1)S(1)}, u32[]{:S(2)}, u32[]{:S(2)}) collective-permute-start(bf16[144,128]{1,0:T(8,128)(2,1)S(1)} %convolution_convert_fusion.21), channel_id=1, source_target_pairs={{0,1},{1,0},{2,3},{3,2},{4,5},{5,4},{6,7},{7,6},{8,9},{9,8},{10,11... | collective-permute-start | bytes 110600 | tf_op jit(solution)/shard_map/ppermute | solution.py:381
  28.7 74.7 %collective-permute-start.4 = (bf16[2,512,1152]{2,1,0:T(8,128)(2,1)}, bf16[2,512,1152]{2,1,0:T(8,128)(2,1)}, u32[]{:S(2)}, u32[]{:S(2)}) collective-permute-start(bf16[2,512,1152]{2,1,0:T(8,128)(2,1)} %bitcast.231), channel_id=1, source_target_pairs={{1,0},{0,1},{3,2},{2,3},{5,4},{4,5},{7,6},{6,7},{9,8},{8,9},{11,10... | collective-permute-start | bytes 7077896 | tf_op jit(solution)/shard_map/ppermute | solution.py:513
  151.8 555.9 %reduce-scatter.3.cloned.1.call-start = ((), (), s32[]{:S(2)}) async-start(), calls=%async_computation.5 | async-start | bytes 10948608 | tf_op jit(solution)/shard_map/reduce_scatter | solution.py:364
  348.1 58.0 %collective-permute-start.10 = (bf16[512,1152]{1,0:T(8,128)(2,1)}, bf16[512,1152]{1,0:T(8,128)(2,1)}, u32[]{:S(2)}, u32[]{:S(2)}) collective-permute-start(bf16[512,1152]{1,0:T(8,128)(2,1)} %get-tuple-element.220), channel_id=1, source_target_pairs={{2,0},{4,2},{6,4},{8,6},{10,8},{12,10},{14,12},{3,1},{5,3},{7,5},{... | collective-permute-start | bytes 3538952 | tf_op jit(solution)/shard_map/ppermute | solution.py:611
  349.4 56.7 %collective-permute-start.9 = (bf16[512,1152]{1,0:T(8,128)(2,1)}, bf16[512,1152]{1,0:T(8,128)(2,1)}, u32[]{:S(2)}, u32[]{:S(2)}) collective-permute-start(bf16[512,1152]{1,0:T(8,128)(2,1)} %get-tuple-element.219), channel_id=1, source_target_pairs={{0,2},{2,4},{4,6},{6,8},{8,10},{10,12},{12,14},{1,3},{3,5},{5,7},{... | collective-permute-start | bytes 3538952 | tf_op jit(solution)/shard_map/ppermute | solution.py:610
  474.6 54.2 %collective-permute-start.11 = (bf16[512,1152]{1,0:T(8,128)(2,1)}, bf16[512,1152]{1,0:T(8,128)(2,1)}, u32[]{:S(2)}, u32[]{:S(2)}) collective-permute-start(bf16[512,1152]{1,0:T(8,128)(2,1)} %fusion.67), channel_id=1, source_target_pairs={{0,2},{2,4},{4,6},{6,8},{8,10},{10,12},{12,14},{1,3},{3,5},{5,7},{... | collective-permute-start | bytes 3538952 | tf_op jit(solution)/shard_map/ppermute | solution.py:645
  478.9 49.9 %collective-permute-start.12 = (bf16[512,1152]{1,0:T(8,128)(2,1)}, bf16[512,1152]{1,0:T(8,128)(2,1)}, u32[]{:S(2)}, u32[]{:S(2)}) collective-permute-start(bf16[512,1152]{1,0:T(8,128)(2,1)} %fusion.64), channel_id=1, source_target_pairs={{2,0},{4,2},{6,4},{8,6},{10,8},{12,10},{14,12},{3,1},{5,3},{7,5},{... | collective-permute-start | bytes 3538952 | tf_op jit(solution)/shard_map/ppermute | solution.py:644
  522.6 504.4 %reduce-scatter.5.cloned.1.call-start = ((), (), s32[]{:S(2)}) async-start(), calls=%async_computation.6 | async-start | bytes 21897216 | tf_op jit(solution)/shard_map/reduce_scatter | solution.py:364
  678.4 29.3 %collective-permute-start.13 = (bf16[2,2,2,144,128]{4,3,2,1,0:T(8,128)(2,1)S(1)}, bf16[2,2,2,144,128]{4,3,2,1,0:T(8,128)(2,1)S(1)}, u32[]{:S(2)}, u32[]{:S(2)}) collective-permute-start(bf16[2,2,2,144,128]{4,3,2,1,0:T(8,128)(2,1)S(1)} %dynamic-slice_bitcast_fusion.9), channel_id=1, source_target_pairs={{0,2},{2,0},{4,6},{6,4},{8,10},{10,8},{12,14},{14,12},{1,3},{3,1},... | collective-permute-start | bytes 884744 | tf_op jit(solution)/shard_map/ppermute | solution.py:381
  708.5 46.1 %collective-permute-start.14 = (bf16[2,2,144,128]{3,2,1,0:T(8,128)(2,1)}, bf16[2,2,144,128]{3,2,1,0:T(8,128)(2,1)}, u32[]{:S(2)}, u32[]{:S(2)}) collective-permute-start(bf16[2,2,144,128]{3,2,1,0:T(8,128)(2,1)} %dynamic-slice_bitcast_fusion.16), channel_id=1, source_target_pairs={{0,4},{2,6},{4,0},{6,2},{8,12},{10,14},{12,8},{14,10},{1,5},{3,7},... | collective-permute-start | bytes 442376 | tf_op jit(solution)/shard_map/ppermute | solution.py:381
  748.8 44.4 %collective-permute-start.15 = (bf16[512,1152]{1,0:T(8,128)(2,1)}, bf16[512,1152]{1,0:T(8,128)(2,1)}, u32[]{:S(2)}, u32[]{:S(2)}) collective-permute-start(bf16[512,1152]{1,0:T(8,128)(2,1)} %get-tuple-element.125), channel_id=1, source_target_pairs={{0,1},{1,0},{2,3},{3,2},{4,5},{5,4},{6,7},{7,6},{8,9},{9,8},{10,11... | collective-permute-start | bytes 3538952 | tf_op jit(solution)/shard_map/ppermute | solution.py:722
  815.5 25.1 %collective-permute-start.17 = (bf16[1152,1152]{1,0:T(8,128)(2,1)}, bf16[1152,1152]{1,0:T(8,128)(2,1)}, u32[]{:S(2)}, u32[]{:S(2)}) collective-permute-start(bf16[1152,1152]{1,0:T(8,128)(2,1)} %broadcast_select_fusion.1), channel_id=1, source_target_pairs={{0,16},{16,0},{1,17},{17,1},{2,18},{18,2},{3,19},{19,3},{4,20},{20... | collective-permute-start | bytes 7962632 | tf_op jit(solution)/shard_map/ppermute | solution.py:477
  820.3 20.3 %collective-permute-start.16 = (bf16[1152,1152]{1,0:T(8,128)(2,1)}, bf16[1152,1152]{1,0:T(8,128)(2,1)S(1)}, u32[]{:S(2)}, u32[]{:S(2)}) collective-permute-start(bf16[1152,1152]{1,0:T(8,128)(2,1)} %get-tuple-element.211), channel_id=1, source_target_pairs={{0,16},{16,0},{1,17},{17,1},{2,18},{18,2},{3,19},{19,3},{4,20},{20... | collective-permute-start | bytes 7962632 | tf_op jit(solution)/shard_map/ppermute | solution.py:477
  820.3 20.3 %collective-permute-start.18 = (bf16[1152,1152]{1,0:T(8,128)(2,1)}, bf16[1152,1152]{1,0:T(8,128)(2,1)S(1)}, u32[]{:S(2)}, u32[]{:S(2)}) collective-permute-start(bf16[1152,1152]{1,0:T(8,128)(2,1)} %get-tuple-element.210), channel_id=1, source_target_pairs={{0,16},{16,0},{1,17},{17,1},{2,18},{18,2},{3,19},{19,3},{4,20},{20... | collective-permute-start | bytes 7962632 | tf_op jit(solution)/shard_map/ppermute | solution.py:477
  829.7 47.7 %collective-permute-start.20 = (bf16[512,1152]{1,0:T(8,128)(2,1)}, bf16[512,1152]{1,0:T(8,128)(2,1)S(1)}, u32[]{:S(2)}, u32[]{:S(2)}) collective-permute-start(bf16[512,1152]{1,0:T(8,128)(2,1)} %get-tuple-element.143), channel_id=1, source_target_pairs={{0,1},{1,0},{2,3},{3,2},{4,5},{5,4},{6,7},{7,6},{8,9},{9,8},{10,11... | collective-permute-start | bytes 3538952 | tf_op jit(solution)/shard_map/ppermute | solution.py:722
  845.6 60.4 %collective-permute-start.22 = (bf16[2,2,2,72,1152]{4,3,2,1,0:T(8,128)(2,1)}, bf16[2,2,2,72,1152]{4,3,2,1,0:T(8,128)(2,1)}, u32[]{:S(2)}, u32[]{:S(2)}) collective-permute-start(bf16[2,2,2,72,1152]{4,3,2,1,0:T(8,128)(2,1)} %dynamic-slice_bitcast_fusion.1), channel_id=1, source_target_pairs={{0,2},{2,0},{4,6},{6,4},{8,10},{10,8},{12,14},{14,12},{1,3},{3,1},... | collective-permute-start | bytes 3981320 | tf_op jit(solution)/shard_map/ppermute | solution.py:381
  851.1 55.0 %collective-permute-start.23 = (bf16[2,2,2,72,1152]{4,3,2,1,0:T(8,128)(2,1)}, bf16[2,2,2,72,1152]{4,3,2,1,0:T(8,128)(2,1)}, u32[]{:S(2)}, u32[]{:S(2)}) collective-permute-start(bf16[2,2,2,72,1152]{4,3,2,1,0:T(8,128)(2,1)} %dynamic-slice_bitcast_fusion), channel_id=1, source_target_pairs={{0,4},{2,6},{4,0},{6,2},{8,12},{10,14},{12,8},{14,10},{1,5},{3,7},... | collective-permute-start | bytes 3981320 | tf_op jit(solution)/shard_map/ppermute | solution.py:381
  853.1 53.0 %collective-permute-start.21 = (bf16[2,2,2,72,1152]{4,3,2,1,0:T(8,128)(2,1)}, bf16[2,2,2,72,1152]{4,3,2,1,0:T(8,128)(2,1)}, u32[]{:S(2)}, u32[]{:S(2)}) collective-permute-start(bf16[2,2,2,72,1152]{4,3,2,1,0:T(8,128)(2,1)} %dynamic-slice_bitcast_fusion.2), channel_id=1, source_target_pairs={{0,1},{1,0},{2,3},{3,2},{4,5},{5,4},{6,7},{7,6},{8,9},{9,8},{10,11... | collective-permute-start | bytes 3981320 | tf_op jit(solution)/shard_map/ppermute | solution.py:381
  875.7 30.4 %collective-permute-start.25 = (f32[2,2,2,1,648]{4,3,2,1,0:T(1,128)S(1)}, f32[2,2,2,1,648]{4,3,2,1,0:T(1,128)S(1)}, u32[]{:S(2)}, u32[]{:S(2)}) collective-permute-start(f32[2,2,2,1,648]{4,3,2,1,0:T(1,128)S(1)} %dynamic-slice_bitcast_fusion.19), channel_id=1, source_target_pairs={{0,1},{1,0},{2,3},{3,2},{4,5},{5,4},{6,7},{7,6},{8,9},{9,8},{10,11... | collective-permute-start | bytes 62216 | tf_op jit(solution)/shard_map/ppermute | solution.py:381
  877.4 28.7 %collective-permute-start.24 = (bf16[144,128]{1,0:T(8,128)(2,1)S(1)}, bf16[144,128]{1,0:T(8,128)(2,1)S(1)}, u32[]{:S(2)}, u32[]{:S(2)}) collective-permute-start(bf16[144,128]{1,0:T(8,128)(2,1)S(1)} %dynamic-slice_bitcast_fusion.18), channel_id=1, source_target_pairs={{0,8},{2,10},{4,12},{6,14},{8,0},{10,2},{12,4},{14,6},{1,9},{3,11}... | collective-permute-start | bytes 110600 | tf_op jit(solution)/shard_map/ppermute | solution.py:381
  906.1 52.0 %collective-permute-start.38 = (bf16[128,4096]{1,0:T(8,128)(2,1)}, bf16[128,4096]{1,0:T(8,128)(2,1)S(1)}, u32[]{:S(2)}, u32[]{:S(2)}) collective-permute-start(bf16[128,4096]{1,0:T(8,128)(2,1)} %bitcast.255), channel_id=1, source_target_pairs={{0,16},{16,0},{1,17},{17,1},{2,18},{18,2},{3,19},{19,3},{4,20},{20... | collective-permute-start | bytes 3145736 | tf_op jit(solution)/shard_map/ppermute | solution.py:477
  907.0 19.5 %collective-permute-start.29 = (f32[2,2,1,648]{3,2,1,0:T(1,128)S(1)}, f32[2,2,1,648]{3,2,1,0:T(1,128)S(1)}, u32[]{:S(2)}, u32[]{:S(2)}) collective-permute-start(f32[2,2,1,648]{3,2,1,0:T(1,128)S(1)} %dynamic-slice_bitcast_fusion.20), channel_id=1, source_target_pairs={{0,2},{2,0},{4,6},{6,4},{8,10},{10,8},{12,14},{14,12},{1,3},{3,1},... | collective-permute-start | bytes 31112 | tf_op jit(solution)/shard_map/ppermute | solution.py:381
  911.2 18.4 %collective-permute-start.28 = (bf16[2,2,72,1152]{3,2,1,0:T(8,128)(2,1)S(1)}, bf16[2,2,72,1152]{3,2,1,0:T(8,128)(2,1)S(1)}, u32[]{:S(2)}, u32[]{:S(2)}) collective-permute-start(bf16[2,2,72,1152]{3,2,1,0:T(8,128)(2,1)S(1)} %dynamic-slice_bitcast_fusion.3), channel_id=1, source_target_pairs={{0,1},{1,0},{2,3},{3,2},{4,5},{5,4},{6,7},{7,6},{8,9},{9,8},{10,11... | collective-permute-start | bytes 1990664 | tf_op jit(solution)/shard_map/ppermute | solution.py:381
  932.7 16.9 %collective-permute-start.32 = (bf16[2,72,1152]{2,1,0:T(8,128)(2,1)S(1)}, bf16[2,72,1152]{2,1,0:T(8,128)(2,1)S(1)}, u32[]{:S(2)}, u32[]{:S(2)}) collective-permute-start(bf16[2,72,1152]{2,1,0:T(8,128)(2,1)S(1)} %dynamic-slice_bitcast_fusion.6), channel_id=1, source_target_pairs={{0,2},{2,0},{4,6},{6,4},{8,10},{10,8},{12,14},{14,12},{1,3},{3,1},... | collective-permute-start | bytes 995336 | tf_op jit(solution)/shard_map/ppermute | solution.py:381
  949.6 78.1 %collective-permute-start.36 = (f32[1,1152]{1,0:T(1,128)S(1)}, f32[1,1152]{1,0:T(1,128)S(1)}, u32[]{:S(2)}, u32[]{:S(2)}) collective-permute-start(f32[1,1152]{1,0:T(1,128)S(1)} %copy-done.74), channel_id=1, source_target_pairs={{0,16},{16,0},{1,17},{17,1},{2,18},{18,2},{3,19},{19,3},{4,20},{20... | collective-permute-start | bytes 13832 | tf_op jit(solution)/shard_map/ppermute | solution.py:477
  950.6 45.0 %collective-permute-start.34 = (bf16[72,3456]{1,0:T(8,128)(2,1)S(1)}, bf16[72,3456]{1,0:T(8,128)(2,1)S(1)}, u32[]{:S(2)}, u32[]{:S(2)}) collective-permute-start(bf16[72,3456]{1,0:T(8,128)(2,1)S(1)} %pad_maximum_fusion.12), channel_id=1, source_target_pairs={{0,8},{2,10},{4,12},{6,14},{8,0},{10,2},{12,4},{14,6},{1,9},{3,11}... | collective-permute-start | bytes 1493000 | tf_op jit(solution)/shard_map/ppermute | solution.py:381
  958.0 37.6 %collective-permute-start.35 = (f32[1,648]{1,0:T(1,128)S(1)}, f32[1,648]{1,0:T(1,128)S(1)}, u32[]{:S(2)}, u32[]{:S(2)}) collective-permute-start(f32[1,648]{1,0:T(1,128)S(1)} %fusion.166), channel_id=1, source_target_pairs={{0,8},{2,10},{4,12},{6,14},{8,0},{10,2},{12,4},{14,6},{1,9},{3,11}... | collective-permute-start | bytes 7784 | tf_op jit(solution)/shard_map/ppermute | solution.py:381
  995.6 32.1 %collective-permute-start.37 = (f32[1,648]{1,0:T(1,128)S(1)}, f32[1,648]{1,0:T(1,128)S(1)}, u32[]{:S(2)}, u32[]{:S(2)}) collective-permute-start(f32[1,648]{1,0:T(1,128)S(1)} %fusion.168), channel_id=1, source_target_pairs={{0,16},{16,0},{1,17},{17,1},{2,18},{18,2},{3,19},{19,3},{4,20},{20... | collective-permute-start | bytes 7784 | tf_op jit(solution)/shard_map/ppermute | solution.py:477
  1027.2 20.7 %collective-permute-start.40 = (bf16[72,3456]{1,0:T(8,128)(2,1)S(1)}, bf16[72,3456]{1,0:T(8,128)(2,1)}, u32[]{:S(2)}, u32[]{:S(2)}) collective-permute-start(bf16[72,3456]{1,0:T(8,128)(2,1)S(1)} %add_convert_fusion.7), channel_id=1, source_target_pairs={{0,16},{16,0},{1,17},{17,1},{2,18},{18,2},{3,19},{19,3},{4,20},{20... | collective-permute-start | bytes 1493000 | tf_op jit(solution)/shard_map/ppermute | solution.py:477
  (136 other events, 1837.0 us)
Sparse Core Ops, SparseCore 0:
  11.4 133.7 all-gather.3
  148.6 134.2 all-gather.5
  286.5 113.7 all-gather.7
  522.8 144.3 reduce-scatter.2
  754.8 272.2 reduce-scatter.4

commit v8 on v6

--- a/solution.py
+++ b/solution.py
@@ -757,7 +757,12 @@
     pair_own = jnp.concatenate(
         [contract(part[:, :row_count], pair_full, 0, 1) for part in pair_grads], axis=0
     )
-    pair_own = tick(pair_own, chains_a + [chain_text])
+    pair_own = together(tick(pair_own, [chain_text]), chains_a)
+    for chain in chains_a:
+        chain.kept = low(
+            chain.kept.astype(jnp.float32) + chain.received.astype(jnp.float32)
+        )
+        chain.received = None
     own_grad = pair_own + contract(query_grad, query_full, 0, 1)
     shift_a_grad = jnp.sum(own_grad, axis=0)
     scale_a_grad = jnp.sum(own_grad * normed_a, axis=0)
@@ -780,25 +785,32 @@
             gate_t_grad,
         ]
     ).reshape(shards, 9 * width // shards)
-    own_grad, mod_grad, rest_received = together(
-        (own_grad, mod_grad, rest_received), chains_a + [chain_text]
-    )
-    for chain in chains_a + [chain_text]:
-        chain.advance()
     chain_mod = Chain(is_first, (mod_grad,), 0)
+    chain_mod.advance()
+    own_grad, rest_received = together((own_grad, rest_received), [chain_text, chain_mod])
+    chain_text.advance()
     chain_mod.advance()
     hidden_a_grad = own_grad + jnp.concatenate(
         [sum(part.astype(jnp.float32) for part in parts) for parts in rest_received], axis=0
     )
     input_grad = grad_a + normalize_back(hidden_a_grad * (1.0 + modulation[1]), normed_a, recip_a)
     latent_grad = input_grad.reshape(latent.shape)
-    latent_grad = together(latent_grad, chains_a + [chain_mod])
+    latent_grad, scattered, kept = together(
+        (latent_grad, scattered, [chain.kept for chain in chains_a]), [chain_mod]
+    )
+    for chain, value in zip(chains_a, kept):
+        chain.kept = value
     while len(chains_a[0].order) > 1:
-        for chain in chains_a + [chain_mod]:
+        for chain in chains_a:
             chain.advance()
-        latent_grad = together(latent_grad, chains_a + [chain_mod])
+        if chain_mod.received is not None:
+            chain_mod.advance()
+        latent_grad = together(
+            latent_grad,
+            chains_a + ([chain_mod] if chain_mod.received is not None else []),
+        )
     chain_last = merged(chains_a)
-    chain_mod.advance()
+    mod_slice = chain_mod.finish()
     lower_b, upper_b = whole_halves(is_first, scattered)
     up_shard = (
         jnp.concatenate([lower_b[:, :half_ff], upper_b[:, :half_ff]], axis=1)
@@ -814,8 +826,7 @@
         ],
         axis=0,
     )
-    latent_grad = together(latent_grad, [chain_last, chain_mod])
-    mod_slice = chain_mod.finish()
+    latent_grad = together(latent_grad, [chain_last])
     own_a = chain_last.finish()
     other_a, up_shard, down_shard = lax.optimization_barrier(
         (swapped(own_a), up_shard, down_shard)

time: 1050 us -> 1090 us (1.038)
  waiting for transfers between devices: 280 us -> 335 us
  other arithmetic: 107 us -> 93.1 us
    optimization_barrier x0 -> x1, waiting for transfers between devices: none -> 78.4 us  [together(): lax.optimization_barrier((main, [chain.received for chain in chains]))]
    ppermute x26, waiting for transfers between devices: 130 us -> 95.9 us  [across(): lax.ppermute(value, axis, [(i, i ^ 1 << step) for i in range(lax.axis_siz...]
    convert_element_type x13 -> x11, other arithmetic: 18.3 us -> 2.72 us  [advance(): value = (value.astype(jnp.float32) + self.received.astype(jnp.float32)).a...]
    ppermute x2, waiting for transfers between devices: 1.57 us -> 13.6 us  [per_device(): lax.ppermute(rest_low[s * row_count:(s + 1) * row_count], 'seq', [(j, i)...]
    convert_element_type x7 -> x9, other arithmetic: 18.1 us -> 27.6 us  [low(): return value.astype(jnp.bfloat16)]
  transfers between devices with their start and end apart: 46 -> 46, of which waited for: 22 -> 26; matrix products, arithmetic and copies ran while one was open for 37% -> 34% of each run, Pallas kernels for 11% -> 11%
where the time goes in v8:
time: 1090 us; the launch traced here: 1080 us
  matrix products  384 us (35%)
  waiting for transfers between devices  335 us (31%)
  Pallas kernels  145 us (13%)
  other arithmetic  93.1 us (9%)
  local copies, waits for them, and re-layouts  52.6 us (5%)
  starting transfers between devices  51.9 us (5%)
  between operations  17.1 us (2%)
    dot_general x43, matrix products, contract(): lax.dot_general(left, right, (((left_dim,), (right_dim,)), ((), ())), pre...  317 us
    all_gather x3, waiting for transfers between devices, gather_halves(): lax.all_gather(jnp.where(is_first, lower, upper), ('bucket', 'frame', 'se...  111 us
    ppermute x26, waiting for transfers between devices, across(): lax.ppermute(value, axis, [(i, i ^ 1 << step) for i in range(lax.axis_siz...  95.9 us
    optimization_barrier x1, waiting for transfers between devices, together(): lax.optimization_barrier((main, [chain.received for chain in chains]))  78.4 us
    dot_general x6, matrix products, product(): return jnp.dot(left, right, preferred_element_type=jnp.float32)  59.8 us
    pallas_call x2, Pallas kernels, spatial_backward(): call(body, (HEADS,), [pl.BlockSpec((head_size, rows), lambda h: (h, frame...  53 us
    pallas_call x1, Pallas kernels, spatial_forward(): call(body, (frame_count, HEADS), [pl.BlockSpec((head_size, rows), lambda...  39.6 us
    ppermute x26, starting transfers between devices, across(): lax.ppermute(value, axis, [(i, i ^ 1 << step) for i in range(lax.axis_siz...  34.7 us
  transfers between devices with their start and end apart: 46, of which 26 were waited for; matrix products, arithmetic and copies ran while one was open for 34% of the time, Pallas kernels for 11%

profile of v8, /device:TPU:0, one launch (start us, length us, event | category | flops | bytes accessed | tf_op | source)
XLA Modules:
  0.0 1078.3 jit_solution(5471979338037298277)
XLA Ops:
  50.4 8.8 collective-permute-done.7
  62.1 13.1 %collective-permute-done.8 = bf16[1152,128]{1,0:T(8,128)(2,1)S(1)} collective-permute-done((bf16[1152,128]{1,0:T(8,128)(2,1)S(1)}, bf16[1152,128]{1,0:T(8,128)(2,1)S(1)}, u32[]{:S(2)}, u32[]{:S(2)}) %collective-permute-start.8) | collective-permute-done | bytes 294944 | tf_op jit(solution)/shard_map/ppermute | solution.py:376
  75.4 28.0 %collective-permute-done.4 = bf16[2,512,1152]{2,1,0:T(8,128)(2,1)} collective-permute-done((bf16[2,512,1152]{2,1,0:T(8,128)(2,1)}, bf16[2,512,1152]{2,1,0:T(8,128)(2,1)}, u32[]{:S(2)}, u32[]{:S(2)}) %collective-permute-start.4) | collective-permute-done | bytes 2359328 | tf_op jit(solution)/shard_map/ppermute | solution.py:508
  114.9 30.3 %all-gather.4.cloned.1.call-done = bf16[2304,3456]{1,0:T(8,128)(2,1)} async-done(((bf16[72,3456]{1,0:T(8,128)(2,1)}), bf16[2304,3456]{1,0:T(8,128)(2,1)}) %all-gather.4.cloned.1.call-update) | async-done | bytes 15925264 | tf_op jit(solution)/shard_map/all_gather | solution.py:322
  153.6 18.5 %convolution_convert_fusion.3.k_ref.v_ref = bf16[2304,2048]{1,0:T(8,128)(2,1)} fusion(bf16[2048,1152]{1,0:T(8,128)(2,1)} %bitcast.253, bf16[2304,3456]{1,0:T(8,128)(2,1)} %all-gather.4.cloned.1.call-done), kind=kOutput, calls=%fused_computation.9 | convolution fusion | flops 10876354560 | bytes 19464192 | tf_op jit(solution)/shard_map/dot_general | solution.py:24
  172.2 39.6 %spatial_forward.1 = (bf16[1152,1024]{1,0:T(8,128)(2,1)S(1)}, f32[1152,1024]{1,0:T(8,128)}, f32[32,1,512]{2,1,0:T(1,128)S(1)}) custom-call(bf16[1152,1024]{1,0:T(8,128)(2,1)S(1)} %convolution_convert_fusion.20.q_ref, bf16[2304,2048]{1,0:T(8,128)(2,1)} %convolution_convert_fusion.3.k_ref.v_ref, bf16[2304,2048]{1,0:T(8,128)(2,1)} %convolution_convert_fusion.3.k_ref.v_ref), custom_call_target="tpu_custom_call" | custom-call | tf_op jit(solution)/shard_map/spatial_forward/pallas_call | solution.py:58
  211.8 10.1 fusion.70
  248.3 34.7 %all-gather.6.cloned.1.call-done = bf16[2304,4608]{1,0:T(8,128)(2,1)} async-done(((bf16[72,4608]{1,0:T(8,128)(2,1)}), bf16[2304,4608]{1,0:T(8,128)(2,1)}) %all-gather.6.cloned.1.call-update) | async-done | bytes 21233680 | tf_op jit(solution)/shard_map/all_gather | solution.py:322
  283.0 12.7 %multiply_convert_fusion.1 = (bf16[1024,2304]{1,0:T(8,128)(2,1)S(1)}, f32[1024,2304]{1,0:T(8,128)}) fusion(bf16[1024,1152]{1,0:T(8,128)(2,1)} %add_convert_fusion.4, bf16[2304,4608]{1,0:T(8,128)(2,1)} %all-gather.6.cloned.1.call-done), kind=kOutput, calls=%fused_computation.33 | convolution fusion | flops 5457051648 | bytes 21823488 | tf_op jit(solution)/shard_map/dot_general | solution.py:20
  309.7 12.7 %multiply_convert_fusion = (bf16[1024,2304]{1,0:T(8,128)(2,1)S(1)}, f32[1024,2304]{1,0:T(8,128)}) fusion(bf16[1024,1152]{1,0:T(8,128)(2,1)S(1)} %copy-done.42, bf16[2304,4608]{1,0:T(8,128)(2,1)} %all-gather.6.cloned.1.call-done), kind=kOutput, calls=%fused_computation.32 | convolution fusion | flops 5457051648 | bytes 21823488 | tf_op jit(solution)/shard_map/dot_general | solution.py:20
  322.5 8.5 fusion.102
  331.0 11.8 %fusion.182 = (f32[1024]{0:T(1024)S(1)}, f32[1024,1152]{1,0:T(8,128)S(1)}, f32[1024,1152]{1,0:T(8,128)}) fusion(f32[1024,1152]{1,0:T(8,128)S(1)} %bitcast.228, f32[1152]{0:T(1024)S(1)} %get-tuple-element.198, bf16[2304,4608]{1,0:T(8,128)(2,1)} %all-gather.6.cloned.1.call-done, bf16[1024,2304]{1,0:T(8,128)(2,1)} %copy-done.44, f32[1024,1152]{1,0:T(8,128)} %fusion.102, ...), kind=kOutput, calls=%fused_computation.369 | convolution fusion | flops 2724985856 | bytes 33333760 | tf_op jit(solution)/shard_map/dot_general | solution.py:20
  356.6 45.7 %all-gather.8.cloned.1.call-done = bf16[2304,2304]{1,0:T(8,128)(2,1)} async-done(((bf16[72,2304]{1,0:T(8,128)(2,1)}), bf16[2304,2304]{1,0:T(8,128)(2,1)}) %all-gather.8.cloned.1.call-update) | async-done | bytes 10616848 | tf_op jit(solution)/shard_map/all_gather | solution.py:322
  408.2 17.3 %convolution_convert_fusion.2.k_ref.v_ref = bf16[2304,2048]{1,0:T(8,128)(2,1)} fusion(bf16[2304,2304]{1,0:T(8,128)(2,1)} %all-gather.8.cloned.1.call-done, bf16[512,1152]{1,0:T(8,128)(2,1)} %collective-permute-done.10, bf16[1024,1152]{1,0:T(8,128)(2,1)S(1)} %copy-done.26, bf16[512,1152]{1,0:T(8,128)(2,1)} %collective-permute-done.9), kind=kOutput, calls=%fused_computation.8 | convolution fusion | flops 10890510336 | bytes 19464192 | tf_op jit(solution)/shard_map/dot_general | solution.py:24
  425.5 10.9 %temporal_forward.1 = bf16[1152,1024]{1,0:T(8,128)(2,1)S(1)} custom-call(s32[2,2]{1,0:T(2,128)S(1)} %add_convert_fusion.8.live_ref, bf16[1152,1024]{1,0:T(8,128)(2,1)S(1)} %convolution_convert_fusion.18.q_ref, bf16[2304,2048]{1,0:T(8,128)(2,1)} %convolution_convert_fusion.2.k_ref.v_ref, bf16[2304,2048]{1,0:T(8,128)(2,1)} %convolution_convert_fusion.2.k_ref.v_ref), custom_call_target="tpu_custom_call" | custom-call | tf_op jit(solution)/shard_map/temporal_forward/pallas_call | solution.py:225
  443.2 16.8 %temporal_backward.1 = (bf16[1152,1024]{1,0:T(8,128)(2,1)S(1)}, bf16[2,1152,2048]{2,1,0:T(8,128)(2,1)}) custom-call(s32[2,2]{1,0:T(2,128)S(1)} %add_convert_fusion.8.live_ref, bf16[1152,1024]{1,0:T(8,128)(2,1)S(1)} %convolution_convert_fusion.18.q_ref, bf16[2304,2048]{1,0:T(8,128)(2,1)} %convolution_convert_fusion.2.k_ref.v_ref, ...), custom_call_target="tpu_custom_call" | custom-call | tf_op jit(solution)/shard_map/temporal_backward/pallas_call | solution.py:280
  485.5 15.8 %fusion.2 = bf16[2304,6912]{1,0:T(8,128)(2,1)} fusion(bf16[2304,6912]{1,0:T(8,128)(2,1)} %fusion.24, bf16[2304,2048]{1,0:T(8,128)(2,1)} %bitcast.280, bf16[512,1152]{1,0:T(8,128)(2,1)} %collective-permute-done.10, bf16[1024,1152]{1,0:T(8,128)(2,1)S(1)} %copy-done.26, bf16[512,1152]{1,0:T(8,128)(2,1)} %collective-permute-done.9), kind=kOutput, calls=%fused_computation.12 | convolution fusion | flops 10888445952 | bytes 19464192 | tf_op jit(solution)/shard_map/dot_general | solution.py:24
  501.3 10.0 fusion.45
  516.8 8.7 collective-permute-done.11
  530.0 12.6 %fusion.29 = (f32[1152]{0:T(1024)}, bf16[1024,1152]{1,0:T(8,128)(2,1)}, f32[1152]{0:T(1024)}, f32[1024,1152]{1,0:T(8,128)}) fusion(bf16[1,2,512,1152]{3,2,1,0:T(8,128)(2,1)S(1)} %copy-done.39, f32[1024]{0:T(1024)S(1)} %bitcast.277, f32[1024,1152]{1,0:T(8,128)S(1)} %bitcast.233, f32[1152]{0:T(1024)S(1)} %get-tuple-element.193, ...), kind=kOutput, calls=%fused_computation.60 | convolution fusion | flops 2740320256 | bytes 28645376 | tf_op jit(solution)/shard_map/dot_general | solution.py:24
  617.5 9.7 fusion.47
  627.2 11.2 %fusion.55 = f32[1024,1152]{1,0:T(8,128)} fusion(f32[1024,1152]{1,0:T(8,128)S(1)} %fusion.47, bf16[1024,2304]{1,0:T(8,128)(2,1)} %copy-done.31, bf16[2304,4608]{1,0:T(8,128)(2,1)} %all-gather.6.cloned.1.call-done), kind=kOutput, calls=%fused_computation.117 | convolution fusion | flops 5436997632 | bytes 19464192 | tf_op jit(solution)/shard_map/dot_general | solution.py:24
  659.6 15.8 %cross_backward.1 = (bf16[1152,1024]{1,0:T(8,128)(2,1)S(1)}, f32[2,1152,128]{2,1,0:T(8,128)S(1)}) custom-call(s32[1]{0:T(128)S(6)} %copy.60.length_ref, bf16[1152,1024]{1,0:T(8,128)(2,1)} %copy-done.2, bf16[2304,128]{1,0:T(8,128)(2,1)S(1)} %pad_maximum_fusion.12.k_ref.v_ref, bf16[2304,128]{1,0:T(8,128)(2,1)S(1)} %pad_maximum_fusion.12.k_ref.v_ref, ...), custom_call_target="tpu_custom_call" | custom-call | tf_op jit(solution)/shard_map/cross_backward/pallas_call | solution.py:171
  715.1 26.6 %spatial_backward.2 = (bf16[1152,512]{1,0:T(8,128)(2,1)S(1)}, bf16[2,1152,1024]{2,1,0:T(8,128)(2,1)}) custom-call(bf16[1152,1024]{1,0:T(8,128)(2,1)S(1)} %convolution_convert_fusion.20.q_ref, bf16[2304,2048]{1,0:T(8,128)(2,1)} %convolution_convert_fusion.3.k_ref.v_ref, bf16[2304,2048]{1,0:T(8,128)(2,1)} %convolution_convert_fusion.3.k_ref.v_ref, ...), custom_call_target="tpu_custom_call" | custom-call | tf_op jit(solution)/shard_map/spatial_backward/pallas_call | solution.py:98
  749.8 26.4 %spatial_backward.3 = (bf16[1152,512]{1,0:T(8,128)(2,1)S(1)}, bf16[2,1152,1024]{2,1,0:T(8,128)(2,1)}) custom-call(bf16[1152,1024]{1,0:T(8,128)(2,1)S(1)} %convolution_convert_fusion.20.q_ref, bf16[2304,2048]{1,0:T(8,128)(2,1)} %convolution_convert_fusion.3.k_ref.v_ref, bf16[2304,2048]{1,0:T(8,128)(2,1)} %convolution_convert_fusion.3.k_ref.v_ref, ...), custom_call_target="tpu_custom_call" | custom-call | tf_op jit(solution)/shard_map/spatial_backward/pallas_call | solution.py:98
  776.2 9.2 fusion.84
  794.1 14.9 %convolution_convert_fusion.4 = bf16[1152,2304]{1,0:T(8,128)(2,1)S(1)} fusion(bf16[2048,1152]{1,0:T(8,128)(2,1)S(1)} %bitcast.256, bf16[2304,1024]{1,0:T(8,128)(2,1)} %bitcast.286, bf16[2304,1024]{1,0:T(8,128)(2,1)} %bitcast.283), kind=kOutput, calls=%fused_computation.10 | convolution fusion | flops 10893164544 | bytes 19464192 | tf_op jit(solution)/shard_map/dot_general | solution.py:24
  859.8 10.8 %collective-permute-done.20 = bf16[512,1152]{1,0:T(8,128)(2,1)S(1)} collective-permute-done((bf16[512,1152]{1,0:T(8,128)(2,1)}, bf16[512,1152]{1,0:T(8,128)(2,1)S(1)}, u32[]{:S(2)}, u32[]{:S(2)}) %collective-permute-start.20) | collective-permute-done | bytes 1179680 | tf_op jit(solution)/shard_map/ppermute | solution.py:726
  884.7 78.4 %reduce-scatter.4.cloned.1.call-done = bf16[72,6912]{1,0:T(8,128)(2,1)} async-done(((bf16[2304,6912]{1,0:T(8,128)(2,1)}), bf16[72,6912]{1,0:T(8,128)(2,1)}) %reduce-scatter.4.cloned.1.call-update) | async-done | bytes 995344 | tf_op jit(solution)/shard_map/optimization_barrier | solution.py:453
  972.7 25.4 %collective-permute-done.25 = bf16[2,2,2,72,1152]{4,3,2,1,0:T(8,128)(2,1)S(1)} collective-permute-done((bf16[2,2,2,72,1152]{4,3,2,1,0:T(8,128)(2,1)S(1)}, bf16[2,2,2,72,1152]{4,3,2,1,0:T(8,128)(2,1)S(1)}, u32[]{:S(2)}, u32[]{:S(2)}) %collective-permute-start.25) | collective-permute-done | bytes 1327136 | tf_op jit(solution)/shard_map/ppermute | solution.py:376
  1008.5 9.5 collective-permute-done.31
  1033.1 18.0 %collective-permute-done.35 = bf16[72,3456]{1,0:T(8,128)(2,1)S(1)} collective-permute-done((bf16[72,3456]{1,0:T(8,128)(2,1)S(1)}, bf16[72,3456]{1,0:T(8,128)(2,1)S(1)}, u32[]{:S(2)}, u32[]{:S(2)}) %collective-permute-start.35) | collective-permute-done | bytes 497696 | tf_op jit(solution)/shard_map/ppermute | solution.py:376
  (515 shorter events, 438.7 us)
Async XLA Ops:
  7.2 138.0 %all-gather.4.cloned.1.call-start = ((), (), s32[]{:S(2)}) async-start(), calls=%async_computation.1 | async-start | bytes 16422912 | tf_op jit(solution)/shard_map/all_gather | solution.py:322
  9.5 273.5 %all-gather.6.cloned.1.call-start = ((), (), s32[]{:S(2)}) async-start(), calls=%async_computation.2 | async-start | bytes 21897216 | tf_op jit(solution)/shard_map/all_gather | solution.py:322
  22.2 380.1 %all-gather.8.cloned.1.call-start = ((), (), s32[]{:S(2)}) async-start(), calls=%async_computation.3 | async-start | bytes 10948608 | tf_op jit(solution)/shard_map/all_gather | solution.py:322
  24.4 18.2 %collective-permute-start.5 = (bf16[144,128]{1,0:T(8,128)(2,1)S(1)}, bf16[144,128]{1,0:T(8,128)(2,1)S(1)}, u32[]{:S(2)}, u32[]{:S(2)}) collective-permute-start(bf16[144,128]{1,0:T(8,128)(2,1)S(1)} %convolution_convert_fusion.21), channel_id=1, source_target_pairs={{0,1},{1,0},{2,3},{3,2},{4,5},{5,4},{6,7},{7,6},{8,9},{9,8},{10,11... | collective-permute-start | bytes 110600 | tf_op jit(solution)/shard_map/ppermute | solution.py:376
  28.7 74.7 %collective-permute-start.4 = (bf16[2,512,1152]{2,1,0:T(8,128)(2,1)}, bf16[2,512,1152]{2,1,0:T(8,128)(2,1)}, u32[]{:S(2)}, u32[]{:S(2)}) collective-permute-start(bf16[2,512,1152]{2,1,0:T(8,128)(2,1)} %bitcast.231), channel_id=1, source_target_pairs={{1,0},{0,1},{3,2},{2,3},{5,4},{4,5},{7,6},{6,7},{9,8},{8,9},{11,10... | collective-permute-start | bytes 7077896 | tf_op jit(solution)/shard_map/ppermute | solution.py:508
  59.3 15.9 %collective-permute-start.8 = (bf16[1152,128]{1,0:T(8,128)(2,1)S(1)}, bf16[1152,128]{1,0:T(8,128)(2,1)S(1)}, u32[]{:S(2)}, u32[]{:S(2)}) collective-permute-start(bf16[1152,128]{1,0:T(8,128)(2,1)S(1)} %pad_maximum_fusion.15), channel_id=1, source_target_pairs={{0,8},{2,10},{4,12},{6,14},{8,0},{10,2},{12,4},{14,6},{1,9},{3,11}... | collective-permute-start | bytes 884744 | tf_op jit(solution)/shard_map/ppermute | solution.py:376
  151.8 811.3 %reduce-scatter.4.cloned.1.call-start = ((), (), s32[]{:S(2)}) async-start(), calls=%async_computation.4 | async-start | bytes 32845824
  347.2 60.9 %collective-permute-start.10 = (bf16[512,1152]{1,0:T(8,128)(2,1)}, bf16[512,1152]{1,0:T(8,128)(2,1)}, u32[]{:S(2)}, u32[]{:S(2)}) collective-permute-start(bf16[512,1152]{1,0:T(8,128)(2,1)} %get-tuple-element.225), channel_id=1, source_target_pairs={{2,0},{4,2},{6,4},{8,6},{10,8},{12,10},{14,12},{3,1},{5,3},{7,5},{... | collective-permute-start | bytes 3538952 | tf_op jit(solution)/shard_map/ppermute | solution.py:606
  348.5 59.6 %collective-permute-start.9 = (bf16[512,1152]{1,0:T(8,128)(2,1)}, bf16[512,1152]{1,0:T(8,128)(2,1)}, u32[]{:S(2)}, u32[]{:S(2)}) collective-permute-start(bf16[512,1152]{1,0:T(8,128)(2,1)} %get-tuple-element.224), channel_id=1, source_target_pairs={{0,2},{2,4},{4,6},{6,8},{8,10},{10,12},{12,14},{1,3},{3,5},{5,7},{... | collective-permute-start | bytes 3538952 | tf_op jit(solution)/shard_map/ppermute | solution.py:605
  473.0 52.5 %collective-permute-start.11 = (bf16[512,1152]{1,0:T(8,128)(2,1)S(1)}, bf16[512,1152]{1,0:T(8,128)(2,1)S(1)}, u32[]{:S(2)}, u32[]{:S(2)}) collective-permute-start(bf16[512,1152]{1,0:T(8,128)(2,1)S(1)} %fusion.67), channel_id=1, source_target_pairs={{0,2},{2,4},{4,6},{6,8},{8,10},{10,12},{12,14},{1,3},{3,5},{5,7},{... | collective-permute-start | bytes 3538952 | tf_op jit(solution)/shard_map/ppermute | solution.py:640
  474.6 50.8 %collective-permute-start.12 = (bf16[512,1152]{1,0:T(8,128)(2,1)S(1)}, bf16[512,1152]{1,0:T(8,128)(2,1)S(1)}, u32[]{:S(2)}, u32[]{:S(2)}) collective-permute-start(bf16[512,1152]{1,0:T(8,128)(2,1)S(1)} %fusion.64), channel_id=1, source_target_pairs={{2,0},{4,2},{6,4},{8,6},{10,8},{12,10},{14,12},{3,1},{5,3},{7,5},{... | collective-permute-start | bytes 3538952 | tf_op jit(solution)/shard_map/ppermute | solution.py:639
  638.5 242.9 %collective-permute-start.38 = (bf16[128,4096]{1,0:T(8,128)(2,1)}, bf16[128,4096]{1,0:T(8,128)(2,1)}, u32[]{:S(2)}, u32[]{:S(2)}) collective-permute-start(bf16[128,4096]{1,0:T(8,128)(2,1)} %bitcast.257), channel_id=1, source_target_pairs={{0,16},{16,0},{1,17},{17,1},{2,18},{18,2},{3,19},{19,3},{4,20},{20... | collective-permute-start | bytes 3145736 | tf_op jit(solution)/shard_map/ppermute | solution.py:472
  675.6 36.3 %collective-permute-start.13 = (bf16[2,2,2,144,128]{4,3,2,1,0:T(8,128)(2,1)S(1)}, bf16[2,2,2,144,128]{4,3,2,1,0:T(8,128)(2,1)S(1)}, u32[]{:S(2)}, u32[]{:S(2)}) collective-permute-start(bf16[2,2,2,144,128]{4,3,2,1,0:T(8,128)(2,1)S(1)} %dynamic-slice_bitcast_fusion.9), channel_id=1, source_target_pairs={{0,2},{2,0},{4,6},{6,4},{8,10},{10,8},{12,14},{14,12},{1,3},{3,1},... | collective-permute-start | bytes 884744 | tf_op jit(solution)/shard_map/ppermute | solution.py:376
  712.0 37.9 %collective-permute-start.14 = (bf16[2,2,144,128]{3,2,1,0:T(8,128)(2,1)S(1)}, bf16[2,2,144,128]{3,2,1,0:T(8,128)(2,1)S(1)}, u32[]{:S(2)}, u32[]{:S(2)}) collective-permute-start(bf16[2,2,144,128]{3,2,1,0:T(8,128)(2,1)S(1)} %dynamic-slice_bitcast_fusion.16), channel_id=1, source_target_pairs={{0,4},{2,6},{4,0},{6,2},{8,12},{10,14},{12,8},{14,10},{1,5},{3,7},... | collective-permute-start | bytes 442376 | tf_op jit(solution)/shard_map/ppermute | solution.py:376
  748.2 40.7 %collective-permute-start.15 = (bf16[512,1152]{1,0:T(8,128)(2,1)S(1)}, bf16[512,1152]{1,0:T(8,128)(2,1)S(1)}, u32[]{:S(2)}, u32[]{:S(2)}) collective-permute-start(bf16[512,1152]{1,0:T(8,128)(2,1)S(1)} %get-tuple-element.125), channel_id=1, source_target_pairs={{0,1},{1,0},{2,3},{3,2},{4,5},{5,4},{6,7},{7,6},{8,9},{9,8},{10,11... | collective-permute-start | bytes 3538952 | tf_op jit(solution)/shard_map/ppermute | solution.py:726
  785.4 43.4 %collective-permute-start.16 = (bf16[2,144,128]{2,1,0:T(8,128)(2,1)S(1)}, bf16[2,144,128]{2,1,0:T(8,128)(2,1)S(1)}, u32[]{:S(2)}, u32[]{:S(2)}) collective-permute-start(bf16[2,144,128]{2,1,0:T(8,128)(2,1)S(1)} %dynamic-slice_bitcast_fusion.17), channel_id=1, source_target_pairs={{0,1},{1,0},{2,3},{3,2},{4,5},{5,4},{6,7},{7,6},{8,9},{9,8},{10,11... | collective-permute-start | bytes 221192 | tf_op jit(solution)/shard_map/ppermute | solution.py:376
  810.8 24.9 %collective-permute-start.18 = (bf16[1152,1152]{1,0:T(8,128)(2,1)}, bf16[1152,1152]{1,0:T(8,128)(2,1)}, u32[]{:S(2)}, u32[]{:S(2)}) collective-permute-start(bf16[1152,1152]{1,0:T(8,128)(2,1)} %broadcast_select_fusion.1), channel_id=1, source_target_pairs={{0,16},{16,0},{1,17},{17,1},{2,18},{18,2},{3,19},{19,3},{4,20},{20... | collective-permute-start | bytes 7962632 | tf_op jit(solution)/shard_map/ppermute | solution.py:472
  815.0 22.2 %collective-permute-start.17 = (bf16[1152,1152]{1,0:T(8,128)(2,1)}, bf16[1152,1152]{1,0:T(8,128)(2,1)S(1)}, u32[]{:S(2)}, u32[]{:S(2)}) collective-permute-start(bf16[1152,1152]{1,0:T(8,128)(2,1)} %get-tuple-element.216), channel_id=1, source_target_pairs={{0,16},{16,0},{1,17},{17,1},{2,18},{18,2},{3,19},{19,3},{4,20},{20... | collective-permute-start | bytes 7962632 | tf_op jit(solution)/shard_map/ppermute | solution.py:472
  815.0 22.2 %collective-permute-start.19 = (bf16[1152,1152]{1,0:T(8,128)(2,1)S(1)}, bf16[1152,1152]{1,0:T(8,128)(2,1)S(1)}, u32[]{:S(2)}, u32[]{:S(2)}) collective-permute-start(bf16[1152,1152]{1,0:T(8,128)(2,1)S(1)} %get-tuple-element.215), channel_id=1, source_target_pairs={{0,16},{16,0},{1,17},{17,1},{2,18},{18,2},{3,19},{19,3},{4,20},{20... | collective-permute-start | bytes 7962632 | tf_op jit(solution)/shard_map/ppermute | solution.py:472
  828.8 235.1 %collective-permute-start.36 = (f32[1,1152]{1,0:T(1,128)S(1)}, f32[1,1152]{1,0:T(1,128)}, u32[]{:S(2)}, u32[]{:S(2)}) collective-permute-start(f32[1,1152]{1,0:T(1,128)S(1)} %divide_multiply_fusion), channel_id=1, source_target_pairs={{0,16},{16,0},{1,17},{17,1},{2,18},{18,2},{3,19},{19,3},{4,20},{20... | collective-permute-start | bytes 13832 | tf_op jit(solution)/shard_map/ppermute | solution.py:472
  835.8 34.9 %collective-permute-start.20 = (bf16[512,1152]{1,0:T(8,128)(2,1)}, bf16[512,1152]{1,0:T(8,128)(2,1)S(1)}, u32[]{:S(2)}, u32[]{:S(2)}) collective-permute-start(bf16[512,1152]{1,0:T(8,128)(2,1)} %get-tuple-element.142), channel_id=1, source_target_pairs={{0,1},{1,0},{2,3},{3,2},{4,5},{5,4},{6,7},{7,6},{8,9},{9,8},{10,11... | collective-permute-start | bytes 3538952 | tf_op jit(solution)/shard_map/ppermute | solution.py:726
  837.2 22.7 %collective-permute-start.21 = (bf16[144,128]{1,0:T(8,128)(2,1)}, bf16[144,128]{1,0:T(8,128)(2,1)}, u32[]{:S(2)}, u32[]{:S(2)}) collective-permute-start(bf16[144,128]{1,0:T(8,128)(2,1)} %dynamic-slice_bitcast_fusion.18), channel_id=1, source_target_pairs={{0,8},{2,10},{4,12},{6,14},{8,0},{10,2},{12,4},{14,6},{1,9},{3,11}... | collective-permute-start | bytes 110600 | tf_op jit(solution)/shard_map/ppermute | solution.py:376
  847.5 23.9 %collective-permute-start.22 = (f32[2,2,2,1,648]{4,3,2,1,0:T(1,128)S(1)}, f32[2,2,2,1,648]{4,3,2,1,0:T(1,128)S(1)}, u32[]{:S(2)}, u32[]{:S(2)}) collective-permute-start(f32[2,2,2,1,648]{4,3,2,1,0:T(1,128)S(1)} %dynamic-slice_bitcast_fusion.19), channel_id=1, source_target_pairs={{0,1},{1,0},{2,3},{3,2},{4,5},{5,4},{6,7},{7,6},{8,9},{9,8},{10,11... | collective-permute-start | bytes 62216 | tf_op jit(solution)/shard_map/ppermute | solution.py:376
  966.9 31.2 %collective-permute-start.25 = (bf16[2,2,2,72,1152]{4,3,2,1,0:T(8,128)(2,1)S(1)}, bf16[2,2,2,72,1152]{4,3,2,1,0:T(8,128)(2,1)S(1)}, u32[]{:S(2)}, u32[]{:S(2)}) collective-permute-start(bf16[2,2,2,72,1152]{4,3,2,1,0:T(8,128)(2,1)S(1)} %dynamic-slice_bitcast_fusion.1), channel_id=1, source_target_pairs={{0,2},{2,0},{4,6},{6,4},{8,10},{10,8},{12,14},{14,12},{1,3},{3,1},... | collective-permute-start | bytes 3981320 | tf_op jit(solution)/shard_map/ppermute | solution.py:376
  969.9 31.0 %collective-permute-start.26 = (bf16[2,2,2,72,1152]{4,3,2,1,0:T(8,128)(2,1)S(1)}, bf16[2,2,2,72,1152]{4,3,2,1,0:T(8,128)(2,1)S(1)}, u32[]{:S(2)}, u32[]{:S(2)}) collective-permute-start(bf16[2,2,2,72,1152]{4,3,2,1,0:T(8,128)(2,1)S(1)} %dynamic-slice_bitcast_fusion), channel_id=1, source_target_pairs={{0,4},{2,6},{4,0},{6,2},{8,12},{10,14},{12,8},{14,10},{1,5},{3,7},... | collective-permute-start | bytes 3981320 | tf_op jit(solution)/shard_map/ppermute | solution.py:376
  970.6 30.7 %collective-permute-start.24 = (bf16[2,2,2,72,1152]{4,3,2,1,0:T(8,128)(2,1)S(1)}, bf16[2,2,2,72,1152]{4,3,2,1,0:T(8,128)(2,1)S(1)}, u32[]{:S(2)}, u32[]{:S(2)}) collective-permute-start(bf16[2,2,2,72,1152]{4,3,2,1,0:T(8,128)(2,1)S(1)} %dynamic-slice_bitcast_fusion.2), channel_id=1, source_target_pairs={{0,1},{1,0},{2,3},{3,2},{4,5},{5,4},{6,7},{7,6},{8,9},{9,8},{10,11... | collective-permute-start | bytes 3981320 | tf_op jit(solution)/shard_map/ppermute | solution.py:376
  1001.7 16.3 %collective-permute-start.30 = (bf16[2,2,72,1152]{3,2,1,0:T(8,128)(2,1)S(1)}, bf16[2,2,72,1152]{3,2,1,0:T(8,128)(2,1)S(1)}, u32[]{:S(2)}, u32[]{:S(2)}) collective-permute-start(bf16[2,2,72,1152]{3,2,1,0:T(8,128)(2,1)S(1)} %dynamic-slice_bitcast_fusion.3), channel_id=1, source_target_pairs={{0,1},{1,0},{2,3},{3,2},{4,5},{5,4},{6,7},{7,6},{8,9},{9,8},{10,11... | collective-permute-start | bytes 1990664 | tf_op jit(solution)/shard_map/ppermute | solution.py:376
  1003.7 15.4 %collective-permute-start.29 = (bf16[2,2,72,1152]{3,2,1,0:T(8,128)(2,1)S(1)}, bf16[2,2,72,1152]{3,2,1,0:T(8,128)(2,1)S(1)}, u32[]{:S(2)}, u32[]{:S(2)}) collective-permute-start(bf16[2,2,72,1152]{3,2,1,0:T(8,128)(2,1)S(1)} %dynamic-slice_bitcast_fusion.4), channel_id=1, source_target_pairs={{0,4},{2,6},{4,0},{6,2},{8,12},{10,14},{12,8},{14,10},{1,5},{3,7},... | collective-permute-start | bytes 1990664 | tf_op jit(solution)/shard_map/ppermute | solution.py:376
  1005.6 15.0 %collective-permute-start.28 = (bf16[2,2,72,1152]{3,2,1,0:T(8,128)(2,1)S(1)}, bf16[2,2,72,1152]{3,2,1,0:T(8,128)(2,1)S(1)}, u32[]{:S(2)}, u32[]{:S(2)}) collective-permute-start(bf16[2,2,72,1152]{3,2,1,0:T(8,128)(2,1)S(1)} %dynamic-slice_bitcast_fusion.5), channel_id=1, source_target_pairs={{0,2},{2,0},{4,6},{6,4},{8,10},{10,8},{12,14},{14,12},{1,3},{3,1},... | collective-permute-start | bytes 1990664 | tf_op jit(solution)/shard_map/ppermute | solution.py:376
  1030.3 20.8 %collective-permute-start.35 = (bf16[72,3456]{1,0:T(8,128)(2,1)S(1)}, bf16[72,3456]{1,0:T(8,128)(2,1)S(1)}, u32[]{:S(2)}, u32[]{:S(2)}) collective-permute-start(bf16[72,3456]{1,0:T(8,128)(2,1)S(1)} %pad_maximum_fusion.13), channel_id=1, source_target_pairs={{0,8},{2,10},{4,12},{6,14},{8,0},{10,2},{12,4},{14,6},{1,9},{3,11}... | collective-permute-start | bytes 1493000 | tf_op jit(solution)/shard_map/ppermute | solution.py:376
  1051.2 18.0 %collective-permute-start.40 = (bf16[72,3456]{1,0:T(8,128)(2,1)S(1)}, bf16[72,3456]{1,0:T(8,128)(2,1)S(1)}, u32[]{:S(2)}, u32[]{:S(2)}) collective-permute-start(bf16[72,3456]{1,0:T(8,128)(2,1)S(1)} %add_convert_fusion.7), channel_id=1, source_target_pairs={{0,16},{16,0},{1,17},{17,1},{2,18},{18,2},{3,19},{19,3},{4,20},{20... | collective-permute-start | bytes 1493000 | tf_op jit(solution)/shard_map/ppermute | solution.py:472
  1051.3 12.6 %collective-permute-start.37 = (f32[1,648]{1,0:T(1,128)S(1)}, f32[1,648]{1,0:T(1,128)S(1)}, u32[]{:S(2)}, u32[]{:S(2)}) collective-permute-start(f32[1,648]{1,0:T(1,128)S(1)} %fusion.166), channel_id=1, source_target_pairs={{0,16},{16,0},{1,17},{17,1},{2,18},{18,2},{3,19},{19,3},{4,20},{20... | collective-permute-start | bytes 7784 | tf_op jit(solution)/shard_map/ppermute | solution.py:472
  (125 other events, 1817.8 us)
Sparse Core Ops, SparseCore 0:
  11.4 133.7 all-gather.3
  148.6 134.2 all-gather.5
  286.5 115.7 all-gather.7
  638.5 324.5 reduce-scatter.3
